TPU v7x, 256 devices: a whole 4x4x8 slice. The times are simulated.
256 devices in a mesh: shot: 4 (over y), gx: 8 (over z_hi, x), gy: 8 (over z_lo, core).
Axes of the slice: x: 4, y: 4, z: 8 (z_hi: 2, z_lo: 4; z = z_hi * 4 + z_lo), core: 2. Of those that a mesh axis runs over, the one named last changes fastest.
Arguments:
- stiffness: float32 [256, 256, 512], P('gx', 'gy'), may hold values from 0.05 to 0.3
- buoyancy: float32 [256, 256, 512], P('gx', 'gy'), may hold values from 0.5 to 1
- older_field: float32 [4, 256, 256, 512], P('shot', 'gx', 'gy'), may hold values from -6 to 6
- current_field: float32 [4, 256, 256, 512], P('shot', 'gx', 'gy'), may hold values from -6 to 6
- stored_tiles: float32 [32, 8, 32, 32, 256], P(('shot', 'gx'), 'gy'), may hold values from -6 to 6
- tile_ids: int32 [32, 8, 32, 32], P(('shot', 'gx'), 'gy'), may hold values from 0 to 511, as said below
- tile_counts: int32 [32, 8, 32], P(('shot', 'gx'), 'gy'), may hold values from 0 to 32, as said below
- receiver_cells: int32 [4, 3, 1024], P('shot'), may hold values from 0 to 255, as said below
- receiver_data: float32 [4, 2, 1024], P('shot'), may hold values from -6 to 6
- source_cell: int32 [4, 3], P('shot'), may hold values from 0 to 255, as said below
Outputs:
- image: float32 [4, 256, 256, 512], P('shot', 'gx', 'gy')
- last_older: float32 [4, 256, 256, 512], P('shot', 'gx', 'gy')
- last_current: float32 [4, 256, 256, 512], P('shot', 'gx', 'gy')
Inputs may be any that keep to these rules, and one draw needn't show every extreme that they name: `tile_counts`: for each owner and second-dimension block, the counts over holders sum to 512; holders of the owner's own shot have none; at least one holder has 32. `tile_ids`: for each owner and second-dimension block, the filled slots over all holders name every tile number once; unfilled slots carry arbitrary tile numbers. `receiver_cells`: depth index 1 to 7; first index below 256, second below 256. `source_cell`: depth index 1 to 3; first index below 256, second below 256.
All inputs are finite; a program needn't handle non-finite values.
Results may differ from a plain program's by a relative error of at most 0.0003.
Values sent between devices are 32-bit elements; how exact they have to be, the bound alone decides.
No kernel may reach another device: no remote copies, remote signals or barrier semaphores. Data moves between devices by JAX's collectives and lax.ppermute only.
A program may use at most 128 MiB of HBM per device.

v0:
```python
import jax
import jax.numpy as jnp
from jax import lax
from jax.sharding import PartitionSpec as P

STEPS = 2


MUTE_RADIUS = 3.0


def with_halo(block, sides, width):
    for axis, dim in sides:
        count = lax.axis_size(axis)
        forward = [(i, i + 1) for i in range(count - 1)]
        backward = [(target, source) for source, target in forward]
        low = lax.ppermute(
            lax.slice_in_dim(block, block.shape[dim] - width, None, axis=dim), axis, forward
        )
        high = lax.ppermute(lax.slice_in_dim(block, 0, width, axis=dim), axis, backward)
        block = jnp.concatenate([low, block, high], axis=dim)
    return block


def from_behind(block, axis, distance):
    devices = range(lax.axis_size(axis))
    route = [(i - distance, i) for i in devices if i - distance in devices]
    return lax.ppermute(block, axis, route)


def operate(padded_f, padded_b):
    centre = padded_f[1:-1, 1:-1, 1:-1]
    coef = padded_b[1:-1, 1:-1, 1:-1]
    upper_x = 0.5 * (coef + padded_b[2:, 1:-1, 1:-1])
    lower_x = 0.5 * (coef + padded_b[:-2, 1:-1, 1:-1])
    result = upper_x * (padded_f[2:, 1:-1, 1:-1] - centre) - lower_x * (
        centre - padded_f[:-2, 1:-1, 1:-1]
    )
    upper_y = 0.5 * (coef + padded_b[1:-1, 2:, 1:-1])
    lower_y = 0.5 * (coef + padded_b[1:-1, :-2, 1:-1])
    result = result + (
        upper_y * (padded_f[1:-1, 2:, 1:-1] - centre)
        - lower_y * (centre - padded_f[1:-1, :-2, 1:-1])
    )
    upper_z = 0.5 * (coef + padded_b[1:-1, 1:-1, 2:])
    lower_z = 0.5 * (coef + padded_b[1:-1, 1:-1, :-2])
    result = result + (
        upper_z * (padded_f[1:-1, 1:-1, 2:] - centre)
        - lower_z * (centre - padded_f[1:-1, 1:-1, :-2])
    )
    return result


def refine(extended, along):
    count = extended.shape[along] - 1
    lower = lax.slice_in_dim(extended, 0, count, axis=along)
    upper = lax.slice_in_dim(extended, 1, count + 1, axis=along)
    middle = 0.5 * (lower + upper)
    paired = jnp.stack([lower, middle], axis=along + 1)
    new_shape = list(lower.shape)
    new_shape[along] = 2 * count
    return paired.reshape(new_shape)


def upsample(extended):
    coarse_z = extended.shape[-1]
    fine_index = jnp.arange(2 * coarse_z, dtype=jnp.int32)
    coarse_index = jnp.arange(coarse_z, dtype=jnp.int32)
    lower_index = fine_index // 2
    is_odd = fine_index % 2 == 1
    same_cell = coarse_index[:, None] == lower_index[None, :]
    next_cell = (coarse_index[:, None] == lower_index[None, :] + 1) & is_odd[None, :]
    weights_z = jnp.where(same_cell, jnp.where(is_odd[None, :], 0.5, 1.0), 0.0) + jnp.where(
        next_cell, 0.5, 0.0
    )
    weights_z = weights_z.astype(jnp.float32)
    along_z = jnp.einsum("abcz,zf->abcf", extended, weights_z, precision=lax.Precision.HIGHEST)
    return refine(refine(along_z, 1), 2)


def assemble(received, plan_ids, plan_counts, half_x, half_y):
    coarse_z = received.shape[-1]
    capacity = received.shape[1]
    tile_total = STEPS * half_x * half_y
    slot_index = jnp.arange(capacity, dtype=jnp.int32)
    filled = slot_index[None, :] < plan_counts[:, None]
    targets = jnp.where(filled, plan_ids, tile_total).reshape(-1)
    tile_rows = jnp.zeros((tile_total, coarse_z), received.dtype)
    tile_rows = tile_rows.at[targets].set(received.reshape(-1, coarse_z), mode="drop")
    return tile_rows.reshape(STEPS, half_x, half_y, coarse_z)


def pad_depth(padded):
    return jnp.pad(padded, ((0, 0), (0, 0), (1, 1)))


def per_device(
    stiffness,
    buoyancy,
    older_field,
    current_field,
    stored_tiles,
    tile_ids,
    tile_counts,
    receiver_cells,
    receiver_data,
    source_cell,
):
    older = older_field[0]
    current = current_field[0]
    block_x, block_y, depth = current.shape
    padded_b = pad_depth(with_halo(buoyancy, (("gx", 0), ("gy", 1)), 1))
    store = stored_tiles[0, 0]
    received = lax.all_to_all(store, ("shot", "gx"), split_axis=0, concat_axis=0, tiled=True)
    coarse = assemble(received, tile_ids[0, 0], tile_counts[0, 0], block_x // 2, block_y // 2)
    rim_x = from_behind(coarse[:, :1], "gx", -1)
    extended = jnp.concatenate([coarse, rim_x], axis=1)
    rim_y = from_behind(extended[:, :, :1], "gy", -1)
    extended = jnp.concatenate([extended, rim_y], axis=2)
    snapshot = upsample(extended)
    gx_index = lax.axis_index("gx")
    gy_index = lax.axis_index("gy")
    global_x = (gx_index * block_x + jnp.arange(block_x, dtype=jnp.int32)).astype(jnp.float32)
    global_y = (gy_index * block_y + jnp.arange(block_y, dtype=jnp.int32)).astype(jnp.float32)
    global_z = jnp.arange(depth, dtype=jnp.int32).astype(jnp.float32)
    source_f = source_cell[0].astype(jnp.float32)
    diff_x = global_x - source_f[0]
    diff_y = global_y - source_f[1]
    diff_z = global_z - source_f[2]
    distance = (
        (diff_x * diff_x)[:, None, None]
        + (diff_y * diff_y)[None, :, None]
        + (diff_z * diff_z)[None, None, :]
    )
    taper = 1.0 - jnp.exp(-distance / (2.0 * MUTE_RADIUS * MUTE_RADIUS))
    cells = receiver_cells[0]
    local_x = cells[0] - gx_index * block_x
    local_y = cells[1] - gy_index * block_y
    inside = (local_x >= 0) & (local_x < block_x) & (local_y >= 0) & (local_y < block_y)
    flat_cells = jnp.where(
        inside, (local_x * block_y + local_y) * depth + cells[2], block_x * block_y * depth
    )
    image_sum = jnp.zeros((block_x, block_y, depth), jnp.float32)
    for section_index in range(STEPS):
        padded_f = pad_depth(with_halo(current, (("gx", 0), ("gy", 1)), 1))
        newer = 2.0 * current - older + stiffness * operate(padded_f, padded_b)
        newer = (
            newer.reshape(-1)
            .at[flat_cells]
            .add(receiver_data[0, section_index], mode="drop")
            .reshape(block_x, block_y, depth)
        )
        image_sum = image_sum + snapshot[section_index] * newer
        older, current = (current, newer)
    return ((taper * image_sum)[None], older[None], current[None])


def solution(mesh):
    in_specs = (
        P("gx", "gy", None),
        P("gx", "gy", None),
        P("shot", "gx", "gy", None),
        P("shot", "gx", "gy", None),
        P(("shot", "gx"), "gy", None, None, None),
        P(("shot", "gx"), "gy", None, None),
        P(("shot", "gx"), "gy", None),
        P("shot", None, None),
        P("shot", None, None),
        P("shot", None),
    )
    out_specs = (
        P("shot", "gx", "gy", None),
        P("shot", "gx", "gy", None),
        P("shot", "gx", "gy", None),
    )
    return jax.shard_map(
        per_device, mesh=mesh, in_specs=in_specs, out_specs=out_specs, check_vma=False
    )
```

profile of v0, /device:TPU:39, one launch (start us, length us, event | category | flops | bytes accessed | tf_op | source)
XLA Modules:
  0.0 177.5 jit_solution(4608731838970485828)
XLA Ops:
  1.7 7.8 %collective-permute-start.4 = (f32[1,32,512]{2,1,0:T(8,128)S(1)}, f32[1,32,512]{2,1,0:T(8,128)S(1)}, u32[]{:S(2)}, u32[]{:S(2)}) collective-permute-start(f32[1,32,512]{2,1,0:T(8,128)S(1)} %get-tuple-element.21), channel_id=1, source_target_pairs={{0,8},{8,16},{16,24},{24,32},{32,40},{40,48},{48,56},{1,9},{9,17},... | collective-permute-start | bytes 196616 | tf_op jit(solution)/shard_map/ppermute | solution.py:17
  14.9 9.4 %collective-permute-start.5 = (f32[1,32,512]{2,1,0:T(8,128)}, f32[1,32,512]{2,1,0:T(8,128)S(1)}, u32[]{:S(2)}, u32[]{:S(2)}) collective-permute-start(f32[1,32,512]{2,1,0:T(8,128)} %get-tuple-element.23), channel_id=1, source_target_pairs={{0,8},{8,16},{16,24},{24,32},{32,40},{40,48},{48,56},{1,9},{9,17},... | collective-permute-start | bytes 196616 | tf_op jit(solution)/shard_map/ppermute | solution.py:17
  24.3 6.8 %all-to-all-start = ((f32[32,32,256]{2,1,0:T(8,128)}), f32[32,32,256]{2,1,0:T(8,128)S(1)}, u32[]{:S(2)}, u32[]{:S(2)}) async-start(f32[32,32,256]{2,1,0:T(8,128)} %bitcast.58), calls=%async_computation | async-start | bytes 2097152 | tf_op jit(solution)/shard_map/all_to_all | solution.py:114
  38.8 4.2 %collective-permute-start.6 = (f32[34,1,512]{2,1,0:T(1,128)S(1)}, f32[34,1,512]{2,1,0:T(1,128)S(1)}, u32[]{:S(2)}, u32[]{:S(2)}) collective-permute-start(f32[34,1,512]{2,1,0:T(1,128)S(1)} %get-tuple-element.14), channel_id=1, source_target_pairs={{1,0},{2,1},{3,2},{4,3},{5,4},{6,5},{7,6},{9,8},{10,9},{11,10},{12... | collective-permute-start | bytes 208904 | tf_op jit(solution)/shard_map/ppermute | solution.py:20
  43.0 2.5 %collective-permute-start.8 = (f32[34,1,512]{2,1,0:T(1,128)S(1)}, f32[34,1,512]{2,1,0:T(1,128)S(1)}, u32[]{:S(2)}, u32[]{:S(2)}) collective-permute-start(f32[34,1,512]{2,1,0:T(1,128)S(1)} %get-tuple-element.13), channel_id=1, source_target_pairs={{0,1},{1,2},{2,3},{3,4},{4,5},{5,6},{6,7},{8,9},{9,10},{10,11},{11... | collective-permute-start | bytes 208904 | tf_op jit(solution)/shard_map/ppermute | solution.py:17
  47.7 3.6 %collective-permute-start.9 = (f32[34,1,512]{2,1,0:T(1,128)S(1)}, f32[34,1,512]{2,1,0:T(1,128)S(1)}, u32[]{:S(2)}, u32[]{:S(2)}) collective-permute-start(f32[34,1,512]{2,1,0:T(1,128)S(1)} %get-tuple-element.15), channel_id=1, source_target_pairs={{0,1},{1,2},{2,3},{3,4},{4,5},{5,6},{6,7},{8,9},{9,10},{10,11},{11... | collective-permute-start | bytes 208904 | tf_op jit(solution)/shard_map/ppermute | solution.py:17
  53.0 5.8 %collective-permute-done.9 = f32[34,1,512]{2,1,0:T(1,128)S(1)} collective-permute-done((f32[34,1,512]{2,1,0:T(1,128)S(1)}, f32[34,1,512]{2,1,0:T(1,128)S(1)}, u32[]{:S(2)}, u32[]{:S(2)}) %collective-permute-start.9) | collective-permute-done | bytes 69664 | tf_op jit(solution)/shard_map/ppermute | solution.py:17
  58.8 4.5 %select_maximum_fusion.2 = f32[34,34,514]{2,1,0:T(8,128)} fusion(f32[34,1,512]{2,1,0:T(1,128)S(1)} %collective-permute-done.7, f32[34,1,512]{2,1,0:T(1,128)S(1)} %collective-permute-done.9, f32[1,32,512]{2,1,0:T(8,128)S(1)} %collective-permute-done.3, f32[32,32,512]{2,1,0:T(8,128)S(1)} %bitcast.47, f32[1,32,512]{2,1,0:T(8,128)S(1)} %collective-permute-done.5), kind=kLoop, calls=%fused_computation.9 | loop fusion | flops 7130208 | bytes 4744224 | tf_op jit(solution)/shard_map/concatenate | solution.py:21
  63.3 9.6 %fusion.23 = f32[32,32,512]{2,1,0:T(8,128)} fusion(f32[32,32,512]{2,1,0:T(8,128)S(1)} %copy-done.7, f32[32,32,512]{2,1,0:T(8,128)S(1)} %bitcast.48, f32[34,34,514]{2,1,0:T(8,128)} %select_maximum_fusion.2, f32[34,1,512]{2,1,0:T(1,128)S(1)} %collective-permute-done.9, f32[1,32,512]{2,1,0:T(8,128)S(1)} %collective-permute-done.3, ...), kind=kLoop, calls=%fused_computation.47 | loop fusion | flops 23592960 | bytes 21643264 | tf_op jit(solution)/shard_map/add | solution.py:146
  75.1 6.8 %scatter_fusion = f32[524288]{0:T(1024)S(1)} fusion(f32[524288]{0:T(1024)S(1)} %bitcast.45, s32[1024]{0:T(1024)S(1)} %bitcast.60, f32[1024]{0:T(1024)S(1)} %bitcast.63), kind=kCustom, calls=%fused_computation.1 | custom fusion | flops 1024 | bytes 16384 | tf_op jit(solution)/shard_map/scatter-add | solution.py:150
  82.6 5.8 %collective-permute-start.11 = (f32[1,32,512]{2,1,0:T(8,128)}, f32[1,32,512]{2,1,0:T(8,128)S(1)}, u32[]{:S(2)}, u32[]{:S(2)}) collective-permute-start(f32[1,32,512]{2,1,0:T(8,128)} %slice.261), channel_id=1, source_target_pairs={{0,8},{8,16},{16,24},{24,32},{32,40},{40,48},{48,56},{1,9},{9,17},... | collective-permute-start | bytes 196616 | tf_op jit(solution)/shard_map/ppermute | solution.py:17
  95.5 8.2 %collective-permute-done.10 = f32[1,32,512]{2,1,0:T(8,128)S(1)} collective-permute-done((f32[1,32,512]{2,1,0:T(8,128)}, f32[1,32,512]{2,1,0:T(8,128)S(1)}, u32[]{:S(2)}, u32[]{:S(2)}) %collective-permute-start.10) | collective-permute-done | bytes 65568 | tf_op jit(solution)/shard_map/ppermute | solution.py:20
  105.8 2.6 %collective-permute-start.12 = (f32[34,1,512]{2,1,0:T(1,128)}, f32[34,1,512]{2,1,0:T(1,128)S(1)}, u32[]{:S(2)}, u32[]{:S(2)}) collective-permute-start(f32[34,1,512]{2,1,0:T(1,128)} %get-tuple-element.12), channel_id=1, source_target_pairs={{1,0},{2,1},{3,2},{4,3},{5,4},{6,5},{7,6},{9,8},{10,9},{11,10},{12... | collective-permute-start | bytes 208904 | tf_op jit(solution)/shard_map/ppermute | solution.py:20
  108.5 3.6 %collective-permute-start.13 = (f32[34,1,512]{2,1,0:T(1,128)}, f32[34,1,512]{2,1,0:T(1,128)}, u32[]{:S(2)}, u32[]{:S(2)}) collective-permute-start(f32[34,1,512]{2,1,0:T(1,128)} %get-tuple-element.11), channel_id=1, source_target_pairs={{0,1},{1,2},{2,3},{3,4},{4,5},{5,6},{6,7},{8,9},{9,10},{10,11},{11... | collective-permute-start | bytes 208904 | tf_op jit(solution)/shard_map/ppermute | solution.py:17
  114.5 5.4 %scatter_custom_fusion = f32[512,256]{1,0:T(8,128)S(1)} fusion(s32[1024]{0:T(1024)} %bitcast.64, f32[1024,256]{1,0:T(8,128)} %bitcast.59, f32[]{:T(128)} %constant.59.clone.1), kind=kCustom, calls=%fused_computation.116 | custom fusion | bytes 524800 | tf_op jit(solution)/shard_map/scatter | solution.py:89
  120.0 2.3 %collective-permute-start = (f32[2,1,16,256]{3,2,1,0:T(8,128)S(1)}, f32[2,1,16,256]{3,2,1,0:T(8,128)S(1)}, u32[]{:S(2)}, u32[]{:S(2)}) collective-permute-start(f32[2,1,16,256]{3,2,1,0:T(8,128)S(1)} %slice.270), channel_id=1, source_target_pairs={{8,0},{16,8},{24,16},{32,24},{40,32},{48,40},{56,48},{9,1},{17,9},... | collective-permute-start | bytes 98312 | tf_op jit(solution)/shard_map/ppermute | solution.py:28
  122.3 3.2 %select_maximum_fusion = f32[34,34,514]{2,1,0:T(8,128)S(1)} fusion(f32[34,1,512]{2,1,0:T(1,128)S(1)} %collective-permute-done.12, f32[34,32,512]{2,1,0:T(8,128)} %copy-done.6, f32[34,1,512]{2,1,0:T(1,128)} %collective-permute-done.13), kind=kLoop, calls=%fused_computation.7 | loop fusion | flops 4753472 | bytes 4744224 | tf_op jit(solution)/shard_map/concatenate | solution.py:21
  125.5 5.4 %collective-permute-done = f32[2,1,16,256]{3,2,1,0:T(8,128)S(1)} collective-permute-done((f32[2,1,16,256]{3,2,1,0:T(8,128)S(1)}, f32[2,1,16,256]{3,2,1,0:T(8,128)S(1)}, u32[]{:S(2)}, u32[]{:S(2)}) %collective-permute-start) | collective-permute-done | bytes 32800 | tf_op jit(solution)/shard_map/ppermute | solution.py:28
  133.2 14.8 %fusion.6 = f32[32,32,512]{2,1,0:T(8,128)S(1)} fusion(f32[32,32,512]{2,1,0:T(8,128)} %param.10, f32[32,32,512]{2,1,0:T(8,128)} %reshape.343, f32[34,34,514]{2,1,0:T(8,128)S(1)} %select_maximum_fusion, f32[34,32,512]{2,1,0:T(8,128)} %copy-done.6, f32[34,1,512]{2,1,0:T(1,128)} %collective-permute-done.13, f32[34,1,512]{2,1,0:T(1,128)S(1)} %collective-permute-done.12, ...), kind=kLoop, calls=%fused_computation.23 | loop fusion | flops 21495808 | bytes 23871488 | tf_op jit(solution)/shard_map/add | solution.py:146
  148.6 7.1 %scatter_fusion.1 = f32[524288]{0:T(1024)S(1)} fusion(f32[524288]{0:T(1024)S(1)} %bitcast.49, s32[1024]{0:T(1024)S(1)} %bitcast.61, f32[1024]{0:T(1024)S(1)} %bitcast.62), kind=kCustom, calls=%fused_computation.2 | custom fusion | flops 1024 | bytes 16384 | tf_op jit(solution)/shard_map/scatter-add | solution.py:150
  161.4 2.3 %slice_bitcast_fusion = (f32[2,32,16,1,512]{4,0,2,1,3:T(2,128)S(1)}, f32[2,32,16,1,512]{4,0,2,1,3:T(2,128)S(1)}) fusion(f32[2,32,17,512]{3,0,2,1:T(2,128)S(1)} %bitcast.50), kind=kLoop, calls=%fused_computation.93 | loop fusion | flops 1048576 | bytes 8388608 | tf_op jit(solution)/shard_map/stack | solution.py:59
  163.7 4.8 %fusion.1 = (f32[1,32,16,2,512]{4,0,2,1,3:T(1,128)S(1)}, f32[1,32,16,2,512]{4,0,2,1,3:T(1,128)S(1)}) fusion(f32[2,32,16,1,512]{4,0,2,1,3:T(2,128)S(1)} %get-tuple-element.17, f32[2,32,16,1,512]{4,0,2,1,3:T(2,128)S(1)} %get-tuple-element.18), kind=kLoop, calls=%fused_computation.17 | loop fusion | flops 1048576 | bytes 8388608 | tf_op jit(solution)/shard_map/stack | solution.py:59
  171.9 3.1 %fusion.49 = f32[1,32,32,512]{3,1,2,0:T(8,128)S(1)} fusion(f32[1,32,32,512]{3,1,2,0:T(8,128)S(1)} %bitcast.54, f32[1,32,32,512]{3,2,1,0:T(8,128)S(1)} %copy-done.9, f32[1,32,32,512]{3,1,2,0:T(8,128)S(1)} %bitcast.53, f32[1,32,32,512]{3,2,1,0:T(8,128)S(1)} %copy-done.8, f32[512]{0:T(512)S(1)} %copy-done.18, f32[32,32]{0,1:T(8,128)S(1)} %copy-done.15), kind=kLoop, calls=%fused_computation.91 | loop fusion | flops 4194304 | bytes 10491904 | tf_op jit(solution)/shard_map/mul | solution.py:155
  175.0 2.5 %copy.26 = f32[1,32,32,512]{3,2,1,0:T(8,128)} copy(f32[1,32,32,512]{3,1,2,0:T(8,128)S(1)} %fusion.49) | data formatting | bytes 4194304
  (105 shorter events, 44.1 us)
Async XLA Ops:
  0.6 37.7 %copy-start.5 = (f32[32,32,512]{2,1,0:T(8,128)S(1)}, f32[32,32,512]{2,1,0:T(8,128)}, u32[]{:S(2)}) copy-start(f32[32,32,512]{2,1,0:T(8,128)} %param.11) | copy-start | bytes 6291460
  0.6 31.0 %copy-start.17 = (f32[1,2,1024]{2,1,0:T(2,128)S(1)}, f32[1,2,1024]{2,1,0:T(2,128)}, u32[]{:S(2)}) copy-start(f32[1,2,1024]{2,1,0:T(2,128)} %param.18) | copy-start | bytes 24580
  0.7 31.6 %copy-start.22 = (s32[1,1,32]{2,1,0:T(1,128)S(1)}, s32[1,1,32]{2,1,0:T(1,128)}, u32[]{:S(2)}) copy-start(s32[1,1,32]{2,1,0:T(1,128)} %param.16) | copy-start | bytes 388
  1.7 36.6 %collective-permute-start.4 = (f32[1,32,512]{2,1,0:T(8,128)S(1)}, f32[1,32,512]{2,1,0:T(8,128)S(1)}, u32[]{:S(2)}, u32[]{:S(2)}) collective-permute-start(f32[1,32,512]{2,1,0:T(8,128)S(1)} %get-tuple-element.21), channel_id=1, source_target_pairs={{0,8},{8,16},{16,24},{24,32},{32,40},{40,48},{48,56},{1,9},{9,17},... | collective-permute-start | bytes 196616 | tf_op jit(solution)/shard_map/ppermute | solution.py:17
  9.5 29.1 %collective-permute-start.2 = (f32[1,32,512]{2,1,0:T(8,128)S(1)}, f32[1,32,512]{2,1,0:T(8,128)S(1)}, u32[]{:S(2)}, u32[]{:S(2)}) collective-permute-start(f32[1,32,512]{2,1,0:T(8,128)S(1)} %get-tuple-element.22), channel_id=1, source_target_pairs={{8,0},{16,8},{24,16},{32,24},{40,32},{48,40},{56,48},{9,1},{17,9},... | collective-permute-start | bytes 196616 | tf_op jit(solution)/shard_map/ppermute | solution.py:20
  13.0 32.6 %collective-permute-start.3 = (f32[1,32,512]{2,1,0:T(8,128)}, f32[1,32,512]{2,1,0:T(8,128)S(1)}, u32[]{:S(2)}, u32[]{:S(2)}) collective-permute-start(f32[1,32,512]{2,1,0:T(8,128)} %get-tuple-element.24), channel_id=1, source_target_pairs={{8,0},{16,8},{24,16},{32,24},{40,32},{48,40},{56,48},{9,1},{17,9},... | collective-permute-start | bytes 196616 | tf_op jit(solution)/shard_map/ppermute | solution.py:20
  14.9 30.7 %collective-permute-start.5 = (f32[1,32,512]{2,1,0:T(8,128)}, f32[1,32,512]{2,1,0:T(8,128)S(1)}, u32[]{:S(2)}, u32[]{:S(2)}) collective-permute-start(f32[1,32,512]{2,1,0:T(8,128)} %get-tuple-element.23), channel_id=1, source_target_pairs={{0,8},{8,16},{16,24},{24,32},{32,40},{40,48},{48,56},{1,9},{9,17},... | collective-permute-start | bytes 196616 | tf_op jit(solution)/shard_map/ppermute | solution.py:17
  24.3 89.2 %all-to-all-start = ((f32[32,32,256]{2,1,0:T(8,128)}), f32[32,32,256]{2,1,0:T(8,128)S(1)}, u32[]{:S(2)}, u32[]{:S(2)}) async-start(f32[32,32,256]{2,1,0:T(8,128)} %bitcast.58), calls=%async_computation | async-start | bytes 2097152 | tf_op jit(solution)/shard_map/all_to_all | solution.py:114
  38.6 24.7 %copy-start.4 = (f32[34,32,512]{2,1,0:T(8,128)}, f32[34,32,512]{2,1,0:T(8,128)S(1)}, u32[]{:S(2)}) copy-start(f32[34,32,512]{2,1,0:T(8,128)S(1)} %constant_dynamic-update-slice_fusion) | copy-start | bytes 6684676
  38.8 12.5 %collective-permute-start.6 = (f32[34,1,512]{2,1,0:T(1,128)S(1)}, f32[34,1,512]{2,1,0:T(1,128)S(1)}, u32[]{:S(2)}, u32[]{:S(2)}) collective-permute-start(f32[34,1,512]{2,1,0:T(1,128)S(1)} %get-tuple-element.14), channel_id=1, source_target_pairs={{1,0},{2,1},{3,2},{4,3},{5,4},{6,5},{7,6},{9,8},{10,9},{11,10},{12... | collective-permute-start | bytes 208904 | tf_op jit(solution)/shard_map/ppermute | solution.py:20
  43.0 8.3 %collective-permute-start.8 = (f32[34,1,512]{2,1,0:T(1,128)S(1)}, f32[34,1,512]{2,1,0:T(1,128)S(1)}, u32[]{:S(2)}, u32[]{:S(2)}) collective-permute-start(f32[34,1,512]{2,1,0:T(1,128)S(1)} %get-tuple-element.13), channel_id=1, source_target_pairs={{0,1},{1,2},{2,3},{3,4},{4,5},{5,6},{6,7},{8,9},{9,10},{10,11},{11... | collective-permute-start | bytes 208904 | tf_op jit(solution)/shard_map/ppermute | solution.py:17
  45.8 7.2 %collective-permute-start.7 = (f32[34,1,512]{2,1,0:T(1,128)S(1)}, f32[34,1,512]{2,1,0:T(1,128)S(1)}, u32[]{:S(2)}, u32[]{:S(2)}) collective-permute-start(f32[34,1,512]{2,1,0:T(1,128)S(1)} %get-tuple-element.16), channel_id=1, source_target_pairs={{1,0},{2,1},{3,2},{4,3},{5,4},{6,5},{7,6},{9,8},{10,9},{11,10},{12... | collective-permute-start | bytes 208904 | tf_op jit(solution)/shard_map/ppermute | solution.py:20
  47.7 11.1 %collective-permute-start.9 = (f32[34,1,512]{2,1,0:T(1,128)S(1)}, f32[34,1,512]{2,1,0:T(1,128)S(1)}, u32[]{:S(2)}, u32[]{:S(2)}) collective-permute-start(f32[34,1,512]{2,1,0:T(1,128)S(1)} %get-tuple-element.15), channel_id=1, source_target_pairs={{0,1},{1,2},{2,3},{3,4},{4,5},{5,6},{6,7},{8,9},{9,10},{10,11},{11... | collective-permute-start | bytes 208904 | tf_op jit(solution)/shard_map/ppermute | solution.py:17
  52.9 10.4 %copy-start = (f32[34,34,514]{2,1,0:T(8,128)}, f32[34,34,514]{2,1,0:T(8,128)S(1)}, u32[]{:S(2)}) copy-start(f32[34,34,514]{2,1,0:T(8,128)S(1)} %select_maximum_fusion.6) | copy-start | bytes 7130212
  82.6 11.1 %collective-permute-start.11 = (f32[1,32,512]{2,1,0:T(8,128)}, f32[1,32,512]{2,1,0:T(8,128)S(1)}, u32[]{:S(2)}, u32[]{:S(2)}) collective-permute-start(f32[1,32,512]{2,1,0:T(8,128)} %slice.261), channel_id=1, source_target_pairs={{0,8},{8,16},{16,24},{24,32},{32,40},{40,48},{48,56},{1,9},{9,17},... | collective-permute-start | bytes 196616 | tf_op jit(solution)/shard_map/ppermute | solution.py:17
  91.7 12.0 %collective-permute-start.10 = (f32[1,32,512]{2,1,0:T(8,128)}, f32[1,32,512]{2,1,0:T(8,128)S(1)}, u32[]{:S(2)}, u32[]{:S(2)}) collective-permute-start(f32[1,32,512]{2,1,0:T(8,128)} %slice.258), channel_id=1, source_target_pairs={{8,0},{16,8},{24,16},{32,24},{40,32},{48,40},{56,48},{9,1},{17,9},... | collective-permute-start | bytes 196616 | tf_op jit(solution)/shard_map/ppermute | solution.py:20
  105.8 16.5 %collective-permute-start.12 = (f32[34,1,512]{2,1,0:T(1,128)}, f32[34,1,512]{2,1,0:T(1,128)S(1)}, u32[]{:S(2)}, u32[]{:S(2)}) collective-permute-start(f32[34,1,512]{2,1,0:T(1,128)} %get-tuple-element.12), channel_id=1, source_target_pairs={{1,0},{2,1},{3,2},{4,3},{5,4},{6,5},{7,6},{9,8},{10,9},{11,10},{12... | collective-permute-start | bytes 208904 | tf_op jit(solution)/shard_map/ppermute | solution.py:20
  108.5 13.9 %collective-permute-start.13 = (f32[34,1,512]{2,1,0:T(1,128)}, f32[34,1,512]{2,1,0:T(1,128)}, u32[]{:S(2)}, u32[]{:S(2)}) collective-permute-start(f32[34,1,512]{2,1,0:T(1,128)} %get-tuple-element.11), channel_id=1, source_target_pairs={{0,1},{1,2},{2,3},{3,4},{4,5},{5,6},{6,7},{8,9},{9,10},{10,11},{11... | collective-permute-start | bytes 208904 | tf_op jit(solution)/shard_map/ppermute | solution.py:17
  119.9 13.3 %copy-start.1 = (f32[34,34,514]{2,1,0:T(8,128)S(1)}, f32[34,34,514]{2,1,0:T(8,128)}, u32[]{:S(2)}) copy-start(f32[34,34,514]{2,1,0:T(8,128)} %copy-done) | copy-start | bytes 7130212
  119.9 13.3 %copy-start.3 = (f32[1,32,32,512]{3,2,1,0:T(8,128)S(1)}, f32[1,32,32,512]{3,2,1,0:T(8,128)}, u32[]{:S(2)}) copy-start(f32[1,32,32,512]{3,2,1,0:T(8,128)} %param.13) | copy-start | bytes 6291460
  120.0 13.3 %copy-start.12 = (f32[1,32,512]{2,1,0:T(8,128)S(1)}, f32[1,32,512]{2,1,0:T(8,128)}, u32[]{:S(2)}) copy-start(f32[1,32,512]{2,1,0:T(8,128)} %copy-done.11) | copy-start | bytes 196612
  120.0 13.3 %copy-start.14 = (f32[1,32,512]{2,1,0:T(8,128)S(1)}, f32[1,32,512]{2,1,0:T(8,128)}, u32[]{:S(2)}) copy-start(f32[1,32,512]{2,1,0:T(8,128)} %copy-done.13) | copy-start | bytes 196612
  120.0 10.9 %collective-permute-start = (f32[2,1,16,256]{3,2,1,0:T(8,128)S(1)}, f32[2,1,16,256]{3,2,1,0:T(8,128)S(1)}, u32[]{:S(2)}, u32[]{:S(2)}) collective-permute-start(f32[2,1,16,256]{3,2,1,0:T(8,128)S(1)} %slice.270), channel_id=1, source_target_pairs={{8,0},{16,8},{24,16},{32,24},{40,32},{48,40},{56,48},{9,1},{17,9},... | collective-permute-start | bytes 98312 | tf_op jit(solution)/shard_map/ppermute | solution.py:28
  130.9 26.2 %collective-permute-start.1 = (f32[2,17,1,256]{3,2,1,0:T(1,128)S(1)}, f32[2,17,1,256]{3,2,1,0:T(1,128)S(1)}, u32[]{:S(2)}, u32[]{:S(2)}) collective-permute-start(f32[2,17,1,256]{3,2,1,0:T(1,128)S(1)} %pad_maximum_fusion.21), channel_id=1, source_target_pairs={{1,0},{2,1},{3,2},{4,3},{5,4},{6,5},{7,6},{9,8},{10,9},{11,10},{12... | collective-permute-start | bytes 104456 | tf_op jit(solution)/shard_map/ppermute | solution.py:28
  (14 other events, 39.2 us)
where the time goes:
time: 178 us; the launch traced here: 177 us
  other arithmetic  64.9 us (36%)
  starting transfers between devices  58.6 us (33%)
  local copies, waits for them, and re-layouts  31.6 us (18%)
  waiting for transfers between devices  19.4 us (11%)
    ppermute x6, starting transfers between devices, with_halo(): lax.ppermute(lax.slice_in_dim(block, block.shape[dim] - width, None, axis...  32.7 us
    add x2, other arithmetic, per_device(): newer = 2.0 * current - older + stiffness * operate(padded_f, padded_b)  24.4 us
    ppermute x6, starting transfers between devices, with_halo(): lax.ppermute(lax.slice_in_dim(block, 0, width, axis=dim), axis, backward)  14.5 us
    scatter-add x2, other arithmetic, per_device(): newer = newer.reshape(-1).at[flat_cells].add(receiver_data[0, section_ind...  13.9 us
    unnamed x53, local copies, waits for them, and re-layouts  10.7 us
    concatenate x4, other arithmetic, with_halo(): block = jnp.concatenate([low, block, high], axis=dim)  9.45 us
    ppermute x6, waiting for transfers between devices, with_halo(): lax.ppermute(lax.slice_in_dim(block, 0, width, axis=dim), axis, backward)  8.22 us
    another operation x4, other arithmetic, refine(): paired = jnp.stack([lower, middle], axis=along + 1)  7.77 us
  transfers between devices with their start and end apart: 15, of which 3 were waited for; matrix products, arithmetic and copies ran while one was open for 42% of the time, Pallas kernels for 0%

commit v1 on v0

v1 whole, which is shorter than its diff:
```python
import jax
import jax.numpy as jnp
from jax import lax
from jax.experimental import pallas as pl
from jax.experimental.pallas import tpu as pltpu
from jax.sharding import PartitionSpec as P

MUTE_RADIUS = 3.0
PLANES = 32
ROWS = 1024
DEPTH = 512
COARSE = 256
CHUNKS = 4
SPAN = ROWS // CHUNKS
VMEM = pl.BlockSpec(memory_space=pltpu.VMEM)
SMEM = pl.BlockSpec(memory_space=pltpu.SMEM)
ANY = pl.BlockSpec(memory_space=pl.ANY)


def rotate(block, axis, step):
    count = lax.axis_size(axis)
    return lax.ppermute(block, axis, [(i, (i + step) % count) for i in range(count)])


def f32(*shape):
    return jax.ShapeDtypeStruct(shape, jnp.float32)


def split_bf16(x):
    high = x.astype(jnp.bfloat16)
    return high, (x - high.astype(jnp.float32)).astype(jnp.bfloat16)


def faces_kernel(fx_lo, fx_hi, fy_lo, fy_hi, bx_lo, bx_hi, by_lo, by_hi, sx_lo, sx_hi, sy_lo, sy_hi):
    for slot, refs in enumerate(((fx_lo, fx_hi, fy_lo, fy_hi), (bx_lo, bx_hi, by_lo, by_hi))):
        sx_lo[slot] = refs[0][0]
        sx_hi[slot] = refs[1][0]
        for x in range(PLANES):
            sy_lo[slot, x : x + 1, :] = refs[2][x, 0:1, :]
            sy_hi[slot, x : x + 1, :] = refs[3][x, 7:8, :]


def faces(field, buoyancy):
    plane_lo = pl.BlockSpec((1, PLANES, DEPTH), lambda i: (0, 0, 0))
    plane_hi = pl.BlockSpec((1, PLANES, DEPTH), lambda i: (PLANES - 1, 0, 0))
    rows_lo = pl.BlockSpec((PLANES, 8, DEPTH), lambda i: (0, 0, 0))
    rows_hi = pl.BlockSpec((PLANES, 8, DEPTH), lambda i: (0, PLANES // 8 - 1, 0))
    out = pl.BlockSpec((2, PLANES, DEPTH), lambda i: (0, 0, 0))
    return pl.pallas_call(
        faces_kernel,
        grid=(1,),
        in_specs=[plane_lo, plane_hi, rows_lo, rows_hi] * 2,
        out_specs=[out] * 4,
        out_shape=[f32(2, PLANES, DEPTH)] * 4,
        cost_estimate=pl.CostEstimate(flops=0, bytes_accessed=3 << 20, transcendentals=0),
        name="faces",
    )(*([field] * 4 + [buoyancy] * 4))


def sources_kernel(cells, data, out):
    base_x = lax.axis_index("gx") * PLANES
    base_y = lax.axis_index("gy") * PLANES
    local_x = cells[0:1, :] - base_x
    local_y = cells[1:2, :] - base_y
    inside = (local_x >= 0) & (local_x < PLANES) & (local_y >= 0) & (local_y < PLANES)
    row = jnp.where(inside, local_x * PLANES + local_y, -1)
    depth_id = lax.broadcasted_iota(jnp.int32, (8, 1024), 0)
    here = depth_id == cells[2:3, :]
    parts = []
    for step in range(2):
        value = jnp.where(here, data[step : step + 1, :], 0.0)
        parts.append(split_bf16(value))
    table = jnp.concatenate([parts[0][0], parts[0][1], parts[1][0], parts[1][1]], axis=0)
    lane = lax.broadcasted_iota(jnp.int32, (128, 128), 1)
    pad = jnp.zeros((96, 1024), jnp.bfloat16)
    table = jnp.concatenate([table, pad], axis=0)
    for start in range(0, ROWS, 128):
        ids = lax.broadcasted_iota(jnp.int32, (128, 1024), 0) + start
        select = jnp.where(ids == row, 1.0, 0.0).astype(jnp.bfloat16)
        product = lax.dot_general(
            select, table, (((1,), (1,)), ((), ())), preferred_element_type=jnp.float32
        )
        for step in range(2):
            high = pltpu.roll(product, (128 - 16 * step) % 128, 1)
            low = pltpu.roll(product, 128 - 16 * step - 8, 1)
            out[step, start : start + 128, :] = jnp.where(lane < 8, high + low, 0.0)


def sources(cells, data):
    return pl.pallas_call(
        sources_kernel,
        in_specs=[VMEM, VMEM],
        out_specs=VMEM,
        out_shape=f32(2, ROWS, 128),
        cost_estimate=pl.CostEstimate(flops=1 << 29, bytes_accessed=2 << 20, transcendentals=0),
        name="sources",
    )(cells, data)


def onehot_kernel(ids, out):
    for start in range(0, 512, 128):
        tile = lax.broadcasted_iota(jnp.int32, (128, 1024), 0) + start
        out[start : start + 128, :] = jnp.where(tile == ids[...], 1.0, 0.0).astype(jnp.bfloat16)


def onehots(ids):
    return pl.pallas_call(
        onehot_kernel,
        in_specs=[VMEM],
        out_specs=VMEM,
        out_shape=jax.ShapeDtypeStruct((512, 1024), jnp.bfloat16),
        cost_estimate=pl.CostEstimate(flops=1 << 20, bytes_accessed=2 << 20, transcendentals=0),
        name="onehots",
    )(ids)


def step_kernel(
    field, older, buoy, stiff, hx_lo, hx_hi, hy_lo, hy_hi, bx_lo, bx_hi, by_lo, by_hi, src,
    out, *rest, step, give_faces,
):
    if give_faces:
        sx_lo, sx_hi, sy_lo, sy_hi = rest[:4]
        rest = rest[4:]
    f_ext, b_ext, s_buf, o_buf, n_buf, in_sem, out_sem = rest
    copies = []
    for chunk in range(CHUNKS):
        part = pl.ds(chunk * SPAN, SPAN)
        shifted = pl.ds(chunk * SPAN + PLANES, SPAN)
        group = [
            pltpu.make_async_copy(field.at[part], f_ext.at[shifted], in_sem.at[chunk, 0]),
            pltpu.make_async_copy(buoy.at[part], b_ext.at[shifted], in_sem.at[chunk, 1]),
            pltpu.make_async_copy(stiff.at[part], s_buf.at[part], in_sem.at[chunk, 2]),
            pltpu.make_async_copy(older.at[part], o_buf.at[part], in_sem.at[chunk, 3]),
        ]
        for copy in group:
            copy.start()
        copies.append(group)
    gx = lax.axis_index("gx")
    gy = lax.axis_index("gy")
    x_lo = jnp.where(gx > 0, 1.0, 0.0)
    x_hi = jnp.where(gx < lax.axis_size("gx") - 1, 1.0, 0.0)
    y_lo = jnp.where(gy > 0, 1.0, 0.0)
    y_hi = jnp.where(gy < lax.axis_size("gy") - 1, 1.0, 0.0)
    f_ext[0:PLANES] = hx_lo[...] * x_lo
    b_ext[0:PLANES] = bx_lo[...] * x_lo
    f_ext[ROWS + PLANES : ROWS + 2 * PLANES] = hx_hi[...] * x_hi
    b_ext[ROWS + PLANES : ROWS + 2 * PLANES] = bx_hi[...] * x_hi
    row_id = lax.broadcasted_iota(jnp.int32, (PLANES, DEPTH), 0)
    lane_id = lax.broadcasted_iota(jnp.int32, (PLANES, DEPTH), 1)
    per = SPAN // PLANES
    out_copies = []
    for group in copies[0][:2]:
        group.wait()
    carry = (b_ext[0:PLANES] + b_ext[PLANES : 2 * PLANES]) * (
        f_ext[PLANES : 2 * PLANES] - f_ext[0:PLANES]
    )
    for chunk in range(CHUNKS):
        for copy in copies[chunk][2:]:
            copy.wait()
        if chunk + 1 < CHUNKS:
            for copy in copies[chunk + 1][:2]:
                copy.wait()
        first = chunk * per

        def plane(k, flux_before, first=first):
            x = first + k
            base = pl.multiple_of((x + 1) * PLANES, PLANES)
            c = f_ext[pl.ds(base, PLANES), :]
            b = b_ext[pl.ds(base, PLANES), :]
            c_next = f_ext[pl.ds(base + PLANES, PLANES), :]
            b_next = b_ext[pl.ds(base + PLANES, PLANES), :]
            flux_x = (b + b_next) * (c_next - c)
            lo_f = hy_lo[pl.ds(x, 1), :] * y_lo
            lo_b = by_lo[pl.ds(x, 1), :] * y_lo
            hi_f = hy_hi[pl.ds(x, 1), :] * y_hi
            hi_b = by_hi[pl.ds(x, 1), :] * y_hi
            c_up = jnp.where(row_id == PLANES - 1, hi_f, pltpu.roll(c, PLANES - 1, 0))
            b_up = jnp.where(row_id == PLANES - 1, hi_b, pltpu.roll(b, PLANES - 1, 0))
            flux_y = (b + b_up) * (c_up - c)
            first_flux = (b[0:1, :] + lo_b) * (c[0:1, :] - lo_f)
            flux_y_before = jnp.where(row_id == 0, first_flux, pltpu.roll(flux_y, 1, 0))
            edge_flux = b * c
            flux_z = (b + pltpu.roll(b, DEPTH - 1, 1)) * (pltpu.roll(c, DEPTH - 1, 1) - c)
            flux_z = jnp.where(lane_id == DEPTH - 1, -edge_flux, flux_z)
            flux_z_before = jnp.where(lane_id == 0, edge_flux, pltpu.roll(flux_z, 1, 1))
            total = (flux_x - flux_before) + (flux_y - flux_y_before) + (flux_z - flux_z_before)
            at = pl.multiple_of(x * PLANES, PLANES)
            new = (2.0 * c - o_buf[pl.ds(at, PLANES), :]) + (
                0.5 * s_buf[pl.ds(at, PLANES), :]
            ) * total
            n_buf[pl.ds(at, PLANES), :] = new
            head = new[:, 0:128] + src[step, pl.ds(at, PLANES), :]
            n_buf[pl.ds(at, PLANES), 0:128] = head
            if give_faces:
                sy_lo[pl.ds(x, 1), :] = n_buf[pl.ds(at, 1), :]
                sy_hi[pl.ds(x, 1), :] = n_buf[pl.ds(at + PLANES - 1, 1), :]
            return flux_x

        carry = lax.fori_loop(0, per, plane, carry)
        part = pl.ds(chunk * SPAN, SPAN)
        copy = pltpu.make_async_copy(n_buf.at[part], out.at[part], out_sem.at[chunk])
        copy.start()
        out_copies.append(copy)
    if give_faces:
        sx_lo[...] = n_buf[0:PLANES]
        sx_hi[...] = n_buf[ROWS - PLANES : ROWS]
    for copy in out_copies:
        copy.wait()


def advance(field, older, buoy, stiff, halos, buoy_halos, src, step, give_faces):
    out_shape = [f32(ROWS, DEPTH)]
    out_specs = [ANY]
    if give_faces:
        out_shape += [f32(PLANES, DEPTH)] * 4
        out_specs += [VMEM] * 4
    return pl.pallas_call(
        lambda *refs: step_kernel(*refs, step=step, give_faces=give_faces),
        in_specs=[ANY] * 4 + [VMEM] * 9,
        out_specs=out_specs,
        out_shape=out_shape,
        scratch_shapes=[
            pltpu.VMEM((ROWS + 2 * PLANES, DEPTH), jnp.float32),
            pltpu.VMEM((ROWS + 2 * PLANES, DEPTH), jnp.float32),
            pltpu.VMEM((ROWS, DEPTH), jnp.float32),
            pltpu.VMEM((ROWS, DEPTH), jnp.float32),
            pltpu.VMEM((ROWS, DEPTH), jnp.float32),
            pltpu.SemaphoreType.DMA((CHUNKS, 4)),
            pltpu.SemaphoreType.DMA((CHUNKS,)),
        ],
        compiler_params=pltpu.CompilerParams(vmem_limit_bytes=32 << 20),
        cost_estimate=pl.CostEstimate(flops=20 << 20, bytes_accessed=10 << 20, transcendentals=0),
        name="advance%d" % step,
    )(field, older, buoy, stiff, *halos, *buoy_halos, src)


def interpolation():
    fine = lax.broadcasted_iota(jnp.int32, (COARSE, DEPTH), 1)
    coarse = lax.broadcasted_iota(jnp.int32, (COARSE, DEPTH), 0)
    gap = jnp.abs(fine - 2 * coarse).astype(jnp.float32)
    return jnp.maximum(1.0 - 0.5 * gap, 0.0).astype(jnp.bfloat16)


def dot(a, b):
    return jnp.dot(a, b, preferred_element_type=jnp.float32)


def coarse_kernel(received, onehot, along, rim_x, rim_y, corner, rows):
    high, low = split_bf16(received[...])
    c_high = dot(onehot[...], high)
    c_low = dot(onehot[...], low)
    coarse = c_high + c_low
    for n in range(2):
        rim_x[n] = coarse[n * 256 : n * 256 + 16, :]
        corner[n] = coarse[n * 256 : n * 256 + 8, :]
    for half in range(2):
        lanes = slice(half * 128, half * 128 + 128)
        rows[half] = coarse[:, lanes]
        for n in range(2):
            rim_y[n, :, lanes] = rows[half, pl.ds(n * 256, 16, stride=16), :]
    weights = interpolation()
    along[...] = dot(c_high.astype(jnp.bfloat16), weights) + dot(c_low.astype(jnp.bfloat16), weights)


def coarse_tiles(received, onehot):
    return pl.pallas_call(
        coarse_kernel,
        in_specs=[VMEM, VMEM],
        out_specs=[VMEM] * 4,
        out_shape=[f32(512, DEPTH), f32(2, 16, COARSE), f32(2, 16, COARSE), f32(2, 8, COARSE)],
        scratch_shapes=[pltpu.VMEM((2, 512, 128), jnp.float32)],
        compiler_params=pltpu.CompilerParams(vmem_limit_bytes=32 << 20),
        cost_estimate=pl.CostEstimate(flops=1 << 30, bytes_accessed=3 << 20, transcendentals=0),
        name="coarse_tiles",
    )(received, onehot)


def image_kernel(source, along, rim_x, rim_y, corner, first, second, out, rims, rim_along, fine):
    gx = lax.axis_index("gx")
    gy = lax.axis_index("gy")
    keep_x = jnp.where(gx < lax.axis_size("gx") - 1, 1.0, 0.0)
    keep_y = jnp.where(gy < lax.axis_size("gy") - 1, 1.0, 0.0)
    for n in range(2):
        rims[n * 40 : n * 40 + 16] = rim_x[n] * keep_x
        rims[n * 40 + 16 : n * 40 + 32] = rim_y[n] * keep_y
        rims[n * 40 + 32 : n * 40 + 40] = corner[n] * (keep_x * keep_y)
    weights = interpolation()
    high, low = split_bf16(rims[...])
    rim_along[...] = dot(high, weights) + dot(low, weights)
    row16 = lax.broadcasted_iota(jnp.int32, (16, DEPTH), 0)
    for n in range(2):
        for k in range(17):
            if k < 16:
                rows = along[n * 256 + k * 16 : n * 256 + k * 16 + 16, :]
                side = rim_along[n * 40 + 16 + k : n * 40 + 17 + k, :]
            else:
                rows = rim_along[n * 40 : n * 40 + 16, :]
                side = rim_along[n * 40 + 32 : n * 40 + 33, :]
            upper = jnp.where(row16 == 15, side, pltpu.roll(rows, 15, 0))
            base = (n * 17 + k) * PLANES
            middle = 0.5 * (rows + upper)
            for part in range(4):
                lanes = slice(part * 128, part * 128 + 128)
                fine[part, pl.ds(base, 16, stride=2), :] = rows[:, lanes]
                fine[part, pl.ds(base + 1, 16, stride=2), :] = middle[:, lanes]
    scale = -1.0 / (2.0 * MUTE_RADIUS * MUTE_RADIUS)
    y = (lax.broadcasted_iota(jnp.int32, (PLANES, DEPTH), 0) + gy * PLANES - source[0, 1]).astype(jnp.float32)
    z = (lax.broadcasted_iota(jnp.int32, (PLANES, DEPTH), 1) - source[0, 2]).astype(jnp.float32)
    decay_yz = jnp.exp((y * y + z * z) * scale)
    x_base = gx * PLANES - source[0, 0]
    for k in range(16):
        for odd in range(2):
            x = 2 * k + odd
            at = slice(x * PLANES, (x + 1) * PLANES)
            dx = jnp.full((1, 128), x_base + x, jnp.int32).astype(jnp.float32)
            decay = jnp.exp((dx * dx) * scale)
            for part in range(4):
                lanes = slice(part * 128, part * 128 + 128)
                taper = 1.0 - decay * decay_yz[:, lanes]
                snaps = []
                for n in range(2):
                    start = (n * 17 + k) * PLANES
                    snap = fine[part, start : start + PLANES, :]
                    if odd:
                        snap = 0.5 * (snap + fine[part, start + PLANES : start + 2 * PLANES, :])
                    snaps.append(snap)
                out[at, lanes] = taper * (
                    snaps[0] * first[at, lanes] + snaps[1] * second[at, lanes]
                )


def imaging(source, along, rims, first, second):
    return pl.pallas_call(
        image_kernel,
        in_specs=[SMEM] + [VMEM] * 6,
        out_specs=VMEM,
        out_shape=f32(ROWS, DEPTH),
        scratch_shapes=[
            pltpu.VMEM((80, COARSE), jnp.float32),
            pltpu.VMEM((80, DEPTH), jnp.float32),
            pltpu.VMEM((4, 2 * 17 * PLANES, 128), jnp.float32),
        ],
        compiler_params=pltpu.CompilerParams(vmem_limit_bytes=32 << 20),
        cost_estimate=pl.CostEstimate(flops=20 << 20, bytes_accessed=8 << 20, transcendentals=0),
        name="imaging",
    )(source, along, *rims, first, second)


def per_device(
    stiffness,
    buoyancy,
    older_field,
    current_field,
    stored_tiles,
    tile_ids,
    tile_counts,
    receiver_cells,
    receiver_data,
    source_cell,
):
    older = older_field[0].reshape(ROWS, DEPTH)
    current = current_field[0].reshape(ROWS, DEPTH)
    stiff = stiffness.reshape(ROWS, DEPTH)
    buoy = buoyancy.reshape(ROWS, DEPTH)

    with jax.named_scope("halo_exchange"):
        sx_lo, sx_hi, sy_lo, sy_hi = faces(current_field[0], buoyancy)
        hx_lo = rotate(sx_hi, "gx", 1)
        hx_hi = rotate(sx_lo, "gx", -1)
        hy_lo = rotate(sy_hi, "gy", 1)
        hy_hi = rotate(sy_lo, "gy", -1)
    both = (hx_lo, hx_hi, hy_lo, hy_hi)
    halos = [h[0] for h in both]
    buoy_halos = [h[1] for h in both]

    received = lax.all_to_all(
        stored_tiles[0, 0], ("shot", "gx"), split_axis=0, concat_axis=0, tiled=True
    ).reshape(1024, COARSE)
    slot = lax.broadcasted_iota(jnp.int32, (32, 32), 1)
    ids = jnp.where(slot < tile_counts[0, 0][:, None], tile_ids[0, 0], -1).reshape(1, 1024)
    onehot = onehots(ids)
    src = sources(receiver_cells[0], receiver_data[0])

    second, sx_lo, sx_hi, sy_lo, sy_hi = advance(
        current, older, buoy, stiff, halos, buoy_halos, src, 0, True
    )
    halos = [
        rotate(sx_hi, "gx", 1),
        rotate(sx_lo, "gx", -1),
        rotate(sy_hi, "gy", 1),
        rotate(sy_lo, "gy", -1),
    ]
    (third,) = advance(second, current, buoy, stiff, halos, buoy_halos, src, 1, False)

    along, rim_x, rim_y, corner = coarse_tiles(received, onehot)
    rims = [
        rotate(rim_x, "gx", -1),
        rotate(rim_y, "gy", -1),
        diagonal(corner),
    ]
    image = imaging(source_cell, along, rims, second, third)
    shape = current_field.shape
    return image.reshape(shape), second.reshape(shape), third.reshape(shape)


def diagonal(block):
    nx, ny = lax.axis_size("gx"), lax.axis_size("gy")
    route = [
        (i * ny + j, ((i - 1) % nx) * ny + (j - 1) % ny) for i in range(nx) for j in range(ny)
    ]
    return lax.ppermute(block, ("gx", "gy"), route)


def solution(mesh):
    in_specs = (
        P("gx", "gy", None),
        P("gx", "gy", None),
        P("shot", "gx", "gy", None),
        P("shot", "gx", "gy", None),
        P(("shot", "gx"), "gy", None, None, None),
        P(("shot", "gx"), "gy", None, None),
        P(("shot", "gx"), "gy", None),
        P("shot", None, None),
        P("shot", None, None),
        P("shot", None),
    )
    out_specs = (
        P("shot", "gx", "gy", None),
        P("shot", "gx", "gy", None),
        P("shot", "gx", "gy", None),
    )
    return jax.shard_map(
        per_device, mesh=mesh, in_specs=in_specs, out_specs=out_specs, check_vma=False
    )
```

time: 178 us -> 103 us (0.58)
  the two profiles are of different devices: /device:TPU:39 before, /device:TPU:49 now
where the time goes in v1:
time: 103 us; the launch traced here: 102 us
  starting transfers between devices  39.9 us (39%)
  Pallas kernels  29.1 us (28%)
  waiting for transfers between devices  18.6 us (18%)
  local copies, waits for them, and re-layouts  13 us (13%)
    ppermute x10, starting transfers between devices, rotate(): lax.ppermute(block, axis, [(i, (i + step) % count) for i in range(count)])  21.5 us
    ppermute x10, waiting for transfers between devices, rotate(): lax.ppermute(block, axis, [(i, (i + step) % count) for i in range(count)])  18.6 us
    pallas_call x2, Pallas kernels, advance(): pl.pallas_call(lambda *refs: step_kernel(*refs, step=step, give_faces=giv...  17 us
    unnamed x31, local copies, waits for them, and re-layouts  12.8 us
    all_to_all x1, starting transfers between devices, per_device(): lax.all_to_all(stored_tiles[0, 0], ('shot', 'gx'), split_axis=0, concat_a...  12.7 us
    ppermute x1, starting transfers between devices, diagonal(): return lax.ppermute(block, ('gx', 'gy'), route)  5.73 us
    pallas_call x1, Pallas kernels, imaging(): pl.pallas_call(image_kernel, in_specs=[SMEM] + [VMEM] * 6, out_specs=VMEM...  3.05 us
    pallas_call x1, Pallas kernels, sources(): pl.pallas_call(sources_kernel, in_specs=[VMEM, VMEM], out_specs=VMEM, out...  2.52 us
  transfers between devices with their start and end apart: 12, of which 1 were waited for; matrix products, arithmetic and copies ran while one was open for 1% of the time, Pallas kernels for 26%

profile of v1, /device:TPU:49, one launch (start us, length us, event | category | flops | bytes accessed | tf_op | source)
XLA Modules:
  0.0 102.0 jit_solution(7577117631498073275)
XLA Ops:
  0.6 12.7 %all-to-all-start = ((f32[32,32,256]{2,1,0:T(8,128)}), f32[32,32,256]{2,1,0:T(8,128)}, u32[]{:S(2)}, u32[]{:S(2)}) async-start(f32[32,32,256]{2,1,0:T(8,128)} %bitcast.47), calls=%async_computation | async-start | bytes 2097152 | tf_op jit(solution)/shard_map/all_to_all | solution.py:376
  13.3 2.5 %faces.1 = (f32[2,32,512]{2,1,0:T(8,128)}, f32[2,32,512]{2,1,0:T(8,128)}, f32[2,32,512]{2,1,0:T(8,128)}, f32[2,32,512]{2,1,0:T(8,128)}) custom-call(f32[32,32,512]{2,1,0:T(8,128)} %bitcast.33, f32[32,32,512]{2,1,0:T(8,128)} %bitcast.34, f32[32,32,512]{2,1,0:T(8,128)} %bitcast.35, f32[32,32,512]{2,1,0:T(8,128)} %bitcast.36, f32[32,32,512]{2,1,0:T(8,128)} %by_hi.1, ...), custom_call_target="tpu_custom_call" | custom-call | bytes 3145728 | tf_op jit(solution)/shard_map/halo_exchange/faces/pallas_call | solution.py:49
  15.8 1.2 %collective-permute-start.3 = (f32[2,32,512]{2,1,0:T(8,128)}, f32[2,32,512]{2,1,0:T(8,128)S(1)}, u32[]{:S(2)}, u32[]{:S(2)}) collective-permute-start(f32[2,32,512]{2,1,0:T(8,128)} %get-tuple-element.20), channel_id=1, source_target_pairs={{0,8},{8,16},{16,24},{24,32},{32,40},{40,48},{48,56},{56,0},{1,9},... | collective-permute-start | bytes 393224 | tf_op jit(solution)/shard_map/halo_exchange/ppermute | solution.py:22
  17.0 6.3 %collective-permute-start.4 = (f32[2,32,512]{2,1,0:T(8,128)}, f32[2,32,512]{2,1,0:T(8,128)S(1)}, u32[]{:S(2)}, u32[]{:S(2)}) collective-permute-start(f32[2,32,512]{2,1,0:T(8,128)} %get-tuple-element.21), channel_id=1, source_target_pairs={{0,56},{8,0},{16,8},{24,16},{32,24},{40,32},{48,40},{56,48},{1,57}... | collective-permute-start | bytes 393224 | tf_op jit(solution)/shard_map/halo_exchange/ppermute | solution.py:22
  23.3 2.4 %collective-permute-start.5 = (f32[2,32,512]{2,1,0:T(8,128)}, f32[2,32,512]{2,1,0:T(8,128)S(1)}, u32[]{:S(2)}, u32[]{:S(2)}) collective-permute-start(f32[2,32,512]{2,1,0:T(8,128)} %get-tuple-element.22), channel_id=1, source_target_pairs={{0,1},{1,2},{2,3},{3,4},{4,5},{5,6},{6,7},{7,0},{8,9},{9,10},{10,1... | collective-permute-start | bytes 393224 | tf_op jit(solution)/shard_map/halo_exchange/ppermute | solution.py:22
  27.2 1.8 %onehots.1.onehot = bf16[512,1024]{1,0:T(8,128)(2,1)} custom-call(s32[1,1024]{1,0:T(1,128)} %broadcast_select_fusion.ids), custom_call_target="tpu_custom_call" | custom-call | flops 1048576 | bytes 2097152 | tf_op jit(solution)/shard_map/onehots/pallas_call | solution.py:107
  29.0 2.5 %sources.1.refs_12_ = f32[2,1024,128]{2,1,0:T(8,128)} custom-call(s32[3,1024]{1,0:T(4,128)} %bitcast.48, f32[2,1024]{1,0:T(2,128)} %bitcast.50), custom_call_target="tpu_custom_call" | custom-call | flops 536870912 | bytes 2097152 | tf_op jit(solution)/shard_map/sources/pallas_call | solution.py:90
  31.5 18.5 %collective-permute-done.3 = f32[2,32,512]{2,1,0:T(8,128)S(1)} collective-permute-done((f32[2,32,512]{2,1,0:T(8,128)}, f32[2,32,512]{2,1,0:T(8,128)S(1)}, u32[]{:S(2)}, u32[]{:S(2)}) %collective-permute-start.3) | collective-permute-done | bytes 131104 | tf_op jit(solution)/shard_map/halo_exchange/ppermute | solution.py:22
  50.2 1.6 %copy-done.1 = f32[32,32,512]{2,1,0:T(8,128)S(1)} copy-done((f32[32,32,512]{2,1,0:T(8,128)S(1)}, f32[32,32,512]{2,1,0:T(8,128)}, u32[]{:S(2)}) %copy-start.1) | copy-done | bytes 2097176
  51.8 1.6 %copy-done.3 = f32[32,32,512]{2,1,0:T(8,128)S(1)} copy-done((f32[32,32,512]{2,1,0:T(8,128)S(1)}, f32[32,32,512]{2,1,0:T(8,128)}, u32[]{:S(2)}) %copy-start.3) | copy-done | bytes 2097176
  53.4 1.2 %copy-done.7 = f32[2,1024,128]{2,1,0:T(8,128)S(1)} copy-done((f32[2,1024,128]{2,1,0:T(8,128)S(1)}, f32[2,1024,128]{2,1,0:T(8,128)}, u32[]{:S(2)}) %copy-start.7) | copy-done | bytes 1048600
  54.6 1.6 %copy-done.9 = f32[1,32,32,512]{3,2,1,0:T(8,128)S(1)} copy-done((f32[1,32,32,512]{3,2,1,0:T(8,128)S(1)}, f32[1,32,32,512]{3,2,1,0:T(8,128)}, u32[]{:S(2)}) %copy-start.9) | copy-done | bytes 2097176
  56.2 8.5 %advance0.1 = (f32[1024,512]{1,0:T(8,128)}, f32[32,512]{1,0:T(8,128)}, f32[32,512]{1,0:T(8,128)}, f32[32,512]{1,0:T(8,128)}, f32[32,512]{1,0:T(8,128)}) custom-call(f32[1024,512]{1,0:T(8,128)S(1)} %bitcast.37, f32[1024,512]{1,0:T(8,128)S(1)} %bitcast.45, f32[1024,512]{1,0:T(8,128)S(1)} %bitcast.39, f32[1024,512]{1,0:T(8,128)S(1)} %bitcast.41, ...), custom_call_target="tpu_custom_call" | custom-call | flops 20971520 | bytes 10485760 | tf_op jit(solution)/shard_map/advance0/pallas_call | solution.py:217
  64.8 7.5 %collective-permute-start.8 = (f32[32,512]{1,0:T(8,128)}, f32[32,512]{1,0:T(8,128)S(1)}, u32[]{:S(2)}, u32[]{:S(2)}) collective-permute-start(f32[32,512]{1,0:T(8,128)} %get-tuple-element.26), channel_id=1, source_target_pairs={{0,56},{8,0},{16,8},{24,16},{32,24},{40,32},{48,40},{56,48},{1,57}... | collective-permute-start | bytes 196616 | tf_op jit(solution)/shard_map/ppermute | solution.py:22
  72.3 3.0 %collective-permute-start.9 = (f32[32,512]{1,0:T(8,128)}, f32[32,512]{1,0:T(8,128)}, u32[]{:S(2)}, u32[]{:S(2)}) collective-permute-start(f32[32,512]{1,0:T(8,128)} %get-tuple-element.27), channel_id=1, source_target_pairs={{0,1},{1,2},{2,3},{3,4},{4,5},{5,6},{6,7},{7,0},{8,9},{9,10},{10,1... | collective-permute-start | bytes 196616 | tf_op jit(solution)/shard_map/ppermute | solution.py:22
  75.3 1.4 %copy-done.10 = bf16[512,1024]{1,0:T(8,128)(2,1)S(1)} copy-done((bf16[512,1024]{1,0:T(8,128)(2,1)S(1)}, bf16[512,1024]{1,0:T(8,128)(2,1)}, u32[]{:S(2)}) %copy-start.10) | copy-done | bytes 1048600
  76.7 2.2 %coarse_tiles.1 = (f32[512,512]{1,0:T(8,128)S(1)}, f32[2,16,256]{2,1,0:T(8,128)S(1)}, f32[2,16,256]{2,1,0:T(8,128)S(1)}, f32[2,8,256]{2,1,0:T(8,128)S(1)}) custom-call(f32[1024,256]{1,0:T(8,128)} %bitcast.1.received, bf16[512,1024]{1,0:T(8,128)(2,1)S(1)} %copy-done.10), custom_call_target="tpu_custom_call" | custom-call | flops 1073741824 | bytes 3145728 | tf_op jit(solution)/shard_map/coarse_tiles/pallas_call | solution.py:266
  79.0 0.9 collective-permute-start.1
  79.9 5.7 %collective-permute-start.2 = (f32[2,8,256]{2,1,0:T(8,128)S(1)}, f32[2,8,256]{2,1,0:T(8,128)S(1)}, u32[]{:S(2)}, u32[]{:S(2)}) collective-permute-start(f32[2,8,256]{2,1,0:T(8,128)S(1)} %get-tuple-element.19), channel_id=1, source_target_pairs={{0,63},{1,56},{2,57},{3,58},{4,59},{5,60},{6,61},{7,62},{8,7},{9,0... | collective-permute-start | bytes 49160 | tf_op jit(solution)/shard_map/ppermute | solution.py:411
  85.7 1.6 %copy-done.4 = f32[32,32,512]{2,1,0:T(8,128)S(1)} copy-done((f32[32,32,512]{2,1,0:T(8,128)S(1)}, f32[32,32,512]{2,1,0:T(8,128)}, u32[]{:S(2)}) %copy-start.4) | copy-done | bytes 2097176
  87.2 1.6 %copy-done.5 = f32[1024,512]{1,0:T(8,128)S(1)} copy-done((f32[1024,512]{1,0:T(8,128)S(1)}, f32[1024,512]{1,0:T(8,128)}, u32[]{:S(2)}) %copy-start.5) | copy-done | bytes 2097176
  88.8 8.5 %advance1.1.second = f32[1024,512]{1,0:T(8,128)} custom-call(f32[1024,512]{1,0:T(8,128)S(1)} %copy-done.5, f32[1024,512]{1,0:T(8,128)S(1)} %bitcast.38, f32[1024,512]{1,0:T(8,128)S(1)} %bitcast.40, f32[1024,512]{1,0:T(8,128)S(1)} %bitcast.42, f32[32,512]{1,0:T(8,128)S(1)} %collective-permute-done.7.refs_4_, f32[32,512]{1,0:T(8,128)S(1)} %collective-permute-done.8.refs_5_, ...), custom_call_target="tpu_custom_call" | custom-call | flops 20971520 | bytes 10485760 | tf_op jit(solution)/shard_map/advance1/pallas_call | solution.py:217
  97.4 1.6 %copy-done.6 = f32[1024,512]{1,0:T(8,128)S(1)} copy-done((f32[1024,512]{1,0:T(8,128)S(1)}, f32[1024,512]{1,0:T(8,128)}, u32[]{:S(2)}) %copy-start.6) | copy-done | bytes 2097176
  99.0 3.1 %imaging.1 = f32[1024,512]{1,0:T(8,128)} custom-call(s32[1,3]{1,0:T(1,128)S(1)} %copy-done.11, f32[512,512]{1,0:T(8,128)S(1)} %get-tuple-element.16.along, f32[2,16,256]{2,1,0:T(8,128)S(1)} %collective-permute-done.rim_x, f32[2,16,256]{2,1,0:T(8,128)S(1)} %collective-permute-done.1.rim_y, f32[2,8,256]{2,1,0:T(8,128)S(1)} %collective-permute-done.2.corner, ...), custom_call_target="tpu_custom_call" | custom-call | flops 20971520 | bytes 8388608 | tf_op jit(solution)/shard_map/imaging/pallas_call | solution.py:333
  (46 shorter events, 1.8 us)
Async XLA Ops:
  0.6 74.7 %all-to-all-start = ((f32[32,32,256]{2,1,0:T(8,128)}), f32[32,32,256]{2,1,0:T(8,128)}, u32[]{:S(2)}, u32[]{:S(2)}) async-start(f32[32,32,256]{2,1,0:T(8,128)} %bitcast.47), calls=%async_computation | async-start | bytes 2097152 | tf_op jit(solution)/shard_map/all_to_all | solution.py:376
  13.3 12.4 %copy-start.12 = (s32[1,1,32,32]{3,2,1,0:T(8,128)S(1)}, s32[1,1,32,32]{3,2,1,0:T(8,128)}, u32[]{:S(2)}) copy-start(s32[1,1,32,32]{3,2,1,0:T(8,128)} %param.15) | copy-start | bytes 12292
  13.3 12.5 %copy-start.14 = (s32[1,1,32]{2,1,0:T(1,128)S(1)}, s32[1,1,32]{2,1,0:T(1,128)}, u32[]{:S(2)}) copy-start(s32[1,1,32]{2,1,0:T(1,128)} %param.16) | copy-start | bytes 388
  13.3 13.2 %copy-start.13 = (s32[1,3,1024]{2,0,1:T(1,128)S(1)}, s32[1,3,1024]{2,0,1:T(1,128)}, u32[]{:S(2)}) copy-start(s32[1,3,1024]{2,0,1:T(1,128)} %param.17) | copy-start | bytes 36868
  15.8 34.3 %collective-permute-start.3 = (f32[2,32,512]{2,1,0:T(8,128)}, f32[2,32,512]{2,1,0:T(8,128)S(1)}, u32[]{:S(2)}, u32[]{:S(2)}) collective-permute-start(f32[2,32,512]{2,1,0:T(8,128)} %get-tuple-element.20), channel_id=1, source_target_pairs={{0,8},{8,16},{16,24},{24,32},{32,40},{40,48},{48,56},{56,0},{1,9},... | collective-permute-start | bytes 393224 | tf_op jit(solution)/shard_map/halo_exchange/ppermute | solution.py:22
  17.0 33.1 %collective-permute-start.4 = (f32[2,32,512]{2,1,0:T(8,128)}, f32[2,32,512]{2,1,0:T(8,128)S(1)}, u32[]{:S(2)}, u32[]{:S(2)}) collective-permute-start(f32[2,32,512]{2,1,0:T(8,128)} %get-tuple-element.21), channel_id=1, source_target_pairs={{0,56},{8,0},{16,8},{24,16},{32,24},{40,32},{48,40},{56,48},{1,57}... | collective-permute-start | bytes 393224 | tf_op jit(solution)/shard_map/halo_exchange/ppermute | solution.py:22
  23.3 26.9 %copy-start = (f32[1,32,32,512]{3,2,1,0:T(8,128)S(1)}, f32[1,32,32,512]{3,2,1,0:T(8,128)}, u32[]{:S(2)}) copy-start(f32[1,32,32,512]{3,2,1,0:T(8,128)} %param.13) | copy-start | bytes 6291460
  23.3 26.8 %collective-permute-start.5 = (f32[2,32,512]{2,1,0:T(8,128)}, f32[2,32,512]{2,1,0:T(8,128)S(1)}, u32[]{:S(2)}, u32[]{:S(2)}) collective-permute-start(f32[2,32,512]{2,1,0:T(8,128)} %get-tuple-element.22), channel_id=1, source_target_pairs={{0,1},{1,2},{2,3},{3,4},{4,5},{5,6},{6,7},{7,0},{8,9},{9,10},{10,1... | collective-permute-start | bytes 393224 | tf_op jit(solution)/shard_map/halo_exchange/ppermute | solution.py:22
  25.7 24.4 %collective-permute-start.6 = (f32[2,32,512]{2,1,0:T(8,128)}, f32[2,32,512]{2,1,0:T(8,128)S(1)}, u32[]{:S(2)}, u32[]{:S(2)}) collective-permute-start(f32[2,32,512]{2,1,0:T(8,128)} %get-tuple-element.23), channel_id=1, source_target_pairs={{0,7},{1,0},{2,1},{3,2},{4,3},{5,4},{6,5},{7,6},{8,15},{9,8},{10,9... | collective-permute-start | bytes 393224 | tf_op jit(solution)/shard_map/halo_exchange/ppermute | solution.py:22
  50.2 1.6 %copy-start.1 = (f32[32,32,512]{2,1,0:T(8,128)S(1)}, f32[32,32,512]{2,1,0:T(8,128)}, u32[]{:S(2)}) copy-start(f32[32,32,512]{2,1,0:T(8,128)} %by_hi.1) | copy-start | bytes 6291460
  51.8 1.6 %copy-start.3 = (f32[32,32,512]{2,1,0:T(8,128)S(1)}, f32[32,32,512]{2,1,0:T(8,128)}, u32[]{:S(2)}) copy-start(f32[32,32,512]{2,1,0:T(8,128)} %param.10) | copy-start | bytes 6291460
  54.6 1.6 %copy-start.9 = (f32[1,32,32,512]{3,2,1,0:T(8,128)S(1)}, f32[1,32,32,512]{3,2,1,0:T(8,128)}, u32[]{:S(2)}) copy-start(f32[1,32,32,512]{3,2,1,0:T(8,128)} %param.12) | copy-start | bytes 6291460
  64.7 20.9 %copy-start.8 = (f32[2,1024,128]{2,1,0:T(8,128)S(1)}, f32[2,1024,128]{2,1,0:T(8,128)}, u32[]{:S(2)}) copy-start(f32[2,1024,128]{2,1,0:T(8,128)} %sources.1.refs_12_) | copy-start | bytes 3145732
  64.7 14.3 %collective-permute-start.7 = (f32[32,512]{1,0:T(8,128)}, f32[32,512]{1,0:T(8,128)S(1)}, u32[]{:S(2)}, u32[]{:S(2)}) collective-permute-start(f32[32,512]{1,0:T(8,128)} %get-tuple-element.25), channel_id=1, source_target_pairs={{0,8},{8,16},{16,24},{24,32},{32,40},{40,48},{48,56},{56,0},{1,9},... | collective-permute-start | bytes 196616 | tf_op jit(solution)/shard_map/ppermute | solution.py:22
  64.8 15.1 %collective-permute-start.8 = (f32[32,512]{1,0:T(8,128)}, f32[32,512]{1,0:T(8,128)S(1)}, u32[]{:S(2)}, u32[]{:S(2)}) collective-permute-start(f32[32,512]{1,0:T(8,128)} %get-tuple-element.26), channel_id=1, source_target_pairs={{0,56},{8,0},{16,8},{24,16},{32,24},{40,32},{48,40},{56,48},{1,57}... | collective-permute-start | bytes 196616 | tf_op jit(solution)/shard_map/ppermute | solution.py:22
  72.3 13.4 %collective-permute-start.9 = (f32[32,512]{1,0:T(8,128)}, f32[32,512]{1,0:T(8,128)}, u32[]{:S(2)}, u32[]{:S(2)}) collective-permute-start(f32[32,512]{1,0:T(8,128)} %get-tuple-element.27), channel_id=1, source_target_pairs={{0,1},{1,2},{2,3},{3,4},{4,5},{5,6},{6,7},{7,0},{8,9},{9,10},{10,1... | collective-permute-start | bytes 196616 | tf_op jit(solution)/shard_map/ppermute | solution.py:22
  75.3 10.3 %collective-permute-start.10 = (f32[32,512]{1,0:T(8,128)}, f32[32,512]{1,0:T(8,128)}, u32[]{:S(2)}, u32[]{:S(2)}) collective-permute-start(f32[32,512]{1,0:T(8,128)} %get-tuple-element.28), channel_id=1, source_target_pairs={{0,7},{1,0},{2,1},{3,2},{4,3},{5,4},{6,5},{7,6},{8,15},{9,8},{10,9... | collective-permute-start | bytes 196616 | tf_op jit(solution)/shard_map/ppermute | solution.py:22
  75.3 10.3 %copy-start.2 = (f32[32,32,512]{2,1,0:T(8,128)S(1)}, f32[32,32,512]{2,1,0:T(8,128)}, u32[]{:S(2)}) copy-start(f32[32,32,512]{2,1,0:T(8,128)} %by_hi.1) | copy-start | bytes 6291460
  78.9 18.5 %collective-permute-start = (f32[2,16,256]{2,1,0:T(8,128)S(1)}, f32[2,16,256]{2,1,0:T(8,128)S(1)}, u32[]{:S(2)}, u32[]{:S(2)}) collective-permute-start(f32[2,16,256]{2,1,0:T(8,128)S(1)} %get-tuple-element.17), channel_id=1, source_target_pairs={{0,56},{8,0},{16,8},{24,16},{32,24},{40,32},{48,40},{56,48},{1,57}... | collective-permute-start | bytes 98312 | tf_op jit(solution)/shard_map/ppermute | solution.py:22
  79.0 18.4 %collective-permute-start.1 = (f32[2,16,256]{2,1,0:T(8,128)S(1)}, f32[2,16,256]{2,1,0:T(8,128)S(1)}, u32[]{:S(2)}, u32[]{:S(2)}) collective-permute-start(f32[2,16,256]{2,1,0:T(8,128)S(1)} %get-tuple-element.18), channel_id=1, source_target_pairs={{0,7},{1,0},{2,1},{3,2},{4,3},{5,4},{6,5},{7,6},{8,15},{9,8},{10,9... | collective-permute-start | bytes 98312 | tf_op jit(solution)/shard_map/ppermute | solution.py:22
  79.9 17.5 %collective-permute-start.2 = (f32[2,8,256]{2,1,0:T(8,128)S(1)}, f32[2,8,256]{2,1,0:T(8,128)S(1)}, u32[]{:S(2)}, u32[]{:S(2)}) collective-permute-start(f32[2,8,256]{2,1,0:T(8,128)S(1)} %get-tuple-element.19), channel_id=1, source_target_pairs={{0,63},{1,56},{2,57},{3,58},{4,59},{5,60},{6,61},{7,62},{8,7},{9,0... | collective-permute-start | bytes 49160 | tf_op jit(solution)/shard_map/ppermute | solution.py:411
  85.6 1.6 %copy-start.4 = (f32[32,32,512]{2,1,0:T(8,128)S(1)}, f32[32,32,512]{2,1,0:T(8,128)}, u32[]{:S(2)}) copy-start(f32[32,32,512]{2,1,0:T(8,128)} %param.10) | copy-start | bytes 6291460
  88.8 8.6 %copy-start.11 = (s32[1,3]{1,0:T(1,128)S(1)}, s32[1,3]{1,0:T(1,128)}, u32[]{:S(2)}) copy-start(s32[1,3]{1,0:T(1,128)} %source.1) | copy-start | bytes 40
  97.4 1.6 %copy-start.6 = (f32[1024,512]{1,0:T(8,128)S(1)}, f32[1024,512]{1,0:T(8,128)}, u32[]{:S(2)}) copy-start(f32[1024,512]{1,0:T(8,128)} %advance1.1.second) | copy-start | bytes 6291460
  (3 other events, 4.2 us)

commit v2 on v1

--- a/solution.py
+++ b/solution.py
@@ -11,10 +11,12 @@
 DEPTH = 512
 COARSE = 256
 CHUNKS = 4
+PER = PLANES // CHUNKS
 SPAN = ROWS // CHUNKS
 VMEM = pl.BlockSpec(memory_space=pltpu.VMEM)
 SMEM = pl.BlockSpec(memory_space=pltpu.SMEM)
 ANY = pl.BlockSpec(memory_space=pl.ANY)
+ROOM = pltpu.CompilerParams(vmem_limit_bytes=16 << 20)
 
 
 def rotate(block, axis, step):
@@ -52,9 +54,10 @@
         in_specs=[plane_lo, plane_hi, rows_lo, rows_hi] * 2,
         out_specs=[out] * 4,
         out_shape=[f32(2, PLANES, DEPTH)] * 4,
+        compiler_params=ROOM,
         cost_estimate=pl.CostEstimate(flops=0, bytes_accessed=3 << 20, transcendentals=0),
         name="faces",
-    )(*([field] * 4 + [buoyancy] * 4))
+    )(*([in_hbm(field)] * 4 + [in_hbm(buoyancy)] * 4))
 
 
 def sources_kernel(cells, data, out):
@@ -93,6 +96,7 @@
         out_specs=VMEM,
         out_shape=f32(2, ROWS, 128),
         cost_estimate=pl.CostEstimate(flops=1 << 29, bytes_accessed=2 << 20, transcendentals=0),
+        compiler_params=ROOM,
         name="sources",
     )(cells, data)
 
@@ -110,128 +114,184 @@
         out_specs=VMEM,
         out_shape=jax.ShapeDtypeStruct((512, 1024), jnp.bfloat16),
         cost_estimate=pl.CostEstimate(flops=1 << 20, bytes_accessed=2 << 20, transcendentals=0),
+        compiler_params=ROOM,
         name="onehots",
     )(ids)
 
 
-def step_kernel(
-    field, older, buoy, stiff, hx_lo, hx_hi, hy_lo, hy_hi, bx_lo, bx_hi, by_lo, by_hi, src,
-    out, *rest, step, give_faces,
-):
-    if give_faces:
-        sx_lo, sx_hi, sy_lo, sy_hi = rest[:4]
-        rest = rest[4:]
-    f_ext, b_ext, s_buf, o_buf, n_buf, in_sem, out_sem = rest
+def in_hbm(x):
+    return pltpu.with_memory_space_constraint(x, pltpu.HBM)
+
+
+def inner_kernel(field, older, buoy, stiff, src, *rest, step):
+    if step == 1:
+        fixed, rest = rest[:4], rest[4:]
+        out, saved, f_buf, b_buf, s_buf, o_buf, in_sem, out_sem = rest
+        n_buf = out
+    else:
+        out, faces_out, stiff_out = rest[0], rest[1:5], rest[5:9]
+        f_buf, b_buf, s_buf, o_buf, n_buf, in_sem, out_sem = rest[9:]
     copies = []
     for chunk in range(CHUNKS):
         part = pl.ds(chunk * SPAN, SPAN)
-        shifted = pl.ds(chunk * SPAN + PLANES, SPAN)
+        pairs = ((field, f_buf), (buoy, b_buf), (stiff, s_buf), (older, o_buf))
         group = [
-            pltpu.make_async_copy(field.at[part], f_ext.at[shifted], in_sem.at[chunk, 0]),
-            pltpu.make_async_copy(buoy.at[part], b_ext.at[shifted], in_sem.at[chunk, 1]),
-            pltpu.make_async_copy(stiff.at[part], s_buf.at[part], in_sem.at[chunk, 2]),
-            pltpu.make_async_copy(older.at[part], o_buf.at[part], in_sem.at[chunk, 3]),
+            pltpu.make_async_copy(hbm.at[part], buf.at[part], in_sem.at[chunk, k])
+            for k, (hbm, buf) in enumerate(pairs)
         ]
         for copy in group:
             copy.start()
         copies.append(group)
-    gx = lax.axis_index("gx")
-    gy = lax.axis_index("gy")
-    x_lo = jnp.where(gx > 0, 1.0, 0.0)
-    x_hi = jnp.where(gx < lax.axis_size("gx") - 1, 1.0, 0.0)
-    y_lo = jnp.where(gy > 0, 1.0, 0.0)
-    y_hi = jnp.where(gy < lax.axis_size("gy") - 1, 1.0, 0.0)
-    f_ext[0:PLANES] = hx_lo[...] * x_lo
-    b_ext[0:PLANES] = bx_lo[...] * x_lo
-    f_ext[ROWS + PLANES : ROWS + 2 * PLANES] = hx_hi[...] * x_hi
-    b_ext[ROWS + PLANES : ROWS + 2 * PLANES] = bx_hi[...] * x_hi
-    row_id = lax.broadcasted_iota(jnp.int32, (PLANES, DEPTH), 0)
-    lane_id = lax.broadcasted_iota(jnp.int32, (PLANES, DEPTH), 1)
-    per = SPAN // PLANES
+    row8 = lax.broadcasted_iota(jnp.int32, (8, DEPTH), 0)
+    lane128 = lax.broadcasted_iota(jnp.int32, (PLANES, 128), 1)
     out_copies = []
-    for group in copies[0][:2]:
-        group.wait()
-    carry = (b_ext[0:PLANES] + b_ext[PLANES : 2 * PLANES]) * (
-        f_ext[PLANES : 2 * PLANES] - f_ext[0:PLANES]
-    )
+
+    def arrive(chunk):
+        for copy in copies[chunk][:2]:
+            copy.wait()
+        if step == 1:
+            if chunk == 0:
+                f_buf[0:PLANES, :] = fixed[0][0]
+            if chunk == CHUNKS - 1:
+                f_buf[ROWS - PLANES : ROWS, :] = fixed[1][0]
+            for x in range(chunk * PER, chunk * PER + PER):
+                f_buf[x * PLANES : x * PLANES + 1, :] = fixed[2][0, x : x + 1, :]
+                f_buf[x * PLANES + 31 : x * PLANES + 32, :] = fixed[3][0, x : x + 1, :]
+            part = pl.ds(chunk * SPAN, SPAN)
+            copy = pltpu.make_async_copy(f_buf.at[part], saved.at[part], out_sem.at[chunk])
+            copy.start()
+            out_copies.append(copy)
+
+    def plane(x, flux_before, last=False):
+        base = pl.multiple_of(x * PLANES, PLANES)
+        at = pl.ds(base, PLANES)
+        c = f_buf[at, :]
+        b = b_buf[at, :]
+        if last:
+            flux_x = jnp.zeros_like(c)
+        else:
+            nearby = pl.ds(base + PLANES, PLANES)
+            flux_x = (b + b_buf[nearby, :]) * (f_buf[nearby, :] - c)
+        flux_y = (b + pltpu.roll(b, PLANES - 1, 0)) * (pltpu.roll(c, PLANES - 1, 0) - c)
+        flux_y = jnp.concatenate(
+            [flux_y[0:24], jnp.where(row8 == 7, 0.0, flux_y[24:32])], axis=0
+        )
+        flux_z = (b + pltpu.roll(b, DEPTH - 1, 1)) * (pltpu.roll(c, DEPTH - 1, 1) - c)
+        flux_z = jnp.concatenate(
+            [flux_z[:, : DEPTH - 128], jnp.where(lane128 == 127, 0.0, flux_z[:, DEPTH - 128 :])],
+            axis=1,
+        )
+        total = (flux_x - flux_before) + (flux_y - pltpu.roll(flux_y, 1, 0))
+        total = total + (flux_z - pltpu.roll(flux_z, 1, 1))
+        head = slice(0, 128)
+        tail = slice(DEPTH - 128, DEPTH)
+        total = jnp.concatenate(
+            [
+                total[:, head] - jnp.where(lane128 == 0, b[:, head] * c[:, head], 0.0),
+                total[:, 128 : DEPTH - 128],
+                total[:, tail] - jnp.where(lane128 == 127, b[:, tail] * c[:, tail], 0.0),
+            ],
+            axis=1,
+        )
+        value = (2.0 * c - o_buf[at, :]) + (0.5 * s_buf[at, :]) * total
+        n_buf[at, 128:DEPTH] = value[:, 128:]
+        n_buf[at, head] = value[:, head] + src[step, at, :]
+        if step == 0:
+            faces_out[2][pl.ds(x, 1), :] = n_buf[pl.ds(base, 1), :]
+            faces_out[3][pl.ds(x, 1), :] = n_buf[pl.ds(base + PLANES - 1, 1), :]
+            stiff_out[2][pl.ds(x, 1), :] = s_buf[pl.ds(base, 1), :]
+            stiff_out[3][pl.ds(x, 1), :] = s_buf[pl.ds(base + PLANES - 1, 1), :]
+        return flux_x
+
+    arrive(0)
+    flux = jnp.zeros((PLANES, DEPTH), jnp.float32)
     for chunk in range(CHUNKS):
         for copy in copies[chunk][2:]:
             copy.wait()
         if chunk + 1 < CHUNKS:
-            for copy in copies[chunk + 1][:2]:
-                copy.wait()
-        first = chunk * per
-
-        def plane(k, flux_before, first=first):
-            x = first + k
-            base = pl.multiple_of((x + 1) * PLANES, PLANES)
-            c = f_ext[pl.ds(base, PLANES), :]
-            b = b_ext[pl.ds(base, PLANES), :]
-            c_next = f_ext[pl.ds(base + PLANES, PLANES), :]
-            b_next = b_ext[pl.ds(base + PLANES, PLANES), :]
-            flux_x = (b + b_next) * (c_next - c)
-            lo_f = hy_lo[pl.ds(x, 1), :] * y_lo
-            lo_b = by_lo[pl.ds(x, 1), :] * y_lo
-            hi_f = hy_hi[pl.ds(x, 1), :] * y_hi
-            hi_b = by_hi[pl.ds(x, 1), :] * y_hi
-            c_up = jnp.where(row_id == PLANES - 1, hi_f, pltpu.roll(c, PLANES - 1, 0))
-            b_up = jnp.where(row_id == PLANES - 1, hi_b, pltpu.roll(b, PLANES - 1, 0))
-            flux_y = (b + b_up) * (c_up - c)
-            first_flux = (b[0:1, :] + lo_b) * (c[0:1, :] - lo_f)
-            flux_y_before = jnp.where(row_id == 0, first_flux, pltpu.roll(flux_y, 1, 0))
-            edge_flux = b * c
-            flux_z = (b + pltpu.roll(b, DEPTH - 1, 1)) * (pltpu.roll(c, DEPTH - 1, 1) - c)
-            flux_z = jnp.where(lane_id == DEPTH - 1, -edge_flux, flux_z)
-            flux_z_before = jnp.where(lane_id == 0, edge_flux, pltpu.roll(flux_z, 1, 1))
-            total = (flux_x - flux_before) + (flux_y - flux_y_before) + (flux_z - flux_z_before)
-            at = pl.multiple_of(x * PLANES, PLANES)
-            new = (2.0 * c - o_buf[pl.ds(at, PLANES), :]) + (
-                0.5 * s_buf[pl.ds(at, PLANES), :]
-            ) * total
-            n_buf[pl.ds(at, PLANES), :] = new
-            head = new[:, 0:128] + src[step, pl.ds(at, PLANES), :]
-            n_buf[pl.ds(at, PLANES), 0:128] = head
-            if give_faces:
-                sy_lo[pl.ds(x, 1), :] = n_buf[pl.ds(at, 1), :]
-                sy_hi[pl.ds(x, 1), :] = n_buf[pl.ds(at + PLANES - 1, 1), :]
-            return flux_x
-
-        carry = lax.fori_loop(0, per, plane, carry)
-        part = pl.ds(chunk * SPAN, SPAN)
-        copy = pltpu.make_async_copy(n_buf.at[part], out.at[part], out_sem.at[chunk])
-        copy.start()
-        out_copies.append(copy)
-    if give_faces:
-        sx_lo[...] = n_buf[0:PLANES]
-        sx_hi[...] = n_buf[ROWS - PLANES : ROWS]
+            arrive(chunk + 1)
+            flux = lax.fori_loop(chunk * PER, chunk * PER + PER, plane, flux, unroll=4)
+        else:
+            flux = lax.fori_loop(chunk * PER, chunk * PER + PER - 4, plane, flux, unroll=4)
+            for x in range(PLANES - 4, PLANES):
+                flux = plane(x, flux, x == PLANES - 1)
+        if step == 0:
+            part = pl.ds(chunk * SPAN, SPAN)
+            copy = pltpu.make_async_copy(n_buf.at[part], out.at[part], out_sem.at[chunk])
+            copy.start()
+            out_copies.append(copy)
+    if step == 0:
+        faces_out[0][...] = n_buf[0:PLANES, :]
+        faces_out[1][...] = n_buf[ROWS - PLANES : ROWS, :]
+        stiff_out[0][...] = s_buf[0:PLANES, :]
+        stiff_out[1][...] = s_buf[ROWS - PLANES : ROWS, :]
     for copy in out_copies:
         copy.wait()
 
 
-def advance(field, older, buoy, stiff, halos, buoy_halos, src, step, give_faces):
-    out_shape = [f32(ROWS, DEPTH)]
-    out_specs = [ANY]
-    if give_faces:
-        out_shape += [f32(PLANES, DEPTH)] * 4
-        out_specs += [VMEM] * 4
-    return pl.pallas_call(
-        lambda *refs: step_kernel(*refs, step=step, give_faces=give_faces),
-        in_specs=[ANY] * 4 + [VMEM] * 9,
+def inner(field, older, buoy, stiff, src, fixed, step):
+    big = pltpu.VMEM((ROWS, DEPTH), jnp.float32)
+    if step == 0:
+        out_shape = [pltpu.HBM((ROWS, DEPTH), jnp.float32)] + [f32(PLANES, DEPTH)] * 8
+        out_specs = [ANY] + [VMEM] * 8
+    else:
+        out_shape = [big, f32(ROWS, DEPTH)]
+        out_specs = [VMEM, ANY]
+    return pl.pallas_call(
+        lambda *refs: inner_kernel(*refs, step=step),
+        in_specs=[ANY] * 4 + [VMEM] * (1 + len(fixed)),
         out_specs=out_specs,
         out_shape=out_shape,
-        scratch_shapes=[
-            pltpu.VMEM((ROWS + 2 * PLANES, DEPTH), jnp.float32),
-            pltpu.VMEM((ROWS + 2 * PLANES, DEPTH), jnp.float32),
-            pltpu.VMEM((ROWS, DEPTH), jnp.float32),
-            pltpu.VMEM((ROWS, DEPTH), jnp.float32),
-            pltpu.VMEM((ROWS, DEPTH), jnp.float32),
-            pltpu.SemaphoreType.DMA((CHUNKS, 4)),
-            pltpu.SemaphoreType.DMA((CHUNKS,)),
-        ],
-        compiler_params=pltpu.CompilerParams(vmem_limit_bytes=32 << 20),
+        scratch_shapes=[big] * (5 - step)
+        + [pltpu.SemaphoreType.DMA((CHUNKS, 4)), pltpu.SemaphoreType.DMA((CHUNKS,))],
+        compiler_params=ROOM,
         cost_estimate=pl.CostEstimate(flops=20 << 20, bytes_accessed=10 << 20, transcendentals=0),
-        name="advance%d" % step,
-    )(field, older, buoy, stiff, *halos, *buoy_halos, src)
+        name="inner%d" % step,
+    )(in_hbm(field), in_hbm(older), in_hbm(buoy), in_hbm(stiff), src, *fixed)
+
+
+def edge_terms(own_b, far_b, own_f, far_f, stiff):
+    gx = lax.axis_index("gx")
+    gy = lax.axis_index("gy")
+    keep = [
+        jnp.where(gx > 0, 1.0, 0.0),
+        jnp.where(gx < lax.axis_size("gx") - 1, 1.0, 0.0),
+        jnp.where(gy > 0, 1.0, 0.0),
+        jnp.where(gy < lax.axis_size("gy") - 1, 1.0, 0.0),
+    ]
+    terms = []
+    for side in range(4):
+        coef = 0.5 * (own_b[side][1] + keep[side] * far_b[side][1])
+        flux = coef * (keep[side] * far_f[side][0] - own_f[side][0])
+        terms.append(stiff[side][...] * flux)
+    return terms
+
+
+def fix_kernel(*refs):
+    own, far, value, stiff, out = (refs[4 * k : 4 * k + 4] for k in range(5))
+    terms = refs[20]
+    for side, term in enumerate(edge_terms(own, far, own, far, stiff)):
+        terms[side] = term
+        out[side][0] = value[side][...] + term
+    for side in range(4):
+        for end in range(2):
+            row = slice(31 * end, 31 * end + 1)
+            other = (2 if side < 2 else 0) + end
+            at = slice(31 * (side % 2), 31 * (side % 2) + 1)
+            out[side][0, row, :] += terms[other, at, :]
+
+
+def fix_faces(own, far, values, stiff):
+    return pl.pallas_call(
+        fix_kernel,
+        in_specs=[VMEM] * 16,
+        out_specs=[VMEM] * 4,
+        out_shape=[f32(1, PLANES, DEPTH)] * 4,
+        scratch_shapes=[pltpu.VMEM((4, PLANES, DEPTH), jnp.float32)],
+        compiler_params=ROOM,
+        cost_estimate=pl.CostEstimate(flops=1 << 20, bytes_accessed=2 << 20, transcendentals=0),
+        name="fix_faces",
+    )(*own, *far, *values, *stiff)
 
 
 def interpolation():
@@ -269,13 +329,19 @@
         out_specs=[VMEM] * 4,
         out_shape=[f32(512, DEPTH), f32(2, 16, COARSE), f32(2, 16, COARSE), f32(2, 8, COARSE)],
         scratch_shapes=[pltpu.VMEM((2, 512, 128), jnp.float32)],
-        compiler_params=pltpu.CompilerParams(vmem_limit_bytes=32 << 20),
+        compiler_params=ROOM,
         cost_estimate=pl.CostEstimate(flops=1 << 30, bytes_accessed=3 << 20, transcendentals=0),
         name="coarse_tiles",
     )(received, onehot)
 
 
-def image_kernel(source, along, rim_x, rim_y, corner, first, second, out, rims, rim_along, fine):
+def image_kernel(source, along, rim_x, rim_y, corner, first_hbm, second, *rest):
+    own, far, own2, far2, stiff = (rest[4 * k : 4 * k + 4] for k in range(5))
+    image, saved, rims, rim_along, fine, out, first, terms, third, sem = rest[20:]
+    load = pltpu.make_async_copy(first_hbm, first, sem.at[0])
+    load.start()
+    for side, term in enumerate(edge_terms(own, far, own2, far2, stiff)):
+        terms[side] = term
     gx = lax.axis_index("gx")
     gy = lax.axis_index("gy")
     keep_x = jnp.where(gx < lax.axis_size("gx") - 1, 1.0, 0.0)
@@ -308,10 +374,20 @@
     z = (lax.broadcasted_iota(jnp.int32, (PLANES, DEPTH), 1) - source[0, 2]).astype(jnp.float32)
     decay_yz = jnp.exp((y * y + z * z) * scale)
     x_base = gx * PLANES - source[0, 0]
+    load.wait()
+    copies = []
     for k in range(16):
         for odd in range(2):
             x = 2 * k + odd
             at = slice(x * PLANES, (x + 1) * PLANES)
+            value = second[at, :]
+            if x == 0:
+                value = value + terms[0]
+            if x == PLANES - 1:
+                value = value + terms[1]
+            third[at, :] = value
+            third[x * PLANES : x * PLANES + 1, :] += terms[2, x : x + 1, :]
+            third[x * PLANES + 31 : x * PLANES + 32, :] += terms[3, x : x + 1, :]
             dx = jnp.full((1, 128), x_base + x, jnp.int32).astype(jnp.float32)
             decay = jnp.exp((dx * dx) * scale)
             for part in range(4):
@@ -325,25 +401,39 @@
                         snap = 0.5 * (snap + fine[part, start + PLANES : start + 2 * PLANES, :])
                     snaps.append(snap)
                 out[at, lanes] = taper * (
-                    snaps[0] * first[at, lanes] + snaps[1] * second[at, lanes]
+                    snaps[0] * first[at, lanes] + snaps[1] * third[at, lanes]
                 )
-
-
-def imaging(source, along, rims, first, second):
+        if k % 4 == 3:
+            rows = pl.ds((k - 3) * 2 * PLANES, 8 * PLANES)
+            for pos, (here, there) in enumerate(((out, image), (third, saved))):
+                slot = 1 + 2 * (k // 4) + pos
+                copies.append(pltpu.make_async_copy(here.at[rows], there.at[rows], sem.at[slot]))
+                copies[-1].start()
+    for copy in copies:
+        copy.wait()
+
+
+def imaging(source, along, rims, first, second, edges):
+    big = pltpu.VMEM((ROWS, DEPTH), jnp.float32)
     return pl.pallas_call(
         image_kernel,
-        in_specs=[SMEM] + [VMEM] * 6,
-        out_specs=VMEM,
-        out_shape=f32(ROWS, DEPTH),
+        in_specs=[SMEM] + [VMEM] * 4 + [ANY] + [VMEM] * 21,
+        out_specs=[ANY, ANY],
+        out_shape=[f32(ROWS, DEPTH)] * 2,
         scratch_shapes=[
             pltpu.VMEM((80, COARSE), jnp.float32),
             pltpu.VMEM((80, DEPTH), jnp.float32),
             pltpu.VMEM((4, 2 * 17 * PLANES, 128), jnp.float32),
+            big,
+            big,
+            pltpu.VMEM((4, PLANES, DEPTH), jnp.float32),
+            big,
+            pltpu.SemaphoreType.DMA((9,)),
         ],
-        compiler_params=pltpu.CompilerParams(vmem_limit_bytes=32 << 20),
+        compiler_params=ROOM,
         cost_estimate=pl.CostEstimate(flops=20 << 20, bytes_accessed=8 << 20, transcendentals=0),
         name="imaging",
-    )(source, along, *rims, first, second)
+    )(source, along, *rims, in_hbm(first), second, *edges)
 
 
 def per_device(
@@ -363,44 +453,33 @@
     stiff = stiffness.reshape(ROWS, DEPTH)
     buoy = buoyancy.reshape(ROWS, DEPTH)
 
-    with jax.named_scope("halo_exchange"):
-        sx_lo, sx_hi, sy_lo, sy_hi = faces(current_field[0], buoyancy)
-        hx_lo = rotate(sx_hi, "gx", 1)
-        hx_hi = rotate(sx_lo, "gx", -1)
-        hy_lo = rotate(sy_hi, "gy", 1)
-        hy_hi = rotate(sy_lo, "gy", -1)
-    both = (hx_lo, hx_hi, hy_lo, hy_hi)
-    halos = [h[0] for h in both]
-    buoy_halos = [h[1] for h in both]
-
+    own = faces(current_field[0], buoyancy)
+    far = exchange(own)
+    tiles, own = lax.optimization_barrier((stored_tiles, own))
     received = lax.all_to_all(
-        stored_tiles[0, 0], ("shot", "gx"), split_axis=0, concat_axis=0, tiled=True
+        tiles[0, 0], ("shot", "gx"), split_axis=0, concat_axis=0, tiled=True
     ).reshape(1024, COARSE)
     slot = lax.broadcasted_iota(jnp.int32, (32, 32), 1)
     ids = jnp.where(slot < tile_counts[0, 0][:, None], tile_ids[0, 0], -1).reshape(1, 1024)
     onehot = onehots(ids)
     src = sources(receiver_cells[0], receiver_data[0])
-
-    second, sx_lo, sx_hi, sy_lo, sy_hi = advance(
-        current, older, buoy, stiff, halos, buoy_halos, src, 0, True
-    )
-    halos = [
-        rotate(sx_hi, "gx", 1),
-        rotate(sx_lo, "gx", -1),
-        rotate(sy_hi, "gy", 1),
-        rotate(sy_lo, "gy", -1),
-    ]
-    (third,) = advance(second, current, buoy, stiff, halos, buoy_halos, src, 1, False)
+    partial, *rest = inner(current, older, buoy, stiff, src, [], 0)
+    values, stiff_faces = rest[:4], rest[4:]
+    own2 = fix_faces(own, far, values, stiff_faces)
+    far2 = exchange(own2)
 
     along, rim_x, rim_y, corner = coarse_tiles(received, onehot)
-    rims = [
-        rotate(rim_x, "gx", -1),
-        rotate(rim_y, "gy", -1),
-        diagonal(corner),
-    ]
-    image = imaging(source_cell, along, rims, second, third)
+    rims = [rotate(rim_x, "gx", -1), rotate(rim_y, "gy", -1), diagonal(corner)]
+    third, last_older = inner(partial, current, buoy, stiff, src, own2, 1)
+    edges = [*own, *far, *own2, *far2, *stiff_faces]
+    image, last_current = imaging(source_cell, along, rims, last_older, third, edges)
     shape = current_field.shape
-    return image.reshape(shape), second.reshape(shape), third.reshape(shape)
+    return image.reshape(shape), last_older.reshape(shape), last_current.reshape(shape)
+
+
+def exchange(own):
+    x_lo, x_hi, y_lo, y_hi = own
+    return [rotate(x_hi, "gx", 1), rotate(x_lo, "gx", -1), rotate(y_hi, "gy", 1), rotate(y_lo, "gy", -1)]
 
 
 def diagonal(block):

time: 103 us -> 87 us (0.84)
  the two profiles are of different devices: /device:TPU:49 before, /device:TPU:1 now
where the time goes in v2:
time: 87 us; the launch traced here: 86.6 us
  starting transfers between devices  44.6 us (51%)
  Pallas kernels  24.8 us (29%)
  waiting for transfers between devices  15.8 us (18%)
  between operations  1.05 us (1%)
    ppermute x10, starting transfers between devices, rotate(): lax.ppermute(block, axis, [(i, (i + step) % count) for i in range(count)])  26.6 us
    ppermute x10, waiting for transfers between devices, rotate(): lax.ppermute(block, axis, [(i, (i + step) % count) for i in range(count)])  15.8 us
    all_to_all x1, starting transfers between devices, per_device(): lax.all_to_all(tiles[0, 0], ('shot', 'gx'), split_axis=0, concat_axis=0,...  14.6 us
    pallas_call x2, Pallas kernels, inner(): pl.pallas_call(lambda *refs: inner_kernel(*refs, step=step), in_specs=[AN...  12.8 us
    pallas_call x1, Pallas kernels, imaging(): pl.pallas_call(image_kernel, in_specs=[SMEM] + [VMEM] * 4 + [ANY] + [VMEM...  5.69 us
    ppermute x1, starting transfers between devices, diagonal(): return lax.ppermute(block, ('gx', 'gy'), route)  3.4 us
    pallas_call x1, Pallas kernels, faces(): pl.pallas_call(faces_kernel, grid=(1,), in_specs=[plane_lo, plane_hi, row...  2.32 us
    pallas_call x1, Pallas kernels, fix_faces(): pl.pallas_call(fix_kernel, in_specs=[VMEM] * 16, out_specs=[VMEM] * 4, ou...  1.94 us
  transfers between devices with their start and end apart: 12, of which 2 were waited for; matrix products, arithmetic and copies ran while one was open for 0% of the time, Pallas kernels for 19%

profile of v2, /device:TPU:1, one launch (start us, length us, event | category | flops | bytes accessed | tf_op | source)
XLA Modules:
  0.0 86.6 jit_solution(746466633919736759)
XLA Ops:
  0.6 2.3 %faces.1 = (f32[2,32,512]{2,1,0:T(8,128)S(1)}, f32[2,32,512]{2,1,0:T(8,128)S(1)}, f32[2,32,512]{2,1,0:T(8,128)S(1)}, f32[2,32,512]{2,1,0:T(8,128)}) custom-call(f32[32,32,512]{2,1,0:T(8,128)} %bitcast.20, f32[32,32,512]{2,1,0:T(8,128)} %bitcast.21, f32[32,32,512]{2,1,0:T(8,128)} %bitcast.22, f32[32,32,512]{2,1,0:T(8,128)} %bitcast.23, f32[32,32,512]{2,1,0:T(8,128)} %by_hi.1, ...), custom_call_target="tpu_custom_call" | custom-call | bytes 3145728 | tf_op jit(solution)/shard_map/faces/pallas_call | solution.py:51
  3.0 0.0 copy-start.9
  3.0 14.6 %all-to-all-start = ((f32[32,32,256]{2,1,0:T(8,128)}), f32[32,32,256]{2,1,0:T(8,128)S(1)}, u32[]{:S(2)}, u32[]{:S(2)}) async-start(f32[32,32,256]{2,1,0:T(8,128)} %bitcast.1), calls=%async_computation | async-start | bytes 2097152 | tf_op jit(solution)/shard_map/all_to_all | solution.py:459
  17.6 7.3 %collective-permute-start.4 = (f32[2,32,512]{2,1,0:T(8,128)S(1)}, f32[2,32,512]{2,1,0:T(8,128)}, u32[]{:S(2)}, u32[]{:S(2)}) collective-permute-start(f32[2,32,512]{2,1,0:T(8,128)S(1)} %get-tuple-element.43.refs_0_.rest_0_), channel_id=1, source_target_pairs={{0,56},{8,0},{16,8},{24,16},{32,24},{40,32},{48,40},{56,48},{1,57}... | collective-permute-start | bytes 393224 | tf_op jit(solution)/shard_map/ppermute | solution.py:24
  24.9 1.5 %collective-permute-start.6 = (f32[2,32,512]{2,1,0:T(8,128)S(1)}, f32[2,32,512]{2,1,0:T(8,128)}, u32[]{:S(2)}, u32[]{:S(2)}) collective-permute-start(f32[2,32,512]{2,1,0:T(8,128)S(1)} %get-tuple-element.45.refs_2_.rest_2_), channel_id=1, source_target_pairs={{0,7},{1,0},{2,1},{3,2},{4,3},{5,4},{6,5},{7,6},{8,15},{9,8},{10,9... | collective-permute-start | bytes 393224 | tf_op jit(solution)/shard_map/ppermute | solution.py:24
  26.5 0.6 collective-permute-start.5
  27.1 0.1 squeeze.17
  27.2 0.1 iota_compare_fusion
  27.2 0.1 lt.23
  27.4 0.2 onehots.1.onehot
  27.6 0.8 sources.1.refs_4_
  28.4 6.3 %inner0.1 = (f32[1024,512]{1,0:T(8,128)}, f32[32,512]{1,0:T(8,128)S(1)}, f32[32,512]{1,0:T(8,128)S(1)}, f32[32,512]{1,0:T(8,128)S(1)}, f32[32,512]{1,0:T(8,128)S...) custom-call(f32[1024,512]{1,0:T(8,128)} %bitcast.24, ...), custom_call_target="tpu_custom_call" | custom-call | flops 20971520 | bytes 10485760 | tf_op jit(solution)/shard_map/inner0/pallas_call | solution.py:240
  34.7 0.0 copy-start
  34.8 8.0 %collective-permute-done.3.refs_4_.rest_4_ = f32[2,32,512]{2,1,0:T(8,128)} collective-permute-done((f32[2,32,512]{2,1,0:T(8,128)S(1)}, f32[2,32,512]{2,1,0:T(8,128)}, u32[]{:S(2)}, u32[]{:S(2)}) %collective-permute-start.3) | collective-permute-done | bytes 131104 | tf_op jit(solution)/shard_map/ppermute | solution.py:24
  42.8 7.8 %collective-permute-done.6.refs_7_.rest_7_ = f32[2,32,512]{2,1,0:T(8,128)} collective-permute-done((f32[2,32,512]{2,1,0:T(8,128)S(1)}, f32[2,32,512]{2,1,0:T(8,128)}, u32[]{:S(2)}, u32[]{:S(2)}) %collective-permute-start.6) | collective-permute-done | bytes 131104 | tf_op jit(solution)/shard_map/ppermute | solution.py:24
  50.6 1.9 %fix_faces.1 = (f32[1,32,512]{2,1,0:T(8,128)}, f32[1,32,512]{2,1,0:T(8,128)}, f32[1,32,512]{2,1,0:T(8,128)}, f32[1,32,512]{2,1,0:T(8,128)}) custom-call(f32[2,32,512]{2,1,0:T(8,128)S(1)} %get-tuple-element.43.refs_0_.rest_0_, f32[2,32,512]{2,1,0:T(8,128)S(1)} %get-tuple-element.44.refs_1_.rest_1_, f32[2,32,512]{2,1,0:T(8,128)S(1)} %get-tuple-element.45.refs_2_.rest_2_, ...), custom_call_target="tpu_custom_call" | custom-call | flops 1048576 | bytes 2097152 | tf_op jit(solution)/shard_map/fix_faces/pallas_call | solution.py:285
  52.5 7.1 %collective-permute-start.8 = (f32[1,32,512]{2,1,0:T(8,128)}, f32[1,32,512]{2,1,0:T(8,128)}, u32[]{:S(2)}, u32[]{:S(2)}) collective-permute-start(f32[1,32,512]{2,1,0:T(8,128)} %get-tuple-element.55.refs_5_.rest_8_), channel_id=1, source_target_pairs={{0,56},{8,0},{16,8},{24,16},{32,24},{40,32},{48,40},{56,48},{1,57}... | collective-permute-start | bytes 196616 | tf_op jit(solution)/shard_map/ppermute | solution.py:24
  59.6 1.8 %collective-permute-start.9 = (f32[1,32,512]{2,1,0:T(8,128)}, f32[1,32,512]{2,1,0:T(8,128)}, u32[]{:S(2)}, u32[]{:S(2)}) collective-permute-start(f32[1,32,512]{2,1,0:T(8,128)} %get-tuple-element.58.refs_8_.rest_11_), channel_id=1, source_target_pairs={{0,1},{1,2},{2,3},{3,4},{4,5},{5,6},{6,7},{7,0},{8,9},{9,10},{10,1... | collective-permute-start | bytes 196616 | tf_op jit(solution)/shard_map/ppermute | solution.py:24
  61.4 1.0 %coarse_tiles.1 = (f32[512,512]{1,0:T(8,128)S(1)}, f32[2,16,256]{2,1,0:T(8,128)S(1)}, f32[2,16,256]{2,1,0:T(8,128)S(1)}, f32[2,8,256]{2,1,0:T(8,128)S(1)}) custom-call(f32[1024,256]{1,0:T(8,128)S(1)} %bitcast.17, bf16[512,1024]{1,0:T(8,128)(2,1)S(1)} %onehots.1.onehot), custom_call_target="tpu_custom_call" | custom-call | flops 1073741824 | bytes 3145728 | tf_op jit(solution)/shard_map/coarse_tiles/pallas_call | solution.py:326
  62.4 7.6 %collective-permute-start = (f32[2,16,256]{2,1,0:T(8,128)S(1)}, f32[2,16,256]{2,1,0:T(8,128)S(1)}, u32[]{:S(2)}, u32[]{:S(2)}) collective-permute-start(f32[2,16,256]{2,1,0:T(8,128)S(1)} %get-tuple-element.39), channel_id=1, source_target_pairs={{0,56},{8,0},{16,8},{24,16},{32,24},{40,32},{48,40},{56,48},{1,57}... | collective-permute-start | bytes 98312 | tf_op jit(solution)/shard_map/ppermute | solution.py:24
  70.0 0.7 collective-permute-start.1
  70.7 3.4 %collective-permute-start.2 = (f32[2,8,256]{2,1,0:T(8,128)S(1)}, f32[2,8,256]{2,1,0:T(8,128)S(1)}, u32[]{:S(2)}, u32[]{:S(2)}) collective-permute-start(f32[2,8,256]{2,1,0:T(8,128)S(1)} %get-tuple-element.41), channel_id=1, source_target_pairs={{0,63},{1,56},{2,57},{3,58},{4,59},{5,60},{6,61},{7,62},{8,7},{9,0... | collective-permute-start | bytes 49160 | tf_op jit(solution)/shard_map/ppermute | solution.py:490
  74.1 6.5 %inner1.1 = (f32[1024,512]{1,0:T(8,128)S(1)}, f32[1024,512]{1,0:T(8,128)}) custom-call(f32[1024,512]{1,0:T(8,128)} %get-tuple-element.42.refs_0_, f32[1024,512]{1,0:T(8,128)} %bitcast.25, f32[1024,512]{1,0:T(8,128)} %bitcast.27, f32[1024,512]{1,0:T(8,128)} %bitcast.29, f32[2,1024,128]{2,1,0:T(8,128)S(1)} %sources.1.refs_4_, ...), custom_call_target="tpu_custom_call" | custom-call | flops 20971520 | bytes 10485760 | tf_op jit(solution)/shard_map/inner1/pallas_call | solution.py:240
  80.7 5.7 %imaging.1 = (f32[1024,512]{1,0:T(8,128)}, f32[1024,512]{1,0:T(8,128)}) custom-call(s32[1,3]{1,0:T(1,128)S(1)} %copy-done.8, f32[512,512]{1,0:T(8,128)S(1)} %get-tuple-element.38.along, f32[2,16,256]{2,1,0:T(8,128)S(1)} %collective-permute-done.rim_x, f32[2,16,256]{2,1,0:T(8,128)S(1)} %collective-permute-done.1.rim_y, ...), custom_call_target="tpu_custom_call" | custom-call | flops 20971520 | bytes 8388608 | tf_op jit(solution)/shard_map/imaging/pallas_call | solution.py:418
  (39 shorter events, 0.1 us)
Async XLA Ops:
  2.9 24.1 %copy-start.10 = (s32[1,1,32,32]{3,2,1,0:T(8,128)S(1)}, s32[1,1,32,32]{3,2,1,0:T(8,128)}, u32[]{:S(2)}) copy-start(s32[1,1,32,32]{3,2,1,0:T(8,128)} %param.15) | copy-start | bytes 12292
  2.9 24.2 %copy-start.12 = (s32[1,1,32]{2,1,0:T(1,128)S(1)}, s32[1,1,32]{2,1,0:T(1,128)}, u32[]{:S(2)}) copy-start(s32[1,1,32]{2,1,0:T(1,128)} %param.16) | copy-start | bytes 388
  3.0 24.4 %copy-start.11 = (s32[1,3,1024]{2,0,1:T(1,128)S(1)}, s32[1,3,1024]{2,0,1:T(1,128)}, u32[]{:S(2)}) copy-start(s32[1,3,1024]{2,0,1:T(1,128)} %param.17) | copy-start | bytes 36868
  3.0 24.6 %copy-start.9 = (f32[1,2,1024]{2,1,0:T(2,128)S(1)}, f32[1,2,1024]{2,1,0:T(2,128)}, u32[]{:S(2)}) copy-start(f32[1,2,1024]{2,1,0:T(2,128)} %param.18) | copy-start | bytes 24580
  3.0 58.5 %all-to-all-start = ((f32[32,32,256]{2,1,0:T(8,128)}), f32[32,32,256]{2,1,0:T(8,128)S(1)}, u32[]{:S(2)}, u32[]{:S(2)}) async-start(f32[32,32,256]{2,1,0:T(8,128)} %bitcast.1), calls=%async_computation | async-start | bytes 2097152 | tf_op jit(solution)/shard_map/all_to_all | solution.py:459
  17.6 17.2 %collective-permute-start.4 = (f32[2,32,512]{2,1,0:T(8,128)S(1)}, f32[2,32,512]{2,1,0:T(8,128)}, u32[]{:S(2)}, u32[]{:S(2)}) collective-permute-start(f32[2,32,512]{2,1,0:T(8,128)S(1)} %get-tuple-element.43.refs_0_.rest_0_), channel_id=1, source_target_pairs={{0,56},{8,0},{16,8},{24,16},{32,24},{40,32},{48,40},{56,48},{1,57}... | collective-permute-start | bytes 393224 | tf_op jit(solution)/shard_map/ppermute | solution.py:24
  24.9 17.8 %collective-permute-start.3 = (f32[2,32,512]{2,1,0:T(8,128)S(1)}, f32[2,32,512]{2,1,0:T(8,128)}, u32[]{:S(2)}, u32[]{:S(2)}) collective-permute-start(f32[2,32,512]{2,1,0:T(8,128)S(1)} %get-tuple-element.44.refs_1_.rest_1_), channel_id=1, source_target_pairs={{0,8},{8,16},{16,24},{24,32},{32,40},{40,48},{48,56},{56,0},{1,9},... | collective-permute-start | bytes 393224 | tf_op jit(solution)/shard_map/ppermute | solution.py:24
  24.9 25.6 %collective-permute-start.6 = (f32[2,32,512]{2,1,0:T(8,128)S(1)}, f32[2,32,512]{2,1,0:T(8,128)}, u32[]{:S(2)}, u32[]{:S(2)}) collective-permute-start(f32[2,32,512]{2,1,0:T(8,128)S(1)} %get-tuple-element.45.refs_2_.rest_2_), channel_id=1, source_target_pairs={{0,7},{1,0},{2,1},{3,2},{4,3},{5,4},{6,5},{7,6},{8,15},{9,8},{10,9... | collective-permute-start | bytes 393224 | tf_op jit(solution)/shard_map/ppermute | solution.py:24
  26.5 24.1 %collective-permute-start.5 = (f32[2,32,512]{2,1,0:T(8,128)}, f32[2,32,512]{2,1,0:T(8,128)}, u32[]{:S(2)}, u32[]{:S(2)}) collective-permute-start(f32[2,32,512]{2,1,0:T(8,128)} %get-tuple-element.46.refs_3_.rest_3_), channel_id=1, source_target_pairs={{0,1},{1,2},{2,3},{3,4},{4,5},{5,6},{6,7},{7,0},{8,9},{9,10},{10,1... | collective-permute-start | bytes 393224 | tf_op jit(solution)/shard_map/ppermute | solution.py:24
  34.7 24.9 %copy-start = (f32[32,512]{1,0:T(8,128)}, f32[32,512]{1,0:T(8,128)S(1)}, u32[]{:S(2)}) copy-start(f32[32,512]{1,0:T(8,128)S(1)} %get-tuple-element.51.refs_12_.rest_16_) | copy-start | bytes 196612
  34.8 24.8 %copy-start.2 = (f32[32,512]{1,0:T(8,128)}, f32[32,512]{1,0:T(8,128)S(1)}, u32[]{:S(2)}) copy-start(f32[32,512]{1,0:T(8,128)S(1)} %get-tuple-element.52.refs_13_.rest_17_) | copy-start | bytes 196612
  34.8 24.8 %copy-start.4 = (f32[32,512]{1,0:T(8,128)}, f32[32,512]{1,0:T(8,128)S(1)}, u32[]{:S(2)}) copy-start(f32[32,512]{1,0:T(8,128)S(1)} %get-tuple-element.53.refs_14_.rest_18_) | copy-start | bytes 196612
  34.8 24.8 %copy-start.6 = (f32[32,512]{1,0:T(8,128)}, f32[32,512]{1,0:T(8,128)S(1)}, u32[]{:S(2)}) copy-start(f32[32,512]{1,0:T(8,128)S(1)} %get-tuple-element.54.refs_15_.rest_19_) | copy-start | bytes 196612
  52.5 17.5 %collective-permute-start.8 = (f32[1,32,512]{2,1,0:T(8,128)}, f32[1,32,512]{2,1,0:T(8,128)}, u32[]{:S(2)}, u32[]{:S(2)}) collective-permute-start(f32[1,32,512]{2,1,0:T(8,128)} %get-tuple-element.55.refs_5_.rest_8_), channel_id=1, source_target_pairs={{0,56},{8,0},{16,8},{24,16},{32,24},{40,32},{48,40},{56,48},{1,57}... | collective-permute-start | bytes 196616 | tf_op jit(solution)/shard_map/ppermute | solution.py:24
  59.6 11.1 %collective-permute-start.7 = (f32[1,32,512]{2,1,0:T(8,128)}, f32[1,32,512]{2,1,0:T(8,128)}, u32[]{:S(2)}, u32[]{:S(2)}) collective-permute-start(f32[1,32,512]{2,1,0:T(8,128)} %get-tuple-element.56.refs_6_.rest_9_), channel_id=1, source_target_pairs={{0,8},{8,16},{16,24},{24,32},{32,40},{40,48},{48,56},{56,0},{1,9},... | collective-permute-start | bytes 196616 | tf_op jit(solution)/shard_map/ppermute | solution.py:24
  59.6 21.0 %collective-permute-start.10 = (f32[1,32,512]{2,1,0:T(8,128)}, f32[1,32,512]{2,1,0:T(8,128)}, u32[]{:S(2)}, u32[]{:S(2)}) collective-permute-start(f32[1,32,512]{2,1,0:T(8,128)} %get-tuple-element.57.refs_7_.rest_10_), channel_id=1, source_target_pairs={{0,7},{1,0},{2,1},{3,2},{4,3},{5,4},{6,5},{7,6},{8,15},{9,8},{10,9... | collective-permute-start | bytes 196616 | tf_op jit(solution)/shard_map/ppermute | solution.py:24
  59.6 21.0 %collective-permute-start.9 = (f32[1,32,512]{2,1,0:T(8,128)}, f32[1,32,512]{2,1,0:T(8,128)}, u32[]{:S(2)}, u32[]{:S(2)}) collective-permute-start(f32[1,32,512]{2,1,0:T(8,128)} %get-tuple-element.58.refs_8_.rest_11_), channel_id=1, source_target_pairs={{0,1},{1,2},{2,3},{3,4},{4,5},{5,6},{6,7},{7,0},{8,9},{9,10},{10,1... | collective-permute-start | bytes 196616 | tf_op jit(solution)/shard_map/ppermute | solution.py:24
  62.4 18.2 %collective-permute-start = (f32[2,16,256]{2,1,0:T(8,128)S(1)}, f32[2,16,256]{2,1,0:T(8,128)S(1)}, u32[]{:S(2)}, u32[]{:S(2)}) collective-permute-start(f32[2,16,256]{2,1,0:T(8,128)S(1)} %get-tuple-element.39), channel_id=1, source_target_pairs={{0,56},{8,0},{16,8},{24,16},{32,24},{40,32},{48,40},{56,48},{1,57}... | collective-permute-start | bytes 98312 | tf_op jit(solution)/shard_map/ppermute | solution.py:24
  70.0 10.7 %collective-permute-start.1 = (f32[2,16,256]{2,1,0:T(8,128)S(1)}, f32[2,16,256]{2,1,0:T(8,128)S(1)}, u32[]{:S(2)}, u32[]{:S(2)}) collective-permute-start(f32[2,16,256]{2,1,0:T(8,128)S(1)} %get-tuple-element.40), channel_id=1, source_target_pairs={{0,7},{1,0},{2,1},{3,2},{4,3},{5,4},{6,5},{7,6},{8,15},{9,8},{10,9... | collective-permute-start | bytes 98312 | tf_op jit(solution)/shard_map/ppermute | solution.py:24
  70.7 10.0 %collective-permute-start.2 = (f32[2,8,256]{2,1,0:T(8,128)S(1)}, f32[2,8,256]{2,1,0:T(8,128)S(1)}, u32[]{:S(2)}, u32[]{:S(2)}) collective-permute-start(f32[2,8,256]{2,1,0:T(8,128)S(1)} %get-tuple-element.41), channel_id=1, source_target_pairs={{0,63},{1,56},{2,57},{3,58},{4,59},{5,60},{6,61},{7,62},{8,7},{9,0... | collective-permute-start | bytes 49160 | tf_op jit(solution)/shard_map/ppermute | solution.py:490
  74.1 6.6 %copy-start.3 = (f32[32,512]{1,0:T(8,128)S(1)}, f32[32,512]{1,0:T(8,128)}, u32[]{:S(2)}) copy-start(f32[32,512]{1,0:T(8,128)} %copy-done.2) | copy-start | bytes 196612
  74.1 6.6 %copy-start.5 = (f32[32,512]{1,0:T(8,128)S(1)}, f32[32,512]{1,0:T(8,128)}, u32[]{:S(2)}) copy-start(f32[32,512]{1,0:T(8,128)} %copy-done.4) | copy-start | bytes 196612
  74.1 6.6 %copy-start.7 = (f32[32,512]{1,0:T(8,128)S(1)}, f32[32,512]{1,0:T(8,128)}, u32[]{:S(2)}) copy-start(f32[32,512]{1,0:T(8,128)} %copy-done.6) | copy-start | bytes 196612
  74.1 6.6 %copy-start.8 = (s32[1,3]{1,0:T(1,128)S(1)}, s32[1,3]{1,0:T(1,128)}, u32[]{:S(2)}) copy-start(s32[1,3]{1,0:T(1,128)} %source.1) | copy-start | bytes 40
  (1 other events, 6.6 us)

commit v3 on v2

--- a/solution.py
+++ b/solution.py
@@ -123,14 +123,29 @@
     return pltpu.with_memory_space_constraint(x, pltpu.HBM)
 
 
+def edge_fluxes(own_b, far_b, own_f, far_f):
+    gx = lax.axis_index("gx")
+    gy = lax.axis_index("gy")
+    keep = [
+        jnp.where(gx > 0, 1.0, 0.0),
+        jnp.where(gx < lax.axis_size("gx") - 1, 1.0, 0.0),
+        jnp.where(gy > 0, 1.0, 0.0),
+        jnp.where(gy < lax.axis_size("gy") - 1, 1.0, 0.0),
+    ]
+    return [
+        (own_b[side][1] + keep[side] * far_b[side][1])
+        * (keep[side] * far_f[side][0] - own_f[side][0])
+        for side in range(4)
+    ]
+
+
 def inner_kernel(field, older, buoy, stiff, src, *rest, step):
-    if step == 1:
-        fixed, rest = rest[:4], rest[4:]
-        out, saved, f_buf, b_buf, s_buf, o_buf, in_sem, out_sem = rest
-        n_buf = out
+    if step == 0:
+        own, far, rest = rest[:4], rest[4:8], rest[8:]
+        out, faces_out, stiff_out = rest[0], rest[1:5], rest[5:9]
+        f_buf, b_buf, s_buf, o_buf, n_buf, edges, in_sem, out_sem = rest[9:]
     else:
-        out, faces_out, stiff_out = rest[0], rest[1:5], rest[5:9]
-        f_buf, b_buf, s_buf, o_buf, n_buf, in_sem, out_sem = rest[9:]
+        n_buf, f_buf, b_buf, s_buf, o_buf, in_sem = rest
     copies = []
     for chunk in range(CHUNKS):
         part = pl.ds(chunk * SPAN, SPAN)
@@ -146,21 +161,13 @@
     lane128 = lax.broadcasted_iota(jnp.int32, (PLANES, 128), 1)
     out_copies = []
 
+    if step == 0:
+        for side, flux in enumerate(edge_fluxes(own, far, own, far)):
+            edges[side] = flux
+
     def arrive(chunk):
         for copy in copies[chunk][:2]:
             copy.wait()
-        if step == 1:
-            if chunk == 0:
-                f_buf[0:PLANES, :] = fixed[0][0]
-            if chunk == CHUNKS - 1:
-                f_buf[ROWS - PLANES : ROWS, :] = fixed[1][0]
-            for x in range(chunk * PER, chunk * PER + PER):
-                f_buf[x * PLANES : x * PLANES + 1, :] = fixed[2][0, x : x + 1, :]
-                f_buf[x * PLANES + 31 : x * PLANES + 32, :] = fixed[3][0, x : x + 1, :]
-            part = pl.ds(chunk * SPAN, SPAN)
-            copy = pltpu.make_async_copy(f_buf.at[part], saved.at[part], out_sem.at[chunk])
-            copy.start()
-            out_copies.append(copy)
 
     def plane(x, flux_before, last=False):
         base = pl.multiple_of(x * PLANES, PLANES)
@@ -168,7 +175,7 @@
         c = f_buf[at, :]
         b = b_buf[at, :]
         if last:
-            flux_x = jnp.zeros_like(c)
+            flux_x = edges[1] if step == 0 else jnp.zeros_like(c)
         else:
             nearby = pl.ds(base + PLANES, PLANES)
             flux_x = (b + b_buf[nearby, :]) * (f_buf[nearby, :] - c)
@@ -183,6 +190,15 @@
         )
         total = (flux_x - flux_before) + (flux_y - pltpu.roll(flux_y, 1, 0))
         total = total + (flux_z - pltpu.roll(flux_z, 1, 1))
+        if step == 0:
+            total = jnp.concatenate(
+                [
+                    total[0:8] + jnp.where(row8 == 0, edges[2, pl.ds(x, 1), :], 0.0),
+                    total[8:24],
+                    total[24:32] + jnp.where(row8 == 7, edges[3, pl.ds(x, 1), :], 0.0),
+                ],
+                axis=0,
+            )
         head = slice(0, 128)
         tail = slice(DEPTH - 128, DEPTH)
         total = jnp.concatenate(
@@ -197,14 +213,14 @@
         n_buf[at, 128:DEPTH] = value[:, 128:]
         n_buf[at, head] = value[:, head] + src[step, at, :]
         if step == 0:
-            faces_out[2][pl.ds(x, 1), :] = n_buf[pl.ds(base, 1), :]
-            faces_out[3][pl.ds(x, 1), :] = n_buf[pl.ds(base + PLANES - 1, 1), :]
+            faces_out[2][0, pl.ds(x, 1), :] = n_buf[pl.ds(base, 1), :]
+            faces_out[3][0, pl.ds(x, 1), :] = n_buf[pl.ds(base + PLANES - 1, 1), :]
             stiff_out[2][pl.ds(x, 1), :] = s_buf[pl.ds(base, 1), :]
             stiff_out[3][pl.ds(x, 1), :] = s_buf[pl.ds(base + PLANES - 1, 1), :]
         return flux_x
 
     arrive(0)
-    flux = jnp.zeros((PLANES, DEPTH), jnp.float32)
+    flux = -edges[0] if step == 0 else jnp.zeros((PLANES, DEPTH), jnp.float32)
     for chunk in range(CHUNKS):
         for copy in copies[chunk][2:]:
             copy.wait()
@@ -221,77 +237,36 @@
             copy.start()
             out_copies.append(copy)
     if step == 0:
-        faces_out[0][...] = n_buf[0:PLANES, :]
-        faces_out[1][...] = n_buf[ROWS - PLANES : ROWS, :]
+        faces_out[0][0] = n_buf[0:PLANES, :]
+        faces_out[1][0] = n_buf[ROWS - PLANES : ROWS, :]
         stiff_out[0][...] = s_buf[0:PLANES, :]
         stiff_out[1][...] = s_buf[ROWS - PLANES : ROWS, :]
     for copy in out_copies:
         copy.wait()
 
 
-def inner(field, older, buoy, stiff, src, fixed, step):
+def inner(field, older, buoy, stiff, src, halos, step):
     big = pltpu.VMEM((ROWS, DEPTH), jnp.float32)
+    scratch = [big] * 4
+    sems = [pltpu.SemaphoreType.DMA((CHUNKS, 4))]
     if step == 0:
-        out_shape = [pltpu.HBM((ROWS, DEPTH), jnp.float32)] + [f32(PLANES, DEPTH)] * 8
+        out_shape = [pltpu.HBM((ROWS, DEPTH), jnp.float32)]
+        out_shape += [f32(1, PLANES, DEPTH)] * 4 + [f32(PLANES, DEPTH)] * 4
         out_specs = [ANY] + [VMEM] * 8
+        scratch = scratch + [big, pltpu.VMEM((4, PLANES, DEPTH), jnp.float32)]
+        sems = sems + [pltpu.SemaphoreType.DMA((CHUNKS,))]
     else:
-        out_shape = [big, f32(ROWS, DEPTH)]
-        out_specs = [VMEM, ANY]
+        out_shape, out_specs = big, VMEM
     return pl.pallas_call(
         lambda *refs: inner_kernel(*refs, step=step),
-        in_specs=[ANY] * 4 + [VMEM] * (1 + len(fixed)),
+        in_specs=[ANY] * 4 + [VMEM] * (1 + len(halos)),
         out_specs=out_specs,
         out_shape=out_shape,
-        scratch_shapes=[big] * (5 - step)
-        + [pltpu.SemaphoreType.DMA((CHUNKS, 4)), pltpu.SemaphoreType.DMA((CHUNKS,))],
-        compiler_params=ROOM,
-        cost_estimate=pl.CostEstimate(flops=20 << 20, bytes_accessed=10 << 20, transcendentals=0),
+        scratch_shapes=scratch + sems,
+        compiler_params=ROOM,
+        cost_estimate=pl.CostEstimate(bytes_accessed=10 << 20, flops=1<<40, transcendentals=0),
         name="inner%d" % step,
-    )(in_hbm(field), in_hbm(older), in_hbm(buoy), in_hbm(stiff), src, *fixed)
-
-
-def edge_terms(own_b, far_b, own_f, far_f, stiff):
-    gx = lax.axis_index("gx")
-    gy = lax.axis_index("gy")
-    keep = [
-        jnp.where(gx > 0, 1.0, 0.0),
-        jnp.where(gx < lax.axis_size("gx") - 1, 1.0, 0.0),
-        jnp.where(gy > 0, 1.0, 0.0),
-        jnp.where(gy < lax.axis_size("gy") - 1, 1.0, 0.0),
-    ]
-    terms = []
-    for side in range(4):
-        coef = 0.5 * (own_b[side][1] + keep[side] * far_b[side][1])
-        flux = coef * (keep[side] * far_f[side][0] - own_f[side][0])
-        terms.append(stiff[side][...] * flux)
-    return terms
-
-
-def fix_kernel(*refs):
-    own, far, value, stiff, out = (refs[4 * k : 4 * k + 4] for k in range(5))
-    terms = refs[20]
-    for side, term in enumerate(edge_terms(own, far, own, far, stiff)):
-        terms[side] = term
-        out[side][0] = value[side][...] + term
-    for side in range(4):
-        for end in range(2):
-            row = slice(31 * end, 31 * end + 1)
-            other = (2 if side < 2 else 0) + end
-            at = slice(31 * (side % 2), 31 * (side % 2) + 1)
-            out[side][0, row, :] += terms[other, at, :]
-
-
-def fix_faces(own, far, values, stiff):
-    return pl.pallas_call(
-        fix_kernel,
-        in_specs=[VMEM] * 16,
-        out_specs=[VMEM] * 4,
-        out_shape=[f32(1, PLANES, DEPTH)] * 4,
-        scratch_shapes=[pltpu.VMEM((4, PLANES, DEPTH), jnp.float32)],
-        compiler_params=ROOM,
-        cost_estimate=pl.CostEstimate(flops=1 << 20, bytes_accessed=2 << 20, transcendentals=0),
-        name="fix_faces",
-    )(*own, *far, *values, *stiff)
+    )(in_hbm(field), in_hbm(older), in_hbm(buoy), in_hbm(stiff), src, *halos)
 
 
 def interpolation():
@@ -340,8 +315,8 @@
     image, saved, rims, rim_along, fine, out, first, terms, third, sem = rest[20:]
     load = pltpu.make_async_copy(first_hbm, first, sem.at[0])
     load.start()
-    for side, term in enumerate(edge_terms(own, far, own2, far2, stiff)):
-        terms[side] = term
+    for side, flux in enumerate(edge_fluxes(own, far, own2, far2)):
+        terms[side] = (0.5 * stiff[side][...]) * flux
     gx = lax.axis_index("gx")
     gy = lax.axis_index("gy")
     keep_x = jnp.where(gx < lax.axis_size("gx") - 1, 1.0, 0.0)
@@ -455,26 +430,27 @@
 
     own = faces(current_field[0], buoyancy)
     far = exchange(own)
-    tiles, own = lax.optimization_barrier((stored_tiles, own))
-    received = lax.all_to_all(
-        tiles[0, 0], ("shot", "gx"), split_axis=0, concat_axis=0, tiled=True
-    ).reshape(1024, COARSE)
     slot = lax.broadcasted_iota(jnp.int32, (32, 32), 1)
     ids = jnp.where(slot < tile_counts[0, 0][:, None], tile_ids[0, 0], -1).reshape(1, 1024)
     onehot = onehots(ids)
     src = sources(receiver_cells[0], receiver_data[0])
-    partial, *rest = inner(current, older, buoy, stiff, src, [], 0)
-    values, stiff_faces = rest[:4], rest[4:]
-    own2 = fix_faces(own, far, values, stiff_faces)
+    tiles, far[2], far[3], onehot, src = lax.optimization_barrier(
+        (stored_tiles, far[2], far[3], onehot, src)
+    )
+    received = lax.all_to_all(
+        tiles[0, 0], ("shot", "gx"), split_axis=0, concat_axis=0, tiled=True
+    ).reshape(1024, COARSE)
+    second, *rest = inner(current, older, buoy, stiff, src, [*own, *far], 0)
+    own2, stiff_faces = rest[:4], rest[4:]
     far2 = exchange(own2)
 
     along, rim_x, rim_y, corner = coarse_tiles(received, onehot)
     rims = [rotate(rim_x, "gx", -1), rotate(rim_y, "gy", -1), diagonal(corner)]
-    third, last_older = inner(partial, current, buoy, stiff, src, own2, 1)
+    third = inner(second, current, buoy, stiff, src, [], 1)
     edges = [*own, *far, *own2, *far2, *stiff_faces]
-    image, last_current = imaging(source_cell, along, rims, last_older, third, edges)
+    image, last_current = imaging(source_cell, along, rims, second, third, edges)
     shape = current_field.shape
-    return image.reshape(shape), last_older.reshape(shape), last_current.reshape(shape)
+    return image.reshape(shape), second.reshape(shape), last_current.reshape(shape)
 
 
 def exchange(own):

time: 87 us -> 77.9 us (0.90)
  the two profiles are of different devices: /device:TPU:1 before, /device:TPU:39 now
where the time goes in v3:
time: 77.9 us; the launch traced here: 77.6 us
  starting transfers between devices  40 us (51%)
  Pallas kernels  23.3 us (30%)
  waiting for transfers between devices  13 us (17%)
  between operations  0.98 us (1%)
    ppermute x10, starting transfers between devices, rotate(): lax.ppermute(block, axis, [(i, (i + step) % count) for i in range(count)])  21.4 us
    pallas_call x2, Pallas kernels, inner(): pl.pallas_call(lambda *refs: inner_kernel(*refs, step=step), in_specs=[AN...  12.5 us
    all_to_all x1, starting transfers between devices, per_device(): lax.all_to_all(tiles[0, 0], ('shot', 'gx'), split_axis=0, concat_axis=0,...  11.6 us
    all_to_all x1, waiting for transfers between devices, per_device(): lax.all_to_all(tiles[0, 0], ('shot', 'gx'), split_axis=0, concat_axis=0,...  10.1 us
    ppermute x1, starting transfers between devices, diagonal(): return lax.ppermute(block, ('gx', 'gy'), route)  7.02 us
    pallas_call x1, Pallas kernels, imaging(): pl.pallas_call(image_kernel, in_specs=[SMEM] + [VMEM] * 4 + [ANY] + [VMEM...  5.38 us
    ppermute x10, waiting for transfers between devices, rotate(): lax.ppermute(block, axis, [(i, (i + step) % count) for i in range(count)])  2.9 us
    pallas_call x1, Pallas kernels, coarse_tiles(): pl.pallas_call(coarse_kernel, in_specs=[VMEM, VMEM], out_specs=[VMEM] * 4...  2.64 us
  transfers between devices with their start and end apart: 12, of which 2 were waited for; matrix products, arithmetic and copies ran while one was open for 0% of the time, Pallas kernels for 21%

profile of v3, /device:TPU:39, one launch (start us, length us, event | category | flops | bytes accessed | tf_op | source)
XLA Modules:
  0.0 77.6 jit_solution(10820808781728000933)
XLA Ops:
  0.7 1.7 %faces.1 = (f32[2,32,512]{2,1,0:T(8,128)S(1)}, f32[2,32,512]{2,1,0:T(8,128)S(1)}, f32[2,32,512]{2,1,0:T(8,128)S(1)}, f32[2,32,512]{2,1,0:T(8,128)S(1)}) custom-call(f32[32,32,512]{2,1,0:T(8,128)} %bitcast.19, f32[32,32,512]{2,1,0:T(8,128)} %bitcast.20, f32[32,32,512]{2,1,0:T(8,128)} %bitcast.21, f32[32,32,512]{2,1,0:T(8,128)} %bitcast.22, ...), custom_call_target="tpu_custom_call" | custom-call | bytes 3145728 | tf_op jit(solution)/shard_map/faces/pallas_call | solution.py:51
  2.4 2.3 %collective-permute-start = (f32[2,32,512]{2,1,0:T(8,128)S(1)}, f32[2,32,512]{2,1,0:T(8,128)S(1)}, u32[]{:S(2)}, u32[]{:S(2)}) collective-permute-start(f32[2,32,512]{2,1,0:T(8,128)S(1)} %get-tuple-element.27.refs_8_.rest_3_), channel_id=1, source_target_pairs={{0,1},{1,2},{2,3},{3,4},{4,5},{5,6},{6,7},{7,0},{8,9},{9,10},{10,1... | collective-permute-start | bytes 393224 | tf_op jit(solution)/shard_map/ppermute | solution.py:24
  4.7 0.5 collective-permute-start.6
  5.2 6.9 %collective-permute-start.5 = (f32[2,32,512]{2,1,0:T(8,128)S(1)}, f32[2,32,512]{2,1,0:T(8,128)S(1)}, u32[]{:S(2)}, u32[]{:S(2)}) collective-permute-start(f32[2,32,512]{2,1,0:T(8,128)S(1)} %get-tuple-element.37.refs_6_.rest_1_), channel_id=1, source_target_pairs={{0,8},{8,16},{16,24},{24,32},{32,40},{40,48},{48,56},{56,0},{1,9},... | collective-permute-start | bytes 393224 | tf_op jit(solution)/shard_map/ppermute | solution.py:24
  12.2 0.1 squeeze.16
  12.2 0.1 iota_compare_fusion
  12.3 0.1 lt.23
  12.5 0.2 onehots.1.onehot
  12.7 0.8 %sources.1.refs_4_ = f32[2,1024,128]{2,1,0:T(8,128)S(1)} custom-call(s32[3,1024]{1,0:T(4,128)S(1)} %bitcast.17, f32[2,1024]{1,0:T(2,128)S(1)} %bitcast.18), custom_call_target="tpu_custom_call" | custom-call | flops 536870912 | bytes 2097152 | tf_op jit(solution)/shard_map/sources/pallas_call | solution.py:93
  13.5 0.0 copy-start.2
  13.5 11.6 %all-to-all-start = ((f32[32,32,256]{2,1,0:T(8,128)}), f32[32,32,256]{2,1,0:T(8,128)}, u32[]{:S(2)}, u32[]{:S(2)}) async-start(f32[32,32,256]{2,1,0:T(8,128)} %bitcast.28), calls=%async_computation | async-start | bytes 2097152 | tf_op jit(solution)/shard_map/all_to_all | solution.py:440
  25.2 7.0 %inner0.1 = (f32[1024,512]{1,0:T(8,128)}, f32[1,32,512]{2,1,0:T(8,128)S(1)}, f32[1,32,512]{2,1,0:T(8,128)S(1)}, f32[1,32,512]{2,1,0:T(8,128)}, f32[1,32,512]{2,1...) custom-call(f32[1024,512]{1,0:T(8,128)} %bitcast.23, ...), custom_call_target="tpu_custom_call" | custom-call | flops 1099511627776 | bytes 10485760 | tf_op jit(solution)/shard_map/inner0/pallas_call | solution.py:260
  32.2 0.7 collective-permute-start.8
  32.8 6.9 %collective-permute-start.7 = (f32[1,32,512]{2,1,0:T(8,128)S(1)}, f32[1,32,512]{2,1,0:T(8,128)S(1)}, u32[]{:S(2)}, u32[]{:S(2)}) collective-permute-start(f32[1,32,512]{2,1,0:T(8,128)S(1)} %get-tuple-element.42.rest_9_), channel_id=1, source_target_pairs={{0,8},{8,16},{16,24},{24,32},{32,40},{40,48},{48,56},{56,0},{1,9},... | collective-permute-start | bytes 196616 | tf_op jit(solution)/shard_map/ppermute | solution.py:24
  39.8 2.8 %collective-permute-start.10 = (f32[1,32,512]{2,1,0:T(8,128)}, f32[1,32,512]{2,1,0:T(8,128)}, u32[]{:S(2)}, u32[]{:S(2)}) collective-permute-start(f32[1,32,512]{2,1,0:T(8,128)} %get-tuple-element.43.rest_10_), channel_id=1, source_target_pairs={{0,7},{1,0},{2,1},{3,2},{4,3},{5,4},{6,5},{7,6},{8,15},{9,8},{10,9... | collective-permute-start | bytes 196616 | tf_op jit(solution)/shard_map/ppermute | solution.py:24
  42.6 0.6 collective-permute-start.9
  43.2 10.1 %all-to-all-done = f32[32,32,256]{2,1,0:T(8,128)} async-done(((f32[32,32,256]{2,1,0:T(8,128)}), f32[32,32,256]{2,1,0:T(8,128)}, u32[]{:S(2)}, u32[]{:S(2)}) %all-to-all-start) | async-done | bytes 1048608 | tf_op jit(solution)/shard_map/all_to_all | solution.py:440
  53.3 2.6 %coarse_tiles.1 = (f32[512,512]{1,0:T(8,128)S(1)}, f32[2,16,256]{2,1,0:T(8,128)}, f32[2,16,256]{2,1,0:T(8,128)}, f32[2,8,256]{2,1,0:T(8,128)}) custom-call(f32[1024,256]{1,0:T(8,128)} %bitcast.4.received, bf16[512,1024]{1,0:T(8,128)(2,1)S(1)} %onehots.1.onehot), custom_call_target="tpu_custom_call" | custom-call | flops 1073741824 | bytes 3145728 | tf_op jit(solution)/shard_map/coarse_tiles/pallas_call | solution.py:301
  55.9 7.0 %collective-permute-start.4 = (f32[2,8,256]{2,1,0:T(8,128)}, f32[2,8,256]{2,1,0:T(8,128)}, u32[]{:S(2)}, u32[]{:S(2)}) collective-permute-start(f32[2,8,256]{2,1,0:T(8,128)} %get-tuple-element.34), channel_id=1, source_target_pairs={{0,63},{1,56},{2,57},{3,58},{4,59},{5,60},{6,61},{7,62},{8,7},{9,0... | collective-permute-start | bytes 49160 | tf_op jit(solution)/shard_map/ppermute | solution.py:466
  62.9 0.2 collective-permute-start.2
  63.1 0.5 collective-permute-start.3
  63.6 5.5 %inner1.1.second = f32[1024,512]{1,0:T(8,128)S(1)} custom-call(f32[1024,512]{1,0:T(8,128)} %get-tuple-element.40.refs_0_.first_hbm, f32[1024,512]{1,0:T(8,128)} %bitcast.24, f32[1024,512]{1,0:T(8,128)} %bitcast.26, f32[1024,512]{1,0:T(8,128)} %bitcast.32, f32[2,1024,128]{2,1,0:T(8,128)S(1)} %copy-done.3), custom_call_target="tpu_custom_call" | custom-call | flops 1099511627776 | bytes 10485760 | tf_op jit(solution)/shard_map/inner1/pallas_call | solution.py:260
  69.1 2.9 %collective-permute-done.2.rim_x = f32[2,16,256]{2,1,0:T(8,128)} collective-permute-done((f32[2,16,256]{2,1,0:T(8,128)}, f32[2,16,256]{2,1,0:T(8,128)}, u32[]{:S(2)}, u32[]{:S(2)}) %collective-permute-start.2) | collective-permute-done | bytes 32800 | tf_op jit(solution)/shard_map/ppermute | solution.py:24
  72.0 5.4 %imaging.1 = (f32[1024,512]{1,0:T(8,128)}, f32[1024,512]{1,0:T(8,128)}) custom-call(s32[1,3]{1,0:T(1,128)S(1)} %copy-done, f32[512,512]{1,0:T(8,128)S(1)} %get-tuple-element.31.along, f32[2,16,256]{2,1,0:T(8,128)} %collective-permute-done.2.rim_x, f32[2,16,256]{2,1,0:T(8,128)} %collective-permute-done.3.rim_y, f32[2,8,256]{2,1,0:T(8,128)} %collective-permute-done.4.corner, ...), custom_call_target="tpu_custom_call" | custom-call | flops 20971520 | bytes 8388608 | tf_op jit(solution)/shard_map/imaging/pallas_call | solution.py:393
  (26 shorter events, 0.1 us)
Async XLA Ops:
  0.6 11.5 %copy-start.4 = (s32[1,1,32,32]{3,2,1,0:T(8,128)S(1)}, s32[1,1,32,32]{3,2,1,0:T(8,128)}, u32[]{:S(2)}) copy-start(s32[1,1,32,32]{3,2,1,0:T(8,128)} %param.15) | copy-start | bytes 12292
  0.6 11.6 %copy-start.6 = (s32[1,1,32]{2,1,0:T(1,128)S(1)}, s32[1,1,32]{2,1,0:T(1,128)}, u32[]{:S(2)}) copy-start(s32[1,1,32]{2,1,0:T(1,128)} %param.16) | copy-start | bytes 388
  0.7 11.8 %copy-start.5 = (s32[1,3,1024]{2,0,1:T(1,128)S(1)}, s32[1,3,1024]{2,0,1:T(1,128)}, u32[]{:S(2)}) copy-start(s32[1,3,1024]{2,0,1:T(1,128)} %param.17) | copy-start | bytes 36868
  0.7 12.0 %copy-start.1 = (f32[1,2,1024]{2,1,0:T(2,128)S(1)}, f32[1,2,1024]{2,1,0:T(2,128)}, u32[]{:S(2)}) copy-start(f32[1,2,1024]{2,1,0:T(2,128)} %param.18) | copy-start | bytes 24580
  2.4 11.1 %collective-permute-start = (f32[2,32,512]{2,1,0:T(8,128)S(1)}, f32[2,32,512]{2,1,0:T(8,128)S(1)}, u32[]{:S(2)}, u32[]{:S(2)}) collective-permute-start(f32[2,32,512]{2,1,0:T(8,128)S(1)} %get-tuple-element.27.refs_8_.rest_3_), channel_id=1, source_target_pairs={{0,1},{1,2},{2,3},{3,4},{4,5},{5,6},{6,7},{7,0},{8,9},{9,10},{10,1... | collective-permute-start | bytes 393224 | tf_op jit(solution)/shard_map/ppermute | solution.py:24
  4.7 8.8 %collective-permute-start.1 = (f32[2,32,512]{2,1,0:T(8,128)S(1)}, f32[2,32,512]{2,1,0:T(8,128)S(1)}, u32[]{:S(2)}, u32[]{:S(2)}) collective-permute-start(f32[2,32,512]{2,1,0:T(8,128)S(1)} %get-tuple-element.28.refs_7_.rest_2_), channel_id=1, source_target_pairs={{0,7},{1,0},{2,1},{3,2},{4,3},{5,4},{6,5},{7,6},{8,15},{9,8},{10,9... | collective-permute-start | bytes 393224 | tf_op jit(solution)/shard_map/ppermute | solution.py:24
  4.7 20.5 %collective-permute-start.6 = (f32[2,32,512]{2,1,0:T(8,128)S(1)}, f32[2,32,512]{2,1,0:T(8,128)S(1)}, u32[]{:S(2)}, u32[]{:S(2)}) collective-permute-start(f32[2,32,512]{2,1,0:T(8,128)S(1)} %get-tuple-element.36.refs_5_.rest_0_), channel_id=1, source_target_pairs={{0,56},{8,0},{16,8},{24,16},{32,24},{40,32},{48,40},{56,48},{1,57}... | collective-permute-start | bytes 393224 | tf_op jit(solution)/shard_map/ppermute | solution.py:24
  5.2 19.9 %collective-permute-start.5 = (f32[2,32,512]{2,1,0:T(8,128)S(1)}, f32[2,32,512]{2,1,0:T(8,128)S(1)}, u32[]{:S(2)}, u32[]{:S(2)}) collective-permute-start(f32[2,32,512]{2,1,0:T(8,128)S(1)} %get-tuple-element.37.refs_6_.rest_1_), channel_id=1, source_target_pairs={{0,8},{8,16},{16,24},{24,32},{32,40},{40,48},{48,56},{56,0},{1,9},... | collective-permute-start | bytes 393224 | tf_op jit(solution)/shard_map/ppermute | solution.py:24
  13.5 18.7 %copy-start.2 = (f32[2,1024,128]{2,1,0:T(8,128)}, f32[2,1024,128]{2,1,0:T(8,128)S(1)}, u32[]{:S(2)}) copy-start(f32[2,1024,128]{2,1,0:T(8,128)S(1)} %sources.1.refs_4_) | copy-start | bytes 3145732
  13.5 39.7 %all-to-all-start = ((f32[32,32,256]{2,1,0:T(8,128)}), f32[32,32,256]{2,1,0:T(8,128)}, u32[]{:S(2)}, u32[]{:S(2)}) async-start(f32[32,32,256]{2,1,0:T(8,128)} %bitcast.28), calls=%async_computation | async-start | bytes 2097152 | tf_op jit(solution)/shard_map/all_to_all | solution.py:440
  32.2 30.7 %collective-permute-start.8 = (f32[1,32,512]{2,1,0:T(8,128)S(1)}, f32[1,32,512]{2,1,0:T(8,128)S(1)}, u32[]{:S(2)}, u32[]{:S(2)}) collective-permute-start(f32[1,32,512]{2,1,0:T(8,128)S(1)} %get-tuple-element.41.rest_8_), channel_id=1, source_target_pairs={{0,56},{8,0},{16,8},{24,16},{32,24},{40,32},{48,40},{56,48},{1,57}... | collective-permute-start | bytes 196616 | tf_op jit(solution)/shard_map/ppermute | solution.py:24
  32.8 30.2 %collective-permute-start.7 = (f32[1,32,512]{2,1,0:T(8,128)S(1)}, f32[1,32,512]{2,1,0:T(8,128)S(1)}, u32[]{:S(2)}, u32[]{:S(2)}) collective-permute-start(f32[1,32,512]{2,1,0:T(8,128)S(1)} %get-tuple-element.42.rest_9_), channel_id=1, source_target_pairs={{0,8},{8,16},{16,24},{24,32},{32,40},{40,48},{48,56},{56,0},{1,9},... | collective-permute-start | bytes 196616 | tf_op jit(solution)/shard_map/ppermute | solution.py:24
  39.8 29.4 %collective-permute-start.10 = (f32[1,32,512]{2,1,0:T(8,128)}, f32[1,32,512]{2,1,0:T(8,128)}, u32[]{:S(2)}, u32[]{:S(2)}) collective-permute-start(f32[1,32,512]{2,1,0:T(8,128)} %get-tuple-element.43.rest_10_), channel_id=1, source_target_pairs={{0,7},{1,0},{2,1},{3,2},{4,3},{5,4},{6,5},{7,6},{8,15},{9,8},{10,9... | collective-permute-start | bytes 196616 | tf_op jit(solution)/shard_map/ppermute | solution.py:24
  42.6 26.6 %collective-permute-start.9 = (f32[1,32,512]{2,1,0:T(8,128)}, f32[1,32,512]{2,1,0:T(8,128)}, u32[]{:S(2)}, u32[]{:S(2)}) collective-permute-start(f32[1,32,512]{2,1,0:T(8,128)} %get-tuple-element.44.rest_11_), channel_id=1, source_target_pairs={{0,1},{1,2},{2,3},{3,4},{4,5},{5,6},{6,7},{7,0},{8,9},{9,10},{10,1... | collective-permute-start | bytes 196616 | tf_op jit(solution)/shard_map/ppermute | solution.py:24
  53.3 10.3 %copy-start.3 = (f32[2,1024,128]{2,1,0:T(8,128)S(1)}, f32[2,1024,128]{2,1,0:T(8,128)}, u32[]{:S(2)}) copy-start(f32[2,1024,128]{2,1,0:T(8,128)} %copy-done.2) | copy-start | bytes 3145732
  55.9 13.2 %collective-permute-start.4 = (f32[2,8,256]{2,1,0:T(8,128)}, f32[2,8,256]{2,1,0:T(8,128)}, u32[]{:S(2)}, u32[]{:S(2)}) collective-permute-start(f32[2,8,256]{2,1,0:T(8,128)} %get-tuple-element.34), channel_id=1, source_target_pairs={{0,63},{1,56},{2,57},{3,58},{4,59},{5,60},{6,61},{7,62},{8,7},{9,0... | collective-permute-start | bytes 49160 | tf_op jit(solution)/shard_map/ppermute | solution.py:466
  62.9 9.1 %collective-permute-start.2 = (f32[2,16,256]{2,1,0:T(8,128)}, f32[2,16,256]{2,1,0:T(8,128)}, u32[]{:S(2)}, u32[]{:S(2)}) collective-permute-start(f32[2,16,256]{2,1,0:T(8,128)} %get-tuple-element.32), channel_id=1, source_target_pairs={{0,56},{8,0},{16,8},{24,16},{32,24},{40,32},{48,40},{56,48},{1,57}... | collective-permute-start | bytes 98312 | tf_op jit(solution)/shard_map/ppermute | solution.py:24
  63.1 8.9 %collective-permute-start.3 = (f32[2,16,256]{2,1,0:T(8,128)}, f32[2,16,256]{2,1,0:T(8,128)}, u32[]{:S(2)}, u32[]{:S(2)}) collective-permute-start(f32[2,16,256]{2,1,0:T(8,128)} %get-tuple-element.33), channel_id=1, source_target_pairs={{0,7},{1,0},{2,1},{3,2},{4,3},{5,4},{6,5},{7,6},{8,15},{9,8},{10,9... | collective-permute-start | bytes 98312 | tf_op jit(solution)/shard_map/ppermute | solution.py:24
  63.6 8.5 %copy-start = (s32[1,3]{1,0:T(1,128)S(1)}, s32[1,3]{1,0:T(1,128)}, u32[]{:S(2)}) copy-start(s32[1,3]{1,0:T(1,128)} %source.1) | copy-start | bytes 40

commit v4 on v3

--- a/solution.py
+++ b/solution.py
@@ -95,7 +95,7 @@
         in_specs=[VMEM, VMEM],
         out_specs=VMEM,
         out_shape=f32(2, ROWS, 128),
-        cost_estimate=pl.CostEstimate(flops=1 << 29, bytes_accessed=2 << 20, transcendentals=0),
+        cost_estimate=pl.CostEstimate(flops=1, bytes_accessed=1, transcendentals=0),
         compiler_params=ROOM,
         name="sources",
     )(cells, data)
@@ -113,7 +113,7 @@
         in_specs=[VMEM],
         out_specs=VMEM,
         out_shape=jax.ShapeDtypeStruct((512, 1024), jnp.bfloat16),
-        cost_estimate=pl.CostEstimate(flops=1 << 20, bytes_accessed=2 << 20, transcendentals=0),
+        cost_estimate=pl.CostEstimate(flops=1, bytes_accessed=1, transcendentals=0),
         compiler_params=ROOM,
         name="onehots",
     )(ids)
@@ -145,7 +145,7 @@
         out, faces_out, stiff_out = rest[0], rest[1:5], rest[5:9]
         f_buf, b_buf, s_buf, o_buf, n_buf, edges, in_sem, out_sem = rest[9:]
     else:
-        n_buf, f_buf, b_buf, s_buf, o_buf, in_sem = rest
+        out, f_buf, b_buf, s_buf, o_buf, n_buf, in_sem, out_sem = rest
     copies = []
     for chunk in range(CHUNKS):
         part = pl.ds(chunk * SPAN, SPAN)
@@ -231,11 +231,10 @@
             flux = lax.fori_loop(chunk * PER, chunk * PER + PER - 4, plane, flux, unroll=4)
             for x in range(PLANES - 4, PLANES):
                 flux = plane(x, flux, x == PLANES - 1)
-        if step == 0:
-            part = pl.ds(chunk * SPAN, SPAN)
-            copy = pltpu.make_async_copy(n_buf.at[part], out.at[part], out_sem.at[chunk])
-            copy.start()
-            out_copies.append(copy)
+        part = pl.ds(chunk * SPAN, SPAN)
+        copy = pltpu.make_async_copy(n_buf.at[part], out.at[part], out_sem.at[chunk])
+        copy.start()
+        out_copies.append(copy)
     if step == 0:
         faces_out[0][0] = n_buf[0:PLANES, :]
         faces_out[1][0] = n_buf[ROWS - PLANES : ROWS, :]
@@ -247,16 +246,14 @@
 
 def inner(field, older, buoy, stiff, src, halos, step):
     big = pltpu.VMEM((ROWS, DEPTH), jnp.float32)
-    scratch = [big] * 4
-    sems = [pltpu.SemaphoreType.DMA((CHUNKS, 4))]
+    scratch = [big] * 5
+    sems = [pltpu.SemaphoreType.DMA((CHUNKS, 4)), pltpu.SemaphoreType.DMA((CHUNKS,))]
+    out_shape = [pltpu.HBM((ROWS, DEPTH), jnp.float32)]
+    out_specs = [ANY]
     if step == 0:
-        out_shape = [pltpu.HBM((ROWS, DEPTH), jnp.float32)]
         out_shape += [f32(1, PLANES, DEPTH)] * 4 + [f32(PLANES, DEPTH)] * 4
-        out_specs = [ANY] + [VMEM] * 8
-        scratch = scratch + [big, pltpu.VMEM((4, PLANES, DEPTH), jnp.float32)]
-        sems = sems + [pltpu.SemaphoreType.DMA((CHUNKS,))]
-    else:
-        out_shape, out_specs = big, VMEM
+        out_specs += [VMEM] * 8
+        scratch = scratch + [pltpu.VMEM((4, PLANES, DEPTH), jnp.float32)]
     return pl.pallas_call(
         lambda *refs: inner_kernel(*refs, step=step),
         in_specs=[ANY] * 4 + [VMEM] * (1 + len(halos)),
@@ -310,11 +307,43 @@
     )(received, onehot)
 
 
-def image_kernel(source, along, rim_x, rim_y, corner, first_hbm, second, *rest):
+def upsample_kernel(along, first_hbm, second_hbm, fine, first, second, sem):
+    loads = [
+        pltpu.make_async_copy(first_hbm, first, sem.at[0]),
+        pltpu.make_async_copy(second_hbm, second, sem.at[1]),
+    ]
+    for copy in loads:
+        copy.start()
+    for n in range(2):
+        for k in range(16):
+            rows = along[n * 256 + k * 16 : n * 256 + k * 16 + 16, :]
+            middle = 0.5 * (rows + pltpu.roll(rows, 15, 0))
+            base = (n * 17 + k) * PLANES
+            for part in range(4):
+                lanes = slice(part * 128, part * 128 + 128)
+                fine[part, pl.ds(base, 16, stride=2), :] = rows[:, lanes]
+                fine[part, pl.ds(base + 1, 16, stride=2), :] = middle[:, lanes]
+    for copy in loads:
+        copy.wait()
+
+
+def upsampling(along, first, second):
+    big = pltpu.VMEM((ROWS, DEPTH), jnp.float32)
+    return pl.pallas_call(
+        upsample_kernel,
+        in_specs=[VMEM, ANY, ANY],
+        out_specs=[VMEM] * 3,
+        out_shape=[pltpu.VMEM((4, 2 * 17 * PLANES, 128), jnp.float32), big, big],
+        scratch_shapes=[pltpu.SemaphoreType.DMA((2,))],
+        compiler_params=ROOM,
+        cost_estimate=pl.CostEstimate(flops=1 << 40, bytes_accessed=8 << 20, transcendentals=0),
+        name="upsampling",
+    )(along, in_hbm(first), in_hbm(second))
+
+
+def image_kernel(source, along, fine_in, rim_x, rim_y, corner, first, second, *rest):
     own, far, own2, far2, stiff = (rest[4 * k : 4 * k + 4] for k in range(5))
-    image, saved, rims, rim_along, fine, out, first, terms, third, sem = rest[20:]
-    load = pltpu.make_async_copy(first_hbm, first, sem.at[0])
-    load.start()
+    image, saved, fine, rims, rim_along, out, terms, third, sem = rest[20:]
     for side, flux in enumerate(edge_fluxes(own, far, own2, far2)):
         terms[side] = (0.5 * stiff[side][...]) * flux
     gx = lax.axis_index("gx")
@@ -330,26 +359,26 @@
     rim_along[...] = dot(high, weights) + dot(low, weights)
     row16 = lax.broadcasted_iota(jnp.int32, (16, DEPTH), 0)
     for n in range(2):
-        for k in range(17):
-            if k < 16:
-                rows = along[n * 256 + k * 16 : n * 256 + k * 16 + 16, :]
-                side = rim_along[n * 40 + 16 + k : n * 40 + 17 + k, :]
-            else:
-                rows = rim_along[n * 40 : n * 40 + 16, :]
-                side = rim_along[n * 40 + 32 : n * 40 + 33, :]
-            upper = jnp.where(row16 == 15, side, pltpu.roll(rows, 15, 0))
-            base = (n * 17 + k) * PLANES
-            middle = 0.5 * (rows + upper)
+        rows = rim_along[n * 40 : n * 40 + 16, :]
+        side = rim_along[n * 40 + 32 : n * 40 + 33, :]
+        middle = 0.5 * (rows + jnp.where(row16 == 15, side, pltpu.roll(rows, 15, 0)))
+        base = (n * 17 + 16) * PLANES
+        for part in range(4):
+            lanes = slice(part * 128, part * 128 + 128)
+            fine[part, pl.ds(base, 16, stride=2), :] = rows[:, lanes]
+            fine[part, pl.ds(base + 1, 16, stride=2), :] = middle[:, lanes]
+        for k in range(16):
+            last = n * 256 + k * 16 + 15
+            pair = n * 40 + 16 + k
+            middle = 0.5 * (along[last : last + 1, :] + rim_along[pair : pair + 1, :])
+            row = (n * 17 + k) * PLANES + 31
             for part in range(4):
-                lanes = slice(part * 128, part * 128 + 128)
-                fine[part, pl.ds(base, 16, stride=2), :] = rows[:, lanes]
-                fine[part, pl.ds(base + 1, 16, stride=2), :] = middle[:, lanes]
+                fine[part, row : row + 1, :] = middle[:, part * 128 : part * 128 + 128]
     scale = -1.0 / (2.0 * MUTE_RADIUS * MUTE_RADIUS)
     y = (lax.broadcasted_iota(jnp.int32, (PLANES, DEPTH), 0) + gy * PLANES - source[0, 1]).astype(jnp.float32)
     z = (lax.broadcasted_iota(jnp.int32, (PLANES, DEPTH), 1) - source[0, 2]).astype(jnp.float32)
     decay_yz = jnp.exp((y * y + z * z) * scale)
     x_base = gx * PLANES - source[0, 0]
-    load.wait()
     copies = []
     for k in range(16):
         for odd in range(2):
@@ -378,37 +407,37 @@
                 out[at, lanes] = taper * (
                     snaps[0] * first[at, lanes] + snaps[1] * third[at, lanes]
                 )
-        if k % 4 == 3:
-            rows = pl.ds((k - 3) * 2 * PLANES, 8 * PLANES)
+        if k % 2 == 1:
+            rows = pl.ds((k - 1) * 2 * PLANES, 4 * PLANES)
             for pos, (here, there) in enumerate(((out, image), (third, saved))):
-                slot = 1 + 2 * (k // 4) + pos
+                slot = 2 * (k // 2) + pos
                 copies.append(pltpu.make_async_copy(here.at[rows], there.at[rows], sem.at[slot]))
                 copies[-1].start()
     for copy in copies:
         copy.wait()
 
 
-def imaging(source, along, rims, first, second, edges):
+def imaging(source, along, fine, rims, first, second, edges):
     big = pltpu.VMEM((ROWS, DEPTH), jnp.float32)
     return pl.pallas_call(
         image_kernel,
-        in_specs=[SMEM] + [VMEM] * 4 + [ANY] + [VMEM] * 21,
-        out_specs=[ANY, ANY],
-        out_shape=[f32(ROWS, DEPTH)] * 2,
+        in_specs=[SMEM] + [VMEM] * 27,
+        out_specs=[ANY, ANY, VMEM],
+        out_shape=[pltpu.HBM((ROWS, DEPTH), jnp.float32)] * 2
+        + [pltpu.VMEM((4, 2 * 17 * PLANES, 128), jnp.float32)],
+        input_output_aliases={2: 2},
         scratch_shapes=[
             pltpu.VMEM((80, COARSE), jnp.float32),
             pltpu.VMEM((80, DEPTH), jnp.float32),
-            pltpu.VMEM((4, 2 * 17 * PLANES, 128), jnp.float32),
-            big,
             big,
             pltpu.VMEM((4, PLANES, DEPTH), jnp.float32),
             big,
-            pltpu.SemaphoreType.DMA((9,)),
+            pltpu.SemaphoreType.DMA((16,)),
         ],
         compiler_params=ROOM,
         cost_estimate=pl.CostEstimate(flops=20 << 20, bytes_accessed=8 << 20, transcendentals=0),
         name="imaging",
-    )(source, along, *rims, in_hbm(first), second, *edges)
+    )(source, along, fine, *rims, first, second, *edges)
 
 
 def per_device(
@@ -428,27 +457,30 @@
     stiff = stiffness.reshape(ROWS, DEPTH)
     buoy = buoyancy.reshape(ROWS, DEPTH)
 
-    own = faces(current_field[0], buoyancy)
+    own = list(faces(current_field[0], buoyancy))
     far = exchange(own)
-    slot = lax.broadcasted_iota(jnp.int32, (32, 32), 1)
-    ids = jnp.where(slot < tile_counts[0, 0][:, None], tile_ids[0, 0], -1).reshape(1, 1024)
-    onehot = onehots(ids)
-    src = sources(receiver_cells[0], receiver_data[0])
-    tiles, far[2], far[3], onehot, src = lax.optimization_barrier(
-        (stored_tiles, far[2], far[3], onehot, src)
-    )
+    tiles, own[0] = lax.optimization_barrier((stored_tiles, own[0]))
     received = lax.all_to_all(
         tiles[0, 0], ("shot", "gx"), split_axis=0, concat_axis=0, tiled=True
     ).reshape(1024, COARSE)
+    numbers, counts, far = lax.optimization_barrier((tile_ids, tile_counts, far))
+    slot = lax.broadcasted_iota(jnp.int32, (32, 32), 1)
+    ids = jnp.where(slot < counts[0, 0][:, None], numbers[0, 0], -1).reshape(1, 1024)
+    onehot = onehots(ids)
+    src = sources(receiver_cells[0], receiver_data[0])
     second, *rest = inner(current, older, buoy, stiff, src, [*own, *far], 0)
     own2, stiff_faces = rest[:4], rest[4:]
     far2 = exchange(own2)
-
+    (third,) = inner(second, current, buoy, stiff, src, [], 1)
+
+    received, third = lax.optimization_barrier((received, third))
     along, rim_x, rim_y, corner = coarse_tiles(received, onehot)
     rims = [rotate(rim_x, "gx", -1), rotate(rim_y, "gy", -1), diagonal(corner)]
-    third = inner(second, current, buoy, stiff, src, [], 1)
+    fine, second_near, third_near = upsampling(along, second, third)
     edges = [*own, *far, *own2, *far2, *stiff_faces]
-    image, last_current = imaging(source_cell, along, rims, second, third, edges)
+    image, last_current, _ = imaging(
+        source_cell, along, fine, rims, second_near, third_near, edges
+    )
     shape = current_field.shape
     return image.reshape(shape), second.reshape(shape), last_current.reshape(shape)
 

time: 77.9 us -> 75.2 us (0.965)
  starting transfers between devices: 40 us -> 37.7 us
  waiting for transfers between devices: 13 us -> 11.1 us
  Pallas kernels: 23.3 us -> 24.8 us
    all_to_all x1, waiting for transfers between devices: 10.1 us -> 4.69 us  [per_device(): lax.all_to_all(tiles[0, 0], ('shot', 'gx'), split_axis=0, concat_axis=0,...]
    ppermute x10, waiting for transfers between devices: 2.9 us -> 6.38 us  [rotate(): lax.ppermute(block, axis, [(i, (i + step) % count) for i in range(count)])]
    ppermute x10, starting transfers between devices: 21.4 us -> 20.1 us  [rotate(): lax.ppermute(block, axis, [(i, (i + step) % count) for i in range(count)])]
    ppermute x1, starting transfers between devices: 7.02 us -> 5.97 us  [diagonal(): return lax.ppermute(block, ('gx', 'gy'), route)]
    pallas_call x2, Pallas kernels: 12.5 us -> 13.4 us  [inner(): pl.pallas_call(lambda *refs: inner_kernel(*refs, step=step), in_specs=[AN...]
    pallas_call x1 -> x2, Pallas kernels: 5.38 us -> 6.13 us  [the longest x1 3.88 us: imaging(): pl.pallas_call(image_kernel, in_specs=[SMEM] + [VMEM] * 27, out_specs=[AN...]
  transfers between devices with their start and end apart: 12 -> 12, of which waited for: 2 -> 2; matrix products, arithmetic and copies ran while one was open for 0% -> 0% of each run, Pallas kernels for 21% -> 26%
where the time goes in v4:
time: 75.2 us; the launch traced here: 74.8 us
  starting transfers between devices  37.7 us (50%)
  Pallas kernels  24.8 us (33%)
  waiting for transfers between devices  11.1 us (15%)
  between operations  0.98 us (1%)
    ppermute x10, starting transfers between devices, rotate(): lax.ppermute(block, axis, [(i, (i + step) % count) for i in range(count)])  20.1 us
    pallas_call x2, Pallas kernels, inner(): pl.pallas_call(lambda *refs: inner_kernel(*refs, step=step), in_specs=[AN...  13.4 us
    all_to_all x1, starting transfers between devices, per_device(): lax.all_to_all(tiles[0, 0], ('shot', 'gx'), split_axis=0, concat_axis=0,...  11.6 us
    ppermute x10, waiting for transfers between devices, rotate(): lax.ppermute(block, axis, [(i, (i + step) % count) for i in range(count)])  6.38 us
    ppermute x1, starting transfers between devices, diagonal(): return lax.ppermute(block, ('gx', 'gy'), route)  5.97 us
    all_to_all x1, waiting for transfers between devices, per_device(): lax.all_to_all(tiles[0, 0], ('shot', 'gx'), split_axis=0, concat_axis=0,...  4.69 us
    pallas_call x1, Pallas kernels, imaging(): pl.pallas_call(image_kernel, in_specs=[SMEM] + [VMEM] * 27, out_specs=[AN...  3.88 us
    pallas_call x1, Pallas kernels, coarse_tiles(): pl.pallas_call(coarse_kernel, in_specs=[VMEM, VMEM], out_specs=[VMEM] * 4...  2.56 us
  transfers between devices with their start and end apart: 12, of which 2 were waited for; matrix products, arithmetic and copies ran while one was open for 0% of the time, Pallas kernels for 26%

profile of v4, /device:TPU:39, one launch (start us, length us, event | category | flops | bytes accessed | tf_op | source)
XLA Modules:
  0.0 74.8 jit_solution(14808669681813676457)
XLA Ops:
  0.6 1.7 %faces.1 = (f32[2,32,512]{2,1,0:T(8,128)S(1)}, f32[2,32,512]{2,1,0:T(8,128)S(1)}, f32[2,32,512]{2,1,0:T(8,128)S(1)}, f32[2,32,512]{2,1,0:T(8,128)S(1)}) custom-call(f32[32,32,512]{2,1,0:T(8,128)} %bitcast.19, f32[32,32,512]{2,1,0:T(8,128)} %bitcast.20, f32[32,32,512]{2,1,0:T(8,128)} %bitcast.21, f32[32,32,512]{2,1,0:T(8,128)} %bitcast.22, ...), custom_call_target="tpu_custom_call" | custom-call | bytes 3145728 | tf_op jit(solution)/shard_map/faces/pallas_call | solution.py:51
  2.4 0.6 collective-permute-start.1
  3.0 6.9 %collective-permute-start = (f32[2,32,512]{2,1,0:T(8,128)S(1)}, f32[2,32,512]{2,1,0:T(8,128)S(1)}, u32[]{:S(2)}, u32[]{:S(2)}) collective-permute-start(f32[2,32,512]{2,1,0:T(8,128)S(1)} %get-tuple-element.38.refs_6_.rest_1_), channel_id=1, source_target_pairs={{0,8},{8,16},{16,24},{24,32},{32,40},{40,48},{48,56},{56,0},{1,9},... | collective-permute-start | bytes 393224 | tf_op jit(solution)/shard_map/ppermute | solution.py:24
  10.0 1.2 %collective-permute-start.3 = (f32[2,32,512]{2,1,0:T(8,128)S(1)}, f32[2,32,512]{2,1,0:T(8,128)S(1)}, u32[]{:S(2)}, u32[]{:S(2)}) collective-permute-start(f32[2,32,512]{2,1,0:T(8,128)S(1)} %get-tuple-element.39.refs_7_.rest_2_), channel_id=1, source_target_pairs={{0,7},{1,0},{2,1},{3,2},{4,3},{5,4},{6,5},{7,6},{8,15},{9,8},{10,9... | collective-permute-start | bytes 393224 | tf_op jit(solution)/shard_map/ppermute | solution.py:24
  11.2 1.5 %collective-permute-start.2 = (f32[2,32,512]{2,1,0:T(8,128)S(1)}, f32[2,32,512]{2,1,0:T(8,128)S(1)}, u32[]{:S(2)}, u32[]{:S(2)}) collective-permute-start(f32[2,32,512]{2,1,0:T(8,128)S(1)} %get-tuple-element.40.refs_8_.rest_3_), channel_id=1, source_target_pairs={{0,1},{1,2},{2,3},{3,4},{4,5},{5,6},{6,7},{7,0},{8,9},{9,10},{10,1... | collective-permute-start | bytes 393224 | tf_op jit(solution)/shard_map/ppermute | solution.py:24
  12.7 11.6 %all-to-all-start = ((f32[32,32,256]{2,1,0:T(8,128)}), f32[32,32,256]{2,1,0:T(8,128)}, u32[]{:S(2)}, u32[]{:S(2)}) async-start(f32[32,32,256]{2,1,0:T(8,128)} %bitcast.1), calls=%async_computation | async-start | bytes 2097152 | tf_op jit(solution)/shard_map/all_to_all | solution.py:463
  24.4 0.1 iota_compare_fusion
  24.5 0.1 lt.23
  24.6 0.1 squeeze.19
  24.7 0.8 %sources.1.refs_4_ = f32[2,1024,128]{2,1,0:T(8,128)S(1)} custom-call(s32[3,1024]{1,0:T(4,128)S(1)} %bitcast.17, f32[2,1024]{1,0:T(2,128)S(1)} %bitcast.18), custom_call_target="tpu_custom_call" | custom-call | flops 1 | bytes 1 | tf_op jit(solution)/shard_map/sources/pallas_call | solution.py:93
  25.5 0.2 onehots.1.onehot
  25.7 7.0 %inner0.1 = (f32[1024,512]{1,0:T(8,128)}, f32[1,32,512]{2,1,0:T(8,128)}, f32[1,32,512]{2,1,0:T(8,128)}, f32[1,32,512]{2,1,0:T(8,128)}, f32[1,32,512]{2,1,0:T(8,1...) custom-call(f32[1024,512]{1,0:T(8,128)} %bitcast.23, ...), custom_call_target="tpu_custom_call" | custom-call | flops 1099511627776 | bytes 10485760 | tf_op jit(solution)/shard_map/inner0/pallas_call | solution.py:257
  32.8 0.6 collective-permute-start.8
  33.4 6.9 %collective-permute-start.7 = (f32[1,32,512]{2,1,0:T(8,128)}, f32[1,32,512]{2,1,0:T(8,128)}, u32[]{:S(2)}, u32[]{:S(2)}) collective-permute-start(f32[1,32,512]{2,1,0:T(8,128)} %get-tuple-element.58.rest_9_), channel_id=1, source_target_pairs={{0,8},{8,16},{16,24},{24,32},{32,40},{40,48},{48,56},{56,0},{1,9},... | collective-permute-start | bytes 196616 | tf_op jit(solution)/shard_map/ppermute | solution.py:24
  40.3 1.0 %collective-permute-start.10 = (f32[1,32,512]{2,1,0:T(8,128)}, f32[1,32,512]{2,1,0:T(8,128)}, u32[]{:S(2)}, u32[]{:S(2)}) collective-permute-start(f32[1,32,512]{2,1,0:T(8,128)} %get-tuple-element.59.rest_10_), channel_id=1, source_target_pairs={{0,7},{1,0},{2,1},{3,2},{4,3},{5,4},{6,5},{7,6},{8,15},{9,8},{10,9... | collective-permute-start | bytes 196616 | tf_op jit(solution)/shard_map/ppermute | solution.py:24
  41.3 0.8 %collective-permute-start.9 = (f32[1,32,512]{2,1,0:T(8,128)}, f32[1,32,512]{2,1,0:T(8,128)}, u32[]{:S(2)}, u32[]{:S(2)}) collective-permute-start(f32[1,32,512]{2,1,0:T(8,128)} %get-tuple-element.60.rest_11_), channel_id=1, source_target_pairs={{0,1},{1,2},{2,3},{3,4},{4,5},{5,6},{6,7},{7,0},{8,9},{9,10},{10,1... | collective-permute-start | bytes 196616 | tf_op jit(solution)/shard_map/ppermute | solution.py:24
  42.1 6.3 %inner1.1.second_hbm = f32[1024,512]{1,0:T(8,128)} custom-call(f32[1024,512]{1,0:T(8,128)} %get-tuple-element.45.refs_0_.first_hbm, f32[1024,512]{1,0:T(8,128)} %bitcast.24, f32[1024,512]{1,0:T(8,128)} %bitcast.26, f32[1024,512]{1,0:T(8,128)} %bitcast.30, f32[2,1024,128]{2,1,0:T(8,128)S(1)} %sources.1.refs_4_), custom_call_target="tpu_custom_call" | custom-call | flops 1099511627776 | bytes 10485760 | tf_op jit(solution)/shard_map/inner1/pallas_call | solution.py:257
  48.4 4.7 %all-to-all-done = f32[32,32,256]{2,1,0:T(8,128)} async-done(((f32[32,32,256]{2,1,0:T(8,128)}), f32[32,32,256]{2,1,0:T(8,128)}, u32[]{:S(2)}, u32[]{:S(2)}) %all-to-all-start) | async-done | bytes 1048608 | tf_op jit(solution)/shard_map/all_to_all | solution.py:463
  53.1 2.6 %coarse_tiles.1 = (f32[512,512]{1,0:T(8,128)S(1)}, f32[2,16,256]{2,1,0:T(8,128)}, f32[2,16,256]{2,1,0:T(8,128)}, f32[2,8,256]{2,1,0:T(8,128)}) custom-call(f32[1024,256]{1,0:T(8,128)} %bitcast.2.received, bf16[512,1024]{1,0:T(8,128)(2,1)S(1)} %onehots.1.onehot), custom_call_target="tpu_custom_call" | custom-call | flops 1073741824 | bytes 3145728 | tf_op jit(solution)/shard_map/coarse_tiles/pallas_call | solution.py:298
  55.7 6.0 %collective-permute-start.6 = (f32[2,8,256]{2,1,0:T(8,128)}, f32[2,8,256]{2,1,0:T(8,128)}, u32[]{:S(2)}, u32[]{:S(2)}) collective-permute-start(f32[2,8,256]{2,1,0:T(8,128)} %get-tuple-element.54), channel_id=1, source_target_pairs={{0,63},{1,56},{2,57},{3,58},{4,59},{5,60},{6,61},{7,62},{8,7},{9,0... | collective-permute-start | bytes 49160 | tf_op jit(solution)/shard_map/ppermute | solution.py:498
  61.7 0.4 collective-permute-start.5
  62.1 2.3 %upsampling.1 = (f32[4,1088,128]{2,1,0:T(8,128)S(1)}, f32[1024,512]{1,0:T(8,128)S(1)}, f32[1024,512]{1,0:T(8,128)S(1)}) custom-call(f32[512,512]{1,0:T(8,128)S(1)} %get-tuple-element.49.along, f32[1024,512]{1,0:T(8,128)} %get-tuple-element.45.refs_0_.first_hbm, f32[1024,512]{1,0:T(8,128)} %inner1.1.second_hbm), custom_call_target="tpu_custom_call" | custom-call | flops 1099511627776 | bytes 8388608 | tf_op jit(solution)/shard_map/upsampling/pallas_call | solution.py:332
  64.4 6.4 %collective-permute-done.4.rim_x = f32[2,16,256]{2,1,0:T(8,128)} collective-permute-done((f32[2,16,256]{2,1,0:T(8,128)}, f32[2,16,256]{2,1,0:T(8,128)}, u32[]{:S(2)}, u32[]{:S(2)}) %collective-permute-start.4) | collective-permute-done | bytes 32800 | tf_op jit(solution)/shard_map/ppermute | solution.py:24
  70.8 3.9 %imaging.1 = (f32[1024,512]{1,0:T(8,128)}, f32[1024,512]{1,0:T(8,128)}, f32[4,1088,128]{2,1,0:T(8,128)S(1)}) custom-call(s32[1,3]{1,0:T(1,128)S(1)} %copy-done.1, f32[512,512]{1,0:T(8,128)S(1)} %get-tuple-element.49.along, f32[4,1088,128]{2,1,0:T(8,128)S(1)} %get-tuple-element.51.fine_in, ...), custom_call_target="tpu_custom_call", output_to_operand_aliasing={{2}: (2, {})} | custom-call | flops 20971520 | bytes 8388608 | tf_op jit(solution)/shard_map/imaging/pallas_call | solution.py:422
  (23 shorter events, 0.1 us)
Async XLA Ops:
  2.3 22.0 %copy-start.3 = (s32[1,3,1024]{2,0,1:T(1,128)S(1)}, s32[1,3,1024]{2,0,1:T(1,128)}, u32[]{:S(2)}) copy-start(s32[1,3,1024]{2,0,1:T(1,128)} %param.17) | copy-start | bytes 36868
  2.4 22.1 %copy-start.4 = (s32[1,1,32]{2,1,0:T(1,128)S(1)}, s32[1,1,32]{2,1,0:T(1,128)}, u32[]{:S(2)}) copy-start(s32[1,1,32]{2,1,0:T(1,128)} %param.16) | copy-start | bytes 388
  2.4 22.2 %copy-start.2 = (s32[1,1,32,32]{3,2,1,0:T(8,128)S(1)}, s32[1,1,32,32]{3,2,1,0:T(8,128)}, u32[]{:S(2)}) copy-start(s32[1,1,32,32]{3,2,1,0:T(8,128)} %param.15) | copy-start | bytes 12292
  2.4 22.3 %copy-start = (f32[1,2,1024]{2,1,0:T(2,128)S(1)}, f32[1,2,1024]{2,1,0:T(2,128)}, u32[]{:S(2)}) copy-start(f32[1,2,1024]{2,1,0:T(2,128)} %param.18) | copy-start | bytes 24580
  2.4 22.0 %collective-permute-start.1 = (f32[2,32,512]{2,1,0:T(8,128)S(1)}, f32[2,32,512]{2,1,0:T(8,128)S(1)}, u32[]{:S(2)}, u32[]{:S(2)}) collective-permute-start(f32[2,32,512]{2,1,0:T(8,128)S(1)} %get-tuple-element.37.refs_5_.rest_0_), channel_id=1, source_target_pairs={{0,56},{8,0},{16,8},{24,16},{32,24},{40,32},{48,40},{56,48},{1,57}... | collective-permute-start | bytes 393224 | tf_op jit(solution)/shard_map/ppermute | solution.py:24
  3.0 21.4 %collective-permute-start = (f32[2,32,512]{2,1,0:T(8,128)S(1)}, f32[2,32,512]{2,1,0:T(8,128)S(1)}, u32[]{:S(2)}, u32[]{:S(2)}) collective-permute-start(f32[2,32,512]{2,1,0:T(8,128)S(1)} %get-tuple-element.38.refs_6_.rest_1_), channel_id=1, source_target_pairs={{0,8},{8,16},{16,24},{24,32},{32,40},{40,48},{48,56},{56,0},{1,9},... | collective-permute-start | bytes 393224 | tf_op jit(solution)/shard_map/ppermute | solution.py:24
  10.0 14.4 %collective-permute-start.3 = (f32[2,32,512]{2,1,0:T(8,128)S(1)}, f32[2,32,512]{2,1,0:T(8,128)S(1)}, u32[]{:S(2)}, u32[]{:S(2)}) collective-permute-start(f32[2,32,512]{2,1,0:T(8,128)S(1)} %get-tuple-element.39.refs_7_.rest_2_), channel_id=1, source_target_pairs={{0,7},{1,0},{2,1},{3,2},{4,3},{5,4},{6,5},{7,6},{8,15},{9,8},{10,9... | collective-permute-start | bytes 393224 | tf_op jit(solution)/shard_map/ppermute | solution.py:24
  11.2 13.2 %collective-permute-start.2 = (f32[2,32,512]{2,1,0:T(8,128)S(1)}, f32[2,32,512]{2,1,0:T(8,128)S(1)}, u32[]{:S(2)}, u32[]{:S(2)}) collective-permute-start(f32[2,32,512]{2,1,0:T(8,128)S(1)} %get-tuple-element.40.refs_8_.rest_3_), channel_id=1, source_target_pairs={{0,1},{1,2},{2,3},{3,4},{4,5},{5,6},{6,7},{7,0},{8,9},{9,10},{10,1... | collective-permute-start | bytes 393224 | tf_op jit(solution)/shard_map/ppermute | solution.py:24
  12.7 40.4 %all-to-all-start = ((f32[32,32,256]{2,1,0:T(8,128)}), f32[32,32,256]{2,1,0:T(8,128)}, u32[]{:S(2)}, u32[]{:S(2)}) async-start(f32[32,32,256]{2,1,0:T(8,128)} %bitcast.1), calls=%async_computation | async-start | bytes 2097152 | tf_op jit(solution)/shard_map/all_to_all | solution.py:463
  32.8 28.9 %collective-permute-start.8 = (f32[1,32,512]{2,1,0:T(8,128)}, f32[1,32,512]{2,1,0:T(8,128)}, u32[]{:S(2)}, u32[]{:S(2)}) collective-permute-start(f32[1,32,512]{2,1,0:T(8,128)} %get-tuple-element.57.rest_8_), channel_id=1, source_target_pairs={{0,56},{8,0},{16,8},{24,16},{32,24},{40,32},{48,40},{56,48},{1,57}... | collective-permute-start | bytes 196616 | tf_op jit(solution)/shard_map/ppermute | solution.py:24
  33.4 28.3 %collective-permute-start.7 = (f32[1,32,512]{2,1,0:T(8,128)}, f32[1,32,512]{2,1,0:T(8,128)}, u32[]{:S(2)}, u32[]{:S(2)}) collective-permute-start(f32[1,32,512]{2,1,0:T(8,128)} %get-tuple-element.58.rest_9_), channel_id=1, source_target_pairs={{0,8},{8,16},{16,24},{24,32},{32,40},{40,48},{48,56},{56,0},{1,9},... | collective-permute-start | bytes 196616 | tf_op jit(solution)/shard_map/ppermute | solution.py:24
  40.3 24.1 %collective-permute-start.10 = (f32[1,32,512]{2,1,0:T(8,128)}, f32[1,32,512]{2,1,0:T(8,128)}, u32[]{:S(2)}, u32[]{:S(2)}) collective-permute-start(f32[1,32,512]{2,1,0:T(8,128)} %get-tuple-element.59.rest_10_), channel_id=1, source_target_pairs={{0,7},{1,0},{2,1},{3,2},{4,3},{5,4},{6,5},{7,6},{8,15},{9,8},{10,9... | collective-permute-start | bytes 196616 | tf_op jit(solution)/shard_map/ppermute | solution.py:24
  41.3 23.1 %collective-permute-start.9 = (f32[1,32,512]{2,1,0:T(8,128)}, f32[1,32,512]{2,1,0:T(8,128)}, u32[]{:S(2)}, u32[]{:S(2)}) collective-permute-start(f32[1,32,512]{2,1,0:T(8,128)} %get-tuple-element.60.rest_11_), channel_id=1, source_target_pairs={{0,1},{1,2},{2,3},{3,4},{4,5},{5,6},{6,7},{7,0},{8,9},{9,10},{10,1... | collective-permute-start | bytes 196616 | tf_op jit(solution)/shard_map/ppermute | solution.py:24
  55.7 8.7 %collective-permute-start.6 = (f32[2,8,256]{2,1,0:T(8,128)}, f32[2,8,256]{2,1,0:T(8,128)}, u32[]{:S(2)}, u32[]{:S(2)}) collective-permute-start(f32[2,8,256]{2,1,0:T(8,128)} %get-tuple-element.54), channel_id=1, source_target_pairs={{0,63},{1,56},{2,57},{3,58},{4,59},{5,60},{6,61},{7,62},{8,7},{9,0... | collective-permute-start | bytes 49160 | tf_op jit(solution)/shard_map/ppermute | solution.py:498
  61.7 9.1 %collective-permute-start.4 = (f32[2,16,256]{2,1,0:T(8,128)}, f32[2,16,256]{2,1,0:T(8,128)}, u32[]{:S(2)}, u32[]{:S(2)}) collective-permute-start(f32[2,16,256]{2,1,0:T(8,128)} %get-tuple-element.52), channel_id=1, source_target_pairs={{0,56},{8,0},{16,8},{24,16},{32,24},{40,32},{48,40},{56,48},{1,57}... | collective-permute-start | bytes 98312 | tf_op jit(solution)/shard_map/ppermute | solution.py:24
  61.7 9.1 %collective-permute-start.5 = (f32[2,16,256]{2,1,0:T(8,128)}, f32[2,16,256]{2,1,0:T(8,128)}, u32[]{:S(2)}, u32[]{:S(2)}) collective-permute-start(f32[2,16,256]{2,1,0:T(8,128)} %get-tuple-element.53), channel_id=1, source_target_pairs={{0,7},{1,0},{2,1},{3,2},{4,3},{5,4},{6,5},{7,6},{8,15},{9,8},{10,9... | collective-permute-start | bytes 98312 | tf_op jit(solution)/shard_map/ppermute | solution.py:24
  62.1 8.7 %copy-start.1 = (s32[1,3]{1,0:T(1,128)S(1)}, s32[1,3]{1,0:T(1,128)}, u32[]{:S(2)}) copy-start(s32[1,3]{1,0:T(1,128)} %source.1) | copy-start | bytes 40

commit v5 on v2

--- a/solution.py
+++ b/solution.py
@@ -95,7 +95,7 @@
         in_specs=[VMEM, VMEM],
         out_specs=VMEM,
         out_shape=f32(2, ROWS, 128),
-        cost_estimate=pl.CostEstimate(flops=1 << 29, bytes_accessed=2 << 20, transcendentals=0),
+        cost_estimate=pl.CostEstimate(flops=1, bytes_accessed=1, transcendentals=0),
         compiler_params=ROOM,
         name="sources",
     )(cells, data)
@@ -113,7 +113,7 @@
         in_specs=[VMEM],
         out_specs=VMEM,
         out_shape=jax.ShapeDtypeStruct((512, 1024), jnp.bfloat16),
-        cost_estimate=pl.CostEstimate(flops=1 << 20, bytes_accessed=2 << 20, transcendentals=0),
+        cost_estimate=pl.CostEstimate(flops=1, bytes_accessed=1, transcendentals=0),
         compiler_params=ROOM,
         name="onehots",
     )(ids)
@@ -121,6 +121,26 @@
 
 def in_hbm(x):
     return pltpu.with_memory_space_constraint(x, pltpu.HBM)
+
+
+def sides():
+    gx = lax.axis_index("gx")
+    gy = lax.axis_index("gy")
+    return [
+        jnp.where(gx > 0, 1.0, 0.0),
+        jnp.where(gx < lax.axis_size("gx") - 1, 1.0, 0.0),
+        jnp.where(gy > 0, 1.0, 0.0),
+        jnp.where(gy < lax.axis_size("gy") - 1, 1.0, 0.0),
+    ]
+
+
+def edge_terms(own_b, far_b, own_f, far_f, stiff):
+    terms = []
+    for side, keep in enumerate(sides()):
+        coef = 0.5 * (own_b[side][1] + keep * far_b[side][1])
+        flux = coef * (keep * far_f[side] - own_f[side])
+        terms.append(stiff[side][...] * flux)
+    return terms
 
 
 def inner_kernel(field, older, buoy, stiff, src, *rest, step):
@@ -151,12 +171,12 @@
             copy.wait()
         if step == 1:
             if chunk == 0:
-                f_buf[0:PLANES, :] = fixed[0][0]
+                f_buf[0:PLANES, :] = fixed[0][0:PLANES]
             if chunk == CHUNKS - 1:
-                f_buf[ROWS - PLANES : ROWS, :] = fixed[1][0]
+                f_buf[ROWS - PLANES : ROWS, :] = fixed[1][0:PLANES]
             for x in range(chunk * PER, chunk * PER + PER):
-                f_buf[x * PLANES : x * PLANES + 1, :] = fixed[2][0, x : x + 1, :]
-                f_buf[x * PLANES + 31 : x * PLANES + 32, :] = fixed[3][0, x : x + 1, :]
+                f_buf[x * PLANES : x * PLANES + 1, :] = fixed[2][x : x + 1, :]
+                f_buf[x * PLANES + 31 : x * PLANES + 32, :] = fixed[3][x : x + 1, :]
             part = pl.ds(chunk * SPAN, SPAN)
             copy = pltpu.make_async_copy(f_buf.at[part], saved.at[part], out_sem.at[chunk])
             copy.start()
@@ -235,7 +255,7 @@
         out_shape = [pltpu.HBM((ROWS, DEPTH), jnp.float32)] + [f32(PLANES, DEPTH)] * 8
         out_specs = [ANY] + [VMEM] * 8
     else:
-        out_shape = [big, f32(ROWS, DEPTH)]
+        out_shape = [big, pltpu.HBM((ROWS, DEPTH), jnp.float32)]
         out_specs = [VMEM, ANY]
     return pl.pallas_call(
         lambda *refs: inner_kernel(*refs, step=step),
@@ -245,53 +265,41 @@
         scratch_shapes=[big] * (5 - step)
         + [pltpu.SemaphoreType.DMA((CHUNKS, 4)), pltpu.SemaphoreType.DMA((CHUNKS,))],
         compiler_params=ROOM,
-        cost_estimate=pl.CostEstimate(flops=20 << 20, bytes_accessed=10 << 20, transcendentals=0),
+        cost_estimate=pl.CostEstimate(flops=1 << 40, bytes_accessed=10 << 20, transcendentals=0),
         name="inner%d" % step,
     )(in_hbm(field), in_hbm(older), in_hbm(buoy), in_hbm(stiff), src, *fixed)
 
 
-def edge_terms(own_b, far_b, own_f, far_f, stiff):
-    gx = lax.axis_index("gx")
-    gy = lax.axis_index("gy")
-    keep = [
-        jnp.where(gx > 0, 1.0, 0.0),
-        jnp.where(gx < lax.axis_size("gx") - 1, 1.0, 0.0),
-        jnp.where(gy > 0, 1.0, 0.0),
-        jnp.where(gy < lax.axis_size("gy") - 1, 1.0, 0.0),
-    ]
-    terms = []
+def fix_kernel(*refs):
+    own, far, value, stiff = (refs[4 * k : 4 * k + 4] for k in range(4))
+    rim_x, rim_y = refs[16:18]
+    out, terms = refs[18:22], refs[22]
+    first = [ref[0] for ref in own]
+    second = [ref[0] for ref in far]
+    for side, term in enumerate(edge_terms(own, far, first, second, stiff)):
+        terms[side] = term
+        out[side][0:PLANES] = value[side][...] + term
     for side in range(4):
-        coef = 0.5 * (own_b[side][1] + keep[side] * far_b[side][1])
-        flux = coef * (keep[side] * far_f[side][0] - own_f[side][0])
-        terms.append(stiff[side][...] * flux)
-    return terms
-
-
-def fix_kernel(*refs):
-    own, far, value, stiff, out = (refs[4 * k : 4 * k + 4] for k in range(5))
-    terms = refs[20]
-    for side, term in enumerate(edge_terms(own, far, own, far, stiff)):
-        terms[side] = term
-        out[side][0] = value[side][...] + term
-    for side in range(4):
+        at = slice(31 * (side % 2), 31 * (side % 2) + 1)
         for end in range(2):
             row = slice(31 * end, 31 * end + 1)
             other = (2 if side < 2 else 0) + end
-            at = slice(31 * (side % 2), 31 * (side % 2) + 1)
-            out[side][0, row, :] += terms[other, at, :]
-
-
-def fix_faces(own, far, values, stiff):
+            out[side][row, :] += terms[other, at, :]
+    out[0][PLANES : PLANES + 16] = rim_x[...]
+    out[2][PLANES : PLANES + 16] = rim_y[...]
+
+
+def fix_faces(own, far, values, stiff, rim_x, rim_y):
     return pl.pallas_call(
         fix_kernel,
-        in_specs=[VMEM] * 16,
+        in_specs=[VMEM] * 18,
         out_specs=[VMEM] * 4,
-        out_shape=[f32(1, PLANES, DEPTH)] * 4,
+        out_shape=[f32(PLANES + 16, DEPTH), f32(PLANES, DEPTH)] * 2,
         scratch_shapes=[pltpu.VMEM((4, PLANES, DEPTH), jnp.float32)],
         compiler_params=ROOM,
         cost_estimate=pl.CostEstimate(flops=1 << 20, bytes_accessed=2 << 20, transcendentals=0),
         name="fix_faces",
-    )(*own, *far, *values, *stiff)
+    )(*own, *far, *values, *stiff, rim_x, rim_y)
 
 
 def interpolation():
@@ -305,19 +313,19 @@
     return jnp.dot(a, b, preferred_element_type=jnp.float32)
 
 
-def coarse_kernel(received, onehot, along, rim_x, rim_y, corner, rows):
+def coarse_kernel(received, onehot, along, rim_x, rim_y, rows):
     high, low = split_bf16(received[...])
     c_high = dot(onehot[...], high)
     c_low = dot(onehot[...], low)
     coarse = c_high + c_low
     for n in range(2):
-        rim_x[n] = coarse[n * 256 : n * 256 + 16, :]
-        corner[n] = coarse[n * 256 : n * 256 + 8, :]
-    for half in range(2):
-        lanes = slice(half * 128, half * 128 + 128)
-        rows[half] = coarse[:, lanes]
-        for n in range(2):
-            rim_y[n, :, lanes] = rows[half, pl.ds(n * 256, 16, stride=16), :]
+        for half in range(2):
+            lanes = slice(half * 128, half * 128 + 128)
+            spot = slice(n * 256 + half * 128, n * 256 + half * 128 + 128)
+            rim_x[:, spot] = coarse[n * 256 : n * 256 + 16, lanes]
+            if n == 0:
+                rows[half] = coarse[:, lanes]
+            rim_y[:, spot] = rows[half, pl.ds(n * 256, 16, stride=16), :]
     weights = interpolation()
     along[...] = dot(c_high.astype(jnp.bfloat16), weights) + dot(c_low.astype(jnp.bfloat16), weights)
 
@@ -326,8 +334,8 @@
     return pl.pallas_call(
         coarse_kernel,
         in_specs=[VMEM, VMEM],
-        out_specs=[VMEM] * 4,
-        out_shape=[f32(512, DEPTH), f32(2, 16, COARSE), f32(2, 16, COARSE), f32(2, 8, COARSE)],
+        out_specs=[VMEM] * 3,
+        out_shape=[f32(512, DEPTH), f32(16, DEPTH), f32(16, DEPTH)],
         scratch_shapes=[pltpu.VMEM((2, 512, 128), jnp.float32)],
         compiler_params=ROOM,
         cost_estimate=pl.CostEstimate(flops=1 << 30, bytes_accessed=3 << 20, transcendentals=0),
@@ -335,46 +343,93 @@
     )(received, onehot)
 
 
-def image_kernel(source, along, rim_x, rim_y, corner, first_hbm, second, *rest):
+def corner_kernel(message, out):
+    out[...] = message[PLANES : PLANES + 8, :]
+
+
+def corner_block(message):
+    return pl.pallas_call(
+        corner_kernel,
+        in_specs=[VMEM],
+        out_specs=VMEM,
+        out_shape=f32(8, DEPTH),
+        compiler_params=ROOM,
+        name="corner_block",
+    )(message)
+
+
+def upsample_kernel(along, first_hbm, fine, first, sem):
+    load = pltpu.make_async_copy(first_hbm, first, sem)
+    load.start()
+    for n in range(2):
+        for k in range(16):
+            rows = along[n * 256 + k * 16 : n * 256 + k * 16 + 16, :]
+            middle = 0.5 * (rows + pltpu.roll(rows, 15, 0))
+            base = (n * 17 + k) * PLANES
+            for part in range(4):
+                lanes = slice(part * 128, part * 128 + 128)
+                fine[part, pl.ds(base, 16, stride=2), :] = rows[:, lanes]
+                fine[part, pl.ds(base + 1, 16, stride=2), :] = middle[:, lanes]
+    load.wait()
+
+
+def upsampling(along, first):
+    return pl.pallas_call(
+        upsample_kernel,
+        in_specs=[VMEM, ANY],
+        out_specs=[VMEM] * 2,
+        out_shape=[
+            pltpu.VMEM((4, 2 * 17 * PLANES, 128), jnp.float32),
+            pltpu.VMEM((ROWS, DEPTH), jnp.float32),
+        ],
+        scratch_shapes=[pltpu.SemaphoreType.DMA],
+        compiler_params=ROOM,
+        cost_estimate=pl.CostEstimate(flops=1 << 40, bytes_accessed=8 << 20, transcendentals=0),
+        name="upsampling",
+    )(along, in_hbm(first))
+
+
+def image_kernel(source, along, fine_in, corner, first, second, *rest):
     own, far, own2, far2, stiff = (rest[4 * k : 4 * k + 4] for k in range(5))
-    image, saved, rims, rim_along, fine, out, first, terms, third, sem = rest[20:]
-    load = pltpu.make_async_copy(first_hbm, first, sem.at[0])
-    load.start()
-    for side, term in enumerate(edge_terms(own, far, own2, far2, stiff)):
+    image, saved, fine, rims, rim_along, out, terms, third, sem = rest[20:]
+    near = [ref[0:PLANES] for ref in own2]
+    distant = [ref[0:PLANES] for ref in far2]
+    for side, term in enumerate(edge_terms(own, far, near, distant, stiff)):
         terms[side] = term
     gx = lax.axis_index("gx")
     gy = lax.axis_index("gy")
     keep_x = jnp.where(gx < lax.axis_size("gx") - 1, 1.0, 0.0)
     keep_y = jnp.where(gy < lax.axis_size("gy") - 1, 1.0, 0.0)
     for n in range(2):
-        rims[n * 40 : n * 40 + 16] = rim_x[n] * keep_x
-        rims[n * 40 + 16 : n * 40 + 32] = rim_y[n] * keep_y
-        rims[n * 40 + 32 : n * 40 + 40] = corner[n] * (keep_x * keep_y)
+        lanes = slice(n * 256, n * 256 + 256)
+        rims[n * 40 : n * 40 + 16] = far2[1][PLANES : PLANES + 16, lanes] * keep_x
+        rims[n * 40 + 16 : n * 40 + 32] = far2[3][PLANES : PLANES + 16, lanes] * keep_y
+        rims[n * 40 + 32 : n * 40 + 40] = corner[:, lanes] * (keep_x * keep_y)
     weights = interpolation()
     high, low = split_bf16(rims[...])
     rim_along[...] = dot(high, weights) + dot(low, weights)
     row16 = lax.broadcasted_iota(jnp.int32, (16, DEPTH), 0)
     for n in range(2):
-        for k in range(17):
-            if k < 16:
-                rows = along[n * 256 + k * 16 : n * 256 + k * 16 + 16, :]
-                side = rim_along[n * 40 + 16 + k : n * 40 + 17 + k, :]
-            else:
-                rows = rim_along[n * 40 : n * 40 + 16, :]
-                side = rim_along[n * 40 + 32 : n * 40 + 33, :]
-            upper = jnp.where(row16 == 15, side, pltpu.roll(rows, 15, 0))
-            base = (n * 17 + k) * PLANES
-            middle = 0.5 * (rows + upper)
+        rows = rim_along[n * 40 : n * 40 + 16, :]
+        side = rim_along[n * 40 + 32 : n * 40 + 33, :]
+        middle = 0.5 * (rows + jnp.where(row16 == 15, side, pltpu.roll(rows, 15, 0)))
+        base = (n * 17 + 16) * PLANES
+        for part in range(4):
+            lanes = slice(part * 128, part * 128 + 128)
+            fine[part, pl.ds(base, 16, stride=2), :] = rows[:, lanes]
+            fine[part, pl.ds(base + 1, 16, stride=2), :] = middle[:, lanes]
+        for k in range(16):
+            last = n * 256 + k * 16 + 15
+            pair = n * 40 + 16 + k
+            middle = 0.5 * (along[last : last + 1, :] + rim_along[pair : pair + 1, :])
+            row = (n * 17 + k) * PLANES + 31
             for part in range(4):
-                lanes = slice(part * 128, part * 128 + 128)
-                fine[part, pl.ds(base, 16, stride=2), :] = rows[:, lanes]
-                fine[part, pl.ds(base + 1, 16, stride=2), :] = middle[:, lanes]
+                fine[part, row : row + 1, :] = middle[:, part * 128 : part * 128 + 128]
     scale = -1.0 / (2.0 * MUTE_RADIUS * MUTE_RADIUS)
     y = (lax.broadcasted_iota(jnp.int32, (PLANES, DEPTH), 0) + gy * PLANES - source[0, 1]).astype(jnp.float32)
     z = (lax.broadcasted_iota(jnp.int32, (PLANES, DEPTH), 1) - source[0, 2]).astype(jnp.float32)
     decay_yz = jnp.exp((y * y + z * z) * scale)
     x_base = gx * PLANES - source[0, 0]
-    load.wait()
     copies = []
     for k in range(16):
         for odd in range(2):
@@ -403,37 +458,37 @@
                 out[at, lanes] = taper * (
                     snaps[0] * first[at, lanes] + snaps[1] * third[at, lanes]
                 )
-        if k % 4 == 3:
-            rows = pl.ds((k - 3) * 2 * PLANES, 8 * PLANES)
+        if k % 2 == 1:
+            rows = pl.ds((k - 1) * 2 * PLANES, 4 * PLANES)
             for pos, (here, there) in enumerate(((out, image), (third, saved))):
-                slot = 1 + 2 * (k // 4) + pos
+                slot = 2 * (k // 2) + pos
                 copies.append(pltpu.make_async_copy(here.at[rows], there.at[rows], sem.at[slot]))
                 copies[-1].start()
     for copy in copies:
         copy.wait()
 
 
-def imaging(source, along, rims, first, second, edges):
+def imaging(source, along, fine, corner, first, second, edges):
     big = pltpu.VMEM((ROWS, DEPTH), jnp.float32)
     return pl.pallas_call(
         image_kernel,
-        in_specs=[SMEM] + [VMEM] * 4 + [ANY] + [VMEM] * 21,
-        out_specs=[ANY, ANY],
-        out_shape=[f32(ROWS, DEPTH)] * 2,
+        in_specs=[SMEM] + [VMEM] * 25,
+        out_specs=[ANY, ANY, VMEM],
+        out_shape=[pltpu.HBM((ROWS, DEPTH), jnp.float32)] * 2
+        + [pltpu.VMEM((4, 2 * 17 * PLANES, 128), jnp.float32)],
+        input_output_aliases={2: 2},
         scratch_shapes=[
             pltpu.VMEM((80, COARSE), jnp.float32),
             pltpu.VMEM((80, DEPTH), jnp.float32),
-            pltpu.VMEM((4, 2 * 17 * PLANES, 128), jnp.float32),
-            big,
             big,
             pltpu.VMEM((4, PLANES, DEPTH), jnp.float32),
             big,
-            pltpu.SemaphoreType.DMA((9,)),
+            pltpu.SemaphoreType.DMA((16,)),
         ],
         compiler_params=ROOM,
         cost_estimate=pl.CostEstimate(flops=20 << 20, bytes_accessed=8 << 20, transcendentals=0),
         name="imaging",
-    )(source, along, *rims, in_hbm(first), second, *edges)
+    )(source, along, fine, corner, first, second, *edges)
 
 
 def per_device(
@@ -453,41 +508,34 @@
     stiff = stiffness.reshape(ROWS, DEPTH)
     buoy = buoyancy.reshape(ROWS, DEPTH)
 
+    received = lax.all_to_all(
+        stored_tiles[0, 0], ("shot", "gx"), split_axis=0, concat_axis=0, tiled=True
+    ).reshape(1024, COARSE)
     own = faces(current_field[0], buoyancy)
     far = exchange(own)
-    tiles, own = lax.optimization_barrier((stored_tiles, own))
-    received = lax.all_to_all(
-        tiles[0, 0], ("shot", "gx"), split_axis=0, concat_axis=0, tiled=True
-    ).reshape(1024, COARSE)
     slot = lax.broadcasted_iota(jnp.int32, (32, 32), 1)
     ids = jnp.where(slot < tile_counts[0, 0][:, None], tile_ids[0, 0], -1).reshape(1, 1024)
     onehot = onehots(ids)
     src = sources(receiver_cells[0], receiver_data[0])
     partial, *rest = inner(current, older, buoy, stiff, src, [], 0)
     values, stiff_faces = rest[:4], rest[4:]
-    own2 = fix_faces(own, far, values, stiff_faces)
+    along, rim_x, rim_y = coarse_tiles(received, onehot)
+    own2 = fix_faces(own, far, values, stiff_faces, rim_x, rim_y)
     far2 = exchange(own2)
-
-    along, rim_x, rim_y, corner = coarse_tiles(received, onehot)
-    rims = [rotate(rim_x, "gx", -1), rotate(rim_y, "gy", -1), diagonal(corner)]
-    third, last_older = inner(partial, current, buoy, stiff, src, own2, 1)
+    third, second = inner(partial, current, buoy, stiff, src, own2, 1)
+    corner = rotate(corner_block(far2[1]), "gy", -1)
+    fine, second_near = upsampling(along, second)
     edges = [*own, *far, *own2, *far2, *stiff_faces]
-    image, last_current = imaging(source_cell, along, rims, last_older, third, edges)
+    image, last_current, _ = imaging(
+        source_cell, along, fine, corner, second_near, third, edges
+    )
     shape = current_field.shape
-    return image.reshape(shape), last_older.reshape(shape), last_current.reshape(shape)
+    return image.reshape(shape), second.reshape(shape), last_current.reshape(shape)
 
 
 def exchange(own):
     x_lo, x_hi, y_lo, y_hi = own
     return [rotate(x_hi, "gx", 1), rotate(x_lo, "gx", -1), rotate(y_hi, "gy", 1), rotate(y_lo, "gy", -1)]
-
-
-def diagonal(block):
-    nx, ny = lax.axis_size("gx"), lax.axis_size("gy")
-    route = [
-        (i * ny + j, ((i - 1) % nx) * ny + (j - 1) % ny) for i in range(nx) for j in range(ny)
-    ]
-    return lax.ppermute(block, ("gx", "gy"), route)
 
 
 def solution(mesh):

time: 87 us -> 80.5 us (0.925)
  starting transfers between devices: 44.6 us -> 39.1 us
  waiting for transfers between devices: 15.8 us -> 11.7 us
  Pallas kernels: 24.8 us -> 28 us
    ppermute x10 -> x9, waiting for transfers between devices: 15.8 us -> 9.15 us  [rotate(): lax.ppermute(block, axis, [(i, (i + step) % count) for i in range(count)])]
    ppermute x1 -> x0, starting transfers between devices: 3.4 us -> none  [diagonal(): return lax.ppermute(block, ('gx', 'gy'), route)]
    pallas_call x3 -> x5, Pallas kernels: 8.62 us -> 11.7 us  [the longest x1 4.25 us: imaging(): pl.pallas_call(image_kernel, in_specs=[SMEM] + [VMEM] * 25, out_specs=[AN...]
    all_to_all x1, waiting for transfers between devices: 0.01 us -> 2.57 us  [per_device(): lax.all_to_all(stored_tiles[0, 0], ('shot', 'gx'), split_axis=0, concat_a...]
    ppermute x10 -> x9, starting transfers between devices: 26.6 us -> 24.5 us  [rotate(): lax.ppermute(block, axis, [(i, (i + step) % count) for i in range(count)])]
  transfers between devices with their start and end apart: 12 -> 10, of which waited for: 2 -> 4; matrix products, arithmetic and copies ran while one was open for 0% -> 0% of each run, Pallas kernels for 19% -> 27%
where the time goes in v5:
time: 80.5 us; the launch traced here: 80.1 us
  starting transfers between devices  39.1 us (49%)
  Pallas kernels  28 us (35%)
  waiting for transfers between devices  11.7 us (15%)
  between operations  0.95 us (1%)
    ppermute x9, starting transfers between devices, rotate(): lax.ppermute(block, axis, [(i, (i + step) % count) for i in range(count)])  24.5 us
    all_to_all x1, starting transfers between devices, per_device(): lax.all_to_all(stored_tiles[0, 0], ('shot', 'gx'), split_axis=0, concat_a...  14.6 us
    pallas_call x2, Pallas kernels, inner(): pl.pallas_call(lambda *refs: inner_kernel(*refs, step=step), in_specs=[AN...  12.8 us
    ppermute x9, waiting for transfers between devices, rotate(): lax.ppermute(block, axis, [(i, (i + step) % count) for i in range(count)])  9.15 us
    pallas_call x1, Pallas kernels, imaging(): pl.pallas_call(image_kernel, in_specs=[SMEM] + [VMEM] * 25, out_specs=[AN...  4.25 us
    all_to_all x1, waiting for transfers between devices, per_device(): lax.all_to_all(stored_tiles[0, 0], ('shot', 'gx'), split_axis=0, concat_a...  2.57 us
    pallas_call x1, Pallas kernels, faces(): pl.pallas_call(faces_kernel, grid=(1,), in_specs=[plane_lo, plane_hi, row...  2.48 us
    pallas_call x1, Pallas kernels, coarse_tiles(): pl.pallas_call(coarse_kernel, in_specs=[VMEM, VMEM], out_specs=[VMEM] * 3...  2.22 us
  transfers between devices with their start and end apart: 10, of which 4 were waited for; matrix products, arithmetic and copies ran while one was open for 0% of the time, Pallas kernels for 27%

profile of v5, /device:TPU:1, one launch (start us, length us, event | category | flops | bytes accessed | tf_op | source)
XLA Modules:
  0.0 80.1 jit_solution(15384289454826982968)
XLA Ops:
  0.6 14.6 %all-to-all-start = ((f32[32,32,256]{2,1,0:T(8,128)}), f32[32,32,256]{2,1,0:T(8,128)}, u32[]{:S(2)}, u32[]{:S(2)}) async-start(f32[32,32,256]{2,1,0:T(8,128)} %bitcast.27), calls=%async_computation | async-start | bytes 2097152 | tf_op jit(solution)/shard_map/all_to_all | solution.py:511
  15.3 2.5 %faces.1 = (f32[2,32,512]{2,1,0:T(8,128)}, f32[2,32,512]{2,1,0:T(8,128)}, f32[2,32,512]{2,1,0:T(8,128)}, f32[2,32,512]{2,1,0:T(8,128)}) custom-call(f32[32,32,512]{2,1,0:T(8,128)} %bitcast.19, f32[32,32,512]{2,1,0:T(8,128)} %bitcast.20, f32[32,32,512]{2,1,0:T(8,128)} %bitcast.21, f32[32,32,512]{2,1,0:T(8,128)} %bitcast.22, f32[32,32,512]{2,1,0:T(8,128)} %by_hi.1, ...), custom_call_target="tpu_custom_call" | custom-call | bytes 3145728 | tf_op jit(solution)/shard_map/faces/pallas_call | solution.py:51
  17.8 7.2 %collective-permute-start.1 = (f32[2,32,512]{2,1,0:T(8,128)}, f32[2,32,512]{2,1,0:T(8,128)}, u32[]{:S(2)}, u32[]{:S(2)}) collective-permute-start(f32[2,32,512]{2,1,0:T(8,128)} %get-tuple-element.31.refs_0_.rest_0_), channel_id=1, source_target_pairs={{0,56},{8,0},{16,8},{24,16},{32,24},{40,32},{48,40},{56,48},{1,57}... | collective-permute-start | bytes 393224 | tf_op jit(solution)/shard_map/ppermute | solution.py:24
  25.0 1.5 %collective-permute-start.3 = (f32[2,32,512]{2,1,0:T(8,128)}, f32[2,32,512]{2,1,0:T(8,128)}, u32[]{:S(2)}, u32[]{:S(2)}) collective-permute-start(f32[2,32,512]{2,1,0:T(8,128)} %get-tuple-element.33.refs_2_.rest_2_), channel_id=1, source_target_pairs={{0,7},{1,0},{2,1},{3,2},{4,3},{5,4},{6,5},{7,6},{8,15},{9,8},{10,9... | collective-permute-start | bytes 393224 | tf_op jit(solution)/shard_map/ppermute | solution.py:24
  26.5 0.6 collective-permute-start.2
  27.1 0.1 squeeze.16
  27.2 0.1 iota_compare_fusion
  27.3 0.1 lt.23
  27.4 0.8 %sources.1.refs_4_ = f32[2,1024,128]{2,1,0:T(8,128)S(1)} custom-call(s32[3,1024]{1,0:T(4,128)S(1)} %bitcast.17, f32[2,1024]{1,0:T(2,128)S(1)} %bitcast.18), custom_call_target="tpu_custom_call" | custom-call | flops 1 | bytes 1 | tf_op jit(solution)/shard_map/sources/pallas_call | solution.py:93
  28.2 6.3 %inner0.1 = (f32[1024,512]{1,0:T(8,128)}, f32[32,512]{1,0:T(8,128)S(1)}, f32[32,512]{1,0:T(8,128)S(1)}, f32[32,512]{1,0:T(8,128)S(1)}, f32[32,512]{1,0:T(8,128)S...) custom-call(f32[1024,512]{1,0:T(8,128)} %bitcast.23, ...), custom_call_target="tpu_custom_call" | custom-call | flops 1099511627776 | bytes 10485760 | tf_op jit(solution)/shard_map/inner0/pallas_call | solution.py:260
  34.6 0.2 onehots.1.onehot
  34.8 2.6 %all-to-all-done = f32[32,32,256]{2,1,0:T(8,128)} async-done(((f32[32,32,256]{2,1,0:T(8,128)}), f32[32,32,256]{2,1,0:T(8,128)}, u32[]{:S(2)}, u32[]{:S(2)}) %all-to-all-start) | async-done | bytes 1048608 | tf_op jit(solution)/shard_map/all_to_all | solution.py:511
  37.3 2.2 %coarse_tiles.1 = (f32[512,512]{1,0:T(8,128)S(1)}, f32[16,512]{1,0:T(8,128)S(1)}, f32[16,512]{1,0:T(8,128)S(1)}) custom-call(f32[1024,256]{1,0:T(8,128)} %bitcast.1.received, bf16[512,1024]{1,0:T(8,128)(2,1)S(1)} %onehots.1.onehot), custom_call_target="tpu_custom_call" | custom-call | flops 1073741824 | bytes 3145728 | tf_op jit(solution)/shard_map/coarse_tiles/pallas_call | solution.py:334
  39.6 0.7 collective-permute-done.refs_4_.rest_4_
  40.2 7.9 %collective-permute-done.3.refs_7_.rest_7_ = f32[2,32,512]{2,1,0:T(8,128)} collective-permute-done((f32[2,32,512]{2,1,0:T(8,128)}, f32[2,32,512]{2,1,0:T(8,128)}, u32[]{:S(2)}, u32[]{:S(2)}) %collective-permute-start.3) | collective-permute-done | bytes 131104 | tf_op jit(solution)/shard_map/ppermute | solution.py:24
  48.1 2.1 %fix_faces.1 = (f32[48,512]{1,0:T(8,128)}, f32[32,512]{1,0:T(8,128)}, f32[48,512]{1,0:T(8,128)}, f32[32,512]{1,0:T(8,128)}) custom-call(f32[2,32,512]{2,1,0:T(8,128)} %get-tuple-element.31.refs_0_.rest_0_, f32[2,32,512]{2,1,0:T(8,128)} %get-tuple-element.32.refs_1_.rest_1_, f32[2,32,512]{2,1,0:T(8,128)} %get-tuple-element.33.refs_2_.rest_2_, ...), custom_call_target="tpu_custom_call" | custom-call | flops 1048576 | bytes 2097152 | tf_op jit(solution)/shard_map/fix_faces/pallas_call | solution.py:293
  50.2 8.0 %collective-permute-start.7 = (f32[32,512]{1,0:T(8,128)}, f32[32,512]{1,0:T(8,128)}, u32[]{:S(2)}, u32[]{:S(2)}) collective-permute-start(f32[32,512]{1,0:T(8,128)} %get-tuple-element.48.refs_8_.rest_11_), channel_id=1, source_target_pairs={{0,1},{1,2},{2,3},{3,4},{4,5},{5,6},{6,7},{7,0},{8,9},{9,10},{10,1... | collective-permute-start | bytes 196616 | tf_op jit(solution)/shard_map/ppermute | solution.py:24
  58.2 6.0 %collective-permute-start.4 = (f32[48,512]{1,0:T(8,128)}, f32[48,512]{1,0:T(8,128)}, u32[]{:S(2)}, u32[]{:S(2)}) collective-permute-start(f32[48,512]{1,0:T(8,128)} %get-tuple-element.45.refs_5_.rest_8_), channel_id=1, source_target_pairs={{0,56},{8,0},{16,8},{24,16},{32,24},{40,32},{48,40},{56,48},{1,57}... | collective-permute-start | bytes 294920 | tf_op jit(solution)/shard_map/ppermute | solution.py:24
  64.2 6.5 %inner1.1 = (f32[1024,512]{1,0:T(8,128)S(1)}, f32[1024,512]{1,0:T(8,128)}) custom-call(f32[1024,512]{1,0:T(8,128)} %get-tuple-element.30.refs_0_, f32[1024,512]{1,0:T(8,128)} %bitcast.24, f32[1024,512]{1,0:T(8,128)} %bitcast.26, f32[1024,512]{1,0:T(8,128)} %bitcast.31, f32[2,1024,128]{2,1,0:T(8,128)S(1)} %sources.1.refs_4_, ...), custom_call_target="tpu_custom_call" | custom-call | flops 1099511627776 | bytes 10485760 | tf_op jit(solution)/shard_map/inner1/pallas_call | solution.py:260
  70.7 1.5 %corner_block.1 = f32[8,512]{1,0:T(8,128)} custom-call(f32[48,512]{1,0:T(8,128)} %collective-permute-done.4.message.rest_13_), custom_call_target="tpu_custom_call" | custom-call | tf_op jit(solution)/shard_map/corner_block/pallas_call | solution.py:351
  72.2 1.2 %collective-permute-start.5 = (f32[8,512]{1,0:T(8,128)}, f32[8,512]{1,0:T(8,128)}, u32[]{:S(2)}, u32[]{:S(2)}) collective-permute-start(f32[8,512]{1,0:T(8,128)} %corner_block.1), channel_id=1, source_target_pairs={{0,7},{1,0},{2,1},{3,2},{4,3},{5,4},{6,5},{7,6},{8,15},{9,8},{10,9... | collective-permute-start | bytes 49160 | tf_op jit(solution)/shard_map/ppermute | solution.py:24
  73.4 1.6 %upsampling.1 = (f32[4,1088,128]{2,1,0:T(8,128)S(1)}, f32[1024,512]{1,0:T(8,128)S(1)}) custom-call(f32[512,512]{1,0:T(8,128)S(1)} %get-tuple-element.29.along, f32[1024,512]{1,0:T(8,128)} %get-tuple-element.49.first_hbm), custom_call_target="tpu_custom_call" | custom-call | flops 1099511627776 | bytes 8388608 | tf_op jit(solution)/shard_map/upsampling/pallas_call | solution.py:377
  75.1 0.6 collective-permute-done.5.corner
  75.7 4.2 %imaging.1 = (f32[1024,512]{1,0:T(8,128)}, f32[1024,512]{1,0:T(8,128)}, f32[4,1088,128]{2,1,0:T(8,128)S(1)}) custom-call(s32[1,3]{1,0:T(1,128)S(1)} %copy-done.1, f32[512,512]{1,0:T(8,128)S(1)} %get-tuple-element.29.along, f32[4,1088,128]{2,1,0:T(8,128)S(1)} %get-tuple-element.50.fine_in, ...), custom_call_target="tpu_custom_call", output_to_operand_aliasing={{2}: (2, {})} | custom-call | flops 20971520 | bytes 8388608 | tf_op jit(solution)/shard_map/imaging/pallas_call | solution.py:473
  (21 shorter events, 0.1 us)
Async XLA Ops:
  0.6 36.7 %all-to-all-start = ((f32[32,32,256]{2,1,0:T(8,128)}), f32[32,32,256]{2,1,0:T(8,128)}, u32[]{:S(2)}, u32[]{:S(2)}) async-start(f32[32,32,256]{2,1,0:T(8,128)} %bitcast.27), calls=%async_computation | async-start | bytes 2097152 | tf_op jit(solution)/shard_map/all_to_all | solution.py:511
  15.3 11.8 %copy-start.2 = (s32[1,1,32,32]{3,2,1,0:T(8,128)S(1)}, s32[1,1,32,32]{3,2,1,0:T(8,128)}, u32[]{:S(2)}) copy-start(s32[1,1,32,32]{3,2,1,0:T(8,128)} %param.15) | copy-start | bytes 12292
  15.3 11.9 %copy-start.4 = (s32[1,1,32]{2,1,0:T(1,128)S(1)}, s32[1,1,32]{2,1,0:T(1,128)}, u32[]{:S(2)}) copy-start(s32[1,1,32]{2,1,0:T(1,128)} %param.16) | copy-start | bytes 388
  15.3 12.1 %copy-start.3 = (s32[1,3,1024]{2,0,1:T(1,128)S(1)}, s32[1,3,1024]{2,0,1:T(1,128)}, u32[]{:S(2)}) copy-start(s32[1,3,1024]{2,0,1:T(1,128)} %param.17) | copy-start | bytes 36868
  15.3 12.1 %copy-start = (f32[1,2,1024]{2,1,0:T(2,128)S(1)}, f32[1,2,1024]{2,1,0:T(2,128)}, u32[]{:S(2)}) copy-start(f32[1,2,1024]{2,1,0:T(2,128)} %param.18) | copy-start | bytes 24580
  17.8 21.8 %collective-permute-start.1 = (f32[2,32,512]{2,1,0:T(8,128)}, f32[2,32,512]{2,1,0:T(8,128)}, u32[]{:S(2)}, u32[]{:S(2)}) collective-permute-start(f32[2,32,512]{2,1,0:T(8,128)} %get-tuple-element.31.refs_0_.rest_0_), channel_id=1, source_target_pairs={{0,56},{8,0},{16,8},{24,16},{32,24},{40,32},{48,40},{56,48},{1,57}... | collective-permute-start | bytes 393224 | tf_op jit(solution)/shard_map/ppermute | solution.py:24
  25.0 15.2 %collective-permute-start = (f32[2,32,512]{2,1,0:T(8,128)}, f32[2,32,512]{2,1,0:T(8,128)}, u32[]{:S(2)}, u32[]{:S(2)}) collective-permute-start(f32[2,32,512]{2,1,0:T(8,128)} %get-tuple-element.32.refs_1_.rest_1_), channel_id=1, source_target_pairs={{0,8},{8,16},{16,24},{24,32},{32,40},{40,48},{48,56},{56,0},{1,9},... | collective-permute-start | bytes 393224 | tf_op jit(solution)/shard_map/ppermute | solution.py:24
  25.0 23.1 %collective-permute-start.3 = (f32[2,32,512]{2,1,0:T(8,128)}, f32[2,32,512]{2,1,0:T(8,128)}, u32[]{:S(2)}, u32[]{:S(2)}) collective-permute-start(f32[2,32,512]{2,1,0:T(8,128)} %get-tuple-element.33.refs_2_.rest_2_), channel_id=1, source_target_pairs={{0,7},{1,0},{2,1},{3,2},{4,3},{5,4},{6,5},{7,6},{8,15},{9,8},{10,9... | collective-permute-start | bytes 393224 | tf_op jit(solution)/shard_map/ppermute | solution.py:24
  26.5 21.6 %collective-permute-start.2 = (f32[2,32,512]{2,1,0:T(8,128)}, f32[2,32,512]{2,1,0:T(8,128)}, u32[]{:S(2)}, u32[]{:S(2)}) collective-permute-start(f32[2,32,512]{2,1,0:T(8,128)} %get-tuple-element.34.refs_3_.rest_3_), channel_id=1, source_target_pairs={{0,1},{1,2},{2,3},{3,4},{4,5},{5,6},{6,7},{7,0},{8,9},{9,10},{10,1... | collective-permute-start | bytes 393224 | tf_op jit(solution)/shard_map/ppermute | solution.py:24
  50.2 24.8 %collective-permute-start.6 = (f32[32,512]{1,0:T(8,128)}, f32[32,512]{1,0:T(8,128)}, u32[]{:S(2)}, u32[]{:S(2)}) collective-permute-start(f32[32,512]{1,0:T(8,128)} %get-tuple-element.46.refs_6_.rest_9_), channel_id=1, source_target_pairs={{0,8},{8,16},{16,24},{24,32},{32,40},{40,48},{48,56},{56,0},{1,9},... | collective-permute-start | bytes 196616 | tf_op jit(solution)/shard_map/ppermute | solution.py:24
  50.2 24.9 %collective-permute-start.7 = (f32[32,512]{1,0:T(8,128)}, f32[32,512]{1,0:T(8,128)}, u32[]{:S(2)}, u32[]{:S(2)}) collective-permute-start(f32[32,512]{1,0:T(8,128)} %get-tuple-element.48.refs_8_.rest_11_), channel_id=1, source_target_pairs={{0,1},{1,2},{2,3},{3,4},{4,5},{5,6},{6,7},{7,0},{8,9},{9,10},{10,1... | collective-permute-start | bytes 196616 | tf_op jit(solution)/shard_map/ppermute | solution.py:24
  58.2 12.5 %collective-permute-start.4 = (f32[48,512]{1,0:T(8,128)}, f32[48,512]{1,0:T(8,128)}, u32[]{:S(2)}, u32[]{:S(2)}) collective-permute-start(f32[48,512]{1,0:T(8,128)} %get-tuple-element.45.refs_5_.rest_8_), channel_id=1, source_target_pairs={{0,56},{8,0},{16,8},{24,16},{32,24},{40,32},{48,40},{56,48},{1,57}... | collective-permute-start | bytes 294920 | tf_op jit(solution)/shard_map/ppermute | solution.py:24
  64.2 10.9 %collective-permute-start.8 = (f32[48,512]{1,0:T(8,128)}, f32[48,512]{1,0:T(8,128)}, u32[]{:S(2)}, u32[]{:S(2)}) collective-permute-start(f32[48,512]{1,0:T(8,128)} %get-tuple-element.47.refs_7_.rest_10_), channel_id=1, source_target_pairs={{0,7},{1,0},{2,1},{3,2},{4,3},{5,4},{6,5},{7,6},{8,15},{9,8},{10,9... | collective-permute-start | bytes 294920 | tf_op jit(solution)/shard_map/ppermute | solution.py:24
  72.2 3.5 %collective-permute-start.5 = (f32[8,512]{1,0:T(8,128)}, f32[8,512]{1,0:T(8,128)}, u32[]{:S(2)}, u32[]{:S(2)}) collective-permute-start(f32[8,512]{1,0:T(8,128)} %corner_block.1), channel_id=1, source_target_pairs={{0,7},{1,0},{2,1},{3,2},{4,3},{5,4},{6,5},{7,6},{8,15},{9,8},{10,9... | collective-permute-start | bytes 49160 | tf_op jit(solution)/shard_map/ppermute | solution.py:24
  73.4 2.3 %copy-start.1 = (s32[1,3]{1,0:T(1,128)S(1)}, s32[1,3]{1,0:T(1,128)}, u32[]{:S(2)}) copy-start(s32[1,3]{1,0:T(1,128)} %source.1) | copy-start | bytes 40

commit v6 on v5

--- a/solution.py
+++ b/solution.py
@@ -24,6 +24,18 @@
     return lax.ppermute(block, axis, [(i, (i + step) % count) for i in range(count)])
 
 
+def swap(block, axis, start):
+    count = lax.axis_size(axis)
+    route = []
+    for low in range(start, count - 1, 2):
+        route += [(low, low + 1), (low + 1, low)]
+    return lax.ppermute(block, axis, route)
+
+
+def parity():
+    return lax.rem(lax.axis_index("gx"), 2)
+
+
 def f32(*shape):
     return jax.ShapeDtypeStruct(shape, jnp.float32)
 
@@ -33,10 +45,12 @@
     return high, (x - high.astype(jnp.float32)).astype(jnp.bfloat16)
 
 
-def faces_kernel(fx_lo, fx_hi, fy_lo, fy_hi, bx_lo, bx_hi, by_lo, by_hi, sx_lo, sx_hi, sy_lo, sy_hi):
+def faces_kernel(fx_lo, fx_hi, fy_lo, fy_hi, bx_lo, bx_hi, by_lo, by_hi, s_first, s_next, sy_lo, sy_hi):
+    even = parity() == 0
     for slot, refs in enumerate(((fx_lo, fx_hi, fy_lo, fy_hi), (bx_lo, bx_hi, by_lo, by_hi))):
-        sx_lo[slot] = refs[0][0]
-        sx_hi[slot] = refs[1][0]
+        low, high = refs[0][0], refs[1][0]
+        s_first[slot] = jnp.where(even, high, low)
+        s_next[slot] = jnp.where(even, low, high)
         for x in range(PLANES):
             sy_lo[slot, x : x + 1, :] = refs[2][x, 0:1, :]
             sy_hi[slot, x : x + 1, :] = refs[3][x, 7:8, :]
@@ -126,9 +140,10 @@
 def sides():
     gx = lax.axis_index("gx")
     gy = lax.axis_index("gy")
+    inside = (gx > 0) & (gx < lax.axis_size("gx") - 1)
     return [
-        jnp.where(gx > 0, 1.0, 0.0),
-        jnp.where(gx < lax.axis_size("gx") - 1, 1.0, 0.0),
+        1.0,
+        jnp.where(inside, 1.0, 0.0),
         jnp.where(gy > 0, 1.0, 0.0),
         jnp.where(gy < lax.axis_size("gy") - 1, 1.0, 0.0),
     ]
@@ -143,44 +158,9 @@
     return terms
 
 
-def inner_kernel(field, older, buoy, stiff, src, *rest, step):
-    if step == 1:
-        fixed, rest = rest[:4], rest[4:]
-        out, saved, f_buf, b_buf, s_buf, o_buf, in_sem, out_sem = rest
-        n_buf = out
-    else:
-        out, faces_out, stiff_out = rest[0], rest[1:5], rest[5:9]
-        f_buf, b_buf, s_buf, o_buf, n_buf, in_sem, out_sem = rest[9:]
-    copies = []
-    for chunk in range(CHUNKS):
-        part = pl.ds(chunk * SPAN, SPAN)
-        pairs = ((field, f_buf), (buoy, b_buf), (stiff, s_buf), (older, o_buf))
-        group = [
-            pltpu.make_async_copy(hbm.at[part], buf.at[part], in_sem.at[chunk, k])
-            for k, (hbm, buf) in enumerate(pairs)
-        ]
-        for copy in group:
-            copy.start()
-        copies.append(group)
+def make_plane(f_buf, b_buf, s_buf, o_buf, n_buf, src, step):
     row8 = lax.broadcasted_iota(jnp.int32, (8, DEPTH), 0)
     lane128 = lax.broadcasted_iota(jnp.int32, (PLANES, 128), 1)
-    out_copies = []
-
-    def arrive(chunk):
-        for copy in copies[chunk][:2]:
-            copy.wait()
-        if step == 1:
-            if chunk == 0:
-                f_buf[0:PLANES, :] = fixed[0][0:PLANES]
-            if chunk == CHUNKS - 1:
-                f_buf[ROWS - PLANES : ROWS, :] = fixed[1][0:PLANES]
-            for x in range(chunk * PER, chunk * PER + PER):
-                f_buf[x * PLANES : x * PLANES + 1, :] = fixed[2][x : x + 1, :]
-                f_buf[x * PLANES + 31 : x * PLANES + 32, :] = fixed[3][x : x + 1, :]
-            part = pl.ds(chunk * SPAN, SPAN)
-            copy = pltpu.make_async_copy(f_buf.at[part], saved.at[part], out_sem.at[chunk])
-            copy.start()
-            out_copies.append(copy)
 
     def plane(x, flux_before, last=False):
         base = pl.multiple_of(x * PLANES, PLANES)
@@ -216,90 +196,144 @@
         value = (2.0 * c - o_buf[at, :]) + (0.5 * s_buf[at, :]) * total
         n_buf[at, 128:DEPTH] = value[:, 128:]
         n_buf[at, head] = value[:, head] + src[step, at, :]
-        if step == 0:
-            faces_out[2][pl.ds(x, 1), :] = n_buf[pl.ds(base, 1), :]
-            faces_out[3][pl.ds(x, 1), :] = n_buf[pl.ds(base + PLANES - 1, 1), :]
-            stiff_out[2][pl.ds(x, 1), :] = s_buf[pl.ds(base, 1), :]
-            stiff_out[3][pl.ds(x, 1), :] = s_buf[pl.ds(base + PLANES - 1, 1), :]
         return flux_x
 
-    arrive(0)
+    return plane
+
+
+def inner0_kernel(field, older, buoy, stiff, src, out, *rest):
+    values, stiff_out = rest[:4], rest[4:8]
+    f_buf, b_buf, s_buf, o_buf, n_buf, in_sem, out_sem = rest[8:]
+    copies = []
+    for chunk in range(CHUNKS):
+        part = pl.ds(chunk * SPAN, SPAN)
+        pairs = ((field, f_buf), (buoy, b_buf), (stiff, s_buf), (older, o_buf))
+        group = [
+            pltpu.make_async_copy(hbm.at[part], buf.at[part], in_sem.at[chunk, k])
+            for k, (hbm, buf) in enumerate(pairs)
+        ]
+        for copy in group:
+            copy.start()
+        copies.append(group)
+    inner_plane = make_plane(f_buf, b_buf, s_buf, o_buf, n_buf, src, 0)
+
+    def plane(x, flux, last=False):
+        flux = inner_plane(x, flux, last)
+        base = pl.multiple_of(x * PLANES, PLANES)
+        for side in range(2):
+            row = pl.ds(base + 31 * side, 1)
+            values[2 + side][pl.ds(x, 1), :] = n_buf[row, :]
+            stiff_out[2 + side][pl.ds(x, 1), :] = s_buf[row, :]
+        return flux
+
+    out_copies = []
+    for copy in copies[0][:2]:
+        copy.wait()
     flux = jnp.zeros((PLANES, DEPTH), jnp.float32)
     for chunk in range(CHUNKS):
         for copy in copies[chunk][2:]:
             copy.wait()
         if chunk + 1 < CHUNKS:
-            arrive(chunk + 1)
+            for copy in copies[chunk + 1][:2]:
+                copy.wait()
             flux = lax.fori_loop(chunk * PER, chunk * PER + PER, plane, flux, unroll=4)
         else:
             flux = lax.fori_loop(chunk * PER, chunk * PER + PER - 4, plane, flux, unroll=4)
             for x in range(PLANES - 4, PLANES):
                 flux = plane(x, flux, x == PLANES - 1)
-        if step == 0:
-            part = pl.ds(chunk * SPAN, SPAN)
-            copy = pltpu.make_async_copy(n_buf.at[part], out.at[part], out_sem.at[chunk])
-            copy.start()
-            out_copies.append(copy)
-    if step == 0:
-        faces_out[0][...] = n_buf[0:PLANES, :]
-        faces_out[1][...] = n_buf[ROWS - PLANES : ROWS, :]
-        stiff_out[0][...] = s_buf[0:PLANES, :]
-        stiff_out[1][...] = s_buf[ROWS - PLANES : ROWS, :]
+        part = pl.ds(chunk * SPAN, SPAN)
+        copy = pltpu.make_async_copy(n_buf.at[part], out.at[part], out_sem.at[chunk])
+        copy.start()
+        out_copies.append(copy)
+    odd = parity()
+    for side in range(2):
+        place = (1 - odd if side == 0 else odd) * (ROWS - PLANES)
+        at = pl.ds(pl.multiple_of(place, PLANES), PLANES)
+        values[side][...] = n_buf[at, :]
+        stiff_out[side][...] = s_buf[at, :]
     for copy in out_copies:
         copy.wait()
 
 
-def inner(field, older, buoy, stiff, src, fixed, step):
+def inner0(field, older, buoy, stiff, src):
     big = pltpu.VMEM((ROWS, DEPTH), jnp.float32)
-    if step == 0:
-        out_shape = [pltpu.HBM((ROWS, DEPTH), jnp.float32)] + [f32(PLANES, DEPTH)] * 8
-        out_specs = [ANY] + [VMEM] * 8
-    else:
-        out_shape = [big, pltpu.HBM((ROWS, DEPTH), jnp.float32)]
-        out_specs = [VMEM, ANY]
-    return pl.pallas_call(
-        lambda *refs: inner_kernel(*refs, step=step),
-        in_specs=[ANY] * 4 + [VMEM] * (1 + len(fixed)),
-        out_specs=out_specs,
-        out_shape=out_shape,
-        scratch_shapes=[big] * (5 - step)
+    return pl.pallas_call(
+        inner0_kernel,
+        in_specs=[ANY] * 4 + [VMEM],
+        out_specs=[ANY] + [VMEM] * 8,
+        out_shape=[pltpu.HBM((ROWS, DEPTH), jnp.float32)] + [f32(PLANES, DEPTH)] * 8,
+        scratch_shapes=[big] * 5
         + [pltpu.SemaphoreType.DMA((CHUNKS, 4)), pltpu.SemaphoreType.DMA((CHUNKS,))],
         compiler_params=ROOM,
         cost_estimate=pl.CostEstimate(flops=1 << 40, bytes_accessed=10 << 20, transcendentals=0),
-        name="inner%d" % step,
-    )(in_hbm(field), in_hbm(older), in_hbm(buoy), in_hbm(stiff), src, *fixed)
+        name="inner0",
+    )(in_hbm(field), in_hbm(older), in_hbm(buoy), in_hbm(stiff), src)
+
+
+def inner1_kernel(given, b_buf, s_buf, o_buf, src, x_first, x_next, y_lo, y_hi, f_buf, n_buf, saved, sem):
+    even = parity() == 0
+    first, following = x_first[0:PLANES], x_next[0:PLANES]
+    f_buf[0:PLANES, :] = jnp.where(even, following, first)
+    f_buf[ROWS - PLANES : ROWS, :] = jnp.where(even, first, following)
+    for x in range(PLANES):
+        f_buf[x * PLANES : x * PLANES + 1, :] = y_lo[x : x + 1, :]
+        f_buf[x * PLANES + 31 : x * PLANES + 32, :] = y_hi[x : x + 1, :]
+    save = pltpu.make_async_copy(f_buf, saved, sem)
+    save.start()
+    plane = make_plane(f_buf, b_buf, s_buf, o_buf, n_buf, src, 1)
+    flux = jnp.zeros((PLANES, DEPTH), jnp.float32)
+    flux = lax.fori_loop(0, PLANES - 4, plane, flux, unroll=4)
+    for x in range(PLANES - 4, PLANES):
+        flux = plane(x, flux, x == PLANES - 1)
+    save.wait()
+
+
+def inner1(given, buoy, stiff, older, src, fixed):
+    big = pltpu.VMEM((ROWS, DEPTH), jnp.float32)
+    return pl.pallas_call(
+        inner1_kernel,
+        in_specs=[VMEM] * 9,
+        out_specs=[VMEM, VMEM, ANY],
+        out_shape=[big, big, pltpu.HBM((ROWS, DEPTH), jnp.float32)],
+        scratch_shapes=[pltpu.SemaphoreType.DMA],
+        input_output_aliases={0: 0},
+        compiler_params=ROOM,
+        cost_estimate=pl.CostEstimate(flops=1 << 40, bytes_accessed=10 << 20, transcendentals=0),
+        name="inner1",
+    )(given, buoy, stiff, older, src, *fixed)
 
 
 def fix_kernel(*refs):
     own, far, value, stiff = (refs[4 * k : 4 * k + 4] for k in range(4))
-    rim_x, rim_y = refs[16:18]
+    rim_x, rim_corner = refs[16:18]
     out, terms = refs[18:22], refs[22]
     first = [ref[0] for ref in own]
     second = [ref[0] for ref in far]
     for side, term in enumerate(edge_terms(own, far, first, second, stiff)):
         terms[side] = term
         out[side][0:PLANES] = value[side][...] + term
-    for side in range(4):
-        at = slice(31 * (side % 2), 31 * (side % 2) + 1)
+    odd = parity()
+    for side in range(2):
+        place = (1 - odd if side == 0 else odd) * (PLANES - 1)
         for end in range(2):
             row = slice(31 * end, 31 * end + 1)
-            other = (2 if side < 2 else 0) + end
-            out[side][row, :] += terms[other, at, :]
-    out[0][PLANES : PLANES + 16] = rim_x[...]
-    out[2][PLANES : PLANES + 16] = rim_y[...]
-
-
-def fix_faces(own, far, values, stiff, rim_x, rim_y):
+            out[side][row, :] += terms[2 + end, pl.ds(place, 1), :]
+            out[2 + end][pl.ds(place, 1), :] += terms[side, row, :]
+        out[side][PLANES : PLANES + 16] = rim_x[...]
+        out[side][PLANES + 16 : PLANES + 24] = rim_corner[0:8, :]
+
+
+def fix_faces(own, far, values, stiff, rim_x, rim_corner):
     return pl.pallas_call(
         fix_kernel,
         in_specs=[VMEM] * 18,
         out_specs=[VMEM] * 4,
-        out_shape=[f32(PLANES + 16, DEPTH), f32(PLANES, DEPTH)] * 2,
+        out_shape=[f32(PLANES + 24, DEPTH)] * 2 + [f32(PLANES, DEPTH)] * 2,
         scratch_shapes=[pltpu.VMEM((4, PLANES, DEPTH), jnp.float32)],
         compiler_params=ROOM,
         cost_estimate=pl.CostEstimate(flops=1 << 20, bytes_accessed=2 << 20, transcendentals=0),
         name="fix_faces",
-    )(*own, *far, *values, *stiff, rim_x, rim_y)
+    )(*own, *far, *values, *stiff, rim_x, rim_corner)
 
 
 def interpolation():
@@ -343,24 +377,11 @@
     )(received, onehot)
 
 
-def corner_kernel(message, out):
-    out[...] = message[PLANES : PLANES + 8, :]
-
-
-def corner_block(message):
-    return pl.pallas_call(
-        corner_kernel,
-        in_specs=[VMEM],
-        out_specs=VMEM,
-        out_shape=f32(8, DEPTH),
-        compiler_params=ROOM,
-        name="corner_block",
-    )(message)
-
-
-def upsample_kernel(along, first_hbm, fine, first, sem):
-    load = pltpu.make_async_copy(first_hbm, first, sem)
-    load.start()
+def upsample_kernel(along, *refs):
+    sources_hbm, fine, near, sem = refs[:4], refs[4], refs[5:9], refs[9]
+    loads = [pltpu.make_async_copy(a, b, sem.at[k]) for k, (a, b) in enumerate(zip(sources_hbm, near))]
+    for copy in loads:
+        copy.start()
     for n in range(2):
         for k in range(16):
             rows = along[n * 256 + k * 16 : n * 256 + k * 16 + 16, :]
@@ -370,28 +391,28 @@
                 lanes = slice(part * 128, part * 128 + 128)
                 fine[part, pl.ds(base, 16, stride=2), :] = rows[:, lanes]
                 fine[part, pl.ds(base + 1, 16, stride=2), :] = middle[:, lanes]
-    load.wait()
-
-
-def upsampling(along, first):
+    for copy in loads:
+        copy.wait()
+
+
+def upsampling(along, *arrays):
+    big = pltpu.VMEM((ROWS, DEPTH), jnp.float32)
     return pl.pallas_call(
         upsample_kernel,
-        in_specs=[VMEM, ANY],
-        out_specs=[VMEM] * 2,
-        out_shape=[
-            pltpu.VMEM((4, 2 * 17 * PLANES, 128), jnp.float32),
-            pltpu.VMEM((ROWS, DEPTH), jnp.float32),
-        ],
-        scratch_shapes=[pltpu.SemaphoreType.DMA],
+        in_specs=[VMEM] + [ANY] * 4,
+        out_specs=[VMEM] * 5,
+        out_shape=[pltpu.VMEM((4, 2 * 17 * PLANES, 128), jnp.float32)] + [big] * 4,
+        scratch_shapes=[pltpu.SemaphoreType.DMA((4,))],
         compiler_params=ROOM,
         cost_estimate=pl.CostEstimate(flops=1 << 40, bytes_accessed=8 << 20, transcendentals=0),
         name="upsampling",
-    )(along, in_hbm(first))
-
-
-def image_kernel(source, along, fine_in, corner, first, second, *rest):
+    )(along, *[in_hbm(a) for a in arrays])
+
+
+def image_kernel(source, along, fine_in, rim_y, first, second, *rest):
     own, far, own2, far2, stiff = (rest[4 * k : 4 * k + 4] for k in range(5))
     image, saved, fine, rims, rim_along, out, terms, third, sem = rest[20:]
+    even = parity() == 0
     near = [ref[0:PLANES] for ref in own2]
     distant = [ref[0:PLANES] for ref in far2]
     for side, term in enumerate(edge_terms(own, far, near, distant, stiff)):
@@ -402,9 +423,10 @@
     keep_y = jnp.where(gy < lax.axis_size("gy") - 1, 1.0, 0.0)
     for n in range(2):
         lanes = slice(n * 256, n * 256 + 256)
-        rims[n * 40 : n * 40 + 16] = far2[1][PLANES : PLANES + 16, lanes] * keep_x
-        rims[n * 40 + 16 : n * 40 + 32] = far2[3][PLANES : PLANES + 16, lanes] * keep_y
-        rims[n * 40 + 32 : n * 40 + 40] = corner[:, lanes] * (keep_x * keep_y)
+        ahead = jnp.where(even, far2[0][PLANES:, lanes], far2[1][PLANES:, lanes])
+        rims[n * 40 : n * 40 + 16] = ahead[0:16] * keep_x
+        rims[n * 40 + 16 : n * 40 + 32] = rim_y[:, lanes] * keep_y
+        rims[n * 40 + 32 : n * 40 + 40] = ahead[16:24] * (keep_x * keep_y)
     weights = interpolation()
     high, low = split_bf16(rims[...])
     rim_along[...] = dot(high, weights) + dot(low, weights)
@@ -437,9 +459,9 @@
             at = slice(x * PLANES, (x + 1) * PLANES)
             value = second[at, :]
             if x == 0:
-                value = value + terms[0]
+                value = value + jnp.where(even, terms[1], terms[0])
             if x == PLANES - 1:
-                value = value + terms[1]
+                value = value + jnp.where(even, terms[0], terms[1])
             third[at, :] = value
             third[x * PLANES : x * PLANES + 1, :] += terms[2, x : x + 1, :]
             third[x * PLANES + 31 : x * PLANES + 32, :] += terms[3, x : x + 1, :]
@@ -468,7 +490,7 @@
         copy.wait()
 
 
-def imaging(source, along, fine, corner, first, second, edges):
+def imaging(source, along, fine, rim_y, first, second, edges):
     big = pltpu.VMEM((ROWS, DEPTH), jnp.float32)
     return pl.pallas_call(
         image_kernel,
@@ -488,7 +510,7 @@
         compiler_params=ROOM,
         cost_estimate=pl.CostEstimate(flops=20 << 20, bytes_accessed=8 << 20, transcendentals=0),
         name="imaging",
-    )(source, along, fine, corner, first, second, *edges)
+    )(source, along, fine, rim_y, first, second, *edges)
 
 
 def per_device(
@@ -508,34 +530,40 @@
     stiff = stiffness.reshape(ROWS, DEPTH)
     buoy = buoyancy.reshape(ROWS, DEPTH)
 
+    own = list(faces(current_field[0], buoyancy))
+    far = exchange(own)
+    tiles, own[0] = lax.optimization_barrier((stored_tiles, own[0]))
     received = lax.all_to_all(
-        stored_tiles[0, 0], ("shot", "gx"), split_axis=0, concat_axis=0, tiled=True
+        tiles[0, 0], ("shot", "gx"), split_axis=0, concat_axis=0, tiled=True
     ).reshape(1024, COARSE)
-    own = faces(current_field[0], buoyancy)
-    far = exchange(own)
     slot = lax.broadcasted_iota(jnp.int32, (32, 32), 1)
     ids = jnp.where(slot < tile_counts[0, 0][:, None], tile_ids[0, 0], -1).reshape(1, 1024)
     onehot = onehots(ids)
     src = sources(receiver_cells[0], receiver_data[0])
-    partial, *rest = inner(current, older, buoy, stiff, src, [], 0)
+    partial, *rest = inner0(current, older, buoy, stiff, src)
     values, stiff_faces = rest[:4], rest[4:]
     along, rim_x, rim_y = coarse_tiles(received, onehot)
-    own2 = fix_faces(own, far, values, stiff_faces, rim_x, rim_y)
+    rim_y_far = rotate(rim_y, "gy", -1)
+    fine, partial, buoy_near, stiff_near, first_near = upsampling(along, partial, buoy, stiff, current)
+    own2 = fix_faces(own, far, values, stiff_faces, rim_x, rim_y_far)
     far2 = exchange(own2)
-    third, second = inner(partial, current, buoy, stiff, src, own2, 1)
-    corner = rotate(corner_block(far2[1]), "gy", -1)
-    fine, second_near = upsampling(along, second)
+    second_near, third, second = inner1(partial, buoy_near, stiff_near, first_near, src, own2)
     edges = [*own, *far, *own2, *far2, *stiff_faces]
     image, last_current, _ = imaging(
-        source_cell, along, fine, corner, second_near, third, edges
+        source_cell, along, fine, rim_y_far, second_near, third, edges
     )
     shape = current_field.shape
     return image.reshape(shape), second.reshape(shape), last_current.reshape(shape)
 
 
 def exchange(own):
-    x_lo, x_hi, y_lo, y_hi = own
-    return [rotate(x_hi, "gx", 1), rotate(x_lo, "gx", -1), rotate(y_hi, "gy", 1), rotate(y_lo, "gy", -1)]
+    first, following, y_lo, y_hi = own
+    return [
+        swap(first, "gx", 0),
+        swap(following, "gx", 1),
+        rotate(y_hi, "gy", 1),
+        rotate(y_lo, "gy", -1),
+    ]
 
 
 def solution(mesh):

time: 80.5 us -> 78.7 us (0.978)
  the two profiles are of different devices: /device:TPU:1 before, /device:TPU:39 now
where the time goes in v6:
time: 78.7 us; the launch traced here: 78.2 us
  starting transfers between devices  34.7 us (44%)
  Pallas kernels  27.3 us (35%)
  waiting for transfers between devices  15 us (19%)
  between operations  0.82 us (1%)
    ppermute x4, starting transfers between devices, swap(): return lax.ppermute(block, axis, route)  15.7 us
    all_to_all x1, starting transfers between devices, per_device(): lax.all_to_all(tiles[0, 0], ('shot', 'gx'), split_axis=0, concat_axis=0,...  13.2 us
    all_to_all x1, waiting for transfers between devices, per_device(): lax.all_to_all(tiles[0, 0], ('shot', 'gx'), split_axis=0, concat_axis=0,...  12.2 us
    pallas_call x1, Pallas kernels, inner0(): pl.pallas_call(inner0_kernel, in_specs=[ANY] * 4 + [VMEM], out_specs=[ANY...  6.7 us
    ppermute x5, starting transfers between devices, rotate(): lax.ppermute(block, axis, [(i, (i + step) % count) for i in range(count)])  5.88 us
    pallas_call x1, Pallas kernels, inner1(): pl.pallas_call(inner1_kernel, in_specs=[VMEM] * 9, out_specs=[VMEM, VMEM,...  4.56 us
    pallas_call x1, Pallas kernels, imaging(): pl.pallas_call(image_kernel, in_specs=[SMEM] + [VMEM] * 25, out_specs=[AN...  4.26 us
    pallas_call x1, Pallas kernels, upsampling(): pl.pallas_call(upsample_kernel, in_specs=[VMEM] + [ANY] * 4, out_specs=[V...  3.58 us
  transfers between devices with their start and end apart: 10, of which 2 were waited for; matrix products, arithmetic and copies ran while one was open for 0% of the time, Pallas kernels for 24%

profile of v6, /device:TPU:39, one launch (start us, length us, event | category | flops | bytes accessed | tf_op | source)
XLA Modules:
  0.0 78.2 jit_solution(15091970217212599100)
XLA Ops:
  0.6 2.5 %faces.1 = (f32[2,32,512]{2,1,0:T(8,128)}, f32[2,32,512]{2,1,0:T(8,128)}, f32[2,32,512]{2,1,0:T(8,128)}, f32[2,32,512]{2,1,0:T(8,128)}) custom-call(f32[32,32,512]{2,1,0:T(8,128)} %bitcast.19, f32[32,32,512]{2,1,0:T(8,128)} %bitcast.20, f32[32,32,512]{2,1,0:T(8,128)} %bitcast.21, f32[32,32,512]{2,1,0:T(8,128)} %bitcast.22, f32[32,32,512]{2,1,0:T(8,128)} %by_hi.1, ...), custom_call_target="tpu_custom_call" | custom-call | bytes 3145728 | tf_op jit(solution)/shard_map/faces/pallas_call | solution.py:65
  3.1 0.6 collective-permute-start.1
  3.8 13.2 %all-to-all-start = ((f32[32,32,256]{2,1,0:T(8,128)}), f32[32,32,256]{2,1,0:T(8,128)}, u32[]{:S(2)}, u32[]{:S(2)}) async-start(f32[32,32,256]{2,1,0:T(8,128)} %bitcast.1), calls=%async_computation | async-start | bytes 2097152 | tf_op jit(solution)/shard_map/all_to_all | solution.py:536
  16.9 7.0 %collective-permute-start.2 = (f32[2,32,512]{2,1,0:T(8,128)}, f32[2,32,512]{2,1,0:T(8,128)}, u32[]{:S(2)}, u32[]{:S(2)}) collective-permute-start(f32[2,32,512]{2,1,0:T(8,128)} %get-tuple-element.46.refs_1_.rest_1_), channel_id=1, source_target_pairs={{8,16},{16,8},{24,32},{32,24},{40,48},{48,40},{9,17},{17,9},{25,33... | collective-permute-start | bytes 393224 | tf_op jit(solution)/shard_map/ppermute | solution.py:32
  23.9 2.5 %collective-permute-start.3 = (f32[2,32,512]{2,1,0:T(8,128)}, f32[2,32,512]{2,1,0:T(8,128)}, u32[]{:S(2)}, u32[]{:S(2)}) collective-permute-start(f32[2,32,512]{2,1,0:T(8,128)} %get-tuple-element.48.refs_3_.rest_3_), channel_id=1, source_target_pairs={{0,1},{1,2},{2,3},{3,4},{4,5},{5,6},{6,7},{7,0},{8,9},{9,10},{10,1... | collective-permute-start | bytes 393224 | tf_op jit(solution)/shard_map/ppermute | solution.py:24
  26.4 0.1 iota_compare_fusion
  26.5 0.1 lt.23
  26.6 0.1 squeeze.17
  26.7 0.8 %sources.1.src = f32[2,1024,128]{2,1,0:T(8,128)S(1)} custom-call(s32[3,1024]{1,0:T(4,128)S(1)} %bitcast.17, f32[2,1024]{1,0:T(2,128)S(1)} %bitcast.18), custom_call_target="tpu_custom_call" | custom-call | flops 1 | bytes 1 | tf_op jit(solution)/shard_map/sources/pallas_call | solution.py:107
  27.5 0.0 copy-start
  27.6 6.7 %inner0.1 = (f32[1024,512]{1,0:T(8,128)}, f32[32,512]{1,0:T(8,128)S(1)}, f32[32,512]{1,0:T(8,128)S(1)}, f32[32,512]{1,0:T(8,128)S(1)}, f32[32,512]{1,0:T(8,128)S...) custom-call(f32[1024,512]{1,0:T(8,128)} %bitcast.23, ...), custom_call_target="tpu_custom_call" | custom-call | flops 1099511627776 | bytes 10485760 | tf_op jit(solution)/shard_map/inner0/pallas_call | solution.py:260
  34.3 0.2 onehots.1.onehot
  34.5 12.2 %all-to-all-done = f32[32,32,256]{2,1,0:T(8,128)} async-done(((f32[32,32,256]{2,1,0:T(8,128)}), f32[32,32,256]{2,1,0:T(8,128)}, u32[]{:S(2)}, u32[]{:S(2)}) %all-to-all-start) | async-done | bytes 1048608 | tf_op jit(solution)/shard_map/all_to_all | solution.py:536
  46.7 2.6 %coarse_tiles.1 = (f32[512,512]{1,0:T(8,128)S(1)}, f32[16,512]{1,0:T(8,128)S(1)}, f32[16,512]{1,0:T(8,128)}) custom-call(f32[1024,256]{1,0:T(8,128)} %bitcast.2.received, bf16[512,1024]{1,0:T(8,128)(2,1)S(1)} %onehots.1.onehot), custom_call_target="tpu_custom_call" | custom-call | flops 1073741824 | bytes 3145728 | tf_op jit(solution)/shard_map/coarse_tiles/pallas_call | solution.py:368
  49.3 2.6 %collective-permute-start = (f32[16,512]{1,0:T(8,128)}, f32[16,512]{1,0:T(8,128)}, u32[]{:S(2)}, u32[]{:S(2)}) collective-permute-start(f32[16,512]{1,0:T(8,128)} %get-tuple-element.40), channel_id=1, source_target_pairs={{0,7},{1,0},{2,1},{3,2},{4,3},{5,4},{6,5},{7,6},{8,15},{9,8},{10,9... | collective-permute-start | bytes 98312 | tf_op jit(solution)/shard_map/ppermute | solution.py:24
  51.9 3.6 %upsampling.1 = (f32[4,1088,128]{2,1,0:T(8,128)S(1)}, f32[1024,512]{1,0:T(8,128)S(1)}, f32[1024,512]{1,0:T(8,128)S(1)}, f32[1024,512]{1,0:T(8,128)S(1)}, f32[1024,512]{1,0:T(8,128)S(1)}) custom-call(f32[512,512]{1,0:T(8,128)S(1)} %get-tuple-element.37.along, f32[1024,512]{1,0:T(8,128)} %get-tuple-element.38.refs_0_, f32[1024,512]{1,0:T(8,128)} %bitcast.26, ...), custom_call_target="tpu_custom_call" | custom-call | flops 1099511627776 | bytes 8388608 | tf_op jit(solution)/shard_map/upsampling/pallas_call | solution.py:400
  55.5 2.2 %fix_faces.1 = (f32[56,512]{1,0:T(8,128)}, f32[56,512]{1,0:T(8,128)}, f32[32,512]{1,0:T(8,128)}, f32[32,512]{1,0:T(8,128)}) custom-call(f32[2,32,512]{2,1,0:T(8,128)} %get-tuple-element.45.refs_0_.rest_0_, f32[2,32,512]{2,1,0:T(8,128)} %get-tuple-element.46.refs_1_.rest_1_, f32[2,32,512]{2,1,0:T(8,128)} %get-tuple-element.47.refs_2_.rest_2_, ...), custom_call_target="tpu_custom_call" | custom-call | flops 1048576 | bytes 2097152 | tf_op jit(solution)/shard_map/fix_faces/pallas_call | solution.py:327
  57.7 1.9 %collective-permute-start.5 = (f32[56,512]{1,0:T(8,128)}, f32[56,512]{1,0:T(8,128)}, u32[]{:S(2)}, u32[]{:S(2)}) collective-permute-start(f32[56,512]{1,0:T(8,128)} %get-tuple-element.58.x_first.rest_8_), channel_id=1, source_target_pairs={{0,8},{8,0},{16,24},{24,16},{32,40},{40,32},{48,56},{56,48},{1,9},... | collective-permute-start | bytes 344072 | tf_op jit(solution)/shard_map/ppermute | solution.py:32
  59.6 6.2 %collective-permute-start.6 = (f32[56,512]{1,0:T(8,128)}, f32[56,512]{1,0:T(8,128)}, u32[]{:S(2)}, u32[]{:S(2)}) collective-permute-start(f32[56,512]{1,0:T(8,128)} %get-tuple-element.59.x_next.rest_9_), channel_id=1, source_target_pairs={{8,16},{16,8},{24,32},{32,24},{40,48},{48,40},{9,17},{17,9},{25,33... | collective-permute-start | bytes 344072 | tf_op jit(solution)/shard_map/ppermute | solution.py:32
  65.8 0.1 collective-permute-start.7
  65.9 0.6 collective-permute-start.8
  66.5 4.6 %inner1.1 = (f32[1024,512]{1,0:T(8,128)S(1)}, f32[1024,512]{1,0:T(8,128)S(1)}, f32[1024,512]{1,0:T(8,128)}) custom-call(f32[1024,512]{1,0:T(8,128)S(1)} %get-tuple-element.41.given, f32[1024,512]{1,0:T(8,128)S(1)} %get-tuple-element.42.b_buf, f32[1024,512]{1,0:T(8,128)S(1)} %get-tuple-element.43.s_buf, ...), custom_call_target="tpu_custom_call", output_to_operand_aliasing={{0}: (0, {})} | custom-call | flops 1099511627776 | bytes 10485760 | tf_op jit(solution)/shard_map/inner1/pallas_call | solution.py:293
  71.1 2.8 %collective-permute-done.6.rest_13_ = f32[56,512]{1,0:T(8,128)} collective-permute-done((f32[56,512]{1,0:T(8,128)}, f32[56,512]{1,0:T(8,128)}, u32[]{:S(2)}, u32[]{:S(2)}) %collective-permute-start.6) | collective-permute-done | bytes 114720 | tf_op jit(solution)/shard_map/ppermute | solution.py:32
  74.0 4.3 %imaging.1 = (f32[1024,512]{1,0:T(8,128)}, f32[1024,512]{1,0:T(8,128)}, f32[4,1088,128]{2,1,0:T(8,128)S(1)}) custom-call(s32[1,3]{1,0:T(1,128)S(1)} %copy-done.3, f32[512,512]{1,0:T(8,128)S(1)} %get-tuple-element.37.along, f32[4,1088,128]{2,1,0:T(8,128)S(1)} %get-tuple-element.39.fine_in, ...), custom_call_target="tpu_custom_call", output_to_operand_aliasing={{2}: (2, {})} | custom-call | flops 20971520 | bytes 8388608 | tf_op jit(solution)/shard_map/imaging/pallas_call | solution.py:495
  (24 shorter events, 0.1 us)
Async XLA Ops:
  3.1 23.3 %copy-start.6 = (s32[1,1,32]{2,1,0:T(1,128)S(1)}, s32[1,1,32]{2,1,0:T(1,128)}, u32[]{:S(2)}) copy-start(s32[1,1,32]{2,1,0:T(1,128)} %param.16) | copy-start | bytes 388
  3.1 23.5 %copy-start.4 = (s32[1,1,32,32]{3,2,1,0:T(8,128)S(1)}, s32[1,1,32,32]{3,2,1,0:T(8,128)}, u32[]{:S(2)}) copy-start(s32[1,1,32,32]{3,2,1,0:T(8,128)} %param.15) | copy-start | bytes 12292
  3.1 23.6 %copy-start.5 = (s32[1,3,1024]{2,0,1:T(1,128)S(1)}, s32[1,3,1024]{2,0,1:T(1,128)}, u32[]{:S(2)}) copy-start(s32[1,3,1024]{2,0,1:T(1,128)} %param.17) | copy-start | bytes 36868
  3.1 23.6 %copy-start.2 = (f32[1,2,1024]{2,1,0:T(2,128)S(1)}, f32[1,2,1024]{2,1,0:T(2,128)}, u32[]{:S(2)}) copy-start(f32[1,2,1024]{2,1,0:T(2,128)} %param.18) | copy-start | bytes 24580
  3.1 52.4 %collective-permute-start.1 = (f32[2,32,512]{2,1,0:T(8,128)}, f32[2,32,512]{2,1,0:T(8,128)}, u32[]{:S(2)}, u32[]{:S(2)}) collective-permute-start(f32[2,32,512]{2,1,0:T(8,128)} %get-tuple-element.45.refs_0_.rest_0_), channel_id=1, source_target_pairs={{0,8},{8,0},{16,24},{24,16},{32,40},{40,32},{48,56},{56,48},{1,9},... | collective-permute-start | bytes 393224 | tf_op jit(solution)/shard_map/ppermute | solution.py:32
  3.8 42.9 %all-to-all-start = ((f32[32,32,256]{2,1,0:T(8,128)}), f32[32,32,256]{2,1,0:T(8,128)}, u32[]{:S(2)}, u32[]{:S(2)}) async-start(f32[32,32,256]{2,1,0:T(8,128)} %bitcast.1), calls=%async_computation | async-start | bytes 2097152 | tf_op jit(solution)/shard_map/all_to_all | solution.py:536
  16.9 38.6 %collective-permute-start.2 = (f32[2,32,512]{2,1,0:T(8,128)}, f32[2,32,512]{2,1,0:T(8,128)}, u32[]{:S(2)}, u32[]{:S(2)}) collective-permute-start(f32[2,32,512]{2,1,0:T(8,128)} %get-tuple-element.46.refs_1_.rest_1_), channel_id=1, source_target_pairs={{8,16},{16,8},{24,32},{32,24},{40,48},{48,40},{9,17},{17,9},{25,33... | collective-permute-start | bytes 393224 | tf_op jit(solution)/shard_map/ppermute | solution.py:32
  23.9 31.6 %collective-permute-start.3 = (f32[2,32,512]{2,1,0:T(8,128)}, f32[2,32,512]{2,1,0:T(8,128)}, u32[]{:S(2)}, u32[]{:S(2)}) collective-permute-start(f32[2,32,512]{2,1,0:T(8,128)} %get-tuple-element.48.refs_3_.rest_3_), channel_id=1, source_target_pairs={{0,1},{1,2},{2,3},{3,4},{4,5},{5,6},{6,7},{7,0},{8,9},{9,10},{10,1... | collective-permute-start | bytes 393224 | tf_op jit(solution)/shard_map/ppermute | solution.py:24
  26.4 29.1 %collective-permute-start.4 = (f32[2,32,512]{2,1,0:T(8,128)}, f32[2,32,512]{2,1,0:T(8,128)}, u32[]{:S(2)}, u32[]{:S(2)}) collective-permute-start(f32[2,32,512]{2,1,0:T(8,128)} %get-tuple-element.47.refs_2_.rest_2_), channel_id=1, source_target_pairs={{0,7},{1,0},{2,1},{3,2},{4,3},{5,4},{6,5},{7,6},{8,15},{9,8},{10,9... | collective-permute-start | bytes 393224 | tf_op jit(solution)/shard_map/ppermute | solution.py:24
  27.5 6.7 %copy-start = (f32[2,1024,128]{2,1,0:T(8,128)}, f32[2,1024,128]{2,1,0:T(8,128)S(1)}, u32[]{:S(2)}) copy-start(f32[2,1024,128]{2,1,0:T(8,128)S(1)} %sources.1.src) | copy-start | bytes 3145732
  49.3 6.3 %collective-permute-start = (f32[16,512]{1,0:T(8,128)}, f32[16,512]{1,0:T(8,128)}, u32[]{:S(2)}, u32[]{:S(2)}) collective-permute-start(f32[16,512]{1,0:T(8,128)} %get-tuple-element.40), channel_id=1, source_target_pairs={{0,7},{1,0},{2,1},{3,2},{4,3},{5,4},{6,5},{7,6},{8,15},{9,8},{10,9... | collective-permute-start | bytes 98312 | tf_op jit(solution)/shard_map/ppermute | solution.py:24
  51.9 14.6 %copy-start.1 = (f32[2,1024,128]{2,1,0:T(8,128)S(1)}, f32[2,1024,128]{2,1,0:T(8,128)}, u32[]{:S(2)}) copy-start(f32[2,1024,128]{2,1,0:T(8,128)} %copy-done) | copy-start | bytes 3145732
  57.7 13.4 %collective-permute-start.5 = (f32[56,512]{1,0:T(8,128)}, f32[56,512]{1,0:T(8,128)}, u32[]{:S(2)}, u32[]{:S(2)}) collective-permute-start(f32[56,512]{1,0:T(8,128)} %get-tuple-element.58.x_first.rest_8_), channel_id=1, source_target_pairs={{0,8},{8,0},{16,24},{24,16},{32,40},{40,32},{48,56},{56,48},{1,9},... | collective-permute-start | bytes 344072 | tf_op jit(solution)/shard_map/ppermute | solution.py:32
  59.6 14.3 %collective-permute-start.6 = (f32[56,512]{1,0:T(8,128)}, f32[56,512]{1,0:T(8,128)}, u32[]{:S(2)}, u32[]{:S(2)}) collective-permute-start(f32[56,512]{1,0:T(8,128)} %get-tuple-element.59.x_next.rest_9_), channel_id=1, source_target_pairs={{8,16},{16,8},{24,32},{32,24},{40,48},{48,40},{9,17},{17,9},{25,33... | collective-permute-start | bytes 344072 | tf_op jit(solution)/shard_map/ppermute | solution.py:32
  65.8 5.3 %collective-permute-start.7 = (f32[32,512]{1,0:T(8,128)}, f32[32,512]{1,0:T(8,128)}, u32[]{:S(2)}, u32[]{:S(2)}) collective-permute-start(f32[32,512]{1,0:T(8,128)} %get-tuple-element.61.y_hi.rest_11_), channel_id=1, source_target_pairs={{0,1},{1,2},{2,3},{3,4},{4,5},{5,6},{6,7},{7,0},{8,9},{9,10},{10,1... | collective-permute-start | bytes 196616 | tf_op jit(solution)/shard_map/ppermute | solution.py:24
  65.9 5.2 %collective-permute-start.8 = (f32[32,512]{1,0:T(8,128)}, f32[32,512]{1,0:T(8,128)}, u32[]{:S(2)}, u32[]{:S(2)}) collective-permute-start(f32[32,512]{1,0:T(8,128)} %get-tuple-element.60.y_lo.rest_10_), channel_id=1, source_target_pairs={{0,7},{1,0},{2,1},{3,2},{4,3},{5,4},{6,5},{7,6},{8,15},{9,8},{10,9... | collective-permute-start | bytes 196616 | tf_op jit(solution)/shard_map/ppermute | solution.py:24
  66.5 7.4 %copy-start.3 = (s32[1,3]{1,0:T(1,128)S(1)}, s32[1,3]{1,0:T(1,128)}, u32[]{:S(2)}) copy-start(s32[1,3]{1,0:T(1,128)} %source.1) | copy-start | bytes 40

commit v7 on v4

--- a/solution.py
+++ b/solution.py
@@ -99,24 +99,6 @@
         compiler_params=ROOM,
         name="sources",
     )(cells, data)
-
-
-def onehot_kernel(ids, out):
-    for start in range(0, 512, 128):
-        tile = lax.broadcasted_iota(jnp.int32, (128, 1024), 0) + start
-        out[start : start + 128, :] = jnp.where(tile == ids[...], 1.0, 0.0).astype(jnp.bfloat16)
-
-
-def onehots(ids):
-    return pl.pallas_call(
-        onehot_kernel,
-        in_specs=[VMEM],
-        out_specs=VMEM,
-        out_shape=jax.ShapeDtypeStruct((512, 1024), jnp.bfloat16),
-        cost_estimate=pl.CostEstimate(flops=1, bytes_accessed=1, transcendentals=0),
-        compiler_params=ROOM,
-        name="onehots",
-    )(ids)
 
 
 def in_hbm(x):
@@ -277,11 +259,25 @@
     return jnp.dot(a, b, preferred_element_type=jnp.float32)
 
 
-def coarse_kernel(received, onehot, along, rim_x, rim_y, corner, rows):
-    high, low = split_bf16(received[...])
-    c_high = dot(onehot[...], high)
-    c_low = dot(onehot[...], low)
-    coarse = c_high + c_low
+def coarse_kernel(received, ids, along, rim_x, rim_y, corner, tiles, c_high, c_low, rows, sem):
+    copies = []
+    for part in range(4):
+        at = pl.ds(part * 256, 256)
+        copies.append(pltpu.make_async_copy(received.at[at], tiles.at[at], sem.at[part]))
+        copies[-1].start()
+    tile = lax.broadcasted_iota(jnp.int32, (512, 256), 0)
+    for part in range(4):
+        at = slice(part * 256, part * 256 + 256)
+        select = jnp.where(tile == ids[:, at], 1.0, 0.0).astype(jnp.bfloat16)
+        copies[part].wait()
+        high, low = split_bf16(tiles[at, :])
+        if part == 0:
+            c_high[...] = dot(select, high)
+            c_low[...] = dot(select, low)
+        else:
+            c_high[...] += dot(select, high)
+            c_low[...] += dot(select, low)
+    coarse = c_high[...] + c_low[...]
     for n in range(2):
         rim_x[n] = coarse[n * 256 : n * 256 + 16, :]
         corner[n] = coarse[n * 256 : n * 256 + 8, :]
@@ -291,153 +287,230 @@
         for n in range(2):
             rim_y[n, :, lanes] = rows[half, pl.ds(n * 256, 16, stride=16), :]
     weights = interpolation()
-    along[...] = dot(c_high.astype(jnp.bfloat16), weights) + dot(c_low.astype(jnp.bfloat16), weights)
-
-
-def coarse_tiles(received, onehot):
+    along[...] = dot(c_high[...].astype(jnp.bfloat16), weights) + dot(
+        c_low[...].astype(jnp.bfloat16), weights
+    )
+
+
+def coarse_tiles(received, ids):
     return pl.pallas_call(
         coarse_kernel,
-        in_specs=[VMEM, VMEM],
+        in_specs=[ANY, VMEM],
         out_specs=[VMEM] * 4,
         out_shape=[f32(512, DEPTH), f32(2, 16, COARSE), f32(2, 16, COARSE), f32(2, 8, COARSE)],
-        scratch_shapes=[pltpu.VMEM((2, 512, 128), jnp.float32)],
+        scratch_shapes=[
+            pltpu.VMEM((1024, COARSE), jnp.float32),
+            pltpu.VMEM((512, COARSE), jnp.float32),
+            pltpu.VMEM((512, COARSE), jnp.float32),
+            pltpu.VMEM((2, 512, 128), jnp.float32),
+            pltpu.SemaphoreType.DMA((4,)),
+        ],
         compiler_params=ROOM,
         cost_estimate=pl.CostEstimate(flops=1 << 30, bytes_accessed=3 << 20, transcendentals=0),
         name="coarse_tiles",
-    )(received, onehot)
-
-
-def upsample_kernel(along, first_hbm, second_hbm, fine, first, second, sem):
-    loads = [
-        pltpu.make_async_copy(first_hbm, first, sem.at[0]),
-        pltpu.make_async_copy(second_hbm, second, sem.at[1]),
-    ]
-    for copy in loads:
-        copy.start()
+    )(in_hbm(received), ids)
+
+
+SCALE = -1.0 / (2.0 * MUTE_RADIUS * MUTE_RADIUS)
+
+
+def picture_kernel(source, along, first_hbm, second_hbm, *rest):
+    own, far, own2, far2, stiff = (rest[4 * k : 4 * k + 4] for k in range(5))
+    image, saved, strip, plane_strip, last_plane, last_rows = rest[20:26]
+    fine, out, first, third, terms, in_sem, sem = rest[26:]
+    loads = []
+    for k in range(4):
+        at = pl.ds(k * SPAN, SPAN)
+        pair = [
+            pltpu.make_async_copy(first_hbm.at[at], first.at[at], in_sem.at[k, 0]),
+            pltpu.make_async_copy(second_hbm.at[at], third.at[at], in_sem.at[k, 1]),
+        ]
+        for copy in pair:
+            copy.start()
+        loads.append(pair)
+    for side, flux in enumerate(edge_fluxes(own, far, own2, far2)):
+        terms[side] = (0.5 * stiff[side][...]) * flux
+    row16 = lax.broadcasted_iota(jnp.int32, (16, DEPTH), 0)
     for n in range(2):
         for k in range(16):
             rows = along[n * 256 + k * 16 : n * 256 + k * 16 + 16, :]
-            middle = 0.5 * (rows + pltpu.roll(rows, 15, 0))
+            middle = 0.5 * (rows + jnp.where(row16 == 15, 0.0, pltpu.roll(rows, 15, 0)))
             base = (n * 17 + k) * PLANES
             for part in range(4):
                 lanes = slice(part * 128, part * 128 + 128)
                 fine[part, pl.ds(base, 16, stride=2), :] = rows[:, lanes]
                 fine[part, pl.ds(base + 1, 16, stride=2), :] = middle[:, lanes]
-    for copy in loads:
+        for part in range(4):
+            base = (n * 17 + 16) * PLANES
+            fine[part, base : base + PLANES, :] = jnp.zeros((PLANES, 128), jnp.float32)
+    gx = lax.axis_index("gx")
+    gy = lax.axis_index("gy")
+    y = (lax.broadcasted_iota(jnp.int32, (PLANES, DEPTH), 0) + gy * PLANES - source[0, 1]).astype(jnp.float32)
+    z = (lax.broadcasted_iota(jnp.int32, (PLANES, DEPTH), 1) - source[0, 2]).astype(jnp.float32)
+    decay_yz = jnp.exp((y * y + z * z) * SCALE)
+    x_base = gx * PLANES - source[0, 0]
+    copies = []
+    for x in range(PLANES):
+        k = x // 2
+        if x % PER == 0:
+            for copy in loads[x // PER]:
+                copy.wait()
+        at = slice(x * PLANES, (x + 1) * PLANES)
+        if x == 0:
+            third[at, :] += terms[0]
+        if x == PLANES - 1:
+            third[at, :] += terms[1]
+        third[x * PLANES : x * PLANES + 1, :] += terms[2, x : x + 1, :]
+        third[x * PLANES + 31 : x * PLANES + 32, :] += terms[3, x : x + 1, :]
+        last_rows[x : x + 1, :] = third[x * PLANES + 31 : x * PLANES + 32, :]
+        dx = jnp.full((1, 128), x_base + x, jnp.int32).astype(jnp.float32)
+        decay = jnp.exp((dx * dx) * SCALE)
+        for part in range(4):
+            lanes = slice(part * 128, part * 128 + 128)
+            taper = 1.0 - decay * decay_yz[:, lanes]
+            snaps = []
+            for n in range(2):
+                start = (n * 17 + k) * PLANES
+                snap = fine[part, start : start + PLANES, :]
+                if x % 2:
+                    snap = 0.5 * (snap + fine[part, start + PLANES : start + 2 * PLANES, :])
+                snaps.append(snap)
+            value = taper * (snaps[0] * first[at, lanes] + snaps[1] * third[at, lanes])
+            out[x, :, lanes] = value
+            strip[x, :, lanes] = value[24:32]
+        if x % 4 == 3:
+            group = pl.ds(x - 3, 3 if x == PLANES - 1 else 4)
+            rows = pl.ds((x - 3) * PLANES, 4 * PLANES)
+            copies.append(
+                pltpu.make_async_copy(
+                    out.at[group, 0:24], image.at[group, 0:24], sem.at[x // 4, 0]
+                )
+            )
+            copies.append(pltpu.make_async_copy(third.at[rows], saved.at[rows], sem.at[x // 4, 1]))
+            for copy in copies[-2:]:
+                copy.start()
+    plane_strip[...] = out[PLANES - 1, 0:24, :]
+    last_plane[...] = third[ROWS - PLANES : ROWS, :]
+    for copy in copies:
         copy.wait()
 
 
-def upsampling(along, first, second):
+def picture(source, along, first, second, edges):
     big = pltpu.VMEM((ROWS, DEPTH), jnp.float32)
     return pl.pallas_call(
-        upsample_kernel,
-        in_specs=[VMEM, ANY, ANY],
-        out_specs=[VMEM] * 3,
-        out_shape=[pltpu.VMEM((4, 2 * 17 * PLANES, 128), jnp.float32), big, big],
-        scratch_shapes=[pltpu.SemaphoreType.DMA((2,))],
+        picture_kernel,
+        in_specs=[SMEM, VMEM, ANY, ANY] + [VMEM] * 20,
+        out_specs=[ANY, ANY] + [VMEM] * 4,
+        out_shape=[
+            pltpu.HBM((PLANES, PLANES, DEPTH), jnp.float32),
+            pltpu.HBM((ROWS, DEPTH), jnp.float32),
+            f32(PLANES, 8, DEPTH),
+            f32(24, DEPTH),
+            f32(PLANES, DEPTH),
+            f32(PLANES, DEPTH),
+        ],
+        scratch_shapes=[
+            pltpu.VMEM((4, 2 * 17 * PLANES, 128), jnp.float32),
+            pltpu.VMEM((PLANES, PLANES, DEPTH), jnp.float32),
+            big,
+            big,
+            pltpu.VMEM((4, PLANES, DEPTH), jnp.float32),
+            pltpu.SemaphoreType.DMA((4, 2)),
+            pltpu.SemaphoreType.DMA((8, 2)),
+        ],
         compiler_params=ROOM,
         cost_estimate=pl.CostEstimate(flops=1 << 40, bytes_accessed=8 << 20, transcendentals=0),
-        name="upsampling",
-    )(along, in_hbm(first), in_hbm(second))
-
-
-def image_kernel(source, along, fine_in, rim_x, rim_y, corner, first, second, *rest):
-    own, far, own2, far2, stiff = (rest[4 * k : 4 * k + 4] for k in range(5))
-    image, saved, fine, rims, rim_along, out, terms, third, sem = rest[20:]
-    for side, flux in enumerate(edge_fluxes(own, far, own2, far2)):
-        terms[side] = (0.5 * stiff[side][...]) * flux
+        name="picture",
+    )(source, along, in_hbm(first), in_hbm(second), *edges)
+
+
+def rims_kernel(
+    source, rim_x, rim_y, corner, strip, plane_strip, q3_plane, q3_rows, q2_plane, q2_rows,
+    image_in, image, rims, along, fine, strip_out, plane_out, delta, sem,
+):
     gx = lax.axis_index("gx")
     gy = lax.axis_index("gy")
     keep_x = jnp.where(gx < lax.axis_size("gx") - 1, 1.0, 0.0)
     keep_y = jnp.where(gy < lax.axis_size("gy") - 1, 1.0, 0.0)
     for n in range(2):
-        rims[n * 40 : n * 40 + 16] = rim_x[n] * keep_x
-        rims[n * 40 + 16 : n * 40 + 32] = rim_y[n] * keep_y
-        rims[n * 40 + 32 : n * 40 + 40] = corner[n] * (keep_x * keep_y)
+        rims[n * 40 : n * 40 + 16] = rim_x[n] * (0.5 * keep_x)
+        rims[n * 40 + 16 : n * 40 + 32] = rim_y[n] * (0.5 * keep_y)
+        rims[n * 40 + 32 : n * 40 + 40] = corner[n] * (0.5 * keep_x * keep_y)
     weights = interpolation()
     high, low = split_bf16(rims[...])
-    rim_along[...] = dot(high, weights) + dot(low, weights)
+    along[...] = dot(high, weights) + dot(low, weights)
     row16 = lax.broadcasted_iota(jnp.int32, (16, DEPTH), 0)
     for n in range(2):
-        rows = rim_along[n * 40 : n * 40 + 16, :]
-        side = rim_along[n * 40 + 32 : n * 40 + 33, :]
-        middle = 0.5 * (rows + jnp.where(row16 == 15, side, pltpu.roll(rows, 15, 0)))
-        base = (n * 17 + 16) * PLANES
-        for part in range(4):
-            lanes = slice(part * 128, part * 128 + 128)
-            fine[part, pl.ds(base, 16, stride=2), :] = rows[:, lanes]
-            fine[part, pl.ds(base + 1, 16, stride=2), :] = middle[:, lanes]
-        for k in range(16):
-            last = n * 256 + k * 16 + 15
-            pair = n * 40 + 16 + k
-            middle = 0.5 * (along[last : last + 1, :] + rim_along[pair : pair + 1, :])
-            row = (n * 17 + k) * PLANES + 31
-            for part in range(4):
-                fine[part, row : row + 1, :] = middle[:, part * 128 : part * 128 + 128]
-    scale = -1.0 / (2.0 * MUTE_RADIUS * MUTE_RADIUS)
-    y = (lax.broadcasted_iota(jnp.int32, (PLANES, DEPTH), 0) + gy * PLANES - source[0, 1]).astype(jnp.float32)
-    z = (lax.broadcasted_iota(jnp.int32, (PLANES, DEPTH), 1) - source[0, 2]).astype(jnp.float32)
-    decay_yz = jnp.exp((y * y + z * z) * scale)
-    x_base = gx * PLANES - source[0, 0]
-    copies = []
-    for k in range(16):
-        for odd in range(2):
-            x = 2 * k + odd
-            at = slice(x * PLANES, (x + 1) * PLANES)
-            value = second[at, :]
-            if x == 0:
-                value = value + terms[0]
-            if x == PLANES - 1:
-                value = value + terms[1]
-            third[at, :] = value
-            third[x * PLANES : x * PLANES + 1, :] += terms[2, x : x + 1, :]
-            third[x * PLANES + 31 : x * PLANES + 32, :] += terms[3, x : x + 1, :]
-            dx = jnp.full((1, 128), x_base + x, jnp.int32).astype(jnp.float32)
-            decay = jnp.exp((dx * dx) * scale)
+        for way in range(2):
+            rows = along[n * 40 + way * 16 : n * 40 + way * 16 + 16, :]
+            end = along[n * 40 + 32 : n * 40 + 33, :] if way == 0 else 0.0
+            middle = 0.5 * (rows + jnp.where(row16 == 15, end, pltpu.roll(rows, 15, 0)))
+            base = (n * 2 + way) * PLANES
             for part in range(4):
                 lanes = slice(part * 128, part * 128 + 128)
-                taper = 1.0 - decay * decay_yz[:, lanes]
-                snaps = []
-                for n in range(2):
-                    start = (n * 17 + k) * PLANES
-                    snap = fine[part, start : start + PLANES, :]
-                    if odd:
-                        snap = 0.5 * (snap + fine[part, start + PLANES : start + 2 * PLANES, :])
-                    snaps.append(snap)
-                out[at, lanes] = taper * (
-                    snaps[0] * first[at, lanes] + snaps[1] * third[at, lanes]
-                )
-        if k % 2 == 1:
-            rows = pl.ds((k - 1) * 2 * PLANES, 4 * PLANES)
-            for pos, (here, there) in enumerate(((out, image), (third, saved))):
-                slot = 2 * (k // 2) + pos
-                copies.append(pltpu.make_async_copy(here.at[rows], there.at[rows], sem.at[slot]))
-                copies[-1].start()
+                fine[part, pl.ds(base, 16, stride=2), :] = rows[:, lanes]
+                fine[part, pl.ds(base + 1, 16, stride=2), :] = middle[:, lanes]
+    index = lax.broadcasted_iota(jnp.int32, (PLANES, 128), 0)
+    last_x = gx * PLANES + (PLANES - 1) - source[0, 0]
+    last_y = gy * PLANES + (PLANES - 1) - source[0, 1]
+    for part in range(4):
+        lanes = slice(part * 128, part * 128 + 128)
+        z = (lax.broadcasted_iota(jnp.int32, (PLANES, 128), 1) + part * 128 - source[0, 2]).astype(jnp.float32)
+        for way in range(2):
+            if way == 0:
+                fixed = last_x
+                moving = (index + gy * PLANES - source[0, 1]).astype(jnp.float32)
+                pair = (q2_plane[0, :, lanes], q3_plane[:, lanes])
+            else:
+                fixed = last_y
+                moving = (index + gx * PLANES - source[0, 0]).astype(jnp.float32)
+                pair = (q2_rows[0, :, lanes], q3_rows[:, lanes])
+            fixed = jnp.full((PLANES, 128), fixed, jnp.int32).astype(jnp.float32)
+            distance = fixed * fixed + moving * moving + z * z
+            taper = 1.0 - jnp.exp(distance * SCALE)
+            total = None
+            for n in range(2):
+                base = (n * 2 + way) * PLANES
+                term = fine[part, base : base + PLANES, :] * pair[n]
+                total = term if total is None else total + term
+            delta[way, :, lanes] = taper * total
+    row8 = lax.broadcasted_iota(jnp.int32, (8, DEPTH), 0)
+    for x in range(PLANES):
+        value = strip[x] + jnp.where(row8 == 7, delta[1, x : x + 1, :], 0.0)
+        if x == PLANES - 1:
+            value = value + delta[0, 24:32, :]
+        strip_out[x] = value
+    plane_out[...] = plane_strip[...] + delta[0, 0:24, :]
+    copies = [
+        pltpu.make_async_copy(strip_out, image.at[:, 24:32], sem.at[0]),
+        pltpu.make_async_copy(plane_out, image.at[PLANES - 1, 0:24], sem.at[1]),
+    ]
+    for copy in copies:
+        copy.start()
     for copy in copies:
         copy.wait()
 
 
-def imaging(source, along, fine, rims, first, second, edges):
-    big = pltpu.VMEM((ROWS, DEPTH), jnp.float32)
+def add_rims(source, rims, strips, faces2, image):
     return pl.pallas_call(
-        image_kernel,
-        in_specs=[SMEM] + [VMEM] * 27,
-        out_specs=[ANY, ANY, VMEM],
-        out_shape=[pltpu.HBM((ROWS, DEPTH), jnp.float32)] * 2
-        + [pltpu.VMEM((4, 2 * 17 * PLANES, 128), jnp.float32)],
-        input_output_aliases={2: 2},
+        rims_kernel,
+        in_specs=[SMEM] + [VMEM] * 9 + [ANY],
+        out_specs=ANY,
+        out_shape=pltpu.HBM((PLANES, PLANES, DEPTH), jnp.float32),
+        input_output_aliases={10: 0},
         scratch_shapes=[
             pltpu.VMEM((80, COARSE), jnp.float32),
             pltpu.VMEM((80, DEPTH), jnp.float32),
-            big,
-            pltpu.VMEM((4, PLANES, DEPTH), jnp.float32),
-            big,
-            pltpu.SemaphoreType.DMA((16,)),
+            pltpu.VMEM((4, 4 * PLANES, 128), jnp.float32),
+            pltpu.VMEM((PLANES, 8, DEPTH), jnp.float32),
+            pltpu.VMEM((24, DEPTH), jnp.float32),
+            pltpu.VMEM((2, PLANES, DEPTH), jnp.float32),
+            pltpu.SemaphoreType.DMA((2,)),
         ],
         compiler_params=ROOM,
-        cost_estimate=pl.CostEstimate(flops=20 << 20, bytes_accessed=8 << 20, transcendentals=0),
-        name="imaging",
-    )(source, along, fine, *rims, first, second, *edges)
+        cost_estimate=pl.CostEstimate(flops=1 << 20, bytes_accessed=2 << 20, transcendentals=0),
+        name="add_rims",
+    )(source, *rims, *strips, *faces2, in_hbm(image))
 
 
 def per_device(
@@ -466,7 +539,6 @@
     numbers, counts, far = lax.optimization_barrier((tile_ids, tile_counts, far))
     slot = lax.broadcasted_iota(jnp.int32, (32, 32), 1)
     ids = jnp.where(slot < counts[0, 0][:, None], numbers[0, 0], -1).reshape(1, 1024)
-    onehot = onehots(ids)
     src = sources(receiver_cells[0], receiver_data[0])
     second, *rest = inner(current, older, buoy, stiff, src, [*own, *far], 0)
     own2, stiff_faces = rest[:4], rest[4:]
@@ -474,13 +546,11 @@
     (third,) = inner(second, current, buoy, stiff, src, [], 1)
 
     received, third = lax.optimization_barrier((received, third))
-    along, rim_x, rim_y, corner = coarse_tiles(received, onehot)
+    along, rim_x, rim_y, corner = coarse_tiles(received, ids)
     rims = [rotate(rim_x, "gx", -1), rotate(rim_y, "gy", -1), diagonal(corner)]
-    fine, second_near, third_near = upsampling(along, second, third)
     edges = [*own, *far, *own2, *far2, *stiff_faces]
-    image, last_current, _ = imaging(
-        source_cell, along, fine, rims, second_near, third_near, edges
-    )
+    image, last_current, *strips = picture(source_cell, along, second, third, edges)
+    image = add_rims(source_cell, rims, strips, [own2[1], own2[3]], image)
     shape = current_field.shape
     return image.reshape(shape), second.reshape(shape), last_current.reshape(shape)
 

time: 75.2 us -> 73 us (0.971)
  waiting for transfers between devices: 11.1 us -> 8.76 us
    ppermute x10, waiting for transfers between devices: 6.38 us -> 4.13 us  [rotate(): lax.ppermute(block, axis, [(i, (i + step) % count) for i in range(count)])]
    pallas_call x4 -> x3, Pallas kernels: 8.88 us -> 9.39 us  [the longest x1 4.46 us: picture(): pl.pallas_call(picture_kernel, in_specs=[SMEM, VMEM, ANY, ANY] + [VMEM] *...]
  transfers between devices with their start and end apart: 12 -> 12, of which waited for: 2 -> 2; matrix products, arithmetic and copies ran while one was open for 0% -> 0% of each run, Pallas kernels for 26% -> 29%
where the time goes in v7:
time: 73 us; the launch traced here: 72.7 us
  starting transfers between devices  37.4 us (51%)
  Pallas kernels  25.3 us (35%)
  waiting for transfers between devices  8.76 us (12%)
  between operations  0.96 us (1%)
    ppermute x10, starting transfers between devices, rotate(): lax.ppermute(block, axis, [(i, (i + step) % count) for i in range(count)])  20.4 us
    pallas_call x2, Pallas kernels, inner(): pl.pallas_call(lambda *refs: inner_kernel(*refs, step=step), in_specs=[AN...  13.4 us
    all_to_all x1, starting transfers between devices, per_device(): lax.all_to_all(tiles[0, 0], ('shot', 'gx'), split_axis=0, concat_axis=0,...  11.6 us
    ppermute x1, starting transfers between devices, diagonal(): return lax.ppermute(block, ('gx', 'gy'), route)  5.34 us
    all_to_all x1, waiting for transfers between devices, per_device(): lax.all_to_all(tiles[0, 0], ('shot', 'gx'), split_axis=0, concat_axis=0,...  4.63 us
    pallas_call x1, Pallas kernels, picture(): pl.pallas_call(picture_kernel, in_specs=[SMEM, VMEM, ANY, ANY] + [VMEM] *...  4.46 us
    ppermute x10, waiting for transfers between devices, rotate(): lax.ppermute(block, axis, [(i, (i + step) % count) for i in range(count)])  4.13 us
    pallas_call x1, Pallas kernels, coarse_tiles(): pl.pallas_call(coarse_kernel, in_specs=[ANY, VMEM], out_specs=[VMEM] * 4,...  2.72 us
  transfers between devices with their start and end apart: 12, of which 2 were waited for; matrix products, arithmetic and copies ran while one was open for 0% of the time, Pallas kernels for 29%

profile of v7, /device:TPU:39, one launch (start us, length us, event | category | flops | bytes accessed | tf_op | source)
XLA Modules:
  0.0 72.7 jit_solution(5755099913710230889)
XLA Ops:
  0.6 1.7 %faces.1 = (f32[2,32,512]{2,1,0:T(8,128)S(1)}, f32[2,32,512]{2,1,0:T(8,128)S(1)}, f32[2,32,512]{2,1,0:T(8,128)S(1)}, f32[2,32,512]{2,1,0:T(8,128)S(1)}) custom-call(f32[32,32,512]{2,1,0:T(8,128)} %bitcast.19, f32[32,32,512]{2,1,0:T(8,128)} %bitcast.20, f32[32,32,512]{2,1,0:T(8,128)} %bitcast.21, f32[32,32,512]{2,1,0:T(8,128)} %bitcast.22, ...), custom_call_target="tpu_custom_call" | custom-call | bytes 3145728 | tf_op jit(solution)/shard_map/faces/pallas_call | solution.py:51
  2.3 0.0 copy-start.3
  2.4 0.6 collective-permute-start.1
  3.0 6.9 %collective-permute-start = (f32[2,32,512]{2,1,0:T(8,128)S(1)}, f32[2,32,512]{2,1,0:T(8,128)S(1)}, u32[]{:S(2)}, u32[]{:S(2)}) collective-permute-start(f32[2,32,512]{2,1,0:T(8,128)S(1)} %get-tuple-element.39.refs_6_.rest_1_), channel_id=1, source_target_pairs={{0,8},{8,16},{16,24},{24,32},{32,40},{40,48},{48,56},{56,0},{1,9},... | collective-permute-start | bytes 393224 | tf_op jit(solution)/shard_map/ppermute | solution.py:24
  9.9 1.2 %collective-permute-start.3 = (f32[2,32,512]{2,1,0:T(8,128)S(1)}, f32[2,32,512]{2,1,0:T(8,128)S(1)}, u32[]{:S(2)}, u32[]{:S(2)}) collective-permute-start(f32[2,32,512]{2,1,0:T(8,128)S(1)} %get-tuple-element.40.refs_7_.rest_2_), channel_id=1, source_target_pairs={{0,7},{1,0},{2,1},{3,2},{4,3},{5,4},{6,5},{7,6},{8,15},{9,8},{10,9... | collective-permute-start | bytes 393224 | tf_op jit(solution)/shard_map/ppermute | solution.py:24
  11.2 1.5 %collective-permute-start.2 = (f32[2,32,512]{2,1,0:T(8,128)S(1)}, f32[2,32,512]{2,1,0:T(8,128)S(1)}, u32[]{:S(2)}, u32[]{:S(2)}) collective-permute-start(f32[2,32,512]{2,1,0:T(8,128)S(1)} %get-tuple-element.41.refs_8_.rest_3_), channel_id=1, source_target_pairs={{0,1},{1,2},{2,3},{3,4},{4,5},{5,6},{6,7},{7,0},{8,9},{9,10},{10,1... | collective-permute-start | bytes 393224 | tf_op jit(solution)/shard_map/ppermute | solution.py:24
  12.7 11.6 %all-to-all-start = ((f32[32,32,256]{2,1,0:T(8,128)}), f32[32,32,256]{2,1,0:T(8,128)}, u32[]{:S(2)}, u32[]{:S(2)}) async-start(f32[32,32,256]{2,1,0:T(8,128)} %bitcast.1), calls=%async_computation | async-start | bytes 2097152 | tf_op jit(solution)/shard_map/all_to_all | solution.py:536
  24.4 0.8 %sources.1.refs_4_ = f32[2,1024,128]{2,1,0:T(8,128)S(1)} custom-call(s32[3,1024]{1,0:T(4,128)S(1)} %bitcast.17, f32[2,1024]{1,0:T(2,128)S(1)} %bitcast.18), custom_call_target="tpu_custom_call" | custom-call | flops 1 | bytes 1 | tf_op jit(solution)/shard_map/sources/pallas_call | solution.py:93
  25.2 7.0 %inner0.1 = (f32[1024,512]{1,0:T(8,128)}, f32[1,32,512]{2,1,0:T(8,128)}, f32[1,32,512]{2,1,0:T(8,128)}, f32[1,32,512]{2,1,0:T(8,128)}, f32[1,32,512]{2,1,0:T(8,1...) custom-call(f32[1024,512]{1,0:T(8,128)} %bitcast.23, ...), custom_call_target="tpu_custom_call" | custom-call | flops 1099511627776 | bytes 10485760 | tf_op jit(solution)/shard_map/inner0/pallas_call | solution.py:239
  32.3 0.7 collective-permute-start.8
  32.9 0.7 %collective-permute-start.10 = (f32[1,32,512]{2,1,0:T(8,128)}, f32[1,32,512]{2,1,0:T(8,128)}, u32[]{:S(2)}, u32[]{:S(2)}) collective-permute-start(f32[1,32,512]{2,1,0:T(8,128)} %get-tuple-element.57.rest_10_), channel_id=1, source_target_pairs={{0,7},{1,0},{2,1},{3,2},{4,3},{5,4},{6,5},{7,6},{8,15},{9,8},{10,9... | collective-permute-start | bytes 196616 | tf_op jit(solution)/shard_map/ppermute | solution.py:24
  33.7 6.9 %collective-permute-start.7 = (f32[1,32,512]{2,1,0:T(8,128)}, f32[1,32,512]{2,1,0:T(8,128)}, u32[]{:S(2)}, u32[]{:S(2)}) collective-permute-start(f32[1,32,512]{2,1,0:T(8,128)} %get-tuple-element.56.rest_9_.q2_plane), channel_id=1, source_target_pairs={{0,8},{8,16},{16,24},{24,32},{32,40},{40,48},{48,56},{56,0},{1,9},... | collective-permute-start | bytes 196616 | tf_op jit(solution)/shard_map/ppermute | solution.py:24
  40.6 1.3 %collective-permute-start.9 = (f32[1,32,512]{2,1,0:T(8,128)}, f32[1,32,512]{2,1,0:T(8,128)}, u32[]{:S(2)}, u32[]{:S(2)}) collective-permute-start(f32[1,32,512]{2,1,0:T(8,128)} %get-tuple-element.58.rest_11_.q2_rows), channel_id=1, source_target_pairs={{0,1},{1,2},{2,3},{3,4},{4,5},{5,6},{6,7},{7,0},{8,9},{9,10},{10,1... | collective-permute-start | bytes 196616 | tf_op jit(solution)/shard_map/ppermute | solution.py:24
  41.9 6.3 %inner1.1.second_hbm = f32[1024,512]{1,0:T(8,128)} custom-call(f32[1024,512]{1,0:T(8,128)} %get-tuple-element.46.refs_0_.first_hbm, f32[1024,512]{1,0:T(8,128)} %bitcast.24, f32[1024,512]{1,0:T(8,128)} %bitcast.26, f32[1024,512]{1,0:T(8,128)} %bitcast.31, f32[2,1024,128]{2,1,0:T(8,128)S(1)} %sources.1.refs_4_), custom_call_target="tpu_custom_call" | custom-call | flops 1099511627776 | bytes 10485760 | tf_op jit(solution)/shard_map/inner1/pallas_call | solution.py:239
  48.2 0.1 iota_compare_fusion
  48.3 0.1 lt.23
  48.4 0.1 squeeze.19
  48.5 4.6 %all-to-all-done = f32[32,32,256]{2,1,0:T(8,128)} async-done(((f32[32,32,256]{2,1,0:T(8,128)}), f32[32,32,256]{2,1,0:T(8,128)}, u32[]{:S(2)}, u32[]{:S(2)}) %all-to-all-start) | async-done | bytes 1048608 | tf_op jit(solution)/shard_map/all_to_all | solution.py:536
  53.1 2.7 %coarse_tiles.1 = (f32[512,512]{1,0:T(8,128)S(1)}, f32[2,16,256]{2,1,0:T(8,128)}, f32[2,16,256]{2,1,0:T(8,128)}, f32[2,8,256]{2,1,0:T(8,128)}) custom-call(f32[1024,256]{1,0:T(8,128)} %bitcast.2.received, s32[1,1024]{1,0:T(1,128)S(1)} %broadcast_select_fusion.ids), custom_call_target="tpu_custom_call" | custom-call | flops 1073741824 | bytes 3145728 | tf_op jit(solution)/shard_map/coarse_tiles/pallas_call | solution.py:296
  55.8 5.3 %collective-permute-start.6 = (f32[2,8,256]{2,1,0:T(8,128)}, f32[2,8,256]{2,1,0:T(8,128)}, u32[]{:S(2)}, u32[]{:S(2)}) collective-permute-start(f32[2,8,256]{2,1,0:T(8,128)} %get-tuple-element.52), channel_id=1, source_target_pairs={{0,63},{1,56},{2,57},{3,58},{4,59},{5,60},{6,61},{7,62},{8,7},{9,0... | collective-permute-start | bytes 49160 | tf_op jit(solution)/shard_map/ppermute | solution.py:568
  61.2 0.5 collective-permute-start.5
  61.7 4.5 %picture.1 = (f32[32,32,512]{2,1,0:T(8,128)}, f32[1024,512]{1,0:T(8,128)}, f32[32,8,512]{2,1,0:T(8,128)S(1)}, f32[24,512]{1,0:T(8,128)S(1)}, f32[32,512]{1,0:T(8,128)S(1)}, /*index=5*/f32[32,512]{1,0:T(8,128)S(1)}) custom-call(s32[1,3]{1,0:T(1,128)S(1)} %copy-done.1, f32[512,512]{1,0:T(8,128)S(1)} %get-tuple-element.53.along, ...), custom_call_target="tpu_custom_call" | custom-call | flops 1099511627776 | bytes 8388608 | tf_op jit(solution)/shard_map/picture/pallas_call | solution.py:400
  66.2 4.1 %collective-permute-done.4.rim_x = f32[2,16,256]{2,1,0:T(8,128)} collective-permute-done((f32[2,16,256]{2,1,0:T(8,128)}, f32[2,16,256]{2,1,0:T(8,128)}, u32[]{:S(2)}, u32[]{:S(2)}) %collective-permute-start.4) | collective-permute-done | bytes 32800 | tf_op jit(solution)/shard_map/ppermute | solution.py:24
  70.3 2.2 %add_rims.1 = f32[32,32,512]{2,1,0:T(8,128)} custom-call(s32[1,3]{1,0:T(1,128)S(1)} %copy-done.1, f32[2,16,256]{2,1,0:T(8,128)} %collective-permute-done.4.rim_x, f32[2,16,256]{2,1,0:T(8,128)} %collective-permute-done.5.rim_y, f32[2,8,256]{2,1,0:T(8,128)} %collective-permute-done.6.corner, ...), custom_call_target="tpu_custom_call", output_to_operand_aliasing={{}: (10, {})} | custom-call | flops 1048576 | bytes 2097152 | tf_op jit(solution)/shard_map/add_rims/pallas_call | solution.py:495
  (22 shorter events, 0.1 us)
Async XLA Ops:
  2.3 22.0 %copy-start.3 = (s32[1,3,1024]{2,0,1:T(1,128)S(1)}, s32[1,3,1024]{2,0,1:T(1,128)}, u32[]{:S(2)}) copy-start(s32[1,3,1024]{2,0,1:T(1,128)} %param.17) | copy-start | bytes 36868
  2.4 22.0 %copy-start = (f32[1,2,1024]{2,1,0:T(2,128)S(1)}, f32[1,2,1024]{2,1,0:T(2,128)}, u32[]{:S(2)}) copy-start(f32[1,2,1024]{2,1,0:T(2,128)} %param.18) | copy-start | bytes 24580
  2.4 22.8 %collective-permute-start.1 = (f32[2,32,512]{2,1,0:T(8,128)S(1)}, f32[2,32,512]{2,1,0:T(8,128)S(1)}, u32[]{:S(2)}, u32[]{:S(2)}) collective-permute-start(f32[2,32,512]{2,1,0:T(8,128)S(1)} %get-tuple-element.38.refs_5_.rest_0_), channel_id=1, source_target_pairs={{0,56},{8,0},{16,8},{24,16},{32,24},{40,32},{48,40},{56,48},{1,57}... | collective-permute-start | bytes 393224 | tf_op jit(solution)/shard_map/ppermute | solution.py:24
  3.0 22.2 %collective-permute-start = (f32[2,32,512]{2,1,0:T(8,128)S(1)}, f32[2,32,512]{2,1,0:T(8,128)S(1)}, u32[]{:S(2)}, u32[]{:S(2)}) collective-permute-start(f32[2,32,512]{2,1,0:T(8,128)S(1)} %get-tuple-element.39.refs_6_.rest_1_), channel_id=1, source_target_pairs={{0,8},{8,16},{16,24},{24,32},{32,40},{40,48},{48,56},{56,0},{1,9},... | collective-permute-start | bytes 393224 | tf_op jit(solution)/shard_map/ppermute | solution.py:24
  9.9 15.3 %collective-permute-start.3 = (f32[2,32,512]{2,1,0:T(8,128)S(1)}, f32[2,32,512]{2,1,0:T(8,128)S(1)}, u32[]{:S(2)}, u32[]{:S(2)}) collective-permute-start(f32[2,32,512]{2,1,0:T(8,128)S(1)} %get-tuple-element.40.refs_7_.rest_2_), channel_id=1, source_target_pairs={{0,7},{1,0},{2,1},{3,2},{4,3},{5,4},{6,5},{7,6},{8,15},{9,8},{10,9... | collective-permute-start | bytes 393224 | tf_op jit(solution)/shard_map/ppermute | solution.py:24
  11.2 14.1 %collective-permute-start.2 = (f32[2,32,512]{2,1,0:T(8,128)S(1)}, f32[2,32,512]{2,1,0:T(8,128)S(1)}, u32[]{:S(2)}, u32[]{:S(2)}) collective-permute-start(f32[2,32,512]{2,1,0:T(8,128)S(1)} %get-tuple-element.41.refs_8_.rest_3_), channel_id=1, source_target_pairs={{0,1},{1,2},{2,3},{3,4},{4,5},{5,6},{6,7},{7,0},{8,9},{9,10},{10,1... | collective-permute-start | bytes 393224 | tf_op jit(solution)/shard_map/ppermute | solution.py:24
  12.7 40.4 %all-to-all-start = ((f32[32,32,256]{2,1,0:T(8,128)}), f32[32,32,256]{2,1,0:T(8,128)}, u32[]{:S(2)}, u32[]{:S(2)}) async-start(f32[32,32,256]{2,1,0:T(8,128)} %bitcast.1), calls=%async_computation | async-start | bytes 2097152 | tf_op jit(solution)/shard_map/all_to_all | solution.py:536
  32.3 28.9 %collective-permute-start.8 = (f32[1,32,512]{2,1,0:T(8,128)}, f32[1,32,512]{2,1,0:T(8,128)}, u32[]{:S(2)}, u32[]{:S(2)}) collective-permute-start(f32[1,32,512]{2,1,0:T(8,128)} %get-tuple-element.55.rest_8_), channel_id=1, source_target_pairs={{0,56},{8,0},{16,8},{24,16},{32,24},{40,32},{48,40},{56,48},{1,57}... | collective-permute-start | bytes 196616 | tf_op jit(solution)/shard_map/ppermute | solution.py:24
  32.9 28.3 %collective-permute-start.10 = (f32[1,32,512]{2,1,0:T(8,128)}, f32[1,32,512]{2,1,0:T(8,128)}, u32[]{:S(2)}, u32[]{:S(2)}) collective-permute-start(f32[1,32,512]{2,1,0:T(8,128)} %get-tuple-element.57.rest_10_), channel_id=1, source_target_pairs={{0,7},{1,0},{2,1},{3,2},{4,3},{5,4},{6,5},{7,6},{8,15},{9,8},{10,9... | collective-permute-start | bytes 196616 | tf_op jit(solution)/shard_map/ppermute | solution.py:24
  33.7 28.0 %collective-permute-start.7 = (f32[1,32,512]{2,1,0:T(8,128)}, f32[1,32,512]{2,1,0:T(8,128)}, u32[]{:S(2)}, u32[]{:S(2)}) collective-permute-start(f32[1,32,512]{2,1,0:T(8,128)} %get-tuple-element.56.rest_9_.q2_plane), channel_id=1, source_target_pairs={{0,8},{8,16},{16,24},{24,32},{32,40},{40,48},{48,56},{56,0},{1,9},... | collective-permute-start | bytes 196616 | tf_op jit(solution)/shard_map/ppermute | solution.py:24
  40.6 21.1 %collective-permute-start.9 = (f32[1,32,512]{2,1,0:T(8,128)}, f32[1,32,512]{2,1,0:T(8,128)}, u32[]{:S(2)}, u32[]{:S(2)}) collective-permute-start(f32[1,32,512]{2,1,0:T(8,128)} %get-tuple-element.58.rest_11_.q2_rows), channel_id=1, source_target_pairs={{0,1},{1,2},{2,3},{3,4},{4,5},{5,6},{6,7},{7,0},{8,9},{9,10},{10,1... | collective-permute-start | bytes 196616 | tf_op jit(solution)/shard_map/ppermute | solution.py:24
  41.9 6.4 %copy-start.4 = (s32[1,1,32]{2,1,0:T(1,128)S(1)}, s32[1,1,32]{2,1,0:T(1,128)}, u32[]{:S(2)}) copy-start(s32[1,1,32]{2,1,0:T(1,128)} %param.16) | copy-start | bytes 388
  41.9 6.5 %copy-start.2 = (s32[1,1,32,32]{3,2,1,0:T(8,128)S(1)}, s32[1,1,32,32]{3,2,1,0:T(8,128)}, u32[]{:S(2)}) copy-start(s32[1,1,32,32]{3,2,1,0:T(8,128)} %param.15) | copy-start | bytes 12292
  48.2 13.5 %copy-start.1 = (s32[1,3]{1,0:T(1,128)S(1)}, s32[1,3]{1,0:T(1,128)}, u32[]{:S(2)}) copy-start(s32[1,3]{1,0:T(1,128)} %source.3) | copy-start | bytes 40
  55.8 10.3 %collective-permute-start.6 = (f32[2,8,256]{2,1,0:T(8,128)}, f32[2,8,256]{2,1,0:T(8,128)}, u32[]{:S(2)}, u32[]{:S(2)}) collective-permute-start(f32[2,8,256]{2,1,0:T(8,128)} %get-tuple-element.52), channel_id=1, source_target_pairs={{0,63},{1,56},{2,57},{3,58},{4,59},{5,60},{6,61},{7,62},{8,7},{9,0... | collective-permute-start | bytes 49160 | tf_op jit(solution)/shard_map/ppermute | solution.py:568
  61.2 9.1 %collective-permute-start.4 = (f32[2,16,256]{2,1,0:T(8,128)}, f32[2,16,256]{2,1,0:T(8,128)}, u32[]{:S(2)}, u32[]{:S(2)}) collective-permute-start(f32[2,16,256]{2,1,0:T(8,128)} %get-tuple-element.50), channel_id=1, source_target_pairs={{0,56},{8,0},{16,8},{24,16},{32,24},{40,32},{48,40},{56,48},{1,57}... | collective-permute-start | bytes 98312 | tf_op jit(solution)/shard_map/ppermute | solution.py:24
  61.2 9.1 %collective-permute-start.5 = (f32[2,16,256]{2,1,0:T(8,128)}, f32[2,16,256]{2,1,0:T(8,128)}, u32[]{:S(2)}, u32[]{:S(2)}) collective-permute-start(f32[2,16,256]{2,1,0:T(8,128)} %get-tuple-element.51), channel_id=1, source_target_pairs={{0,7},{1,0},{2,1},{3,2},{4,3},{5,4},{6,5},{7,6},{8,15},{9,8},{10,9... | collective-permute-start | bytes 98312 | tf_op jit(solution)/shard_map/ppermute | solution.py:24

commit v8 on v7

--- a/solution.py
+++ b/solution.py
@@ -243,7 +243,7 @@
         out_shape=out_shape,
         scratch_shapes=scratch + sems,
         compiler_params=ROOM,
-        cost_estimate=pl.CostEstimate(bytes_accessed=10 << 20, flops=1<<40, transcendentals=0),
+        cost_estimate=pl.CostEstimate(flops=(1 << 40) >> (6 * step), bytes_accessed=1, transcendentals=0),
         name="inner%d" % step,
     )(in_hbm(field), in_hbm(older), in_hbm(buoy), in_hbm(stiff), src, *halos)
 
@@ -259,65 +259,52 @@
     return jnp.dot(a, b, preferred_element_type=jnp.float32)
 
 
-def coarse_kernel(received, ids, along, rim_x, rim_y, corner, tiles, c_high, c_low, rows, sem):
+def rim_rows_kernel(received, ids, rim_x, rim_y, corner, tiles, sem):
     copies = []
     for part in range(4):
         at = pl.ds(part * 256, 256)
         copies.append(pltpu.make_async_copy(received.at[at], tiles.at[at], sem.at[part]))
         copies[-1].start()
-    tile = lax.broadcasted_iota(jnp.int32, (512, 256), 0)
+    row = lax.broadcasted_iota(jnp.int32, (16, 1024), 0)
+    wanted = jnp.concatenate([row, row * 16, row + 256, row * 16 + 256], axis=0)
+    select = jnp.where(wanted == ids[...], 1.0, 0.0).astype(jnp.bfloat16)
+    total = jnp.zeros((64, COARSE), jnp.float32)
     for part in range(4):
         at = slice(part * 256, part * 256 + 256)
-        select = jnp.where(tile == ids[:, at], 1.0, 0.0).astype(jnp.bfloat16)
         copies[part].wait()
         high, low = split_bf16(tiles[at, :])
-        if part == 0:
-            c_high[...] = dot(select, high)
-            c_low[...] = dot(select, low)
-        else:
-            c_high[...] += dot(select, high)
-            c_low[...] += dot(select, low)
-    coarse = c_high[...] + c_low[...]
+        total = total + (dot(select[:, at], high) + dot(select[:, at], low))
     for n in range(2):
-        rim_x[n] = coarse[n * 256 : n * 256 + 16, :]
-        corner[n] = coarse[n * 256 : n * 256 + 8, :]
-    for half in range(2):
-        lanes = slice(half * 128, half * 128 + 128)
-        rows[half] = coarse[:, lanes]
-        for n in range(2):
-            rim_y[n, :, lanes] = rows[half, pl.ds(n * 256, 16, stride=16), :]
-    weights = interpolation()
-    along[...] = dot(c_high[...].astype(jnp.bfloat16), weights) + dot(
-        c_low[...].astype(jnp.bfloat16), weights
-    )
-
-
-def coarse_tiles(received, ids):
+        rim_x[n] = total[n * 32 : n * 32 + 16]
+        rim_y[n] = total[n * 32 + 16 : n * 32 + 32]
+        corner[n] = total[n * 32 : n * 32 + 8]
+
+
+def rim_rows(received, ids):
     return pl.pallas_call(
-        coarse_kernel,
+        rim_rows_kernel,
         in_specs=[ANY, VMEM],
-        out_specs=[VMEM] * 4,
-        out_shape=[f32(512, DEPTH), f32(2, 16, COARSE), f32(2, 16, COARSE), f32(2, 8, COARSE)],
-        scratch_shapes=[
-            pltpu.VMEM((1024, COARSE), jnp.float32),
-            pltpu.VMEM((512, COARSE), jnp.float32),
-            pltpu.VMEM((512, COARSE), jnp.float32),
-            pltpu.VMEM((2, 512, 128), jnp.float32),
-            pltpu.SemaphoreType.DMA((4,)),
-        ],
+        out_specs=[VMEM] * 3,
+        out_shape=[f32(2, 16, COARSE), f32(2, 16, COARSE), f32(2, 8, COARSE)],
+        scratch_shapes=[pltpu.VMEM((1024, COARSE), jnp.float32), pltpu.SemaphoreType.DMA((4,))],
         compiler_params=ROOM,
         cost_estimate=pl.CostEstimate(flops=1 << 30, bytes_accessed=3 << 20, transcendentals=0),
-        name="coarse_tiles",
+        name="rim_rows",
     )(in_hbm(received), ids)
 
 
 SCALE = -1.0 / (2.0 * MUTE_RADIUS * MUTE_RADIUS)
 
 
-def picture_kernel(source, along, first_hbm, second_hbm, *rest):
+def picture_kernel(source, received, ids, first_hbm, second_hbm, *rest):
     own, far, own2, far2, stiff = (rest[4 * k : 4 * k + 4] for k in range(5))
-    image, saved, strip, plane_strip, last_plane, last_rows = rest[20:26]
-    fine, out, first, third, terms, in_sem, sem = rest[26:]
+    image, saved, strip, plane_strip, factors = rest[20:25]
+    fine, out, first, third, terms, tiles, onehot, along, tile_sem, in_sem, sem = rest[25:]
+    tile_copies = []
+    for part in range(4):
+        at = pl.ds(part * 256, 256)
+        tile_copies.append(pltpu.make_async_copy(received.at[at], tiles.at[at], tile_sem.at[part]))
+        tile_copies[-1].start()
     loads = []
     for k in range(4):
         at = pl.ds(k * SPAN, SPAN)
@@ -330,6 +317,16 @@
         loads.append(pair)
     for side, flux in enumerate(edge_fluxes(own, far, own2, far2)):
         terms[side] = (0.5 * stiff[side][...]) * flux
+    for start in range(0, 512, 128):
+        tile = lax.broadcasted_iota(jnp.int32, (128, 1024), 0) + start
+        onehot[start : start + 128, :] = jnp.where(tile == ids[...], 1.0, 0.0).astype(jnp.bfloat16)
+    for copy in tile_copies:
+        copy.wait()
+    weights = interpolation()
+    high, low = split_bf16(tiles[...])
+    c_high = dot(onehot[...], high).astype(jnp.bfloat16)
+    c_low = dot(onehot[...], low).astype(jnp.bfloat16)
+    along[...] = dot(c_high, weights) + dot(c_low, weights)
     row16 = lax.broadcasted_iota(jnp.int32, (16, DEPTH), 0)
     for n in range(2):
         for k in range(16):
@@ -362,7 +359,7 @@
             third[at, :] += terms[1]
         third[x * PLANES : x * PLANES + 1, :] += terms[2, x : x + 1, :]
         third[x * PLANES + 31 : x * PLANES + 32, :] += terms[3, x : x + 1, :]
-        last_rows[x : x + 1, :] = third[x * PLANES + 31 : x * PLANES + 32, :]
+        factors[1, 1, x : x + 1, :] = third[x * PLANES + 31 : x * PLANES + 32, :]
         dx = jnp.full((1, 128), x_base + x, jnp.int32).astype(jnp.float32)
         decay = jnp.exp((dx * dx) * SCALE)
         for part in range(4):
@@ -390,24 +387,30 @@
             for copy in copies[-2:]:
                 copy.start()
     plane_strip[...] = out[PLANES - 1, 0:24, :]
-    last_plane[...] = third[ROWS - PLANES : ROWS, :]
+    last_x = jnp.full((PLANES, DEPTH), x_base + PLANES - 1, jnp.int32).astype(jnp.float32)
+    last_y = jnp.full((PLANES, DEPTH), gy * PLANES + 31 - source[0, 1], jnp.int32).astype(jnp.float32)
+    x = (lax.broadcasted_iota(jnp.int32, (PLANES, DEPTH), 0) + x_base).astype(jnp.float32)
+    for way, (a, b) in enumerate(((last_x, y), (x, last_y))):
+        taper = 1.0 - jnp.exp((a * a + b * b + z * z) * SCALE)
+        newest = third[ROWS - PLANES : ROWS, :] if way == 0 else factors[1, 1]
+        factors[way, 1] = taper * newest
+        factors[way, 0] = taper * own2[1 + 2 * way][0]
     for copy in copies:
         copy.wait()
 
 
-def picture(source, along, first, second, edges):
+def picture(source, received, ids, first, second, edges):
     big = pltpu.VMEM((ROWS, DEPTH), jnp.float32)
     return pl.pallas_call(
         picture_kernel,
-        in_specs=[SMEM, VMEM, ANY, ANY] + [VMEM] * 20,
-        out_specs=[ANY, ANY] + [VMEM] * 4,
+        in_specs=[SMEM, ANY, VMEM, ANY, ANY] + [VMEM] * 20,
+        out_specs=[ANY, ANY] + [VMEM] * 3,
         out_shape=[
             pltpu.HBM((PLANES, PLANES, DEPTH), jnp.float32),
             pltpu.HBM((ROWS, DEPTH), jnp.float32),
             f32(PLANES, 8, DEPTH),
             f32(24, DEPTH),
-            f32(PLANES, DEPTH),
-            f32(PLANES, DEPTH),
+            f32(2, 2, PLANES, DEPTH),
         ],
         scratch_shapes=[
             pltpu.VMEM((4, 2 * 17 * PLANES, 128), jnp.float32),
@@ -415,28 +418,38 @@
             big,
             big,
             pltpu.VMEM((4, PLANES, DEPTH), jnp.float32),
+            pltpu.VMEM((1024, COARSE), jnp.float32),
+            pltpu.VMEM((512, 1024), jnp.bfloat16),
+            pltpu.VMEM((512, DEPTH), jnp.float32),
+            pltpu.SemaphoreType.DMA((4,)),
             pltpu.SemaphoreType.DMA((4, 2)),
             pltpu.SemaphoreType.DMA((8, 2)),
         ],
         compiler_params=ROOM,
         cost_estimate=pl.CostEstimate(flops=1 << 40, bytes_accessed=8 << 20, transcendentals=0),
         name="picture",
-    )(source, along, in_hbm(first), in_hbm(second), *edges)
+    )(source, in_hbm(received), ids, in_hbm(first), in_hbm(second), *edges)
 
 
 def rims_kernel(
-    source, rim_x, rim_y, corner, strip, plane_strip, q3_plane, q3_rows, q2_plane, q2_rows,
-    image_in, image, rims, along, fine, strip_out, plane_out, delta, sem,
+    rim_x_hbm, rim_y_hbm, corner_hbm, strip, plane_strip, factors,
+    image_in, image, rim_x, rim_y, corner, rims, along, fine, strip_out, plane_out, delta, sem,
 ):
+    pairs = ((rim_x_hbm, rim_x), (rim_y_hbm, rim_y), (corner_hbm, corner))
+    loads = [pltpu.make_async_copy(a, b, sem.at[2 + k]) for k, (a, b) in enumerate(pairs)]
+    for copy in loads:
+        copy.start()
+    weights = interpolation()
     gx = lax.axis_index("gx")
     gy = lax.axis_index("gy")
     keep_x = jnp.where(gx < lax.axis_size("gx") - 1, 1.0, 0.0)
     keep_y = jnp.where(gy < lax.axis_size("gy") - 1, 1.0, 0.0)
+    for copy in loads:
+        copy.wait()
     for n in range(2):
         rims[n * 40 : n * 40 + 16] = rim_x[n] * (0.5 * keep_x)
         rims[n * 40 + 16 : n * 40 + 32] = rim_y[n] * (0.5 * keep_y)
         rims[n * 40 + 32 : n * 40 + 40] = corner[n] * (0.5 * keep_x * keep_y)
-    weights = interpolation()
     high, low = split_bf16(rims[...])
     along[...] = dot(high, weights) + dot(low, weights)
     row16 = lax.broadcasted_iota(jnp.int32, (16, DEPTH), 0)
@@ -450,30 +463,13 @@
                 lanes = slice(part * 128, part * 128 + 128)
                 fine[part, pl.ds(base, 16, stride=2), :] = rows[:, lanes]
                 fine[part, pl.ds(base + 1, 16, stride=2), :] = middle[:, lanes]
-    index = lax.broadcasted_iota(jnp.int32, (PLANES, 128), 0)
-    last_x = gx * PLANES + (PLANES - 1) - source[0, 0]
-    last_y = gy * PLANES + (PLANES - 1) - source[0, 1]
     for part in range(4):
         lanes = slice(part * 128, part * 128 + 128)
-        z = (lax.broadcasted_iota(jnp.int32, (PLANES, 128), 1) + part * 128 - source[0, 2]).astype(jnp.float32)
         for way in range(2):
-            if way == 0:
-                fixed = last_x
-                moving = (index + gy * PLANES - source[0, 1]).astype(jnp.float32)
-                pair = (q2_plane[0, :, lanes], q3_plane[:, lanes])
-            else:
-                fixed = last_y
-                moving = (index + gx * PLANES - source[0, 0]).astype(jnp.float32)
-                pair = (q2_rows[0, :, lanes], q3_rows[:, lanes])
-            fixed = jnp.full((PLANES, 128), fixed, jnp.int32).astype(jnp.float32)
-            distance = fixed * fixed + moving * moving + z * z
-            taper = 1.0 - jnp.exp(distance * SCALE)
-            total = None
-            for n in range(2):
-                base = (n * 2 + way) * PLANES
-                term = fine[part, base : base + PLANES, :] * pair[n]
-                total = term if total is None else total + term
-            delta[way, :, lanes] = taper * total
+            delta[way, :, lanes] = (
+                fine[part, way * PLANES : (way + 1) * PLANES, :] * factors[way, 0, :, lanes]
+                + fine[part, (2 + way) * PLANES : (3 + way) * PLANES, :] * factors[way, 1, :, lanes]
+            )
     row8 = lax.broadcasted_iota(jnp.int32, (8, DEPTH), 0)
     for x in range(PLANES):
         value = strip[x] + jnp.where(row8 == 7, delta[1, x : x + 1, :], 0.0)
@@ -491,26 +487,29 @@
         copy.wait()
 
 
-def add_rims(source, rims, strips, faces2, image):
+def add_rims(rims, strips, image):
     return pl.pallas_call(
         rims_kernel,
-        in_specs=[SMEM] + [VMEM] * 9 + [ANY],
+        in_specs=[ANY] * 3 + [VMEM] * 3 + [ANY],
         out_specs=ANY,
         out_shape=pltpu.HBM((PLANES, PLANES, DEPTH), jnp.float32),
-        input_output_aliases={10: 0},
+        input_output_aliases={6: 0},
         scratch_shapes=[
+            pltpu.VMEM((2, 16, COARSE), jnp.float32),
+            pltpu.VMEM((2, 16, COARSE), jnp.float32),
+            pltpu.VMEM((2, 8, COARSE), jnp.float32),
             pltpu.VMEM((80, COARSE), jnp.float32),
             pltpu.VMEM((80, DEPTH), jnp.float32),
             pltpu.VMEM((4, 4 * PLANES, 128), jnp.float32),
             pltpu.VMEM((PLANES, 8, DEPTH), jnp.float32),
             pltpu.VMEM((24, DEPTH), jnp.float32),
             pltpu.VMEM((2, PLANES, DEPTH), jnp.float32),
-            pltpu.SemaphoreType.DMA((2,)),
+            pltpu.SemaphoreType.DMA((5,)),
         ],
         compiler_params=ROOM,
         cost_estimate=pl.CostEstimate(flops=1 << 20, bytes_accessed=2 << 20, transcendentals=0),
         name="add_rims",
-    )(source, *rims, *strips, *faces2, in_hbm(image))
+    )(*rims, *strips, in_hbm(image))
 
 
 def per_device(
@@ -536,7 +535,7 @@
     received = lax.all_to_all(
         tiles[0, 0], ("shot", "gx"), split_axis=0, concat_axis=0, tiled=True
     ).reshape(1024, COARSE)
-    numbers, counts, far = lax.optimization_barrier((tile_ids, tile_counts, far))
+    numbers, counts, far[0], far[1] = lax.optimization_barrier((tile_ids, tile_counts, far[0], far[1]))
     slot = lax.broadcasted_iota(jnp.int32, (32, 32), 1)
     ids = jnp.where(slot < counts[0, 0][:, None], numbers[0, 0], -1).reshape(1, 1024)
     src = sources(receiver_cells[0], receiver_data[0])
@@ -546,11 +545,11 @@
     (third,) = inner(second, current, buoy, stiff, src, [], 1)
 
     received, third = lax.optimization_barrier((received, third))
-    along, rim_x, rim_y, corner = coarse_tiles(received, ids)
+    rim_x, rim_y, corner = rim_rows(received, ids)
     rims = [rotate(rim_x, "gx", -1), rotate(rim_y, "gy", -1), diagonal(corner)]
     edges = [*own, *far, *own2, *far2, *stiff_faces]
-    image, last_current, *strips = picture(source_cell, along, second, third, edges)
-    image = add_rims(source_cell, rims, strips, [own2[1], own2[3]], image)
+    image, last_current, *strips = picture(source_cell, received, ids, second, third, edges)
+    image = add_rims(rims, strips, image)
     shape = current_field.shape
     return image.reshape(shape), second.reshape(shape), last_current.reshape(shape)
 

time: 73 us -> 70.7 us (0.968)
  starting transfers between devices: 37.4 us -> 34.5 us
    ppermute x1, starting transfers between devices: 5.34 us -> 0.01 us  [diagonal(): return lax.ppermute(block, ('gx', 'gy'), route)]
    ppermute x10, waiting for transfers between devices: 4.13 us -> 0.03 us  [rotate(): lax.ppermute(block, axis, [(i, (i + step) % count) for i in range(count)])]
    ppermute x1, waiting for transfers between devices: 0.01 us -> 2.78 us  [diagonal(): return lax.ppermute(block, ('gx', 'gy'), route)]
    ppermute x10, starting transfers between devices: 20.4 us -> 22.4 us  [rotate(): lax.ppermute(block, axis, [(i, (i + step) % count) for i in range(count)])]
    all_to_all x1, waiting for transfers between devices: 4.63 us -> 6.37 us  [per_device(): lax.all_to_all(tiles[0, 0], ('shot', 'gx'), split_axis=0, concat_axis=0,...]
    pallas_call x3, Pallas kernels: 9.39 us -> 10.2 us  [the longest x1 6.07 us: picture(): pl.pallas_call(picture_kernel, in_specs=[SMEM, ANY, VMEM, ANY, ANY] + [VM...]
  transfers between devices with their start and end apart: 12 -> 12, of which waited for: 2 -> 2; matrix products, arithmetic and copies ran while one was open for 0% -> 0% of each run, Pallas kernels for 29% -> 31%
where the time goes in v8:
time: 70.7 us; the launch traced here: 70.4 us
  starting transfers between devices  34.5 us (49%)
  Pallas kernels  25.4 us (36%)
  waiting for transfers between devices  9.18 us (13%)
  between operations  0.97 us (1%)
    ppermute x10, starting transfers between devices, rotate(): lax.ppermute(block, axis, [(i, (i + step) % count) for i in range(count)])  22.4 us
    pallas_call x2, Pallas kernels, inner(): pl.pallas_call(lambda *refs: inner_kernel(*refs, step=step), in_specs=[AN...  12.6 us
    all_to_all x1, starting transfers between devices, per_device(): lax.all_to_all(tiles[0, 0], ('shot', 'gx'), split_axis=0, concat_axis=0,...  12.2 us
    all_to_all x1, waiting for transfers between devices, per_device(): lax.all_to_all(tiles[0, 0], ('shot', 'gx'), split_axis=0, concat_axis=0,...  6.37 us
    pallas_call x1, Pallas kernels, picture(): pl.pallas_call(picture_kernel, in_specs=[SMEM, ANY, VMEM, ANY, ANY] + [VM...  6.07 us
    ppermute x1, waiting for transfers between devices, diagonal(): return lax.ppermute(block, ('gx', 'gy'), route)  2.78 us
    pallas_call x1, Pallas kernels, rim_rows(): pl.pallas_call(rim_rows_kernel, in_specs=[ANY, VMEM], out_specs=[VMEM] *...  2.21 us
    pallas_call x1, Pallas kernels, add_rims(): pl.pallas_call(rims_kernel, in_specs=[ANY] * 3 + [VMEM] * 3 + [ANY], out_...  1.94 us
  transfers between devices with their start and end apart: 12, of which 2 were waited for; matrix products, arithmetic and copies ran while one was open for 0% of the time, Pallas kernels for 31%

profile of v8, /device:TPU:39, one launch (start us, length us, event | category | flops | bytes accessed | tf_op | source)
XLA Modules:
  0.0 70.4 jit_solution(2090493702899262854)
XLA Ops:
  0.6 1.7 %faces.1 = (f32[2,32,512]{2,1,0:T(8,128)S(1)}, f32[2,32,512]{2,1,0:T(8,128)S(1)}, f32[2,32,512]{2,1,0:T(8,128)S(1)}, f32[2,32,512]{2,1,0:T(8,128)S(1)}) custom-call(f32[32,32,512]{2,1,0:T(8,128)} %bitcast.19, f32[32,32,512]{2,1,0:T(8,128)} %bitcast.20, f32[32,32,512]{2,1,0:T(8,128)} %bitcast.21, f32[32,32,512]{2,1,0:T(8,128)} %bitcast.22, ...), custom_call_target="tpu_custom_call" | custom-call | bytes 3145728 | tf_op jit(solution)/shard_map/faces/pallas_call | solution.py:51
  2.3 0.0 copy-start.3
  2.4 0.0 copy-start
  2.4 6.0 %collective-permute-start = (f32[2,32,512]{2,1,0:T(8,128)S(1)}, f32[2,32,512]{2,1,0:T(8,128)S(1)}, u32[]{:S(2)}, u32[]{:S(2)}) collective-permute-start(f32[2,32,512]{2,1,0:T(8,128)S(1)} %get-tuple-element.35.refs_6_.rest_1_), channel_id=1, source_target_pairs={{0,8},{8,16},{16,24},{24,32},{32,40},{40,48},{48,56},{56,0},{1,9},... | collective-permute-start | bytes 393224 | tf_op jit(solution)/shard_map/ppermute | solution.py:24
  8.4 1.6 %collective-permute-start.2 = (f32[2,32,512]{2,1,0:T(8,128)S(1)}, f32[2,32,512]{2,1,0:T(8,128)S(1)}, u32[]{:S(2)}, u32[]{:S(2)}) collective-permute-start(f32[2,32,512]{2,1,0:T(8,128)S(1)} %get-tuple-element.37.refs_8_.rest_3_), channel_id=1, source_target_pairs={{0,1},{1,2},{2,3},{3,4},{4,5},{5,6},{6,7},{7,0},{8,9},{9,10},{10,1... | collective-permute-start | bytes 393224 | tf_op jit(solution)/shard_map/ppermute | solution.py:24
  10.0 12.2 %all-to-all-start = ((f32[32,32,256]{2,1,0:T(8,128)}), f32[32,32,256]{2,1,0:T(8,128)}, u32[]{:S(2)}, u32[]{:S(2)}) async-start(f32[32,32,256]{2,1,0:T(8,128)} %bitcast.1), calls=%async_computation | async-start | bytes 2097152 | tf_op jit(solution)/shard_map/all_to_all | solution.py:535
  22.2 0.8 %sources.1.refs_4_ = f32[2,1024,128]{2,1,0:T(8,128)S(1)} custom-call(s32[3,1024]{1,0:T(4,128)S(1)} %bitcast.17, f32[2,1024]{1,0:T(2,128)S(1)} %bitcast.18), custom_call_target="tpu_custom_call" | custom-call | flops 1 | bytes 1 | tf_op jit(solution)/shard_map/sources/pallas_call | solution.py:93
  23.1 0.0 copy-start.2
  23.1 6.3 %inner0.1 = (f32[1024,512]{1,0:T(8,128)}, f32[1,32,512]{2,1,0:T(8,128)S(1)}, f32[1,32,512]{2,1,0:T(8,128)S(1)}, f32[1,32,512]{2,1,0:T(8,128)S(1)}, f32[1,32,512]...) custom-call(f32[1024,512]{1,0:T(8,128)} %bitcast.23, ...), custom_call_target="tpu_custom_call" | custom-call | flops 1099511627776 | bytes 1 | tf_op jit(solution)/shard_map/inner0/pallas_call | solution.py:239
  29.4 1.8 %collective-permute-start.10 = (f32[1,32,512]{2,1,0:T(8,128)S(1)}, f32[1,32,512]{2,1,0:T(8,128)S(1)}, u32[]{:S(2)}, u32[]{:S(2)}) collective-permute-start(f32[1,32,512]{2,1,0:T(8,128)S(1)} %get-tuple-element.50.rest_10_), channel_id=1, source_target_pairs={{0,7},{1,0},{2,1},{3,2},{4,3},{5,4},{6,5},{7,6},{8,15},{9,8},{10,9... | collective-permute-start | bytes 196616 | tf_op jit(solution)/shard_map/ppermute | solution.py:24
  31.2 5.1 %collective-permute-start.7 = (f32[1,32,512]{2,1,0:T(8,128)S(1)}, f32[1,32,512]{2,1,0:T(8,128)S(1)}, u32[]{:S(2)}, u32[]{:S(2)}) collective-permute-start(f32[1,32,512]{2,1,0:T(8,128)S(1)} %get-tuple-element.49.rest_9_), channel_id=1, source_target_pairs={{0,8},{8,16},{16,24},{24,32},{32,40},{40,48},{48,56},{56,0},{1,9},... | collective-permute-start | bytes 196616 | tf_op jit(solution)/shard_map/ppermute | solution.py:24
  36.3 1.0 %collective-permute-start.9 = (f32[1,32,512]{2,1,0:T(8,128)S(1)}, f32[1,32,512]{2,1,0:T(8,128)S(1)}, u32[]{:S(2)}, u32[]{:S(2)}) collective-permute-start(f32[1,32,512]{2,1,0:T(8,128)S(1)} %get-tuple-element.51.rest_11_), channel_id=1, source_target_pairs={{0,1},{1,2},{2,3},{3,4},{4,5},{5,6},{6,7},{7,0},{8,9},{9,10},{10,1... | collective-permute-start | bytes 196616 | tf_op jit(solution)/shard_map/ppermute | solution.py:24
  37.3 0.1 iota_compare_fusion
  37.3 0.1 lt.23
  37.4 0.1 squeeze.19
  37.5 6.3 %inner1.1.second_hbm = f32[1024,512]{1,0:T(8,128)} custom-call(f32[1024,512]{1,0:T(8,128)} %get-tuple-element.40.refs_0_.first_hbm, f32[1024,512]{1,0:T(8,128)} %bitcast.24, f32[1024,512]{1,0:T(8,128)} %bitcast.26, f32[1024,512]{1,0:T(8,128)} %bitcast.31, f32[2,1024,128]{2,1,0:T(8,128)S(1)} %sources.1.refs_4_), custom_call_target="tpu_custom_call" | custom-call | flops 17179869184 | bytes 1 | tf_op jit(solution)/shard_map/inner1/pallas_call | solution.py:239
  43.8 0.0 copy-start.1
  43.8 6.4 %all-to-all-done = f32[32,32,256]{2,1,0:T(8,128)} async-done(((f32[32,32,256]{2,1,0:T(8,128)}), f32[32,32,256]{2,1,0:T(8,128)}, u32[]{:S(2)}, u32[]{:S(2)}) %all-to-all-start) | async-done | bytes 1048608 | tf_op jit(solution)/shard_map/all_to_all | solution.py:535
  50.2 2.2 %rim_rows.1 = (f32[2,16,256]{2,1,0:T(8,128)}, f32[2,16,256]{2,1,0:T(8,128)}, f32[2,8,256]{2,1,0:T(8,128)}) custom-call(f32[1024,256]{1,0:T(8,128)} %bitcast.2.received, s32[1,1024]{1,0:T(1,128)S(1)} %broadcast_select_fusion.ids), custom_call_target="tpu_custom_call" | custom-call | flops 1073741824 | bytes 3145728 | tf_op jit(solution)/shard_map/rim_rows/pallas_call | solution.py:284
  52.4 3.0 %collective-permute-start.4 = (f32[2,16,256]{2,1,0:T(8,128)}, f32[2,16,256]{2,1,0:T(8,128)}, u32[]{:S(2)}, u32[]{:S(2)}) collective-permute-start(f32[2,16,256]{2,1,0:T(8,128)} %get-tuple-element.44), channel_id=1, source_target_pairs={{0,56},{8,0},{16,8},{24,16},{32,24},{40,32},{48,40},{56,48},{1,57}... | collective-permute-start | bytes 98312 | tf_op jit(solution)/shard_map/ppermute | solution.py:24
  55.5 3.9 %collective-permute-start.5 = (f32[2,16,256]{2,1,0:T(8,128)}, f32[2,16,256]{2,1,0:T(8,128)}, u32[]{:S(2)}, u32[]{:S(2)}) collective-permute-start(f32[2,16,256]{2,1,0:T(8,128)} %get-tuple-element.45), channel_id=1, source_target_pairs={{0,7},{1,0},{2,1},{3,2},{4,3},{5,4},{6,5},{7,6},{8,15},{9,8},{10,9... | collective-permute-start | bytes 98312 | tf_op jit(solution)/shard_map/ppermute | solution.py:24
  59.4 6.1 %picture.1 = (f32[32,32,512]{2,1,0:T(8,128)}, f32[1024,512]{1,0:T(8,128)}, f32[32,8,512]{2,1,0:T(8,128)S(1)}, f32[24,512]{1,0:T(8,128)S(1)}, f32[2,2,32,512]{3,2,1,0:T(8,128)S(1)}) custom-call(s32[1,3]{1,0:T(1,128)S(1)} %copy-done.1, f32[1024,256]{1,0:T(8,128)} %bitcast.2.received, s32[1,1024]{1,0:T(1,128)S(1)} %broadcast_select_fusion.ids, ...), custom_call_target="tpu_custom_call" | custom-call | flops 1099511627776 | bytes 8388608 | tf_op jit(solution)/shard_map/picture/pallas_call | solution.py:404
  65.5 2.8 %collective-permute-done.6.corner_hbm = f32[2,8,256]{2,1,0:T(8,128)} collective-permute-done((f32[2,8,256]{2,1,0:T(8,128)}, f32[2,8,256]{2,1,0:T(8,128)}, u32[]{:S(2)}, u32[]{:S(2)}) %collective-permute-start.6) | collective-permute-done | bytes 16416 | tf_op jit(solution)/shard_map/ppermute | solution.py:567
  68.3 1.9 %add_rims.1 = f32[32,32,512]{2,1,0:T(8,128)} custom-call(f32[2,16,256]{2,1,0:T(8,128)} %collective-permute-done.4.rim_x_hbm, f32[2,16,256]{2,1,0:T(8,128)} %collective-permute-done.5.rim_y_hbm, f32[2,8,256]{2,1,0:T(8,128)} %collective-permute-done.6.corner_hbm, f32[32,8,512]{2,1,0:T(8,128)S(1)} %get-tuple-element.56.strip, ...), custom_call_target="tpu_custom_call", output_to_operand_aliasing={{}: (6, {})} | custom-call | flops 1048576 | bytes 2097152 | tf_op jit(solution)/shard_map/add_rims/pallas_call | solution.py:491
  (22 shorter events, 0.1 us)
Async XLA Ops:
  2.3 19.8 %copy-start.3 = (s32[1,3,1024]{2,0,1:T(1,128)S(1)}, s32[1,3,1024]{2,0,1:T(1,128)}, u32[]{:S(2)}) copy-start(s32[1,3,1024]{2,0,1:T(1,128)} %param.17) | copy-start | bytes 36868
  2.4 19.8 %copy-start = (f32[1,2,1024]{2,1,0:T(2,128)S(1)}, f32[1,2,1024]{2,1,0:T(2,128)}, u32[]{:S(2)}) copy-start(f32[1,2,1024]{2,1,0:T(2,128)} %param.18) | copy-start | bytes 24580
  2.4 20.6 %collective-permute-start = (f32[2,32,512]{2,1,0:T(8,128)S(1)}, f32[2,32,512]{2,1,0:T(8,128)S(1)}, u32[]{:S(2)}, u32[]{:S(2)}) collective-permute-start(f32[2,32,512]{2,1,0:T(8,128)S(1)} %get-tuple-element.35.refs_6_.rest_1_), channel_id=1, source_target_pairs={{0,8},{8,16},{16,24},{24,32},{32,40},{40,48},{48,56},{56,0},{1,9},... | collective-permute-start | bytes 393224 | tf_op jit(solution)/shard_map/ppermute | solution.py:24
  8.4 14.6 %collective-permute-start.1 = (f32[2,32,512]{2,1,0:T(8,128)S(1)}, f32[2,32,512]{2,1,0:T(8,128)S(1)}, u32[]{:S(2)}, u32[]{:S(2)}) collective-permute-start(f32[2,32,512]{2,1,0:T(8,128)S(1)} %get-tuple-element.34.refs_5_.rest_0_), channel_id=1, source_target_pairs={{0,56},{8,0},{16,8},{24,16},{32,24},{40,32},{48,40},{56,48},{1,57}... | collective-permute-start | bytes 393224 | tf_op jit(solution)/shard_map/ppermute | solution.py:24
  8.4 14.6 %collective-permute-start.2 = (f32[2,32,512]{2,1,0:T(8,128)S(1)}, f32[2,32,512]{2,1,0:T(8,128)S(1)}, u32[]{:S(2)}, u32[]{:S(2)}) collective-permute-start(f32[2,32,512]{2,1,0:T(8,128)S(1)} %get-tuple-element.37.refs_8_.rest_3_), channel_id=1, source_target_pairs={{0,1},{1,2},{2,3},{3,4},{4,5},{5,6},{6,7},{7,0},{8,9},{9,10},{10,1... | collective-permute-start | bytes 393224 | tf_op jit(solution)/shard_map/ppermute | solution.py:24
  10.0 13.1 %collective-permute-start.3 = (f32[2,32,512]{2,1,0:T(8,128)S(1)}, f32[2,32,512]{2,1,0:T(8,128)S(1)}, u32[]{:S(2)}, u32[]{:S(2)}) collective-permute-start(f32[2,32,512]{2,1,0:T(8,128)S(1)} %get-tuple-element.36.refs_7_.rest_2_), channel_id=1, source_target_pairs={{0,7},{1,0},{2,1},{3,2},{4,3},{5,4},{6,5},{7,6},{8,15},{9,8},{10,9... | collective-permute-start | bytes 393224 | tf_op jit(solution)/shard_map/ppermute | solution.py:24
  10.0 40.3 %all-to-all-start = ((f32[32,32,256]{2,1,0:T(8,128)}), f32[32,32,256]{2,1,0:T(8,128)}, u32[]{:S(2)}, u32[]{:S(2)}) async-start(f32[32,32,256]{2,1,0:T(8,128)} %bitcast.1), calls=%async_computation | async-start | bytes 2097152 | tf_op jit(solution)/shard_map/all_to_all | solution.py:535
  23.0 14.2 %copy-start.4 = (s32[1,1,32]{2,1,0:T(1,128)S(1)}, s32[1,1,32]{2,1,0:T(1,128)}, u32[]{:S(2)}) copy-start(s32[1,1,32]{2,1,0:T(1,128)} %param.16) | copy-start | bytes 388
  23.1 14.4 %copy-start.2 = (s32[1,1,32,32]{3,2,1,0:T(8,128)S(1)}, s32[1,1,32,32]{3,2,1,0:T(8,128)}, u32[]{:S(2)}) copy-start(s32[1,1,32,32]{3,2,1,0:T(8,128)} %param.15) | copy-start | bytes 12292
  29.4 26.1 %collective-permute-start.10 = (f32[1,32,512]{2,1,0:T(8,128)S(1)}, f32[1,32,512]{2,1,0:T(8,128)S(1)}, u32[]{:S(2)}, u32[]{:S(2)}) collective-permute-start(f32[1,32,512]{2,1,0:T(8,128)S(1)} %get-tuple-element.50.rest_10_), channel_id=1, source_target_pairs={{0,7},{1,0},{2,1},{3,2},{4,3},{5,4},{6,5},{7,6},{8,15},{9,8},{10,9... | collective-permute-start | bytes 196616 | tf_op jit(solution)/shard_map/ppermute | solution.py:24
  31.2 28.2 %collective-permute-start.7 = (f32[1,32,512]{2,1,0:T(8,128)S(1)}, f32[1,32,512]{2,1,0:T(8,128)S(1)}, u32[]{:S(2)}, u32[]{:S(2)}) collective-permute-start(f32[1,32,512]{2,1,0:T(8,128)S(1)} %get-tuple-element.49.rest_9_), channel_id=1, source_target_pairs={{0,8},{8,16},{16,24},{24,32},{32,40},{40,48},{48,56},{56,0},{1,9},... | collective-permute-start | bytes 196616 | tf_op jit(solution)/shard_map/ppermute | solution.py:24
  36.3 23.1 %collective-permute-start.8 = (f32[1,32,512]{2,1,0:T(8,128)S(1)}, f32[1,32,512]{2,1,0:T(8,128)S(1)}, u32[]{:S(2)}, u32[]{:S(2)}) collective-permute-start(f32[1,32,512]{2,1,0:T(8,128)S(1)} %get-tuple-element.48.rest_8_), channel_id=1, source_target_pairs={{0,56},{8,0},{16,8},{24,16},{32,24},{40,32},{48,40},{56,48},{1,57}... | collective-permute-start | bytes 196616 | tf_op jit(solution)/shard_map/ppermute | solution.py:24
  36.3 23.1 %collective-permute-start.9 = (f32[1,32,512]{2,1,0:T(8,128)S(1)}, f32[1,32,512]{2,1,0:T(8,128)S(1)}, u32[]{:S(2)}, u32[]{:S(2)}) collective-permute-start(f32[1,32,512]{2,1,0:T(8,128)S(1)} %get-tuple-element.51.rest_11_), channel_id=1, source_target_pairs={{0,1},{1,2},{2,3},{3,4},{4,5},{5,6},{6,7},{7,0},{8,9},{9,10},{10,1... | collective-permute-start | bytes 196616 | tf_op jit(solution)/shard_map/ppermute | solution.py:24
  43.8 15.6 %copy-start.1 = (s32[1,3]{1,0:T(1,128)S(1)}, s32[1,3]{1,0:T(1,128)}, u32[]{:S(2)}) copy-start(s32[1,3]{1,0:T(1,128)} %source.1) | copy-start | bytes 40
  52.4 15.8 %collective-permute-start.4 = (f32[2,16,256]{2,1,0:T(8,128)}, f32[2,16,256]{2,1,0:T(8,128)}, u32[]{:S(2)}, u32[]{:S(2)}) collective-permute-start(f32[2,16,256]{2,1,0:T(8,128)} %get-tuple-element.44), channel_id=1, source_target_pairs={{0,56},{8,0},{16,8},{24,16},{32,24},{40,32},{48,40},{56,48},{1,57}... | collective-permute-start | bytes 98312 | tf_op jit(solution)/shard_map/ppermute | solution.py:24
  55.5 12.8 %collective-permute-start.5 = (f32[2,16,256]{2,1,0:T(8,128)}, f32[2,16,256]{2,1,0:T(8,128)}, u32[]{:S(2)}, u32[]{:S(2)}) collective-permute-start(f32[2,16,256]{2,1,0:T(8,128)} %get-tuple-element.45), channel_id=1, source_target_pairs={{0,7},{1,0},{2,1},{3,2},{4,3},{5,4},{6,5},{7,6},{8,15},{9,8},{10,9... | collective-permute-start | bytes 98312 | tf_op jit(solution)/shard_map/ppermute | solution.py:24
  59.4 8.9 %collective-permute-start.6 = (f32[2,8,256]{2,1,0:T(8,128)}, f32[2,8,256]{2,1,0:T(8,128)}, u32[]{:S(2)}, u32[]{:S(2)}) collective-permute-start(f32[2,8,256]{2,1,0:T(8,128)} %get-tuple-element.46), channel_id=1, source_target_pairs={{0,63},{1,56},{2,57},{3,58},{4,59},{5,60},{6,61},{7,62},{8,7},{9,0... | collective-permute-start | bytes 49160 | tf_op jit(solution)/shard_map/ppermute | solution.py:567

commit v9 on v8

--- a/solution.py
+++ b/solution.py
@@ -19,9 +19,24 @@
 ROOM = pltpu.CompilerParams(vmem_limit_bytes=16 << 20)
 
 
-def rotate(block, axis, step):
+def swap(block, axis, start):
     count = lax.axis_size(axis)
-    return lax.ppermute(block, axis, [(i, (i + step) % count) for i in range(count)])
+    route = []
+    for low in range(start, count - 1, 2):
+        route += [(low, low + 1), (low + 1, low)]
+    return lax.ppermute(block, axis, route)
+
+
+def parity(axis):
+    return lax.rem(lax.axis_index(axis), 2)
+
+
+def by_side(messages):
+    values = []
+    for axis, pair in (("gx", messages[:2]), ("gy", messages[2:])):
+        odd = parity(axis) == 1
+        values += [jnp.where(odd, pair[0], pair[1]), jnp.where(odd, pair[1], pair[0])]
+    return values
 
 
 def f32(*shape):
@@ -33,13 +48,17 @@
     return high, (x - high.astype(jnp.float32)).astype(jnp.bfloat16)
 
 
-def faces_kernel(fx_lo, fx_hi, fy_lo, fy_hi, bx_lo, bx_hi, by_lo, by_hi, sx_lo, sx_hi, sy_lo, sy_hi):
+def faces_kernel(fx_lo, fx_hi, fy_lo, fy_hi, bx_lo, bx_hi, by_lo, by_hi, x_first, x_next, y_first, y_next):
+    odd_x = parity("gx") == 1
+    odd_y = parity("gy") == 1
     for slot, refs in enumerate(((fx_lo, fx_hi, fy_lo, fy_hi), (bx_lo, bx_hi, by_lo, by_hi))):
-        sx_lo[slot] = refs[0][0]
-        sx_hi[slot] = refs[1][0]
+        low, high = refs[0][0], refs[1][0]
+        x_first[slot] = jnp.where(odd_x, low, high)
+        x_next[slot] = jnp.where(odd_x, high, low)
         for x in range(PLANES):
-            sy_lo[slot, x : x + 1, :] = refs[2][x, 0:1, :]
-            sy_hi[slot, x : x + 1, :] = refs[3][x, 7:8, :]
+            low, high = refs[2][x, 0:1, :], refs[3][x, 7:8, :]
+            y_first[slot, x : x + 1, :] = jnp.where(odd_y, low, high)
+            y_next[slot, x : x + 1, :] = jnp.where(odd_y, high, low)
 
 
 def faces(field, buoyancy):
@@ -115,8 +134,8 @@
         jnp.where(gy < lax.axis_size("gy") - 1, 1.0, 0.0),
     ]
     return [
-        (own_b[side][1] + keep[side] * far_b[side][1])
-        * (keep[side] * far_f[side][0] - own_f[side][0])
+        (own_b[side] + keep[side] * far_b[side])
+        * (keep[side] * far_f[side] - own_f[side])
         for side in range(4)
     ]
 
@@ -144,7 +163,9 @@
     out_copies = []
 
     if step == 0:
-        for side, flux in enumerate(edge_fluxes(own, far, own, far)):
+        near_b, away_b = by_side([m[1] for m in own]), by_side([m[1] for m in far])
+        near_f, away_f = by_side([m[0] for m in own]), by_side([m[0] for m in far])
+        for side, flux in enumerate(edge_fluxes(near_b, away_b, near_f, away_f)):
             edges[side] = flux
 
     def arrive(chunk):
@@ -195,8 +216,9 @@
         n_buf[at, 128:DEPTH] = value[:, 128:]
         n_buf[at, head] = value[:, head] + src[step, at, :]
         if step == 0:
-            faces_out[2][0, pl.ds(x, 1), :] = n_buf[pl.ds(base, 1), :]
-            faces_out[3][0, pl.ds(x, 1), :] = n_buf[pl.ds(base + PLANES - 1, 1), :]
+            odd = parity("gy")
+            faces_out[2][0, pl.ds(x, 1), :] = n_buf[pl.ds(base + 31 * (1 - odd), 1), :]
+            faces_out[3][0, pl.ds(x, 1), :] = n_buf[pl.ds(base + 31 * odd, 1), :]
             stiff_out[2][pl.ds(x, 1), :] = s_buf[pl.ds(base, 1), :]
             stiff_out[3][pl.ds(x, 1), :] = s_buf[pl.ds(base + PLANES - 1, 1), :]
         return flux_x
@@ -218,8 +240,10 @@
         copy.start()
         out_copies.append(copy)
     if step == 0:
-        faces_out[0][0] = n_buf[0:PLANES, :]
-        faces_out[1][0] = n_buf[ROWS - PLANES : ROWS, :]
+        low, high = n_buf[0:PLANES, :], n_buf[ROWS - PLANES : ROWS, :]
+        odd = parity("gx") == 1
+        faces_out[0][0] = jnp.where(odd, low, high)
+        faces_out[1][0] = jnp.where(odd, high, low)
         stiff_out[0][...] = s_buf[0:PLANES, :]
         stiff_out[1][...] = s_buf[ROWS - PLANES : ROWS, :]
     for copy in out_copies:
@@ -315,8 +339,12 @@
         for copy in pair:
             copy.start()
         loads.append(pair)
-    for side, flux in enumerate(edge_fluxes(own, far, own2, far2)):
+    near_b, away_b = by_side([m[1] for m in own]), by_side([m[1] for m in far])
+    near_f, away_f = by_side([m[0] for m in own2]), by_side([m[0] for m in far2])
+    for side, flux in enumerate(edge_fluxes(near_b, away_b, near_f, away_f)):
         terms[side] = (0.5 * stiff[side][...]) * flux
+    factors[0, 0] = near_f[1]
+    factors[1, 0] = near_f[3]
     for start in range(0, 512, 128):
         tile = lax.broadcasted_iota(jnp.int32, (128, 1024), 0) + start
         onehot[start : start + 128, :] = jnp.where(tile == ids[...], 1.0, 0.0).astype(jnp.bfloat16)
@@ -394,7 +422,7 @@
         taper = 1.0 - jnp.exp((a * a + b * b + z * z) * SCALE)
         newest = third[ROWS - PLANES : ROWS, :] if way == 0 else factors[1, 1]
         factors[way, 1] = taper * newest
-        factors[way, 0] = taper * own2[1 + 2 * way][0]
+        factors[way, 0] = taper * factors[way, 0]
     for copy in copies:
         copy.wait()
 
@@ -546,7 +574,7 @@
 
     received, third = lax.optimization_barrier((received, third))
     rim_x, rim_y, corner = rim_rows(received, ids)
-    rims = [rotate(rim_x, "gx", -1), rotate(rim_y, "gy", -1), diagonal(corner)]
+    rims = [down(rim_x, "gx"), down(rim_y, "gy"), diagonal(corner)]
     edges = [*own, *far, *own2, *far2, *stiff_faces]
     image, last_current, *strips = picture(source_cell, received, ids, second, third, edges)
     image = add_rims(rims, strips, image)
@@ -555,15 +583,21 @@
 
 
 def exchange(own):
-    x_lo, x_hi, y_lo, y_hi = own
-    return [rotate(x_hi, "gx", 1), rotate(x_lo, "gx", -1), rotate(y_hi, "gy", 1), rotate(y_lo, "gy", -1)]
+    return [
+        swap(own[0], "gx", 0),
+        swap(own[1], "gx", 1),
+        swap(own[2], "gy", 0),
+        swap(own[3], "gy", 1),
+    ]
+
+
+def down(block, axis):
+    return lax.ppermute(block, axis, [(i, i - 1) for i in range(1, lax.axis_size(axis))])
 
 
 def diagonal(block):
     nx, ny = lax.axis_size("gx"), lax.axis_size("gy")
-    route = [
-        (i * ny + j, ((i - 1) % nx) * ny + (j - 1) % ny) for i in range(nx) for j in range(ny)
-    ]
+    route = [(i * ny + j, (i - 1) * ny + j - 1) for i in range(1, nx) for j in range(1, ny)]
     return lax.ppermute(block, ("gx", "gy"), route)
 
 

time: 70.7 us -> 74.6 us (1.055)
  starting transfers between devices: 34.5 us -> 42.1 us
  waiting for transfers between devices: 9.18 us -> 5.41 us
    ppermute x10, starting transfers between devices: 22.4 us -> 30.8 us  [the longest x8 23.4 us: swap(): return lax.ppermute(block, axis, route)]
    all_to_all x1, starting transfers between devices: 12.2 us -> 8.21 us  [per_device(): lax.all_to_all(tiles[0, 0], ('shot', 'gx'), split_axis=0, concat_axis=0,...]
    ppermute x1, starting transfers between devices: 0.01 us -> 3.1 us  [diagonal(): return lax.ppermute(block, ('gx', 'gy'), route)]
    all_to_all x1, waiting for transfers between devices: 6.37 us -> 3.68 us  [per_device(): lax.all_to_all(tiles[0, 0], ('shot', 'gx'), split_axis=0, concat_axis=0,...]
    ppermute x1, waiting for transfers between devices: 2.78 us -> 1.7 us  [diagonal(): return lax.ppermute(block, ('gx', 'gy'), route)]
  transfers between devices with their start and end apart: 12 -> 12, of which waited for: 2 -> 2; matrix products, arithmetic and copies ran while one was open for 0% -> 0% of each run, Pallas kernels for 31% -> 29%
where the time goes in v9:
time: 74.6 us; the launch traced here: 74.1 us
  starting transfers between devices  42.1 us (56%)
  Pallas kernels  25.4 us (34%)
  waiting for transfers between devices  5.41 us (7%)
  between operations  0.91 us (1%)
    ppermute x8, starting transfers between devices, swap(): return lax.ppermute(block, axis, route)  23.4 us
    pallas_call x2, Pallas kernels, inner(): pl.pallas_call(lambda *refs: inner_kernel(*refs, step=step), in_specs=[AN...  12.6 us
    all_to_all x1, starting transfers between devices, per_device(): lax.all_to_all(tiles[0, 0], ('shot', 'gx'), split_axis=0, concat_axis=0,...  8.21 us
    ppermute x2, starting transfers between devices, down(): lax.ppermute(block, axis, [(i, i - 1) for i in range(1, lax.axis_size(axi...  7.44 us
    pallas_call x1, Pallas kernels, picture(): pl.pallas_call(picture_kernel, in_specs=[SMEM, ANY, VMEM, ANY, ANY] + [VM...  6.08 us
    all_to_all x1, waiting for transfers between devices, per_device(): lax.all_to_all(tiles[0, 0], ('shot', 'gx'), split_axis=0, concat_axis=0,...  3.68 us
    ppermute x1, starting transfers between devices, diagonal(): return lax.ppermute(block, ('gx', 'gy'), route)  3.1 us
    pallas_call x1, Pallas kernels, rim_rows(): pl.pallas_call(rim_rows_kernel, in_specs=[ANY, VMEM], out_specs=[VMEM] *...  2.21 us
  transfers between devices with their start and end apart: 12, of which 2 were waited for; matrix products, arithmetic and copies ran while one was open for 0% of the time, Pallas kernels for 29%

profile of v9, /device:TPU:39, one launch (start us, length us, event | category | flops | bytes accessed | tf_op | source)
XLA Modules:
  0.0 74.1 jit_solution(15645687593196386929)
XLA Ops:
  0.6 1.7 %faces.1 = (f32[2,32,512]{2,1,0:T(8,128)S(1)}, f32[2,32,512]{2,1,0:T(8,128)S(1)}, f32[2,32,512]{2,1,0:T(8,128)S(1)}, f32[2,32,512]{2,1,0:T(8,128)S(1)}) custom-call(f32[32,32,512]{2,1,0:T(8,128)} %bitcast.19, f32[32,32,512]{2,1,0:T(8,128)} %bitcast.20, f32[32,32,512]{2,1,0:T(8,128)} %bitcast.21, f32[32,32,512]{2,1,0:T(8,128)} %bitcast.22, ...), custom_call_target="tpu_custom_call" | custom-call | bytes 3145728 | tf_op jit(solution)/shard_map/faces/pallas_call | solution.py:70
  2.4 7.8 %collective-permute-start.1 = (f32[2,32,512]{2,1,0:T(8,128)S(1)}, f32[2,32,512]{2,1,0:T(8,128)S(1)}, u32[]{:S(2)}, u32[]{:S(2)}) collective-permute-start(f32[2,32,512]{2,1,0:T(8,128)S(1)} %get-tuple-element.35.refs_6_.rest_1_), channel_id=1, source_target_pairs={{8,16},{16,8},{24,32},{32,24},{40,48},{48,40},{9,17},{17,9},{25,33... | collective-permute-start | bytes 393224 | tf_op jit(solution)/shard_map/ppermute | solution.py:27
  10.2 0.1 collective-permute-start
  10.3 1.0 %collective-permute-start.2 = (f32[2,32,512]{2,1,0:T(8,128)S(1)}, f32[2,32,512]{2,1,0:T(8,128)S(1)}, u32[]{:S(2)}, u32[]{:S(2)}) collective-permute-start(f32[2,32,512]{2,1,0:T(8,128)S(1)} %get-tuple-element.36.refs_7_.rest_2_), channel_id=1, source_target_pairs={{0,1},{1,0},{2,3},{3,2},{4,5},{5,4},{6,7},{7,6},{8,9},{9,8},{10,11... | collective-permute-start | bytes 393224 | tf_op jit(solution)/shard_map/ppermute | solution.py:27
  11.4 2.5 %collective-permute-start.3 = (f32[2,32,512]{2,1,0:T(8,128)S(1)}, f32[2,32,512]{2,1,0:T(8,128)S(1)}, u32[]{:S(2)}, u32[]{:S(2)}) collective-permute-start(f32[2,32,512]{2,1,0:T(8,128)S(1)} %get-tuple-element.37.refs_8_.rest_3_), channel_id=1, source_target_pairs={{1,2},{2,1},{3,4},{4,3},{5,6},{6,5},{9,10},{10,9},{11,12},{12,11},... | collective-permute-start | bytes 393224 | tf_op jit(solution)/shard_map/ppermute | solution.py:27
  13.9 8.2 %all-to-all-start = ((f32[32,32,256]{2,1,0:T(8,128)}), f32[32,32,256]{2,1,0:T(8,128)}, u32[]{:S(2)}, u32[]{:S(2)}) async-start(f32[32,32,256]{2,1,0:T(8,128)} %bitcast.1), calls=%async_computation | async-start | bytes 2097152 | tf_op jit(solution)/shard_map/all_to_all | solution.py:563
  22.2 0.8 %sources.1.refs_4_ = f32[2,1024,128]{2,1,0:T(8,128)S(1)} custom-call(s32[3,1024]{1,0:T(4,128)S(1)} %bitcast.17, f32[2,1024]{1,0:T(2,128)S(1)} %bitcast.18), custom_call_target="tpu_custom_call" | custom-call | flops 1 | bytes 1 | tf_op jit(solution)/shard_map/sources/pallas_call | solution.py:112
  23.1 6.3 %inner0.1 = (f32[1024,512]{1,0:T(8,128)}, f32[1,32,512]{2,1,0:T(8,128)S(1)}, f32[1,32,512]{2,1,0:T(8,128)S(1)}, f32[1,32,512]{2,1,0:T(8,128)S(1)}, f32[1,32,512]...) custom-call(f32[1024,512]{1,0:T(8,128)} %bitcast.23, ...), custom_call_target="tpu_custom_call" | custom-call | flops 1099511627776 | bytes 1 | tf_op jit(solution)/shard_map/inner0/pallas_call | solution.py:263
  29.4 3.5 %collective-permute-start.10 = (f32[1,32,512]{2,1,0:T(8,128)S(1)}, f32[1,32,512]{2,1,0:T(8,128)S(1)}, u32[]{:S(2)}, u32[]{:S(2)}) collective-permute-start(f32[1,32,512]{2,1,0:T(8,128)S(1)} %get-tuple-element.51.rest_11_), channel_id=1, source_target_pairs={{1,2},{2,1},{3,4},{4,3},{5,6},{6,5},{9,10},{10,9},{11,12},{12,11},... | collective-permute-start | bytes 196616 | tf_op jit(solution)/shard_map/ppermute | solution.py:27
  32.9 0.7 collective-permute-start.7
  33.6 7.6 %collective-permute-start.8 = (f32[1,32,512]{2,1,0:T(8,128)S(1)}, f32[1,32,512]{2,1,0:T(8,128)S(1)}, u32[]{:S(2)}, u32[]{:S(2)}) collective-permute-start(f32[1,32,512]{2,1,0:T(8,128)S(1)} %get-tuple-element.49.rest_9_), channel_id=1, source_target_pairs={{8,16},{16,8},{24,32},{32,24},{40,48},{48,40},{9,17},{17,9},{25,33... | collective-permute-start | bytes 196616 | tf_op jit(solution)/shard_map/ppermute | solution.py:27
  41.2 0.1 collective-permute-start.9
  41.3 0.1 iota_compare_fusion
  41.4 0.1 lt.23
  41.4 0.1 squeeze.19
  41.5 6.3 %inner1.1.second_hbm = f32[1024,512]{1,0:T(8,128)} custom-call(f32[1024,512]{1,0:T(8,128)} %get-tuple-element.40.refs_0_.first_hbm, f32[1024,512]{1,0:T(8,128)} %bitcast.24, f32[1024,512]{1,0:T(8,128)} %bitcast.26, f32[1024,512]{1,0:T(8,128)} %bitcast.31, f32[2,1024,128]{2,1,0:T(8,128)S(1)} %sources.1.refs_4_), custom_call_target="tpu_custom_call" | custom-call | flops 17179869184 | bytes 1 | tf_op jit(solution)/shard_map/inner1/pallas_call | solution.py:263
  47.9 3.7 %all-to-all-done = f32[32,32,256]{2,1,0:T(8,128)} async-done(((f32[32,32,256]{2,1,0:T(8,128)}), f32[32,32,256]{2,1,0:T(8,128)}, u32[]{:S(2)}, u32[]{:S(2)}) %all-to-all-start) | async-done | bytes 1048608 | tf_op jit(solution)/shard_map/all_to_all | solution.py:563
  51.5 2.2 %rim_rows.1 = (f32[2,16,256]{2,1,0:T(8,128)}, f32[2,16,256]{2,1,0:T(8,128)}, f32[2,8,256]{2,1,0:T(8,128)}) custom-call(f32[1024,256]{1,0:T(8,128)} %bitcast.2.received, s32[1,1024]{1,0:T(1,128)S(1)} %broadcast_select_fusion.ids), custom_call_target="tpu_custom_call" | custom-call | flops 1073741824 | bytes 3145728 | tf_op jit(solution)/shard_map/rim_rows/pallas_call | solution.py:308
  53.8 4.7 %collective-permute-start.4 = (f32[2,16,256]{2,1,0:T(8,128)}, f32[2,16,256]{2,1,0:T(8,128)}, u32[]{:S(2)}, u32[]{:S(2)}) collective-permute-start(f32[2,16,256]{2,1,0:T(8,128)} %get-tuple-element.44), channel_id=1, source_target_pairs={{8,0},{16,8},{24,16},{32,24},{40,32},{48,40},{56,48},{9,1},{17,9},... | collective-permute-start | bytes 98312 | tf_op jit(solution)/shard_map/ppermute | solution.py:595
  58.5 2.8 %collective-permute-start.5 = (f32[2,16,256]{2,1,0:T(8,128)}, f32[2,16,256]{2,1,0:T(8,128)}, u32[]{:S(2)}, u32[]{:S(2)}) collective-permute-start(f32[2,16,256]{2,1,0:T(8,128)} %get-tuple-element.45), channel_id=1, source_target_pairs={{1,0},{2,1},{3,2},{4,3},{5,4},{6,5},{7,6},{9,8},{10,9},{11,10},{12... | collective-permute-start | bytes 98312 | tf_op jit(solution)/shard_map/ppermute | solution.py:595
  61.2 3.1 %collective-permute-start.6 = (f32[2,8,256]{2,1,0:T(8,128)}, f32[2,8,256]{2,1,0:T(8,128)}, u32[]{:S(2)}, u32[]{:S(2)}) collective-permute-start(f32[2,8,256]{2,1,0:T(8,128)} %get-tuple-element.46), channel_id=1, source_target_pairs={{9,0},{10,1},{11,2},{12,3},{13,4},{14,5},{15,6},{17,8},{18,9},{19,... | collective-permute-start | bytes 49160 | tf_op jit(solution)/shard_map/ppermute | solution.py:601
  64.4 6.1 %picture.1 = (f32[32,32,512]{2,1,0:T(8,128)}, f32[1024,512]{1,0:T(8,128)}, f32[32,8,512]{2,1,0:T(8,128)S(1)}, f32[24,512]{1,0:T(8,128)S(1)}, f32[2,2,32,512]{3,2,1,0:T(8,128)S(1)}) custom-call(s32[1,3]{1,0:T(1,128)S(1)} %copy-done.1, f32[1024,256]{1,0:T(8,128)} %bitcast.2.received, s32[1,1024]{1,0:T(1,128)S(1)} %broadcast_select_fusion.ids, ...), custom_call_target="tpu_custom_call" | custom-call | flops 1099511627776 | bytes 8388608 | tf_op jit(solution)/shard_map/picture/pallas_call | solution.py:432
  70.5 1.7 %collective-permute-done.6.corner_hbm = f32[2,8,256]{2,1,0:T(8,128)} collective-permute-done((f32[2,8,256]{2,1,0:T(8,128)}, f32[2,8,256]{2,1,0:T(8,128)}, u32[]{:S(2)}, u32[]{:S(2)}) %collective-permute-start.6) | collective-permute-done | bytes 16416 | tf_op jit(solution)/shard_map/ppermute | solution.py:601
  72.2 1.9 %add_rims.1 = f32[32,32,512]{2,1,0:T(8,128)} custom-call(f32[2,16,256]{2,1,0:T(8,128)} %collective-permute-done.4.rim_x_hbm, f32[2,16,256]{2,1,0:T(8,128)} %collective-permute-done.5.rim_y_hbm, f32[2,8,256]{2,1,0:T(8,128)} %collective-permute-done.6.corner_hbm, f32[32,8,512]{2,1,0:T(8,128)S(1)} %get-tuple-element.56.strip, ...), custom_call_target="tpu_custom_call", output_to_operand_aliasing={{}: (6, {})} | custom-call | flops 1048576 | bytes 2097152 | tf_op jit(solution)/shard_map/add_rims/pallas_call | solution.py:519
  (22 shorter events, 0.1 us)
Async XLA Ops:
  2.4 19.8 %copy-start.3 = (s32[1,3,1024]{2,0,1:T(1,128)S(1)}, s32[1,3,1024]{2,0,1:T(1,128)}, u32[]{:S(2)}) copy-start(s32[1,3,1024]{2,0,1:T(1,128)} %param.17) | copy-start | bytes 36868
  2.4 19.8 %copy-start = (f32[1,2,1024]{2,1,0:T(2,128)S(1)}, f32[1,2,1024]{2,1,0:T(2,128)}, u32[]{:S(2)}) copy-start(f32[1,2,1024]{2,1,0:T(2,128)} %param.18) | copy-start | bytes 24580
  2.4 20.6 %collective-permute-start.1 = (f32[2,32,512]{2,1,0:T(8,128)S(1)}, f32[2,32,512]{2,1,0:T(8,128)S(1)}, u32[]{:S(2)}, u32[]{:S(2)}) collective-permute-start(f32[2,32,512]{2,1,0:T(8,128)S(1)} %get-tuple-element.35.refs_6_.rest_1_), channel_id=1, source_target_pairs={{8,16},{16,8},{24,32},{32,24},{40,48},{48,40},{9,17},{17,9},{25,33... | collective-permute-start | bytes 393224 | tf_op jit(solution)/shard_map/ppermute | solution.py:27
  10.2 12.8 %collective-permute-start = (f32[2,32,512]{2,1,0:T(8,128)S(1)}, f32[2,32,512]{2,1,0:T(8,128)S(1)}, u32[]{:S(2)}, u32[]{:S(2)}) collective-permute-start(f32[2,32,512]{2,1,0:T(8,128)S(1)} %get-tuple-element.34.refs_5_.rest_0_), channel_id=1, source_target_pairs={{0,8},{8,0},{16,24},{24,16},{32,40},{40,32},{48,56},{56,48},{1,9},... | collective-permute-start | bytes 393224 | tf_op jit(solution)/shard_map/ppermute | solution.py:27
  10.3 12.7 %collective-permute-start.2 = (f32[2,32,512]{2,1,0:T(8,128)S(1)}, f32[2,32,512]{2,1,0:T(8,128)S(1)}, u32[]{:S(2)}, u32[]{:S(2)}) collective-permute-start(f32[2,32,512]{2,1,0:T(8,128)S(1)} %get-tuple-element.36.refs_7_.rest_2_), channel_id=1, source_target_pairs={{0,1},{1,0},{2,3},{3,2},{4,5},{5,4},{6,7},{7,6},{8,9},{9,8},{10,11... | collective-permute-start | bytes 393224 | tf_op jit(solution)/shard_map/ppermute | solution.py:27
  11.4 11.7 %collective-permute-start.3 = (f32[2,32,512]{2,1,0:T(8,128)S(1)}, f32[2,32,512]{2,1,0:T(8,128)S(1)}, u32[]{:S(2)}, u32[]{:S(2)}) collective-permute-start(f32[2,32,512]{2,1,0:T(8,128)S(1)} %get-tuple-element.37.refs_8_.rest_3_), channel_id=1, source_target_pairs={{1,2},{2,1},{3,4},{4,3},{5,6},{6,5},{9,10},{10,9},{11,12},{12,11},... | collective-permute-start | bytes 393224 | tf_op jit(solution)/shard_map/ppermute | solution.py:27
  13.9 37.6 %all-to-all-start = ((f32[32,32,256]{2,1,0:T(8,128)}), f32[32,32,256]{2,1,0:T(8,128)}, u32[]{:S(2)}, u32[]{:S(2)}) async-start(f32[32,32,256]{2,1,0:T(8,128)} %bitcast.1), calls=%async_computation | async-start | bytes 2097152 | tf_op jit(solution)/shard_map/all_to_all | solution.py:563
  23.0 18.2 %copy-start.4 = (s32[1,1,32]{2,1,0:T(1,128)S(1)}, s32[1,1,32]{2,1,0:T(1,128)}, u32[]{:S(2)}) copy-start(s32[1,1,32]{2,1,0:T(1,128)} %param.16) | copy-start | bytes 388
  23.1 18.4 %copy-start.2 = (s32[1,1,32,32]{3,2,1,0:T(8,128)S(1)}, s32[1,1,32,32]{3,2,1,0:T(8,128)}, u32[]{:S(2)}) copy-start(s32[1,1,32,32]{3,2,1,0:T(8,128)} %param.15) | copy-start | bytes 12292
  29.4 29.1 %collective-permute-start.10 = (f32[1,32,512]{2,1,0:T(8,128)S(1)}, f32[1,32,512]{2,1,0:T(8,128)S(1)}, u32[]{:S(2)}, u32[]{:S(2)}) collective-permute-start(f32[1,32,512]{2,1,0:T(8,128)S(1)} %get-tuple-element.51.rest_11_), channel_id=1, source_target_pairs={{1,2},{2,1},{3,4},{4,3},{5,6},{6,5},{9,10},{10,9},{11,12},{12,11},... | collective-permute-start | bytes 196616 | tf_op jit(solution)/shard_map/ppermute | solution.py:27
  32.9 28.3 %collective-permute-start.7 = (f32[1,32,512]{2,1,0:T(8,128)S(1)}, f32[1,32,512]{2,1,0:T(8,128)S(1)}, u32[]{:S(2)}, u32[]{:S(2)}) collective-permute-start(f32[1,32,512]{2,1,0:T(8,128)S(1)} %get-tuple-element.48.rest_8_), channel_id=1, source_target_pairs={{0,8},{8,0},{16,24},{24,16},{32,40},{40,32},{48,56},{56,48},{1,9},... | collective-permute-start | bytes 196616 | tf_op jit(solution)/shard_map/ppermute | solution.py:27
  33.6 30.8 %collective-permute-start.8 = (f32[1,32,512]{2,1,0:T(8,128)S(1)}, f32[1,32,512]{2,1,0:T(8,128)S(1)}, u32[]{:S(2)}, u32[]{:S(2)}) collective-permute-start(f32[1,32,512]{2,1,0:T(8,128)S(1)} %get-tuple-element.49.rest_9_), channel_id=1, source_target_pairs={{8,16},{16,8},{24,32},{32,24},{40,48},{48,40},{9,17},{17,9},{25,33... | collective-permute-start | bytes 196616 | tf_op jit(solution)/shard_map/ppermute | solution.py:27
  41.2 23.2 %collective-permute-start.9 = (f32[1,32,512]{2,1,0:T(8,128)S(1)}, f32[1,32,512]{2,1,0:T(8,128)S(1)}, u32[]{:S(2)}, u32[]{:S(2)}) collective-permute-start(f32[1,32,512]{2,1,0:T(8,128)S(1)} %get-tuple-element.50.rest_10_), channel_id=1, source_target_pairs={{0,1},{1,0},{2,3},{3,2},{4,5},{5,4},{6,7},{7,6},{8,9},{9,8},{10,11... | collective-permute-start | bytes 196616 | tf_op jit(solution)/shard_map/ppermute | solution.py:27
  47.9 16.5 %copy-start.1 = (s32[1,3]{1,0:T(1,128)S(1)}, s32[1,3]{1,0:T(1,128)}, u32[]{:S(2)}) copy-start(s32[1,3]{1,0:T(1,128)} %source.1) | copy-start | bytes 40
  53.8 18.4 %collective-permute-start.4 = (f32[2,16,256]{2,1,0:T(8,128)}, f32[2,16,256]{2,1,0:T(8,128)}, u32[]{:S(2)}, u32[]{:S(2)}) collective-permute-start(f32[2,16,256]{2,1,0:T(8,128)} %get-tuple-element.44), channel_id=1, source_target_pairs={{8,0},{16,8},{24,16},{32,24},{40,32},{48,40},{56,48},{9,1},{17,9},... | collective-permute-start | bytes 98312 | tf_op jit(solution)/shard_map/ppermute | solution.py:595
  58.5 13.7 %collective-permute-start.5 = (f32[2,16,256]{2,1,0:T(8,128)}, f32[2,16,256]{2,1,0:T(8,128)}, u32[]{:S(2)}, u32[]{:S(2)}) collective-permute-start(f32[2,16,256]{2,1,0:T(8,128)} %get-tuple-element.45), channel_id=1, source_target_pairs={{1,0},{2,1},{3,2},{4,3},{5,4},{6,5},{7,6},{9,8},{10,9},{11,10},{12... | collective-permute-start | bytes 98312 | tf_op jit(solution)/shard_map/ppermute | solution.py:595
  61.2 10.9 %collective-permute-start.6 = (f32[2,8,256]{2,1,0:T(8,128)}, f32[2,8,256]{2,1,0:T(8,128)}, u32[]{:S(2)}, u32[]{:S(2)}) collective-permute-start(f32[2,8,256]{2,1,0:T(8,128)} %get-tuple-element.46), channel_id=1, source_target_pairs={{9,0},{10,1},{11,2},{12,3},{13,4},{14,5},{15,6},{17,8},{18,9},{19,... | collective-permute-start | bytes 49160 | tf_op jit(solution)/shard_map/ppermute | solution.py:601

commit v10 on v9

--- a/solution.py
+++ b/solution.py
@@ -592,12 +592,15 @@
 
 
 def down(block, axis):
-    return lax.ppermute(block, axis, [(i, i - 1) for i in range(1, lax.axis_size(axis))])
+    count = lax.axis_size(axis)
+    return lax.ppermute(block, axis, [(i, (i - 1) % count) for i in range(count)])
 
 
 def diagonal(block):
     nx, ny = lax.axis_size("gx"), lax.axis_size("gy")
-    route = [(i * ny + j, (i - 1) * ny + j - 1) for i in range(1, nx) for j in range(1, ny)]
+    route = [
+        (i * ny + j, ((i - 1) % nx) * ny + (j - 1) % ny) for i in range(nx) for j in range(ny)
+    ]
     return lax.ppermute(block, ("gx", "gy"), route)
 
 

time: 74.6 us -> 69.1 us (0.926)
  starting transfers between devices: 42.1 us -> 36.7 us
    ppermute x2, starting transfers between devices: 7.44 us -> 3.69 us  [down(): lax.ppermute(block, axis, [(i, (i - 1) % count) for i in range(count)])]
    ppermute x1, starting transfers between devices: 3.1 us -> 1.45 us  [diagonal(): return lax.ppermute(block, ('gx', 'gy'), route)]
  transfers between devices with their start and end apart: 12 -> 12, of which waited for: 2 -> 2; matrix products, arithmetic and copies ran while one was open for 0% -> 0% of each run, Pallas kernels for 29% -> 32%
where the time goes in v10:
time: 69.1 us; the launch traced here: 68.6 us
  starting transfers between devices  36.7 us (53%)
  Pallas kernels  25.4 us (37%)
  waiting for transfers between devices  5.19 us (8%)
  between operations  1.01 us (1%)
    ppermute x8, starting transfers between devices, swap(): return lax.ppermute(block, axis, route)  23.4 us
    pallas_call x2, Pallas kernels, inner(): pl.pallas_call(lambda *refs: inner_kernel(*refs, step=step), in_specs=[AN...  12.6 us
    all_to_all x1, starting transfers between devices, per_device(): lax.all_to_all(tiles[0, 0], ('shot', 'gx'), split_axis=0, concat_axis=0,...  8.21 us
    pallas_call x1, Pallas kernels, picture(): pl.pallas_call(picture_kernel, in_specs=[SMEM, ANY, VMEM, ANY, ANY] + [VM...  6.08 us
    ppermute x2, starting transfers between devices, down(): lax.ppermute(block, axis, [(i, (i - 1) % count) for i in range(count)])  3.69 us
    all_to_all x1, waiting for transfers between devices, per_device(): lax.all_to_all(tiles[0, 0], ('shot', 'gx'), split_axis=0, concat_axis=0,...  3.68 us
    pallas_call x1, Pallas kernels, rim_rows(): pl.pallas_call(rim_rows_kernel, in_specs=[ANY, VMEM], out_specs=[VMEM] *...  2.21 us
    pallas_call x1, Pallas kernels, add_rims(): pl.pallas_call(rims_kernel, in_specs=[ANY] * 3 + [VMEM] * 3 + [ANY], out_...  1.94 us
  transfers between devices with their start and end apart: 12, of which 2 were waited for; matrix products, arithmetic and copies ran while one was open for 0% of the time, Pallas kernels for 32%

profile of v10, /device:TPU:39, one launch (start us, length us, event | category | flops | bytes accessed | tf_op | source)
XLA Modules:
  0.0 68.6 jit_solution(3073784804435776561)
XLA Ops:
  0.6 1.7 %faces.1 = (f32[2,32,512]{2,1,0:T(8,128)S(1)}, f32[2,32,512]{2,1,0:T(8,128)S(1)}, f32[2,32,512]{2,1,0:T(8,128)S(1)}, f32[2,32,512]{2,1,0:T(8,128)S(1)}) custom-call(f32[32,32,512]{2,1,0:T(8,128)} %bitcast.19, f32[32,32,512]{2,1,0:T(8,128)} %bitcast.20, f32[32,32,512]{2,1,0:T(8,128)} %bitcast.21, f32[32,32,512]{2,1,0:T(8,128)} %bitcast.22, ...), custom_call_target="tpu_custom_call" | custom-call | bytes 3145728 | tf_op jit(solution)/shard_map/faces/pallas_call | solution.py:70
  2.4 7.8 %collective-permute-start.1 = (f32[2,32,512]{2,1,0:T(8,128)S(1)}, f32[2,32,512]{2,1,0:T(8,128)S(1)}, u32[]{:S(2)}, u32[]{:S(2)}) collective-permute-start(f32[2,32,512]{2,1,0:T(8,128)S(1)} %get-tuple-element.35.refs_6_.rest_1_), channel_id=1, source_target_pairs={{8,16},{16,8},{24,32},{32,24},{40,48},{48,40},{9,17},{17,9},{25,33... | collective-permute-start | bytes 393224 | tf_op jit(solution)/shard_map/ppermute | solution.py:27
  10.2 0.1 collective-permute-start
  10.3 1.0 %collective-permute-start.2 = (f32[2,32,512]{2,1,0:T(8,128)S(1)}, f32[2,32,512]{2,1,0:T(8,128)S(1)}, u32[]{:S(2)}, u32[]{:S(2)}) collective-permute-start(f32[2,32,512]{2,1,0:T(8,128)S(1)} %get-tuple-element.36.refs_7_.rest_2_), channel_id=1, source_target_pairs={{0,1},{1,0},{2,3},{3,2},{4,5},{5,4},{6,7},{7,6},{8,9},{9,8},{10,11... | collective-permute-start | bytes 393224 | tf_op jit(solution)/shard_map/ppermute | solution.py:27
  11.4 2.5 %collective-permute-start.3 = (f32[2,32,512]{2,1,0:T(8,128)S(1)}, f32[2,32,512]{2,1,0:T(8,128)S(1)}, u32[]{:S(2)}, u32[]{:S(2)}) collective-permute-start(f32[2,32,512]{2,1,0:T(8,128)S(1)} %get-tuple-element.37.refs_8_.rest_3_), channel_id=1, source_target_pairs={{1,2},{2,1},{3,4},{4,3},{5,6},{6,5},{9,10},{10,9},{11,12},{12,11},... | collective-permute-start | bytes 393224 | tf_op jit(solution)/shard_map/ppermute | solution.py:27
  13.9 8.2 %all-to-all-start = ((f32[32,32,256]{2,1,0:T(8,128)}), f32[32,32,256]{2,1,0:T(8,128)}, u32[]{:S(2)}, u32[]{:S(2)}) async-start(f32[32,32,256]{2,1,0:T(8,128)} %bitcast.1), calls=%async_computation | async-start | bytes 2097152 | tf_op jit(solution)/shard_map/all_to_all | solution.py:563
  22.2 0.8 %sources.1.refs_4_ = f32[2,1024,128]{2,1,0:T(8,128)S(1)} custom-call(s32[3,1024]{1,0:T(4,128)S(1)} %bitcast.17, f32[2,1024]{1,0:T(2,128)S(1)} %bitcast.18), custom_call_target="tpu_custom_call" | custom-call | flops 1 | bytes 1 | tf_op jit(solution)/shard_map/sources/pallas_call | solution.py:112
  23.1 6.3 %inner0.1 = (f32[1024,512]{1,0:T(8,128)}, f32[1,32,512]{2,1,0:T(8,128)S(1)}, f32[1,32,512]{2,1,0:T(8,128)S(1)}, f32[1,32,512]{2,1,0:T(8,128)S(1)}, f32[1,32,512]...) custom-call(f32[1024,512]{1,0:T(8,128)} %bitcast.23, ...), custom_call_target="tpu_custom_call" | custom-call | flops 1099511627776 | bytes 1 | tf_op jit(solution)/shard_map/inner0/pallas_call | solution.py:263
  29.4 3.5 %collective-permute-start.10 = (f32[1,32,512]{2,1,0:T(8,128)S(1)}, f32[1,32,512]{2,1,0:T(8,128)S(1)}, u32[]{:S(2)}, u32[]{:S(2)}) collective-permute-start(f32[1,32,512]{2,1,0:T(8,128)S(1)} %get-tuple-element.51.rest_11_), channel_id=1, source_target_pairs={{1,2},{2,1},{3,4},{4,3},{5,6},{6,5},{9,10},{10,9},{11,12},{12,11},... | collective-permute-start | bytes 196616 | tf_op jit(solution)/shard_map/ppermute | solution.py:27
  32.9 0.7 collective-permute-start.7
  33.6 7.6 %collective-permute-start.8 = (f32[1,32,512]{2,1,0:T(8,128)S(1)}, f32[1,32,512]{2,1,0:T(8,128)S(1)}, u32[]{:S(2)}, u32[]{:S(2)}) collective-permute-start(f32[1,32,512]{2,1,0:T(8,128)S(1)} %get-tuple-element.49.rest_9_), channel_id=1, source_target_pairs={{8,16},{16,8},{24,32},{32,24},{40,48},{48,40},{9,17},{17,9},{25,33... | collective-permute-start | bytes 196616 | tf_op jit(solution)/shard_map/ppermute | solution.py:27
  41.2 0.1 collective-permute-start.9
  41.3 0.1 iota_compare_fusion
  41.4 0.1 lt.23
  41.4 0.1 squeeze.19
  41.5 6.3 %inner1.1.second_hbm = f32[1024,512]{1,0:T(8,128)} custom-call(f32[1024,512]{1,0:T(8,128)} %get-tuple-element.40.refs_0_.first_hbm, f32[1024,512]{1,0:T(8,128)} %bitcast.24, f32[1024,512]{1,0:T(8,128)} %bitcast.26, f32[1024,512]{1,0:T(8,128)} %bitcast.31, f32[2,1024,128]{2,1,0:T(8,128)S(1)} %sources.1.refs_4_), custom_call_target="tpu_custom_call" | custom-call | flops 17179869184 | bytes 1 | tf_op jit(solution)/shard_map/inner1/pallas_call | solution.py:263
  47.9 3.7 %all-to-all-done = f32[32,32,256]{2,1,0:T(8,128)} async-done(((f32[32,32,256]{2,1,0:T(8,128)}), f32[32,32,256]{2,1,0:T(8,128)}, u32[]{:S(2)}, u32[]{:S(2)}) %all-to-all-start) | async-done | bytes 1048608 | tf_op jit(solution)/shard_map/all_to_all | solution.py:563
  51.5 2.2 %rim_rows.1 = (f32[2,16,256]{2,1,0:T(8,128)}, f32[2,16,256]{2,1,0:T(8,128)}, f32[2,8,256]{2,1,0:T(8,128)}) custom-call(f32[1024,256]{1,0:T(8,128)} %bitcast.2.received, s32[1,1024]{1,0:T(1,128)S(1)} %broadcast_select_fusion.ids), custom_call_target="tpu_custom_call" | custom-call | flops 1073741824 | bytes 3145728 | tf_op jit(solution)/shard_map/rim_rows/pallas_call | solution.py:308
  53.8 2.8 %collective-permute-start.4 = (f32[2,16,256]{2,1,0:T(8,128)}, f32[2,16,256]{2,1,0:T(8,128)}, u32[]{:S(2)}, u32[]{:S(2)}) collective-permute-start(f32[2,16,256]{2,1,0:T(8,128)} %get-tuple-element.44), channel_id=1, source_target_pairs={{0,56},{8,0},{16,8},{24,16},{32,24},{40,32},{48,40},{56,48},{1,57}... | collective-permute-start | bytes 98312 | tf_op jit(solution)/shard_map/ppermute | solution.py:596
  56.6 0.9 %collective-permute-start.5 = (f32[2,16,256]{2,1,0:T(8,128)}, f32[2,16,256]{2,1,0:T(8,128)}, u32[]{:S(2)}, u32[]{:S(2)}) collective-permute-start(f32[2,16,256]{2,1,0:T(8,128)} %get-tuple-element.45), channel_id=1, source_target_pairs={{0,7},{1,0},{2,1},{3,2},{4,3},{5,4},{6,5},{7,6},{8,15},{9,8},{10,9... | collective-permute-start | bytes 98312 | tf_op jit(solution)/shard_map/ppermute | solution.py:596
  57.5 1.4 %collective-permute-start.6 = (f32[2,8,256]{2,1,0:T(8,128)}, f32[2,8,256]{2,1,0:T(8,128)}, u32[]{:S(2)}, u32[]{:S(2)}) collective-permute-start(f32[2,8,256]{2,1,0:T(8,128)} %get-tuple-element.46), channel_id=1, source_target_pairs={{0,63},{1,56},{2,57},{3,58},{4,59},{5,60},{6,61},{7,62},{8,7},{9,0... | collective-permute-start | bytes 49160 | tf_op jit(solution)/shard_map/ppermute | solution.py:604
  58.9 6.1 %picture.1 = (f32[32,32,512]{2,1,0:T(8,128)}, f32[1024,512]{1,0:T(8,128)}, f32[32,8,512]{2,1,0:T(8,128)S(1)}, f32[24,512]{1,0:T(8,128)S(1)}, f32[2,2,32,512]{3,2,1,0:T(8,128)S(1)}) custom-call(s32[1,3]{1,0:T(1,128)S(1)} %copy-done.1, f32[1024,256]{1,0:T(8,128)} %bitcast.2.received, s32[1,1024]{1,0:T(1,128)S(1)} %broadcast_select_fusion.ids, ...), custom_call_target="tpu_custom_call" | custom-call | flops 1099511627776 | bytes 8388608 | tf_op jit(solution)/shard_map/picture/pallas_call | solution.py:432
  65.0 1.5 %collective-permute-done.6.corner_hbm = f32[2,8,256]{2,1,0:T(8,128)} collective-permute-done((f32[2,8,256]{2,1,0:T(8,128)}, f32[2,8,256]{2,1,0:T(8,128)}, u32[]{:S(2)}, u32[]{:S(2)}) %collective-permute-start.6) | collective-permute-done | bytes 16416 | tf_op jit(solution)/shard_map/ppermute | solution.py:604
  66.5 1.9 %add_rims.1 = f32[32,32,512]{2,1,0:T(8,128)} custom-call(f32[2,16,256]{2,1,0:T(8,128)} %collective-permute-done.4.rim_x_hbm, f32[2,16,256]{2,1,0:T(8,128)} %collective-permute-done.5.rim_y_hbm, f32[2,8,256]{2,1,0:T(8,128)} %collective-permute-done.6.corner_hbm, f32[32,8,512]{2,1,0:T(8,128)S(1)} %get-tuple-element.56.strip, ...), custom_call_target="tpu_custom_call", output_to_operand_aliasing={{}: (6, {})} | custom-call | flops 1048576 | bytes 2097152 | tf_op jit(solution)/shard_map/add_rims/pallas_call | solution.py:519
  (22 shorter events, 0.1 us)
Async XLA Ops:
  2.4 19.8 %copy-start.3 = (s32[1,3,1024]{2,0,1:T(1,128)S(1)}, s32[1,3,1024]{2,0,1:T(1,128)}, u32[]{:S(2)}) copy-start(s32[1,3,1024]{2,0,1:T(1,128)} %param.17) | copy-start | bytes 36868
  2.4 19.8 %copy-start = (f32[1,2,1024]{2,1,0:T(2,128)S(1)}, f32[1,2,1024]{2,1,0:T(2,128)}, u32[]{:S(2)}) copy-start(f32[1,2,1024]{2,1,0:T(2,128)} %param.18) | copy-start | bytes 24580
  2.4 20.6 %collective-permute-start.1 = (f32[2,32,512]{2,1,0:T(8,128)S(1)}, f32[2,32,512]{2,1,0:T(8,128)S(1)}, u32[]{:S(2)}, u32[]{:S(2)}) collective-permute-start(f32[2,32,512]{2,1,0:T(8,128)S(1)} %get-tuple-element.35.refs_6_.rest_1_), channel_id=1, source_target_pairs={{8,16},{16,8},{24,32},{32,24},{40,48},{48,40},{9,17},{17,9},{25,33... | collective-permute-start | bytes 393224 | tf_op jit(solution)/shard_map/ppermute | solution.py:27
  10.2 12.8 %collective-permute-start = (f32[2,32,512]{2,1,0:T(8,128)S(1)}, f32[2,32,512]{2,1,0:T(8,128)S(1)}, u32[]{:S(2)}, u32[]{:S(2)}) collective-permute-start(f32[2,32,512]{2,1,0:T(8,128)S(1)} %get-tuple-element.34.refs_5_.rest_0_), channel_id=1, source_target_pairs={{0,8},{8,0},{16,24},{24,16},{32,40},{40,32},{48,56},{56,48},{1,9},... | collective-permute-start | bytes 393224 | tf_op jit(solution)/shard_map/ppermute | solution.py:27
  10.3 12.7 %collective-permute-start.2 = (f32[2,32,512]{2,1,0:T(8,128)S(1)}, f32[2,32,512]{2,1,0:T(8,128)S(1)}, u32[]{:S(2)}, u32[]{:S(2)}) collective-permute-start(f32[2,32,512]{2,1,0:T(8,128)S(1)} %get-tuple-element.36.refs_7_.rest_2_), channel_id=1, source_target_pairs={{0,1},{1,0},{2,3},{3,2},{4,5},{5,4},{6,7},{7,6},{8,9},{9,8},{10,11... | collective-permute-start | bytes 393224 | tf_op jit(solution)/shard_map/ppermute | solution.py:27
  11.4 11.7 %collective-permute-start.3 = (f32[2,32,512]{2,1,0:T(8,128)S(1)}, f32[2,32,512]{2,1,0:T(8,128)S(1)}, u32[]{:S(2)}, u32[]{:S(2)}) collective-permute-start(f32[2,32,512]{2,1,0:T(8,128)S(1)} %get-tuple-element.37.refs_8_.rest_3_), channel_id=1, source_target_pairs={{1,2},{2,1},{3,4},{4,3},{5,6},{6,5},{9,10},{10,9},{11,12},{12,11},... | collective-permute-start | bytes 393224 | tf_op jit(solution)/shard_map/ppermute | solution.py:27
  13.9 37.6 %all-to-all-start = ((f32[32,32,256]{2,1,0:T(8,128)}), f32[32,32,256]{2,1,0:T(8,128)}, u32[]{:S(2)}, u32[]{:S(2)}) async-start(f32[32,32,256]{2,1,0:T(8,128)} %bitcast.1), calls=%async_computation | async-start | bytes 2097152 | tf_op jit(solution)/shard_map/all_to_all | solution.py:563
  23.0 18.2 %copy-start.4 = (s32[1,1,32]{2,1,0:T(1,128)S(1)}, s32[1,1,32]{2,1,0:T(1,128)}, u32[]{:S(2)}) copy-start(s32[1,1,32]{2,1,0:T(1,128)} %param.16) | copy-start | bytes 388
  23.1 18.4 %copy-start.2 = (s32[1,1,32,32]{3,2,1,0:T(8,128)S(1)}, s32[1,1,32,32]{3,2,1,0:T(8,128)}, u32[]{:S(2)}) copy-start(s32[1,1,32,32]{3,2,1,0:T(8,128)} %param.15) | copy-start | bytes 12292
  29.4 27.2 %collective-permute-start.10 = (f32[1,32,512]{2,1,0:T(8,128)S(1)}, f32[1,32,512]{2,1,0:T(8,128)S(1)}, u32[]{:S(2)}, u32[]{:S(2)}) collective-permute-start(f32[1,32,512]{2,1,0:T(8,128)S(1)} %get-tuple-element.51.rest_11_), channel_id=1, source_target_pairs={{1,2},{2,1},{3,4},{4,3},{5,6},{6,5},{9,10},{10,9},{11,12},{12,11},... | collective-permute-start | bytes 196616 | tf_op jit(solution)/shard_map/ppermute | solution.py:27
  32.9 24.6 %collective-permute-start.7 = (f32[1,32,512]{2,1,0:T(8,128)S(1)}, f32[1,32,512]{2,1,0:T(8,128)S(1)}, u32[]{:S(2)}, u32[]{:S(2)}) collective-permute-start(f32[1,32,512]{2,1,0:T(8,128)S(1)} %get-tuple-element.48.rest_8_), channel_id=1, source_target_pairs={{0,8},{8,0},{16,24},{24,16},{32,40},{40,32},{48,56},{56,48},{1,9},... | collective-permute-start | bytes 196616 | tf_op jit(solution)/shard_map/ppermute | solution.py:27
  33.6 25.3 %collective-permute-start.8 = (f32[1,32,512]{2,1,0:T(8,128)S(1)}, f32[1,32,512]{2,1,0:T(8,128)S(1)}, u32[]{:S(2)}, u32[]{:S(2)}) collective-permute-start(f32[1,32,512]{2,1,0:T(8,128)S(1)} %get-tuple-element.49.rest_9_), channel_id=1, source_target_pairs={{8,16},{16,8},{24,32},{32,24},{40,48},{48,40},{9,17},{17,9},{25,33... | collective-permute-start | bytes 196616 | tf_op jit(solution)/shard_map/ppermute | solution.py:27
  41.2 17.7 %collective-permute-start.9 = (f32[1,32,512]{2,1,0:T(8,128)S(1)}, f32[1,32,512]{2,1,0:T(8,128)S(1)}, u32[]{:S(2)}, u32[]{:S(2)}) collective-permute-start(f32[1,32,512]{2,1,0:T(8,128)S(1)} %get-tuple-element.50.rest_10_), channel_id=1, source_target_pairs={{0,1},{1,0},{2,3},{3,2},{4,5},{5,4},{6,7},{7,6},{8,9},{9,8},{10,11... | collective-permute-start | bytes 196616 | tf_op jit(solution)/shard_map/ppermute | solution.py:27
  47.9 11.1 %copy-start.1 = (s32[1,3]{1,0:T(1,128)S(1)}, s32[1,3]{1,0:T(1,128)}, u32[]{:S(2)}) copy-start(s32[1,3]{1,0:T(1,128)} %source.1) | copy-start | bytes 40
  53.8 12.7 %collective-permute-start.4 = (f32[2,16,256]{2,1,0:T(8,128)}, f32[2,16,256]{2,1,0:T(8,128)}, u32[]{:S(2)}, u32[]{:S(2)}) collective-permute-start(f32[2,16,256]{2,1,0:T(8,128)} %get-tuple-element.44), channel_id=1, source_target_pairs={{0,56},{8,0},{16,8},{24,16},{32,24},{40,32},{48,40},{56,48},{1,57}... | collective-permute-start | bytes 98312 | tf_op jit(solution)/shard_map/ppermute | solution.py:596
  56.6 9.9 %collective-permute-start.5 = (f32[2,16,256]{2,1,0:T(8,128)}, f32[2,16,256]{2,1,0:T(8,128)}, u32[]{:S(2)}, u32[]{:S(2)}) collective-permute-start(f32[2,16,256]{2,1,0:T(8,128)} %get-tuple-element.45), channel_id=1, source_target_pairs={{0,7},{1,0},{2,1},{3,2},{4,3},{5,4},{6,5},{7,6},{8,15},{9,8},{10,9... | collective-permute-start | bytes 98312 | tf_op jit(solution)/shard_map/ppermute | solution.py:596
  57.5 9.0 %collective-permute-start.6 = (f32[2,8,256]{2,1,0:T(8,128)}, f32[2,8,256]{2,1,0:T(8,128)}, u32[]{:S(2)}, u32[]{:S(2)}) collective-permute-start(f32[2,8,256]{2,1,0:T(8,128)} %get-tuple-element.46), channel_id=1, source_target_pairs={{0,63},{1,56},{2,57},{3,58},{4,59},{5,60},{6,61},{7,62},{8,7},{9,0... | collective-permute-start | bytes 49160 | tf_op jit(solution)/shard_map/ppermute | solution.py:604
